TPU v7x, 32 devices: a whole 2x2x4 slice. The times are simulated.
32 devices in a mesh: section: 2 (over x), dp: 16 (over z, y, core).
Axes of the slice: x: 2, y: 2, z: 4, core: 2. Of those that a mesh axis runs over, the one named last changes fastest.
Arguments:
- section_inputs: bfloat16 [2, 2048, 8192], P('section', 'dp'), may hold values from -6 to 6
- teacher_states: bfloat16 [2048, 8192], P('dp'), may hold values from -6 to 6
- confidence: int32 [2048], P('dp'), may hold values from 1 to 256
- gains: float32 [2, 8192], P('section'), may hold values from 0.1 to 1.9
- w_down: bfloat16 [2, 8192, 256], P('section', 'dp'), may hold values from -0.0625 to 0.0625
- w_up: bfloat16 [2, 8192, 256], P('section', 'dp'), may hold values from -0.375 to 0.375
Outputs:
- input_grads: bfloat16 [2, 2048, 8192], P('section', 'dp')
- grad_down: float32 [2, 8192, 256], P('section', 'dp')
- grad_up: float32 [2, 8192, 256], P('section', 'dp')
- grad_gain: float32 [2, 8192], P('section', 'dp')
All inputs are finite; a program needn't handle non-finite values.
Results may differ from a plain program's by a relative error of at most 0.013.
Values may be sent and summed in bfloat16 or wider, within the bound.
No kernel may reach another device: no remote copies, remote signals or barrier semaphores. Data moves between devices by JAX's collectives and lax.ppermute only.
A program may use at most 64 MiB of HBM per device.

v0:
```python
import jax
import jax.numpy as jnp
from jax import lax
from jax.sharding import PartitionSpec as P

MICRO = 4
ROWS = 32
TOK_DEV = 128


EPSILON = 1e-05


def shifted(block, axis, distance):
    devices = range(lax.axis_size(axis))
    route = [(i - distance, i) for i in devices if i - distance in devices]
    return lax.ppermute(block, axis, route)


def write_rows(buffer, fresh, first_row, active_step):
    previous = lax.dynamic_slice_in_dim(buffer, first_row, fresh.shape[0], 0)
    return lax.dynamic_update_slice_in_dim(
        buffer, jnp.where(active_step, fresh, previous), first_row, 0
    )


def local(section_inputs, teacher_states, confidence, gains, w_down, w_up):
    sections = lax.axis_size("section")
    section_index = lax.axis_index("section")
    layer_inputs = section_inputs[0]
    gain = gains[0]
    down_matrix, up_matrix = (
        lax.all_gather(w_down[0], "dp", axis=0, tiled=True),
        lax.all_gather(w_up[0], "dp", axis=0, tiled=True),
    )
    is_last = section_index == sections - 1
    rank_width = down_matrix.shape[1]
    width = down_matrix.shape[0]

    def run_step(step_index, carry):
        incoming, scaled_all, cot_all, pre_all, hidden_all, grads_all, gain_term = carry
        micro_index = step_index - (sections - 1 - section_index)
        active_step = (micro_index >= 0) & (micro_index < MICRO)
        first_row = jnp.clip(micro_index, 0, MICRO - 1) * ROWS
        rows_in = lax.dynamic_slice_in_dim(layer_inputs, first_row, ROWS, 0)
        teacher_rows = lax.dynamic_slice_in_dim(teacher_states, first_row, ROWS, 0)
        weight_rows = (
            lax.dynamic_slice_in_dim(confidence, first_row, ROWS, 0).astype(jnp.float32) / 256.0
        )
        values = rows_in.astype(jnp.float32)
        inverse = lax.rsqrt(jnp.mean(values * values, axis=-1, keepdims=True) + EPSILON)
        normed = values * inverse
        scaled = (normed * gain).astype(jnp.bfloat16)
        preact = jnp.dot(scaled, down_matrix, preferred_element_type=jnp.float32)
        hidden = jax.nn.silu(preact).astype(jnp.bfloat16)
        branch = jnp.einsum("tr,dr->td", hidden, up_matrix, preferred_element_type=jnp.float32)
        top_grad = (
            weight_rows[:, None] * (values + branch - teacher_rows.astype(jnp.float32))
        ).astype(jnp.bfloat16)
        cotangent = jnp.where(is_last, top_grad, incoming)
        hidden_grad = jnp.dot(cotangent, up_matrix, preferred_element_type=jnp.float32)
        sigmoid_val = jax.nn.sigmoid(preact)
        pre_grad = (hidden_grad * sigmoid_val * (1.0 + preact * (1.0 - sigmoid_val))).astype(
            jnp.bfloat16
        )
        normed_grad = jnp.einsum(
            "tr,dr->td", pre_grad, down_matrix, preferred_element_type=jnp.float32
        )
        scaled_grad = normed_grad * gain
        input_grad = cotangent.astype(jnp.float32) + inverse * (
            scaled_grad - normed * jnp.mean(scaled_grad * normed, axis=-1, keepdims=True)
        )
        input_grad = input_grad.astype(jnp.bfloat16)
        gain_term = gain_term + jnp.where(active_step, jnp.sum(normed_grad * normed, axis=0), 0.0)
        scaled_all = write_rows(scaled_all, scaled, first_row, active_step)
        cot_all = write_rows(cot_all, cotangent, first_row, active_step)
        pre_all = write_rows(pre_all, pre_grad, first_row, active_step)
        hidden_all = write_rows(hidden_all, hidden, first_row, active_step)
        grads_all = write_rows(grads_all, input_grad, first_row, active_step)
        outgoing = shifted(input_grad, "section", -1)
        return (outgoing, scaled_all, cot_all, pre_all, hidden_all, grads_all, gain_term)

    token_count = layer_inputs.shape[0]
    start_carry = (
        jnp.zeros((ROWS, width), jnp.bfloat16),
        jnp.zeros((token_count, width), jnp.bfloat16),
        jnp.zeros((token_count, width), jnp.bfloat16),
        jnp.zeros((token_count, rank_width), jnp.bfloat16),
        jnp.zeros((token_count, rank_width), jnp.bfloat16),
        jnp.zeros((token_count, width), jnp.bfloat16),
        jnp.zeros((width,), jnp.float32),
    )
    final_carry = lax.fori_loop(0, MICRO + sections - 1, run_step, start_carry)
    _, scaled_all, cot_all, pre_all, hidden_all, grads_all, gain_term = final_carry
    down_part = jnp.einsum("td,tr->dr", scaled_all, pre_all, preferred_element_type=jnp.float32)
    up_part = jnp.einsum("td,tr->dr", cot_all, hidden_all, preferred_element_type=jnp.float32)
    stacked = lax.psum_scatter(
        jnp.concatenate([down_part, up_part], axis=1).astype(jnp.bfloat16),
        "dp",
        scatter_dimension=0,
        tiled=True,
    ).astype(jnp.float32)
    gain_sum = lax.psum_scatter(gain_term, "dp", scatter_dimension=0, tiled=True)
    stacked = stacked / TOK_DEV
    grad_down = stacked[:, :rank_width]
    grad_up = stacked[:, rank_width:]
    return (grads_all[None], grad_down[None], grad_up[None], (gain_sum / TOK_DEV)[None])


def solution(mesh):
    in_specs = (
        P("section", "dp", None),
        P("dp", None),
        P("dp"),
        P("section", None),
        P("section", "dp", None),
        P("section", "dp", None),
    )
    out_specs = (
        P("section", "dp", None),
        P("section", "dp", None),
        P("section", "dp", None),
        P("section", "dp"),
    )
    return jax.shard_map(local, mesh=mesh, in_specs=in_specs, out_specs=out_specs, check_vma=False)
```

profile of v0, /device:TPU:0, one launch (start us, length us, event | category | flops | bytes accessed | tf_op | source)
XLA Modules:
  0.0 383.3 jit_solution(15505079731274536532)
XLA Ops:
  7.2 0.7 all-gather.5.cloned.1.call-update
  7.9 0.7 all-gather.7.cloned.1.call-update
  8.7 54.7 %all-gather.5.cloned.1.call-done = bf16[1,8192,256]{2,1,0:T(8,128)(2,1)} async-done(((bf16[1,512,256]{2,1,0:T(8,128)(2,1)}), bf16[1,8192,256]{2,1,0:T(8,128)(2,1)}) %all-gather.5.cloned.1.call-update) | async-done | bytes 4194320 | tf_op jit(solution)/shard_map/all_gather | solution.py:33
  63.5 51.2 %all-gather.7.cloned.1.call-done = bf16[1,8192,256]{2,1,0:T(8,128)(2,1)} async-done(((bf16[1,512,256]{2,1,0:T(8,128)(2,1)}), bf16[1,8192,256]{2,1,0:T(8,128)(2,1)}) %all-gather.7.cloned.1.call-update) | async-done | bytes 4194320 | tf_op jit(solution)/shard_map/all_gather | solution.py:34
  114.8 1.5 broadcast.67.clone.1
  116.3 1.5 broadcast.67.clone
  117.8 1.5 broadcast.67
  119.3 135.4 %while.28 = (s32[]{:T(128)}, bf16[32,8192]{1,0:T(8,128)(2,1)S(1)}, bf16[128,8192]{1,0:T(8,128)(2,1)}, bf16[128,8192]{1,0:T(8,128)(2,1)}, bf16[128,256]{1,0:T(8,1...) while((s32[]{:T(128)}, bf16[32,8192]{1,0:T(8,128)(2,1)S(1)}, ...), condition=%wide.region_4.5_spmd.clone, body=%wide.region_0.4_spmd.clone.sunk | while | flops 546234496 | bytes 63868848 | solution.py:93
  119.4 0.2 fusion.47
  119.7 3.2 select_dynamic-update-slice_fusion.8
  123.1 2.4 fusion.48
  125.6 0.8 select_dynamic-update-slice_fusion.9
  126.4 1.3 copy-done
  127.7 1.5 fusion.49
  129.2 3.0 select_dynamic-update-slice_fusion.10
  132.2 1.3 collective-permute-start
  133.5 14.7 %collective-permute-done = bf16[32,8192]{1,0:T(8,128)(2,1)S(1)} collective-permute-done((bf16[32,8192]{1,0:T(8,128)(2,1)S(1)}, bf16[32,8192]{1,0:T(8,128)(2,1)S(1)}, u32[]{:S(2)}, u32[]{:S(2)}) %collective-permute-start) | collective-permute-done | bytes 524320 | tf_op jit(solution)/shard_map/while/body/eval_jaxpr/ppermute | solution.py:17
  148.3 0.2 fusion.47
  148.5 3.2 select_dynamic-update-slice_fusion.8
  152.0 2.4 fusion.48
  154.4 0.8 select_dynamic-update-slice_fusion.9
  155.2 1.3 copy-done
  156.6 1.5 fusion.49
  158.1 3.0 select_dynamic-update-slice_fusion.10
  161.1 1.3 collective-permute-start
  162.4 13.8 %collective-permute-done = bf16[32,8192]{1,0:T(8,128)(2,1)S(1)} collective-permute-done((bf16[32,8192]{1,0:T(8,128)(2,1)S(1)}, bf16[32,8192]{1,0:T(8,128)(2,1)S(1)}, u32[]{:S(2)}, u32[]{:S(2)}) %collective-permute-start) | collective-permute-done | bytes 524320 | tf_op jit(solution)/shard_map/while/body/eval_jaxpr/ppermute | solution.py:17
  176.3 0.2 fusion.47
  176.6 3.2 select_dynamic-update-slice_fusion.8
  180.0 2.4 fusion.48
  182.4 0.8 select_dynamic-update-slice_fusion.9
  183.3 1.3 copy-done
  184.6 1.5 fusion.49
  186.1 3.0 select_dynamic-update-slice_fusion.10
  189.1 1.3 collective-permute-start
  190.4 12.9 %collective-permute-done = bf16[32,8192]{1,0:T(8,128)(2,1)S(1)} collective-permute-done((bf16[32,8192]{1,0:T(8,128)(2,1)S(1)}, bf16[32,8192]{1,0:T(8,128)(2,1)S(1)}, u32[]{:S(2)}, u32[]{:S(2)}) %collective-permute-start) | collective-permute-done | bytes 524320 | tf_op jit(solution)/shard_map/while/body/eval_jaxpr/ppermute | solution.py:17
  203.4 0.2 fusion.47
  203.7 3.2 select_dynamic-update-slice_fusion.8
  207.1 2.4 fusion.48
  209.5 0.8 select_dynamic-update-slice_fusion.9
  210.4 1.3 copy-done
  211.7 1.5 fusion.49
  213.2 3.0 select_dynamic-update-slice_fusion.10
  216.2 1.3 collective-permute-start
  217.5 12.0 %collective-permute-done = bf16[32,8192]{1,0:T(8,128)(2,1)S(1)} collective-permute-done((bf16[32,8192]{1,0:T(8,128)(2,1)S(1)}, bf16[32,8192]{1,0:T(8,128)(2,1)S(1)}, u32[]{:S(2)}, u32[]{:S(2)}) %collective-permute-start) | collective-permute-done | bytes 524320 | tf_op jit(solution)/shard_map/while/body/eval_jaxpr/ppermute | solution.py:17
  229.6 0.2 fusion.47
  229.8 3.2 select_dynamic-update-slice_fusion.8
  233.3 2.4 fusion.48
  235.7 0.8 select_dynamic-update-slice_fusion.9
  236.5 1.3 copy-done
  237.9 1.5 fusion.49
  239.3 3.0 select_dynamic-update-slice_fusion.10
  242.4 1.3 collective-permute-start
  243.7 11.1 %collective-permute-done = bf16[32,8192]{1,0:T(8,128)(2,1)S(1)} collective-permute-done((bf16[32,8192]{1,0:T(8,128)(2,1)S(1)}, bf16[32,8192]{1,0:T(8,128)(2,1)S(1)}, u32[]{:S(2)}, u32[]{:S(2)}) %collective-permute-start) | collective-permute-done | bytes 524320 | tf_op jit(solution)/shard_map/while/body/eval_jaxpr/ppermute | solution.py:17
  254.8 5.0 %convolution_convert_fusion.1 = bf16[8192,256]{0,1:T(8,128)(2,1)} fusion(bf16[128,8192]{1,0:T(8,128)(2,1)} %get-tuple-element.369, bf16[128,256]{1,0:T(8,128)(2,1)S(1)} %get-tuple-element.370), kind=kOutput, calls=%fused_computation.36 | convolution fusion | flops 538968064 | bytes 6356992 | tf_op jit(solution)/shard_map/td,tr->dr/dot_general | solution.py:95
  259.7 3.2 convolution_convert_fusion
  263.0 7.7 %pad_maximum_fusion = bf16[8192,512]{0,1:T(8,128)(2,1)} fusion(bf16[8192,256]{0,1:T(8,128)(2,1)} %convolution_convert_fusion, bf16[8192,256]{0,1:T(8,128)(2,1)} %convolution_convert_fusion.1), kind=kLoop, calls=%fused_computation.37 | loop fusion | flops 16777216 | bytes 16777216 | tf_op jit(solution)/shard_map/concatenate | solution.py:98
  270.7 0.6 copy-done.6
  271.3 0.6 dynamic-slice
  272.5 59.9 %all-reduce = f32[8192]{0:T(1024)S(1)} all-reduce(f32[8192]{0:T(1024)S(1)} %get-tuple-element.373), channel_id=5, replica_groups=mesh['section'=2,'dp'=16] {'dp'}, use_global_device_ids=true, to_apply=%region_6.7.clone | all-reduce | flops 8192 | bytes 65536
  332.5 0.7 dynamic-slice_multiply_fusion
  333.1 40.4 %reduce-scatter.2.cloned.1.call-done = bf16[512,512]{0,1:T(8,128)(2,1)} async-done(((bf16[8192,512]{0,1:T(8,128)(2,1)}), bf16[512,512]{0,1:T(8,128)(2,1)}) %reduce-scatter.2.cloned.1.call-update) | async-done | bytes 524304 | tf_op jit(solution)/shard_map/reduce_scatter | solution.py:97
  373.5 1.2 convert_multiply_fusion.3
  374.8 1.0 copy.13
  375.8 1.0 copy.12
  (53 shorter events, 1.8 us)
Async XLA Ops:
  7.2 56.3 %all-gather.5.cloned.1.call-start = ((), (), s32[]{:S(2)}) async-start(), calls=%async_computation.2 | async-start | bytes 4456448 | tf_op jit(solution)/shard_map/all_gather | solution.py:33
  7.9 106.8 %all-gather.7.cloned.1.call-start = ((), (), s32[]{:S(2)}) async-start(), calls=%async_computation.3 | async-start | bytes 4456448 | tf_op jit(solution)/shard_map/all_gather | solution.py:34
  8.6 364.9 %reduce-scatter.2.cloned.1.call-start = ((), (), s32[]{:S(2)}) async-start(), calls=%async_computation.1 | async-start | bytes 8912896 | tf_op jit(solution)/shard_map/reduce_scatter | solution.py:97
  116.3 3.0 copy-start.2
  116.3 3.0 copy-start.4
  116.3 3.0 copy-start.5
  119.7 3.5 copy-start.1
  125.6 2.2 copy-start
  132.2 16.0 %collective-permute-start = (bf16[32,8192]{1,0:T(8,128)(2,1)S(1)}, bf16[32,8192]{1,0:T(8,128)(2,1)S(1)}, u32[]{:S(2)}, u32[]{:S(2)}) collective-permute-start(bf16[32,8192]{1,0:T(8,128)(2,1)S(1)} %get-tuple-element.590), channel_id=1, source_target_pairs={{16,0},{17,1},{18,2},{19,3},{20,4},{21,5},{22,6},{23,7},{24,8},{25... | collective-permute-start | bytes 1572872 | tf_op jit(solution)/shard_map/while/body/eval_jaxpr/ppermute | solution.py:17
  148.5 3.5 copy-start.1
  154.4 2.2 copy-start
  161.1 15.2 %collective-permute-start = (bf16[32,8192]{1,0:T(8,128)(2,1)S(1)}, bf16[32,8192]{1,0:T(8,128)(2,1)S(1)}, u32[]{:S(2)}, u32[]{:S(2)}) collective-permute-start(bf16[32,8192]{1,0:T(8,128)(2,1)S(1)} %get-tuple-element.590), channel_id=1, source_target_pairs={{16,0},{17,1},{18,2},{19,3},{20,4},{21,5},{22,6},{23,7},{24,8},{25... | collective-permute-start | bytes 1572872 | tf_op jit(solution)/shard_map/while/body/eval_jaxpr/ppermute | solution.py:17
  176.5 3.5 copy-start.1
  182.4 2.2 copy-start
  189.1 14.2 %collective-permute-start = (bf16[32,8192]{1,0:T(8,128)(2,1)S(1)}, bf16[32,8192]{1,0:T(8,128)(2,1)S(1)}, u32[]{:S(2)}, u32[]{:S(2)}) collective-permute-start(bf16[32,8192]{1,0:T(8,128)(2,1)S(1)} %get-tuple-element.590), channel_id=1, source_target_pairs={{16,0},{17,1},{18,2},{19,3},{20,4},{21,5},{22,6},{23,7},{24,8},{25... | collective-permute-start | bytes 1572872 | tf_op jit(solution)/shard_map/while/body/eval_jaxpr/ppermute | solution.py:17
  203.6 3.5 copy-start.1
  209.5 2.2 copy-start
  216.2 13.3 %collective-permute-start = (bf16[32,8192]{1,0:T(8,128)(2,1)S(1)}, bf16[32,8192]{1,0:T(8,128)(2,1)S(1)}, u32[]{:S(2)}, u32[]{:S(2)}) collective-permute-start(bf16[32,8192]{1,0:T(8,128)(2,1)S(1)} %get-tuple-element.590), channel_id=1, source_target_pairs={{16,0},{17,1},{18,2},{19,3},{20,4},{21,5},{22,6},{23,7},{24,8},{25... | collective-permute-start | bytes 1572872 | tf_op jit(solution)/shard_map/while/body/eval_jaxpr/ppermute | solution.py:17
  229.8 3.5 copy-start.1
  235.7 2.2 copy-start
  242.4 12.4 %collective-permute-start = (bf16[32,8192]{1,0:T(8,128)(2,1)S(1)}, bf16[32,8192]{1,0:T(8,128)(2,1)S(1)}, u32[]{:S(2)}, u32[]{:S(2)}) collective-permute-start(bf16[32,8192]{1,0:T(8,128)(2,1)S(1)} %get-tuple-element.590), channel_id=1, source_target_pairs={{16,0},{17,1},{18,2},{19,3},{20,4},{21,5},{22,6},{23,7},{24,8},{25... | collective-permute-start | bytes 1572872 | tf_op jit(solution)/shard_map/while/body/eval_jaxpr/ppermute | solution.py:17
  254.8 5.0 %copy-start.3 = (bf16[128,8192]{1,0:T(8,128)(2,1)S(1)}, bf16[128,8192]{1,0:T(8,128)(2,1)}, u32[]{:S(2)}) copy-start(bf16[128,8192]{1,0:T(8,128)(2,1)} %get-tuple-element.371) | copy-start | bytes 6291460
  270.7 0.7 copy-start.6
Sparse Core Ops, SparseCore 0:
  10.2 53.2 all-gather.4
  65.6 49.0 all-gather.6
  270.8 102.6 reduce-scatter.1
where the time goes:
time: 384 us; the launch traced here: 383 us
  waiting for transfers between devices  212 us (55%)
  blocking collectives  59.9 us (16%)
  matrix products  47.9 us (12%)
  other arithmetic  26.3 us (7%)
  local copies, waits for them, and re-layouts  15.7 us (4%)
  between operations  14.5 us (4%)
  starting transfers between devices  6.52 us (2%)
    ppermute x5, waiting for transfers between devices, shifted(): return lax.ppermute(block, axis, route)  64.5 us
    unnamed x1, blocking collectives  59.9 us
    all_gather x1, waiting for transfers between devices, local(): lax.all_gather(w_down[0], 'dp', axis=0, tiled=True)  54.7 us
    all_gather x1, waiting for transfers between devices, local(): lax.all_gather(w_up[0], 'dp', axis=0, tiled=True)  51.2 us
    reduce_scatter x1, waiting for transfers between devices, local(): lax.psum_scatter(jnp.concatenate([down_part, up_part], axis=1).astype(jnp...  40.4 us
    dot_general x5, matrix products, run_step(): preact = jnp.dot(scaled, down_matrix, preferred_element_type=jnp.float32)  16.2 us
    dynamic_update_slice x5, other arithmetic, write_rows(): lax.dynamic_update_slice_in_dim(buffer, jnp.where(active_step, fresh, pre...  15.1 us
    dot_general x5, matrix products, run_step(): jnp.einsum('tr,dr->td', hidden, up_matrix, preferred_element_type=jnp.flo...  12 us
  transfers between devices with their start and end apart: 8, of which 8 were waited for; matrix products, arithmetic and copies ran while one was open for 0% of the time, Pallas kernels for 0%

commit v1 on v0

v1 whole, which is shorter than its diff:
```python
import jax
import jax.numpy as jnp
import numpy as np
from jax import lax
from jax.experimental import pallas as pl
from jax.experimental.pallas import tpu as pltpu
from jax.sharding import PartitionSpec as P

Z_CHIPS = 4
CORES = 2
EPSILON = 1e-05
F32 = jnp.float32
BF16 = jnp.bfloat16


def ring_of_chips(chips):
    rows = chips // Z_CHIPS
    cycle = []
    for z in range(Z_CHIPS):
        ys = range(1, rows) if z % 2 == 0 else range(rows - 1, 0, -1)
        cycle += [z * rows + y for y in ys]
    return cycle + [z * rows for z in range(Z_CHIPS - 1, -1, -1)]


class Routes:
    def __init__(self, devices):
        self.ring = ring_of_chips(devices // CORES)
        n = self.n = len(self.ring)
        self.half = n // 2
        self.partner = [(i, i ^ 1) for i in range(devices)]
        self.onward_by_core = [
            [(self.ring[i] * CORES + c, self.ring[(i + 1 - 2 * c) % n] * CORES + c) for i in range(n)]
            for c in range(CORES)
        ]
        self.onward = self.onward_by_core[0] + self.onward_by_core[1]
        table = np.zeros((devices, n), np.int32)
        for i, chip in enumerate(self.ring):
            for c in range(CORES):
                sign = 1 - 2 * c
                steps = [0] + [-k for k in range(1, self.half)] + list(range(1, self.half)) + [self.half]
                table[chip * CORES + c] = [self.ring[(i + sign * s) % n] for s in steps]
        self.table = table

    def behind(self, k):
        return k

    def ahead(self, k):
        return self.half - 1 + k

    @property
    def opposite(self):
        return self.n - 1


def arrange_kernel(ids, x_ref, t_ref, gain_ref, inv_ref, x_out, t_out, scaled_out, gain_out):
    x = x_ref[...]
    x_out[0] = x
    t_out[0] = t_ref[...]
    gain = gain_ref[...]
    gain_out[0] = gain
    scaled_out[0] = ((x.astype(F32) * inv_ref[...]) * gain).astype(BF16)


def arrange(ids, x, teacher, gain, inverse):
    tokens, width = x.shape
    n = ids.shape[0]
    block = width // n
    return pl.pallas_call(
        arrange_kernel,
        grid_spec=pltpu.PrefetchScalarGridSpec(
            num_scalar_prefetch=1,
            grid=(n,),
            in_specs=[
                pl.BlockSpec((tokens, block), lambda j, ids: (0, ids[j])),
                pl.BlockSpec((tokens, block), lambda j, ids: (0, ids[j])),
                pl.BlockSpec((1, block), lambda j, ids: (0, ids[j])),
                pl.BlockSpec((tokens, 1), lambda j, ids: (0, 0)),
            ],
            out_specs=[
                pl.BlockSpec((1, tokens, block), lambda j, ids: (j, 0, 0)),
                pl.BlockSpec((1, tokens, block), lambda j, ids: (j, 0, 0)),
                pl.BlockSpec((1, tokens, block), lambda j, ids: (j, 0, 0)),
                pl.BlockSpec((1, 1, block), lambda j, ids: (j, 0, 0)),
            ],
        ),
        out_shape=[
            jax.ShapeDtypeStruct((n, tokens, block), BF16),
            jax.ShapeDtypeStruct((n, tokens, block), BF16),
            jax.ShapeDtypeStruct((n, tokens, block), BF16),
            jax.ShapeDtypeStruct((n, 1, block), F32),
        ],
        cost_estimate=pl.CostEstimate(flops=4 * tokens * width, bytes_accessed=10 * tokens * width, transcendentals=0),
        name="arrange",
    )(ids, x, teacher, gain, inverse)


def finish_kernel(ids, cot_ref, x_ref, down_ref, gain_ref, pre_ref, inv_ref, mean_ref, out_ref):
    grad = lax.dot_general(pre_ref[...], down_ref[0], (((1,), (1,)), ((), ())), preferred_element_type=F32)
    normed = x_ref[0].astype(F32) * inv_ref[...]
    out = cot_ref[0].astype(F32) + inv_ref[...] * (grad * gain_ref[0] - normed * mean_ref[...])
    out_ref[...] = out.astype(BF16)


def finish(ids, cot, x, down, gain, pre_grad, inverse, mean):
    n, tokens, block = cot.shape
    rank = pre_grad.shape[1]
    return pl.pallas_call(
        finish_kernel,
        grid_spec=pltpu.PrefetchScalarGridSpec(
            num_scalar_prefetch=1,
            grid=(n,),
            in_specs=[
                pl.BlockSpec((1, tokens, block), lambda j, ids: (j, 0, 0)),
                pl.BlockSpec((1, tokens, block), lambda j, ids: (j, 0, 0)),
                pl.BlockSpec((1, block, rank), lambda j, ids: (j, 0, 0)),
                pl.BlockSpec((1, 1, block), lambda j, ids: (j, 0, 0)),
                pl.BlockSpec((tokens, rank), lambda j, ids: (0, 0)),
                pl.BlockSpec((tokens, 1), lambda j, ids: (0, 0)),
                pl.BlockSpec((tokens, 1), lambda j, ids: (0, 0)),
            ],
            out_specs=pl.BlockSpec((tokens, block), lambda j, ids: (0, ids[j])),
        ),
        out_shape=jax.ShapeDtypeStruct((tokens, n * block), BF16),
        cost_estimate=pl.CostEstimate(
            flops=2 * tokens * n * block * rank, bytes_accessed=6 * tokens * n * block, transcendentals=0
        ),
        name="finish",
    )(ids, cot, x, down, gain, pre_grad, inverse, mean)


def gathered(routes, down, up, core):
    def send(block, route):
        return lax.ppermute(block, "dp", route)

    first = core == 0

    def of_chip(block):
        other = send(block, routes.partner)
        return jnp.where(first, jnp.concatenate([block, other]), jnp.concatenate([other, block]))

    downs, ups = {}, {}
    travelling = {}
    for slots, block, key in ((downs, down, "down"), (ups, up, "up")):
        travelling[key] = slots[0] = of_chip(block)
    for k in range(1, routes.half):
        for slots, key in ((downs, "down"), (ups, "up")):
            travelling[key] = slots[routes.behind(k)] = send(travelling[key], routes.onward)
            slots[routes.ahead(k)] = send(travelling[key], routes.partner)
    mine = send(jnp.where(first, travelling["down"], travelling["up"]), routes.onward)
    other = send(mine, routes.partner)
    downs[routes.opposite] = jnp.where(first, mine, other)
    ups[routes.opposite] = jnp.where(first, other, mine)
    return downs, ups


def scattered(routes, parts, core, far_core):
    def send(block, route):
        return lax.ppermute(block, "dp", route)

    opposite = parts[routes.opposite]
    to_far = [(a, b) for a, b in routes.partner if b % CORES == far_core]
    total = opposite.astype(F32) + send(opposite, to_far).astype(F32)
    total = send(total.astype(BF16), routes.onward_by_core[far_core]).astype(F32)
    for k in range(routes.half - 1, 0, -1):
        other = send(parts[routes.behind(k)], routes.partner).astype(F32)
        total = total + (other + parts[routes.ahead(k)].astype(F32))
        total = send(total.astype(BF16), routes.onward).astype(F32)
    total = total + parts[0].astype(F32)
    rows = total.shape[0] // CORES
    low, high = total[:rows], total[rows:]
    first = core == 0
    other = send(jnp.where(first, high, low).astype(BF16), routes.partner)
    return jnp.where(first, low, high) + other.astype(F32)


def local(section_inputs, teacher_states, confidence, gains, w_down, w_up):
    sections = lax.axis_size("section")
    devices = lax.axis_size("dp")
    section_index = lax.axis_index("section")
    dp_index = lax.axis_index("dp")
    core = dp_index % CORES
    is_last = section_index == sections - 1
    routes = Routes(devices)
    x = section_inputs[0]
    tokens, width = x.shape
    slots = range(routes.n)

    downs, ups = gathered(routes, w_down[0], w_up[0], core)

    ids = lax.dynamic_slice_in_dim(jnp.asarray(routes.table), dp_index, 1, 0)[0]
    values = x.astype(F32)
    inverse = lax.rsqrt(jnp.mean(values * values, axis=-1, keepdims=True) + EPSILON)
    x_slots, teacher_slots, scaled_slots, gain_slots = arrange(ids, x, teacher_states, gains, inverse)
    weight_rows = (confidence.astype(F32) / 256.0)[:, None]

    order = [0]
    for k in range(1, routes.half):
        order += [routes.behind(k), routes.ahead(k)]
    order.append(routes.opposite)
    preact = 0.0
    for j in order:
        preact = preact + jnp.dot(scaled_slots[j], downs[j], preferred_element_type=F32)
    hidden = jax.nn.silu(preact).astype(BF16)
    sigmoid_val = jax.nn.sigmoid(preact)
    slope = sigmoid_val * (1.0 + preact * (1.0 - sigmoid_val))

    def top_of(j):
        branch = jnp.einsum("tr,dr->td", hidden, ups[j], preferred_element_type=F32)
        return (weight_rows * (x_slots[j].astype(F32) + branch - teacher_slots[j].astype(F32))).astype(BF16)

    tops = {j: top_of(j) for j in order}
    leaving = order[::-1]

    def pre_grad_of(cots):
        hidden_grad = 0.0
        for j in leaving:
            hidden_grad = hidden_grad + jnp.dot(cots[j], ups[j], preferred_element_type=F32)
        pre_grad = (hidden_grad * slope).astype(BF16)
        mean = jnp.sum(pre_grad.astype(F32) * preact, axis=-1, keepdims=True) / width
        return pre_grad, mean

    def input_grad_of(j, cots, pre_grad, mean):
        grad = jnp.einsum("tr,dr->td", pre_grad, downs[j], preferred_element_type=F32)
        normed = x_slots[j].astype(F32) * inverse
        return (
            cots[j].astype(F32) + inverse * (grad * gain_slots[j] - normed * mean)
        ).astype(BF16)

    cots = tops
    back = [(s, s - 1) for s in range(1, sections)]
    for _ in range(sections - 1):
        pre_grad, mean = pre_grad_of(cots)
        arrived = {}
        for j in leaving:
            arrived[j] = lax.ppermute(input_grad_of(j, cots, pre_grad, mean), "section", back)
        cots = {j: jnp.where(is_last, tops[j], arrived[j]) for j in slots}

    def product(a, b):
        return lax.dot_general(a, b, (((0,), (0,)), ((), ())), preferred_element_type=F32).astype(BF16)

    up_sum = scattered(routes, {j: product(cots[j], hidden) for j in leaving}, core, 1)
    pre_grad, mean = pre_grad_of(cots)
    down_sum = scattered(routes, {j: product(scaled_slots[j], pre_grad) for j in leaving}, core, 0)
    input_grads = finish(
        ids,
        jnp.stack([cots[j] for j in slots]),
        x_slots,
        jnp.stack([downs[j] for j in slots]),
        gain_slots,
        pre_grad,
        inverse,
        mean,
    )
    grad_down = down_sum / tokens
    grad_up = up_sum / tokens
    own_gain = lax.dynamic_slice_in_dim(gains[0], dp_index * w_down.shape[1], w_down.shape[1], 0)
    grad_gain = jnp.sum(grad_down * w_down[0].astype(F32), axis=1) / own_gain
    return input_grads[None], grad_down[None], grad_up[None], grad_gain[None]


def solution(mesh):
    in_specs = (
        P("section", "dp", None),
        P("dp", None),
        P("dp"),
        P("section", None),
        P("section", "dp", None),
        P("section", "dp", None),
    )
    out_specs = (
        P("section", "dp", None),
        P("section", "dp", None),
        P("section", "dp", None),
        P("section", "dp"),
    )
    return jax.shard_map(local, mesh=mesh, in_specs=in_specs, out_specs=out_specs, check_vma=False)
```

time: 384 us -> 197 us (0.51)
  waiting for transfers between devices: 212 us -> 87.8 us
  blocking collectives: 59.9 us -> 0 us
  starting transfers between devices: 6.52 us -> 48.1 us
  matrix products: 47.9 us -> 26.3 us
  Pallas kernels: 0 us -> 16.8 us
  other arithmetic: 26.3 us -> 10.6 us
  between operations: 14.5 us -> 1.66 us
  local copies, waits for them, and re-layouts: 15.7 us -> 4.75 us
    all_gather x2 -> x0, waiting for transfers between devices: 106 us -> none  [the longest x1 54.7 us: local(): lax.all_gather(w_down[0], 'dp', axis=0, tiled=True)]
    unnamed x1 -> x0, blocking collectives: 59.9 us -> none
    ppermute x5 -> x42, starting transfers between devices: 6.4 us -> 48.1 us  [the longest x34 37.6 us: send(): return lax.ppermute(block, 'dp', route)]
    reduce_scatter x1 -> x0, waiting for transfers between devices: 40.4 us -> none  [local(): lax.psum_scatter(jnp.concatenate([down_part, up_part], axis=1).astype(jnp...]
    ppermute x5 -> x42, waiting for transfers between devices: 64.5 us -> 87.8 us  [the longest x34 51.2 us: send(): return lax.ppermute(block, 'dp', route)]
    dot_general x22 -> x56, matrix products: 47.9 us -> 26.3 us  [the longest x16 15.2 us: product(): lax.dot_general(a, b, (((0,), (0,)), ((), ())), preferred_element_type=F32)]
    pallas_call x0 -> x2, Pallas kernels: none -> 16.8 us  [the longest x1 8.92 us: finish(): pl.pallas_call(finish_kernel, grid_spec=pltpu.PrefetchScalarGridSpec(num_...]
    dynamic_update_slice x5 -> x0, other arithmetic: 15.1 us -> none  [write_rows(): lax.dynamic_update_slice_in_dim(buffer, jnp.where(active_step, fresh, pre...]
  transfers between devices with their start and end apart: 8 -> 42, of which waited for: 8 -> 19; matrix products, arithmetic and copies ran while one was open for 0% -> 16% of each run, Pallas kernels for 0% -> 9%
where the time goes in v1:
time: 197 us; the launch traced here: 196 us
  waiting for transfers between devices  87.8 us (45%)
  starting transfers between devices  48.1 us (24%)
  matrix products  26.3 us (13%)
  Pallas kernels  16.8 us (9%)
  other arithmetic  10.6 us (5%)
  local copies, waits for them, and re-layouts  4.75 us (2%)
    ppermute x34, waiting for transfers between devices, send(): return lax.ppermute(block, 'dp', route)  51.2 us
    ppermute x34, starting transfers between devices, send(): return lax.ppermute(block, 'dp', route)  37.6 us
    ppermute x8, waiting for transfers between devices, local(): lax.ppermute(input_grad_of(j, cots, pre_grad, mean), 'section', back)  36.6 us
    dot_general x16, matrix products, product(): lax.dot_general(a, b, (((0,), (0,)), ((), ())), preferred_element_type=F32)  15.2 us
    ppermute x8, starting transfers between devices, local(): lax.ppermute(input_grad_of(j, cots, pre_grad, mean), 'section', back)  10.5 us
    pallas_call x1, Pallas kernels, finish(): pl.pallas_call(finish_kernel, grid_spec=pltpu.PrefetchScalarGridSpec(num_...  8.92 us
    pallas_call x1, Pallas kernels, arrange(): pl.pallas_call(arrange_kernel, grid_spec=pltpu.PrefetchScalarGridSpec(num...  7.92 us
    dot_general x16, matrix products, pre_grad_of(): jnp.dot(cots[j], ups[j], preferred_element_type=F32)  3.95 us
  transfers between devices with their start and end apart: 42, of which 19 were waited for; matrix products, arithmetic and copies ran while one was open for 16% of the time, Pallas kernels for 9%

profile of v1, /device:TPU:0, one launch (start us, length us, event | category | flops | bytes accessed | tf_op | source)
XLA Modules:
  0.0 196.0 jit_solution(14988177333674193511)
XLA Ops:
  1.2 2.1 %multiply_reduce_fusion = f32[128]{0:T(128)S(1)} fusion(bf16[1,128,8192]{2,1,0:T(8,128)(2,1)} %param.7), kind=kLoop, calls=%fused_computation | loop fusion | flops 3145600 | bytes 2097664 | tf_op jit(solution)/shard_map/reduce_sum | solution.py:192
  4.1 1.2 dynamic-slice_bitcast_fusion.ids
  5.3 7.9 %arrange.1 = (bf16[8,128,1024]{2,1,0:T(8,128)(2,1)}, bf16[8,128,1024]{2,1,0:T(8,128)(2,1)}, bf16[8,128,1024]{2,1,0:T(8,128)(2,1)}, f32[8,1,1024]{2,1,0:T(1,128)}) custom-call(s32[8]{0:T(128)} %dynamic-slice_bitcast_fusion.ids, bf16[128,8192]{1,0:T(8,128)(2,1)} %bitcast.250, bf16[128,8192]{1,0:T(8,128)(2,1)} %t_ref.1, f32[1,8192]{1,0:T(1,128)} %gain_ref.1, ...), custom_call_target="tpu_custom_call" | custom-call | flops 4194304 | bytes 10485760 | tf_op jit(solution)/shard_map/arrange/pallas_call | solution.py:68
  13.5 3.0 %collective-permute-start.1 = (bf16[1024,256]{1,0:T(8,128)(2,1)S(1)}, bf16[1024,256]{1,0:T(8,128)(2,1)S(1)}, u32[]{:S(2)}, u32[]{:S(2)}) collective-permute-start(bf16[1024,256]{1,0:T(8,128)(2,1)S(1)} %maximum_select_fusion), channel_id=1, source_target_pairs={{2,6},{6,10},{10,14},{14,12},{12,8},{8,4},{4,0},{0,2},{3,1},{7,3},... | collective-permute-start | bytes 1572872 | tf_op jit(solution)/shard_map/ppermute | solution.py:133
  16.7 1.6 collective-permute-start.8
  19.2 4.5 %collective-permute-done.1 = bf16[1024,256]{1,0:T(8,128)(2,1)S(1)} collective-permute-done((bf16[1024,256]{1,0:T(8,128)(2,1)S(1)}, bf16[1024,256]{1,0:T(8,128)(2,1)S(1)}, u32[]{:S(2)}, u32[]{:S(2)}) %collective-permute-start.1) | collective-permute-done | bytes 524320 | tf_op jit(solution)/shard_map/ppermute | solution.py:133
  23.7 2.0 %collective-permute-start.3 = (bf16[1024,256]{1,0:T(8,128)(2,1)S(1)}, bf16[1024,256]{1,0:T(8,128)(2,1)S(1)}, u32[]{:S(2)}, u32[]{:S(2)}) collective-permute-start(bf16[1024,256]{1,0:T(8,128)(2,1)S(1)} %collective-permute-done.1), channel_id=1, source_target_pairs={{2,6},{6,10},{10,14},{14,12},{12,8},{8,4},{4,0},{0,2},{3,1},{7,3},... | collective-permute-start | bytes 1572872 | tf_op jit(solution)/shard_map/ppermute | solution.py:133
  25.6 3.7 %collective-permute-done.8 = bf16[1024,256]{1,0:T(8,128)(2,1)S(1)} collective-permute-done((bf16[1024,256]{1,0:T(8,128)(2,1)S(1)}, bf16[1024,256]{1,0:T(8,128)(2,1)S(1)}, u32[]{:S(2)}, u32[]{:S(2)}) %collective-permute-start.8) | collective-permute-done | bytes 524320 | tf_op jit(solution)/shard_map/ppermute | solution.py:133
  29.3 2.0 %collective-permute-start.9 = (bf16[1024,256]{1,0:T(8,128)(2,1)S(1)}, bf16[1024,256]{1,0:T(8,128)(2,1)S(1)}, u32[]{:S(2)}, u32[]{:S(2)}) collective-permute-start(bf16[1024,256]{1,0:T(8,128)(2,1)S(1)} %collective-permute-done.8), channel_id=1, source_target_pairs={{2,6},{6,10},{10,14},{14,12},{12,8},{8,4},{4,0},{0,2},{3,1},{7,3},... | collective-permute-start | bytes 1572872 | tf_op jit(solution)/shard_map/ppermute | solution.py:133
  31.8 3.1 %collective-permute-done.3 = bf16[1024,256]{1,0:T(8,128)(2,1)S(1)} collective-permute-done((bf16[1024,256]{1,0:T(8,128)(2,1)S(1)}, bf16[1024,256]{1,0:T(8,128)(2,1)S(1)}, u32[]{:S(2)}, u32[]{:S(2)}) %collective-permute-start.3) | collective-permute-done | bytes 524320 | tf_op jit(solution)/shard_map/ppermute | solution.py:133
  34.9 2.0 %collective-permute-start.5 = (bf16[1024,256]{1,0:T(8,128)(2,1)S(1)}, bf16[1024,256]{1,0:T(8,128)(2,1)S(1)}, u32[]{:S(2)}, u32[]{:S(2)}) collective-permute-start(bf16[1024,256]{1,0:T(8,128)(2,1)S(1)} %collective-permute-done.3), channel_id=1, source_target_pairs={{2,6},{6,10},{10,14},{14,12},{12,8},{8,4},{4,0},{0,2},{3,1},{7,3},... | collective-permute-start | bytes 1572872 | tf_op jit(solution)/shard_map/ppermute | solution.py:133
  36.9 3.7 %collective-permute-done.9 = bf16[1024,256]{1,0:T(8,128)(2,1)S(1)} collective-permute-done((bf16[1024,256]{1,0:T(8,128)(2,1)S(1)}, bf16[1024,256]{1,0:T(8,128)(2,1)S(1)}, u32[]{:S(2)}, u32[]{:S(2)}) %collective-permute-start.9) | collective-permute-done | bytes 524320 | tf_op jit(solution)/shard_map/ppermute | solution.py:133
  40.5 2.0 %collective-permute-start.10 = (bf16[1024,256]{1,0:T(8,128)(2,1)S(1)}, bf16[1024,256]{1,0:T(8,128)(2,1)S(1)}, u32[]{:S(2)}, u32[]{:S(2)}) collective-permute-start(bf16[1024,256]{1,0:T(8,128)(2,1)S(1)} %collective-permute-done.9), channel_id=1, source_target_pairs={{2,6},{6,10},{10,14},{14,12},{12,8},{8,4},{4,0},{0,2},{3,1},{7,3},... | collective-permute-start | bytes 1572872 | tf_op jit(solution)/shard_map/ppermute | solution.py:133
  43.1 3.0 %collective-permute-done.5 = bf16[1024,256]{1,0:T(8,128)(2,1)S(1)} collective-permute-done((bf16[1024,256]{1,0:T(8,128)(2,1)S(1)}, bf16[1024,256]{1,0:T(8,128)(2,1)S(1)}, u32[]{:S(2)}, u32[]{:S(2)}) %collective-permute-start.5) | collective-permute-done | bytes 524320 | tf_op jit(solution)/shard_map/ppermute | solution.py:133
  46.1 5.6 %collective-permute-done.10 = bf16[1024,256]{1,0:T(8,128)(2,1)S(1)} collective-permute-done((bf16[1024,256]{1,0:T(8,128)(2,1)S(1)}, bf16[1024,256]{1,0:T(8,128)(2,1)S(1)}, u32[]{:S(2)}, u32[]{:S(2)}) %collective-permute-start.10) | collective-permute-done | bytes 524320 | tf_op jit(solution)/shard_map/ppermute | solution.py:133
  51.8 2.0 %collective-permute-start.11 = (bf16[1024,256]{1,0:T(8,128)(2,1)S(1)}, bf16[1024,256]{1,0:T(8,128)(2,1)S(1)}, u32[]{:S(2)}, u32[]{:S(2)}) collective-permute-start(bf16[1024,256]{1,0:T(8,128)(2,1)S(1)} %broadcast_select_fusion.2), channel_id=1, source_target_pairs={{2,6},{6,10},{10,14},{14,12},{12,8},{8,4},{4,0},{0,2},{3,1},{7,3},... | collective-permute-start | bytes 1572872 | tf_op jit(solution)/shard_map/ppermute | solution.py:133
  54.5 6.5 %collective-permute-done.11 = bf16[1024,256]{1,0:T(8,128)(2,1)S(1)} collective-permute-done((bf16[1024,256]{1,0:T(8,128)(2,1)S(1)}, bf16[1024,256]{1,0:T(8,128)(2,1)S(1)}, u32[]{:S(2)}, u32[]{:S(2)}) %collective-permute-start.11) | collective-permute-done | bytes 524320 | tf_op jit(solution)/shard_map/ppermute | solution.py:133
  61.6 1.3 collective-permute-done.12
  70.1 1.3 collective-permute-start.16
  71.4 1.3 collective-permute-start.23
  73.1 1.3 collective-permute-start.22
  74.7 1.3 collective-permute-start.21
  76.4 1.3 collective-permute-start.17
  78.7 2.5 %collective-permute-done.16 = bf16[128,1024]{1,0:T(8,128)(2,1)S(1)} collective-permute-done((bf16[128,1024]{1,0:T(8,128)(2,1)S(1)}, bf16[128,1024]{1,0:T(8,128)(2,1)S(1)}, u32[]{:S(2)}, u32[]{:S(2)}) %collective-permute-start.16) | collective-permute-done | bytes 262176 | tf_op jit(solution)/shard_map/ppermute | solution.py:235
  81.2 1.3 collective-permute-start.18
  82.6 21.1 %collective-permute-done.17 = bf16[128,1024]{1,0:T(8,128)(2,1)S(1)} collective-permute-done((bf16[128,1024]{1,0:T(8,128)(2,1)S(1)}, bf16[128,1024]{1,0:T(8,128)(2,1)S(1)}, u32[]{:S(2)}, u32[]{:S(2)}) %collective-permute-start.17) | collective-permute-done | bytes 262176 | tf_op jit(solution)/shard_map/ppermute | solution.py:235
  103.6 1.3 collective-permute-start.19
  105.0 4.2 %collective-permute-done.18 = bf16[128,1024]{1,0:T(8,128)(2,1)S(1)} collective-permute-done((bf16[128,1024]{1,0:T(8,128)(2,1)S(1)}, bf16[128,1024]{1,0:T(8,128)(2,1)S(1)}, u32[]{:S(2)}, u32[]{:S(2)}) %collective-permute-start.18) | collective-permute-done | bytes 262176 | tf_op jit(solution)/shard_map/ppermute | solution.py:235
  109.3 1.5 collective-permute-start.20
  110.8 4.1 %collective-permute-done.19 = bf16[128,1024]{1,0:T(8,128)(2,1)S(1)} collective-permute-done((bf16[128,1024]{1,0:T(8,128)(2,1)S(1)}, bf16[128,1024]{1,0:T(8,128)(2,1)S(1)}, u32[]{:S(2)}, u32[]{:S(2)}) %collective-permute-start.19) | collective-permute-done | bytes 262176 | tf_op jit(solution)/shard_map/ppermute | solution.py:235
  114.9 4.7 %collective-permute-done.20 = bf16[128,1024]{1,0:T(8,128)(2,1)S(1)} collective-permute-done((bf16[128,1024]{1,0:T(8,128)(2,1)S(1)}, bf16[128,1024]{1,0:T(8,128)(2,1)S(1)}, u32[]{:S(2)}, u32[]{:S(2)}) %collective-permute-start.20) | collective-permute-done | bytes 262176 | tf_op jit(solution)/shard_map/ppermute | solution.py:235
  120.4 1.2 convolution_convert_fusion.7
  121.8 1.2 convolution_convert_fusion.6
  124.9 1.1 convolution_convert_fusion.10
  126.0 1.1 convolution_convert_fusion.12
  127.1 1.3 collective-permute-start.24
  128.4 1.1 convolution_convert_fusion.14
  129.5 1.2 collective-permute-start.26
  130.7 2.7 %collective-permute-start.33 = (bf16[1024,256]{1,0:T(8,128)(2,1)}, bf16[1024,256]{1,0:T(8,128)(2,1)}, u32[]{:S(2)}, u32[]{:S(2)}) collective-permute-start(bf16[1024,256]{1,0:T(8,128)(2,1)} %convolution_convert_fusion.7), channel_id=1, source_target_pairs={{0,1},{2,3},{4,5},{6,7},{8,9},{10,11},{12,13},{14,15},{16,17},{18,... | collective-permute-start | bytes 1572872 | tf_op jit(solution)/shard_map/ppermute | solution.py:158
  133.4 1.1 convolution_convert_fusion.2
  135.0 3.9 %collective-permute-start.25 = (bf16[1024,256]{1,0:T(8,128)(2,1)S(1)}, bf16[1024,256]{1,0:T(8,128)(2,1)}, u32[]{:S(2)}, u32[]{:S(2)}) collective-permute-start(bf16[1024,256]{1,0:T(8,128)(2,1)S(1)} %add_convert_fusion.7), channel_id=1, source_target_pairs={{2,6},{6,10},{10,14},{14,12},{12,8},{8,4},{4,0},{0,2},{18,22},{22,... | collective-permute-start | bytes 1572872 | tf_op jit(solution)/shard_map/ppermute | solution.py:158
  140.1 1.3 fusion.7
  141.5 2.1 %add_convert_fusion.3 = bf16[1024,256]{1,0:T(8,128)(2,1)} fusion(bf16[1024,256]{1,0:T(8,128)(2,1)} %collective-permute-done.33, bf16[1024,256]{1,0:T(8,128)(2,1)} %convolution_convert_fusion.7), kind=kLoop, calls=%fused_computation.126 | loop fusion | flops 1048576 | bytes 1572864 | tf_op jit(solution)/shard_map/convert_element_type | solution.py:163
  143.6 1.4 collective-permute-start.34
  145.0 1.1 collective-permute-done.25
  146.1 1.2 add_convert_fusion.6
  147.3 2.0 %collective-permute-start.27 = (bf16[1024,256]{1,0:T(8,128)(2,1)S(1)}, bf16[1024,256]{1,0:T(8,128)(2,1)S(1)}, u32[]{:S(2)}, u32[]{:S(2)}) collective-permute-start(bf16[1024,256]{1,0:T(8,128)(2,1)S(1)} %add_convert_fusion.6), channel_id=1, source_target_pairs={{2,6},{6,10},{10,14},{14,12},{12,8},{8,4},{4,0},{0,2},{3,1},{7,3},... | collective-permute-start | bytes 1572872 | tf_op jit(solution)/shard_map/ppermute | solution.py:158
  149.4 8.9 %finish.1 = bf16[128,8192]{1,0:T(8,128)(2,1)} custom-call(s32[8]{0:T(128)} %dynamic-slice_bitcast_fusion.ids, bf16[8,128,1024]{2,1,0:T(8,128)(2,1)} %copy-done.5, bf16[8,128,1024]{2,1,0:T(8,128)(2,1)} %get-tuple-element.8.x_ref, bf16[8,1024,256]{2,1,0:T(8,128)(2,1)} %copy-done.4, f32[8,1,1024]{2,1,0:T(1,128)} %get-tuple-element.11.gain_ref, ...), custom_call_target="tpu_custom_call" | custom-call | flops 536870912 | bytes 6291456 | tf_op jit(solution)/shard_map/finish/pallas_call | solution.py:107
  159.2 1.5 add_convert_fusion.2
  160.8 1.6 collective-permute-start.36
  162.6 1.6 collective-permute-start.29
  164.2 1.3 fusion.5
  165.5 4.5 %collective-permute-done.36 = bf16[1024,256]{1,0:T(8,128)(2,1)S(1)} collective-permute-done((bf16[1024,256]{1,0:T(8,128)(2,1)S(1)}, bf16[1024,256]{1,0:T(8,128)(2,1)S(1)}, u32[]{:S(2)}, u32[]{:S(2)}) %collective-permute-start.36) | collective-permute-done | bytes 524320 | tf_op jit(solution)/shard_map/ppermute | solution.py:158
  170.4 1.6 collective-permute-start.38
  172.0 3.6 %collective-permute-done.29 = bf16[1024,256]{1,0:T(8,128)(2,1)S(1)} collective-permute-done((bf16[1024,256]{1,0:T(8,128)(2,1)S(1)}, bf16[1024,256]{1,0:T(8,128)(2,1)S(1)}, u32[]{:S(2)}, u32[]{:S(2)}) %collective-permute-start.29) | collective-permute-done | bytes 524320 | tf_op jit(solution)/shard_map/ppermute | solution.py:158
  175.8 1.6 collective-permute-start.31
  177.4 1.3 fusion.4
  178.7 2.5 %collective-permute-done.38 = bf16[1024,256]{1,0:T(8,128)(2,1)S(1)} collective-permute-done((bf16[1024,256]{1,0:T(8,128)(2,1)S(1)}, bf16[1024,256]{1,0:T(8,128)(2,1)S(1)}, u32[]{:S(2)}, u32[]{:S(2)}) %collective-permute-start.38) | collective-permute-done | bytes 524320 | tf_op jit(solution)/shard_map/ppermute | solution.py:158
  181.2 1.4 add_convert_fusion
  182.7 1.6 collective-permute-start.40
  184.3 2.6 %collective-permute-done.31 = bf16[1024,256]{1,0:T(8,128)(2,1)S(1)} collective-permute-done((bf16[1024,256]{1,0:T(8,128)(2,1)S(1)}, bf16[1024,256]{1,0:T(8,128)(2,1)S(1)}, u32[]{:S(2)}, u32[]{:S(2)}) %collective-permute-start.31) | collective-permute-done | bytes 524320 | tf_op jit(solution)/shard_map/ppermute | solution.py:158
  187.1 5.4 %collective-permute-done.40 = bf16[1024,256]{1,0:T(8,128)(2,1)S(1)} collective-permute-done((bf16[1024,256]{1,0:T(8,128)(2,1)S(1)}, bf16[1024,256]{1,0:T(8,128)(2,1)S(1)}, u32[]{:S(2)}, u32[]{:S(2)}) %collective-permute-start.40) | collective-permute-done | bytes 524320 | tf_op jit(solution)/shard_map/ppermute | solution.py:158
  193.0 0.9 multiply_reduce_fusion.1
  193.9 1.3 dynamic-slice_divide_fusion
  (156 shorter events, 21.9 us)
Async XLA Ops:
  0.6 15.8 %collective-permute-start.7 = (bf16[512,256]{1,0:T(8,128)(2,1)}, bf16[512,256]{1,0:T(8,128)(2,1)S(1)}, u32[]{:S(2)}, u32[]{:S(2)}) collective-permute-start(bf16[512,256]{1,0:T(8,128)(2,1)} %bitcast.255), channel_id=1, source_target_pairs={{0,1},{1,0},{2,3},{3,2},{4,5},{5,4},{6,7},{7,6},{8,9},{9,8},{10,11... | collective-permute-start | bytes 786440 | tf_op jit(solution)/shard_map/ppermute | solution.py:133
  1.1 12.1 %collective-permute-start = (bf16[512,256]{1,0:T(8,128)(2,1)}, bf16[512,256]{1,0:T(8,128)(2,1)S(1)}, u32[]{:S(2)}, u32[]{:S(2)}) collective-permute-start(bf16[512,256]{1,0:T(8,128)(2,1)} %bitcast.251), channel_id=1, source_target_pairs={{0,1},{1,0},{2,3},{3,2},{4,5},{5,4},{6,7},{7,6},{8,9},{9,8},{10,11... | collective-permute-start | bytes 786440 | tf_op jit(solution)/shard_map/ppermute | solution.py:133
  5.3 8.0 %copy-start.12 = (bf16[1,512,256]{2,1,0:T(8,128)(2,1)S(1)}, bf16[1,512,256]{2,1,0:T(8,128)(2,1)}, u32[]{:S(2)}) copy-start(bf16[1,512,256]{2,1,0:T(8,128)(2,1)} %param.11) | copy-start | bytes 786436
  5.3 11.2 %copy-start.17 = (bf16[1,512,256]{2,1,0:T(8,128)(2,1)S(1)}, bf16[1,512,256]{2,1,0:T(8,128)(2,1)}, u32[]{:S(2)}) copy-start(bf16[1,512,256]{2,1,0:T(8,128)(2,1)} %param.12) | copy-start | bytes 786436
  13.2 5.1 %copy-start.18 = (s32[128]{0:T(128)S(1)}, s32[128]{0:T(128)}, u32[]{:S(2)}) copy-start(s32[128]{0:T(128)} %param.9) | copy-start | bytes 1540
  13.2 18.1 %copy-start.1 = (bf16[8,128,1024]{2,1,0:T(8,128)(2,1)S(1)}, bf16[8,128,1024]{2,1,0:T(8,128)(2,1)}, u32[]{:S(2)}) copy-start(bf16[8,128,1024]{2,1,0:T(8,128)(2,1)} %get-tuple-element.9) | copy-start | bytes 6291460
  13.5 10.2 %collective-permute-start.1 = (bf16[1024,256]{1,0:T(8,128)(2,1)S(1)}, bf16[1024,256]{1,0:T(8,128)(2,1)S(1)}, u32[]{:S(2)}, u32[]{:S(2)}) collective-permute-start(bf16[1024,256]{1,0:T(8,128)(2,1)S(1)} %maximum_select_fusion), channel_id=1, source_target_pairs={{2,6},{6,10},{10,14},{14,12},{12,8},{8,4},{4,0},{0,2},{3,1},{7,3},... | collective-permute-start | bytes 1572872 | tf_op jit(solution)/shard_map/ppermute | solution.py:133
  16.7 12.6 %collective-permute-start.8 = (bf16[1024,256]{1,0:T(8,128)(2,1)S(1)}, bf16[1024,256]{1,0:T(8,128)(2,1)S(1)}, u32[]{:S(2)}, u32[]{:S(2)}) collective-permute-start(bf16[1024,256]{1,0:T(8,128)(2,1)S(1)} %maximum_select_fusion.1), channel_id=1, source_target_pairs={{2,6},{6,10},{10,14},{14,12},{12,8},{8,4},{4,0},{0,2},{3,1},{7,3},... | collective-permute-start | bytes 1572872 | tf_op jit(solution)/shard_map/ppermute | solution.py:133
  23.7 11.2 %collective-permute-start.3 = (bf16[1024,256]{1,0:T(8,128)(2,1)S(1)}, bf16[1024,256]{1,0:T(8,128)(2,1)S(1)}, u32[]{:S(2)}, u32[]{:S(2)}) collective-permute-start(bf16[1024,256]{1,0:T(8,128)(2,1)S(1)} %collective-permute-done.1), channel_id=1, source_target_pairs={{2,6},{6,10},{10,14},{14,12},{12,8},{8,4},{4,0},{0,2},{3,1},{7,3},... | collective-permute-start | bytes 1572872 | tf_op jit(solution)/shard_map/ppermute | solution.py:133
  25.6 17.1 %collective-permute-start.2 = (bf16[1024,256]{1,0:T(8,128)(2,1)S(1)}, bf16[1024,256]{1,0:T(8,128)(2,1)S(1)}, u32[]{:S(2)}, u32[]{:S(2)}) collective-permute-start(bf16[1024,256]{1,0:T(8,128)(2,1)S(1)} %collective-permute-done.1), channel_id=1, source_target_pairs={{0,1},{1,0},{2,3},{3,2},{4,5},{5,4},{6,7},{7,6},{8,9},{9,8},{10,11... | collective-permute-start | bytes 1572872 | tf_op jit(solution)/shard_map/ppermute | solution.py:133
  29.3 36.9 %collective-permute-start.15 = (bf16[1024,256]{1,0:T(8,128)(2,1)S(1)}, bf16[1024,256]{1,0:T(8,128)(2,1)S(1)}, u32[]{:S(2)}, u32[]{:S(2)}) collective-permute-start(bf16[1024,256]{1,0:T(8,128)(2,1)S(1)} %collective-permute-done.8), channel_id=1, source_target_pairs={{0,1},{1,0},{2,3},{3,2},{4,5},{5,4},{6,7},{7,6},{8,9},{9,8},{10,11... | collective-permute-start | bytes 1572872 | tf_op jit(solution)/shard_map/ppermute | solution.py:133
  29.3 11.2 %collective-permute-start.9 = (bf16[1024,256]{1,0:T(8,128)(2,1)S(1)}, bf16[1024,256]{1,0:T(8,128)(2,1)S(1)}, u32[]{:S(2)}, u32[]{:S(2)}) collective-permute-start(bf16[1024,256]{1,0:T(8,128)(2,1)S(1)} %collective-permute-done.8), channel_id=1, source_target_pairs={{2,6},{6,10},{10,14},{14,12},{12,8},{8,4},{4,0},{0,2},{3,1},{7,3},... | collective-permute-start | bytes 1572872 | tf_op jit(solution)/shard_map/ppermute | solution.py:133
  34.9 11.2 %collective-permute-start.5 = (bf16[1024,256]{1,0:T(8,128)(2,1)S(1)}, bf16[1024,256]{1,0:T(8,128)(2,1)S(1)}, u32[]{:S(2)}, u32[]{:S(2)}) collective-permute-start(bf16[1024,256]{1,0:T(8,128)(2,1)S(1)} %collective-permute-done.3), channel_id=1, source_target_pairs={{2,6},{6,10},{10,14},{14,12},{12,8},{8,4},{4,0},{0,2},{3,1},{7,3},... | collective-permute-start | bytes 1572872 | tf_op jit(solution)/shard_map/ppermute | solution.py:133
  36.9 17.1 %collective-permute-start.4 = (bf16[1024,256]{1,0:T(8,128)(2,1)S(1)}, bf16[1024,256]{1,0:T(8,128)(2,1)S(1)}, u32[]{:S(2)}, u32[]{:S(2)}) collective-permute-start(bf16[1024,256]{1,0:T(8,128)(2,1)S(1)} %collective-permute-done.3), channel_id=1, source_target_pairs={{0,1},{1,0},{2,3},{3,2},{4,5},{5,4},{6,7},{7,6},{8,9},{9,8},{10,11... | collective-permute-start | bytes 1572872 | tf_op jit(solution)/shard_map/ppermute | solution.py:133
  40.5 11.2 %collective-permute-start.10 = (bf16[1024,256]{1,0:T(8,128)(2,1)S(1)}, bf16[1024,256]{1,0:T(8,128)(2,1)S(1)}, u32[]{:S(2)}, u32[]{:S(2)}) collective-permute-start(bf16[1024,256]{1,0:T(8,128)(2,1)S(1)} %collective-permute-done.9), channel_id=1, source_target_pairs={{2,6},{6,10},{10,14},{14,12},{12,8},{8,4},{4,0},{0,2},{3,1},{7,3},... | collective-permute-start | bytes 1572872 | tf_op jit(solution)/shard_map/ppermute | solution.py:133
  42.8 24.6 %collective-permute-start.14 = (bf16[1024,256]{1,0:T(8,128)(2,1)S(1)}, bf16[1024,256]{1,0:T(8,128)(2,1)S(1)}, u32[]{:S(2)}, u32[]{:S(2)}) collective-permute-start(bf16[1024,256]{1,0:T(8,128)(2,1)S(1)} %collective-permute-done.9), channel_id=1, source_target_pairs={{0,1},{1,0},{2,3},{3,2},{4,5},{5,4},{6,7},{7,6},{8,9},{9,8},{10,11... | collective-permute-start | bytes 1572872 | tf_op jit(solution)/shard_map/ppermute | solution.py:133
  51.8 9.2 %collective-permute-start.11 = (bf16[1024,256]{1,0:T(8,128)(2,1)S(1)}, bf16[1024,256]{1,0:T(8,128)(2,1)S(1)}, u32[]{:S(2)}, u32[]{:S(2)}) collective-permute-start(bf16[1024,256]{1,0:T(8,128)(2,1)S(1)} %broadcast_select_fusion.2), channel_id=1, source_target_pairs={{2,6},{6,10},{10,14},{14,12},{12,8},{8,4},{4,0},{0,2},{3,1},{7,3},... | collective-permute-start | bytes 1572872 | tf_op jit(solution)/shard_map/ppermute | solution.py:133
  53.8 7.7 %collective-permute-start.6 = (bf16[1024,256]{1,0:T(8,128)(2,1)S(1)}, bf16[1024,256]{1,0:T(8,128)(2,1)S(1)}, u32[]{:S(2)}, u32[]{:S(2)}) collective-permute-start(bf16[1024,256]{1,0:T(8,128)(2,1)S(1)} %collective-permute-done.5), channel_id=1, source_target_pairs={{0,1},{1,0},{2,3},{3,2},{4,5},{5,4},{6,7},{7,6},{8,9},{9,8},{10,11... | collective-permute-start | bytes 1572872 | tf_op jit(solution)/shard_map/ppermute | solution.py:133
  53.9 14.6 %collective-permute-start.13 = (bf16[1024,256]{1,0:T(8,128)(2,1)S(1)}, bf16[1024,256]{1,0:T(8,128)(2,1)S(1)}, u32[]{:S(2)}, u32[]{:S(2)}) collective-permute-start(bf16[1024,256]{1,0:T(8,128)(2,1)S(1)} %collective-permute-done.10), channel_id=1, source_target_pairs={{0,1},{1,0},{2,3},{3,2},{4,5},{5,4},{6,7},{7,6},{8,9},{9,8},{10,11... | collective-permute-start | bytes 1572872 | tf_op jit(solution)/shard_map/ppermute | solution.py:133
  61.1 1.9 collective-permute-start.12
  61.6 2.0 %copy-start = (bf16[8,128,1024]{2,1,0:T(8,128)(2,1)S(1)}, bf16[8,128,1024]{2,1,0:T(8,128)(2,1)}, u32[]{:S(2)}) copy-start(bf16[8,128,1024]{2,1,0:T(8,128)(2,1)} %get-tuple-element.8.x_ref) | copy-start | bytes 6291460
  61.6 2.2 %copy-start.16 = (bf16[8,128,1024]{2,1,0:T(8,128)(2,1)S(1)}, bf16[8,128,1024]{2,1,0:T(8,128)(2,1)}, u32[]{:S(2)}) copy-start(bf16[8,128,1024]{2,1,0:T(8,128)(2,1)} %get-tuple-element.10) | copy-start | bytes 6291460
  63.1 2.0 %copy-start.4 = (bf16[8,1024,256]{2,1,0:T(8,128)(2,1)}, bf16[8,1024,256]{2,1,0:T(8,128)(2,1)S(1)}, u32[]{:S(2)}) copy-start(bf16[8,1024,256]{2,1,0:T(8,128)(2,1)S(1)} %get-tuple-element.12.down_ref) | copy-start | bytes 12582916
  70.1 11.0 %collective-permute-start.16 = (bf16[128,1024]{1,0:T(8,128)(2,1)S(1)}, bf16[128,1024]{1,0:T(8,128)(2,1)S(1)}, u32[]{:S(2)}, u32[]{:S(2)}) collective-permute-start(bf16[128,1024]{1,0:T(8,128)(2,1)S(1)} %fusion.56), channel_id=1, source_target_pairs={{16,0},{17,1},{18,2},{19,3},{20,4},{21,5},{22,6},{23,7},{24,8},{25... | collective-permute-start | bytes 786440 | tf_op jit(solution)/shard_map/ppermute | solution.py:235
  71.4 48.6 %collective-permute-start.23 = (bf16[128,1024]{1,0:T(8,128)(2,1)S(1)}, bf16[128,1024]{1,0:T(8,128)(2,1)S(1)}, u32[]{:S(2)}, u32[]{:S(2)}) collective-permute-start(bf16[128,1024]{1,0:T(8,128)(2,1)S(1)} %fusion.63), channel_id=1, source_target_pairs={{16,0},{17,1},{18,2},{19,3},{20,4},{21,5},{22,6},{23,7},{24,8},{25... | collective-permute-start | bytes 786440 | tf_op jit(solution)/shard_map/ppermute | solution.py:235
  73.1 46.8 %collective-permute-start.22 = (bf16[128,1024]{1,0:T(8,128)(2,1)S(1)}, bf16[128,1024]{1,0:T(8,128)(2,1)S(1)}, u32[]{:S(2)}, u32[]{:S(2)}) collective-permute-start(bf16[128,1024]{1,0:T(8,128)(2,1)S(1)} %fusion.62), channel_id=1, source_target_pairs={{16,0},{17,1},{18,2},{19,3},{20,4},{21,5},{22,6},{23,7},{24,8},{25... | collective-permute-start | bytes 786440 | tf_op jit(solution)/shard_map/ppermute | solution.py:235
  74.7 45.1 %collective-permute-start.21 = (bf16[128,1024]{1,0:T(8,128)(2,1)S(1)}, bf16[128,1024]{1,0:T(8,128)(2,1)S(1)}, u32[]{:S(2)}, u32[]{:S(2)}) collective-permute-start(bf16[128,1024]{1,0:T(8,128)(2,1)S(1)} %fusion.61), channel_id=1, source_target_pairs={{16,0},{17,1},{18,2},{19,3},{20,4},{21,5},{22,6},{23,7},{24,8},{25... | collective-permute-start | bytes 786440 | tf_op jit(solution)/shard_map/ppermute | solution.py:235
  76.4 27.3 %collective-permute-start.17 = (bf16[128,1024]{1,0:T(8,128)(2,1)S(1)}, bf16[128,1024]{1,0:T(8,128)(2,1)S(1)}, u32[]{:S(2)}, u32[]{:S(2)}) collective-permute-start(bf16[128,1024]{1,0:T(8,128)(2,1)S(1)} %fusion.57), channel_id=1, source_target_pairs={{16,0},{17,1},{18,2},{19,3},{20,4},{21,5},{22,6},{23,7},{24,8},{25... | collective-permute-start | bytes 786440 | tf_op jit(solution)/shard_map/ppermute | solution.py:235
  81.2 28.1 %collective-permute-start.18 = (bf16[128,1024]{1,0:T(8,128)(2,1)S(1)}, bf16[128,1024]{1,0:T(8,128)(2,1)S(1)}, u32[]{:S(2)}, u32[]{:S(2)}) collective-permute-start(bf16[128,1024]{1,0:T(8,128)(2,1)S(1)} %fusion.58), channel_id=1, source_target_pairs={{16,0},{17,1},{18,2},{19,3},{20,4},{21,5},{22,6},{23,7},{24,8},{25... | collective-permute-start | bytes 786440 | tf_op jit(solution)/shard_map/ppermute | solution.py:235
  82.5 39.0 %copy-start.6 = (bf16[128,1024]{1,0:T(8,128)(2,1)}, bf16[128,1024]{1,0:T(8,128)(2,1)S(1)}, u32[]{:S(2)}) copy-start(bf16[128,1024]{1,0:T(8,128)(2,1)S(1)} %get-tuple-element.29) | copy-start | bytes 786436
  103.6 11.2 %collective-permute-start.19 = (bf16[128,1024]{1,0:T(8,128)(2,1)S(1)}, bf16[128,1024]{1,0:T(8,128)(2,1)S(1)}, u32[]{:S(2)}, u32[]{:S(2)}) collective-permute-start(bf16[128,1024]{1,0:T(8,128)(2,1)S(1)} %fusion.59), channel_id=1, source_target_pairs={{16,0},{17,1},{18,2},{19,3},{20,4},{21,5},{22,6},{23,7},{24,8},{25... | collective-permute-start | bytes 786440 | tf_op jit(solution)/shard_map/ppermute | solution.py:235
  109.3 10.4 %collective-permute-start.20 = (bf16[128,1024]{1,0:T(8,128)(2,1)S(1)}, bf16[128,1024]{1,0:T(8,128)(2,1)S(1)}, u32[]{:S(2)}, u32[]{:S(2)}) collective-permute-start(bf16[128,1024]{1,0:T(8,128)(2,1)S(1)} %fusion.60), channel_id=1, source_target_pairs={{16,0},{17,1},{18,2},{19,3},{20,4},{21,5},{22,6},{23,7},{24,8},{25... | collective-permute-start | bytes 786440 | tf_op jit(solution)/shard_map/ppermute | solution.py:235
  119.8 3.7 %copy-start.8 = (bf16[128,1024]{1,0:T(8,128)(2,1)}, bf16[128,1024]{1,0:T(8,128)(2,1)S(1)}, u32[]{:S(2)}) copy-start(bf16[128,1024]{1,0:T(8,128)(2,1)S(1)} %get-tuple-element.21) | copy-start | bytes 786436
  119.9 3.8 %copy-start.10 = (bf16[128,1024]{1,0:T(8,128)(2,1)}, bf16[128,1024]{1,0:T(8,128)(2,1)S(1)}, u32[]{:S(2)}) copy-start(bf16[128,1024]{1,0:T(8,128)(2,1)S(1)} %get-tuple-element.19) | copy-start | bytes 786436
  120.0 4.0 %copy-start.14 = (bf16[128,1024]{1,0:T(8,128)(2,1)}, bf16[128,1024]{1,0:T(8,128)(2,1)S(1)}, u32[]{:S(2)}) copy-start(bf16[128,1024]{1,0:T(8,128)(2,1)S(1)} %get-tuple-element.17) | copy-start | bytes 786436
  120.1 3.1 %copy-start.5 = (bf16[8,128,1024]{2,1,0:T(8,128)(2,1)}, bf16[8,128,1024]{2,1,0:T(8,128)(2,1)S(1)}, u32[]{:S(2)}) copy-start(bf16[8,128,1024]{2,1,0:T(8,128)(2,1)S(1)} %get-tuple-element.14.cot_ref) | copy-start | bytes 6291460
  124.6 15.5 %copy-start.2 = (bf16[128,256]{1,0:T(8,128)(2,1)}, bf16[128,256]{1,0:T(8,128)(2,1)S(1)}, u32[]{:S(2)}) copy-start(bf16[128,256]{1,0:T(8,128)(2,1)S(1)} %get-tuple-element.47.pre_ref) | copy-start | bytes 196612
  127.1 7.7 %collective-permute-start.24 = (bf16[1024,256]{1,0:T(8,128)(2,1)S(1)}, bf16[1024,256]{1,0:T(8,128)(2,1)S(1)}, u32[]{:S(2)}, u32[]{:S(2)}) collective-permute-start(bf16[1024,256]{1,0:T(8,128)(2,1)S(1)} %convolution_convert_fusion.15), channel_id=1, source_target_pairs={{1,0},{3,2},{5,4},{7,6},{9,8},{11,10},{13,12},{15,14},{17,16},{19,... | collective-permute-start | bytes 1572872 | tf_op jit(solution)/shard_map/ppermute | solution.py:158
  129.5 14.1 %collective-permute-start.26 = (bf16[1024,256]{1,0:T(8,128)(2,1)}, bf16[1024,256]{1,0:T(8,128)(2,1)S(1)}, u32[]{:S(2)}, u32[]{:S(2)}) collective-permute-start(bf16[1024,256]{1,0:T(8,128)(2,1)} %convolution_convert_fusion.14), channel_id=1, source_target_pairs={{0,1},{1,0},{2,3},{3,2},{4,5},{5,4},{6,7},{7,6},{8,9},{9,8},{10,11... | collective-permute-start | bytes 1572872 | tf_op jit(solution)/shard_map/ppermute | solution.py:158
  130.7 10.7 %collective-permute-start.33 = (bf16[1024,256]{1,0:T(8,128)(2,1)}, bf16[1024,256]{1,0:T(8,128)(2,1)}, u32[]{:S(2)}, u32[]{:S(2)}) collective-permute-start(bf16[1024,256]{1,0:T(8,128)(2,1)} %convolution_convert_fusion.7), channel_id=1, source_target_pairs={{0,1},{2,3},{4,5},{6,7},{8,9},{10,11},{12,13},{14,15},{16,17},{18,... | collective-permute-start | bytes 1572872 | tf_op jit(solution)/shard_map/ppermute | solution.py:158
  135.0 11.2 %collective-permute-start.25 = (bf16[1024,256]{1,0:T(8,128)(2,1)S(1)}, bf16[1024,256]{1,0:T(8,128)(2,1)}, u32[]{:S(2)}, u32[]{:S(2)}) collective-permute-start(bf16[1024,256]{1,0:T(8,128)(2,1)S(1)} %add_convert_fusion.7), channel_id=1, source_target_pairs={{2,6},{6,10},{10,14},{14,12},{12,8},{8,4},{4,0},{0,2},{18,22},{22,... | collective-permute-start | bytes 1572872 | tf_op jit(solution)/shard_map/ppermute | solution.py:158
  139.6 39.1 %collective-permute-start.39 = (bf16[1024,256]{1,0:T(8,128)(2,1)}, bf16[1024,256]{1,0:T(8,128)(2,1)}, u32[]{:S(2)}, u32[]{:S(2)}) collective-permute-start(bf16[1024,256]{1,0:T(8,128)(2,1)} %convolution_convert_fusion.2), channel_id=1, source_target_pairs={{0,1},{1,0},{2,3},{3,2},{4,5},{5,4},{6,7},{7,6},{8,9},{9,8},{10,11... | collective-permute-start | bytes 1572872 | tf_op jit(solution)/shard_map/ppermute | solution.py:158
  139.6 21.2 %collective-permute-start.28 = (bf16[1024,256]{1,0:T(8,128)(2,1)}, bf16[1024,256]{1,0:T(8,128)(2,1)S(1)}, u32[]{:S(2)}, u32[]{:S(2)}) collective-permute-start(bf16[1024,256]{1,0:T(8,128)(2,1)} %convolution_convert_fusion.12), channel_id=1, source_target_pairs={{0,1},{1,0},{2,3},{3,2},{4,5},{5,4},{6,7},{7,6},{8,9},{9,8},{10,11... | collective-permute-start | bytes 1572872 | tf_op jit(solution)/shard_map/ppermute | solution.py:158
  141.4 17.2 %collective-permute-start.35 = (bf16[1024,256]{1,0:T(8,128)(2,1)}, bf16[1024,256]{1,0:T(8,128)(2,1)}, u32[]{:S(2)}, u32[]{:S(2)}) collective-permute-start(bf16[1024,256]{1,0:T(8,128)(2,1)} %convolution_convert_fusion.6), channel_id=1, source_target_pairs={{0,1},{1,0},{2,3},{3,2},{4,5},{5,4},{6,7},{7,6},{8,9},{9,8},{10,11... | collective-permute-start | bytes 1572872 | tf_op jit(solution)/shard_map/ppermute | solution.py:158
  143.6 15.1 %collective-permute-start.34 = (bf16[1024,256]{1,0:T(8,128)(2,1)}, bf16[1024,256]{1,0:T(8,128)(2,1)}, u32[]{:S(2)}, u32[]{:S(2)}) collective-permute-start(bf16[1024,256]{1,0:T(8,128)(2,1)} %add_convert_fusion.3), channel_id=1, source_target_pairs={{3,1},{7,3},{11,7},{15,11},{13,15},{9,13},{5,9},{1,5},{19,17},{23,... | collective-permute-start | bytes 1572872 | tf_op jit(solution)/shard_map/ppermute | solution.py:158
  147.3 15.1 %collective-permute-start.27 = (bf16[1024,256]{1,0:T(8,128)(2,1)S(1)}, bf16[1024,256]{1,0:T(8,128)(2,1)S(1)}, u32[]{:S(2)}, u32[]{:S(2)}) collective-permute-start(bf16[1024,256]{1,0:T(8,128)(2,1)S(1)} %add_convert_fusion.6), channel_id=1, source_target_pairs={{2,6},{6,10},{10,14},{14,12},{12,8},{8,4},{4,0},{0,2},{3,1},{7,3},... | collective-permute-start | bytes 1572872 | tf_op jit(solution)/shard_map/ppermute | solution.py:158
  149.4 9.8 %copy-start.15 = (bf16[128,1024]{1,0:T(8,128)(2,1)S(1)}, bf16[128,1024]{1,0:T(8,128)(2,1)}, u32[]{:S(2)}) copy-start(bf16[128,1024]{1,0:T(8,128)(2,1)} %copy-done.14) | copy-start | bytes 786436
  158.6 5.6 %copy-start.3 = (bf16[128,256]{1,0:T(8,128)(2,1)S(1)}, bf16[128,256]{1,0:T(8,128)(2,1)}, u32[]{:S(2)}) copy-start(bf16[128,256]{1,0:T(8,128)(2,1)} %copy-done.2) | copy-start | bytes 196612
  158.6 6.8 %collective-permute-start.37 = (bf16[1024,256]{1,0:T(8,128)(2,1)S(1)}, bf16[1024,256]{1,0:T(8,128)(2,1)S(1)}, u32[]{:S(2)}, u32[]{:S(2)}) collective-permute-start(bf16[1024,256]{1,0:T(8,128)(2,1)S(1)} %convolution_convert_fusion.4), channel_id=1, source_target_pairs={{0,1},{1,0},{2,3},{3,2},{4,5},{5,4},{6,7},{7,6},{8,9},{9,8},{10,11... | collective-permute-start | bytes 1572872 | tf_op jit(solution)/shard_map/ppermute | solution.py:158
  158.7 13.3 %collective-permute-start.30 = (bf16[1024,256]{1,0:T(8,128)(2,1)}, bf16[1024,256]{1,0:T(8,128)(2,1)S(1)}, u32[]{:S(2)}, u32[]{:S(2)}) collective-permute-start(bf16[1024,256]{1,0:T(8,128)(2,1)} %convolution_convert_fusion.10), channel_id=1, source_target_pairs={{0,1},{1,0},{2,3},{3,2},{4,5},{5,4},{6,7},{7,6},{8,9},{9,8},{10,11... | collective-permute-start | bytes 1572872 | tf_op jit(solution)/shard_map/ppermute | solution.py:158
  160.8 9.3 %copy-start.11 = (bf16[128,1024]{1,0:T(8,128)(2,1)S(1)}, bf16[128,1024]{1,0:T(8,128)(2,1)}, u32[]{:S(2)}) copy-start(bf16[128,1024]{1,0:T(8,128)(2,1)} %copy-done.10) | copy-start | bytes 786436
  160.8 9.2 %collective-permute-start.36 = (bf16[1024,256]{1,0:T(8,128)(2,1)S(1)}, bf16[1024,256]{1,0:T(8,128)(2,1)S(1)}, u32[]{:S(2)}, u32[]{:S(2)}) collective-permute-start(bf16[1024,256]{1,0:T(8,128)(2,1)S(1)} %add_convert_fusion.2), channel_id=1, source_target_pairs={{2,6},{6,10},{10,14},{14,12},{12,8},{8,4},{4,0},{0,2},{3,1},{7,3},... | collective-permute-start | bytes 1572872 | tf_op jit(solution)/shard_map/ppermute | solution.py:158
  162.6 13.1 %collective-permute-start.29 = (bf16[1024,256]{1,0:T(8,128)(2,1)S(1)}, bf16[1024,256]{1,0:T(8,128)(2,1)S(1)}, u32[]{:S(2)}, u32[]{:S(2)}) collective-permute-start(bf16[1024,256]{1,0:T(8,128)(2,1)S(1)} %add_convert_fusion.5), channel_id=1, source_target_pairs={{2,6},{6,10},{10,14},{14,12},{12,8},{8,4},{4,0},{0,2},{3,1},{7,3},... | collective-permute-start | bytes 1572872 | tf_op jit(solution)/shard_map/ppermute | solution.py:158
  170.4 10.9 %copy-start.9 = (bf16[128,1024]{1,0:T(8,128)(2,1)S(1)}, bf16[128,1024]{1,0:T(8,128)(2,1)}, u32[]{:S(2)}) copy-start(bf16[128,1024]{1,0:T(8,128)(2,1)} %copy-done.8) | copy-start | bytes 786436
  170.4 10.9 %collective-permute-start.38 = (bf16[1024,256]{1,0:T(8,128)(2,1)S(1)}, bf16[1024,256]{1,0:T(8,128)(2,1)S(1)}, u32[]{:S(2)}, u32[]{:S(2)}) collective-permute-start(bf16[1024,256]{1,0:T(8,128)(2,1)S(1)} %add_convert_fusion.1), channel_id=1, source_target_pairs={{2,6},{6,10},{10,14},{14,12},{12,8},{8,4},{4,0},{0,2},{3,1},{7,3},... | collective-permute-start | bytes 1572872 | tf_op jit(solution)/shard_map/ppermute | solution.py:158
  175.8 11.1 %collective-permute-start.31 = (bf16[1024,256]{1,0:T(8,128)(2,1)S(1)}, bf16[1024,256]{1,0:T(8,128)(2,1)S(1)}, u32[]{:S(2)}, u32[]{:S(2)}) collective-permute-start(bf16[1024,256]{1,0:T(8,128)(2,1)S(1)} %add_convert_fusion.4), channel_id=1, source_target_pairs={{2,6},{6,10},{10,14},{14,12},{12,8},{8,4},{4,0},{0,2},{3,1},{7,3},... | collective-permute-start | bytes 1572872 | tf_op jit(solution)/shard_map/ppermute | solution.py:158
  182.6 9.8 %copy-start.7 = (bf16[128,1024]{1,0:T(8,128)(2,1)S(1)}, bf16[128,1024]{1,0:T(8,128)(2,1)}, u32[]{:S(2)}) copy-start(bf16[128,1024]{1,0:T(8,128)(2,1)} %copy-done.6) | copy-start | bytes 786436
  182.7 9.8 %collective-permute-start.40 = (bf16[1024,256]{1,0:T(8,128)(2,1)S(1)}, bf16[1024,256]{1,0:T(8,128)(2,1)S(1)}, u32[]{:S(2)}, u32[]{:S(2)}) collective-permute-start(bf16[1024,256]{1,0:T(8,128)(2,1)S(1)} %add_convert_fusion), channel_id=1, source_target_pairs={{2,6},{6,10},{10,14},{14,12},{12,8},{8,4},{4,0},{0,2},{3,1},{7,3},... | collective-permute-start | bytes 1572872 | tf_op jit(solution)/shard_map/ppermute | solution.py:158
  187.0 6.0 %copy-start.13 = (bf16[1,512,256]{2,1,0:T(8,128)(2,1)S(1)}, bf16[1,512,256]{2,1,0:T(8,128)(2,1)}, u32[]{:S(2)}) copy-start(bf16[1,512,256]{2,1,0:T(8,128)(2,1)} %param.11) | copy-start | bytes 786436
  187.0 5.9 %collective-permute-start.32 = (bf16[512,256]{1,0:T(8,128)(2,1)S(1)}, bf16[512,256]{1,0:T(8,128)(2,1)S(1)}, u32[]{:S(2)}, u32[]{:S(2)}) collective-permute-start(bf16[512,256]{1,0:T(8,128)(2,1)S(1)} %select_convert_fusion.1), channel_id=1, source_target_pairs={{0,1},{1,0},{2,3},{3,2},{4,5},{5,4},{6,7},{7,6},{8,9},{9,8},{10,11... | collective-permute-start | bytes 786440 | tf_op jit(solution)/shard_map/ppermute | solution.py:158
  192.9 2.3 %collective-permute-start.41 = (bf16[512,256]{1,0:T(8,128)(2,1)S(1)}, bf16[512,256]{1,0:T(8,128)(2,1)S(1)}, u32[]{:S(2)}, u32[]{:S(2)}) collective-permute-start(bf16[512,256]{1,0:T(8,128)(2,1)S(1)} %select_convert_fusion), channel_id=1, source_target_pairs={{0,1},{1,0},{2,3},{3,2},{4,5},{5,4},{6,7},{7,6},{8,9},{9,8},{10,11... | collective-permute-start | bytes 786440 | tf_op jit(solution)/shard_map/ppermute | solution.py:158

commit v2 on v1

v2 whole, which is shorter than its diff:
```python
import jax
import jax.numpy as jnp
import numpy as np
from jax import lax
from jax.experimental import pallas as pl
from jax.experimental.pallas import tpu as pltpu
from jax.sharding import PartitionSpec as P

Z_CHIPS = 4
CORES = 2
EPSILON = 1e-05
F32 = jnp.float32
BF16 = jnp.bfloat16


def ring_of_chips(chips):
    rows = chips // Z_CHIPS
    cycle = []
    for z in range(Z_CHIPS):
        ys = range(1, rows) if z % 2 == 0 else range(rows - 1, 0, -1)
        cycle += [z * rows + y for y in ys]
    return cycle + [z * rows for z in range(Z_CHIPS - 1, -1, -1)]


class Routes:
    def __init__(self, devices):
        ring = ring_of_chips(devices // CORES)
        n = self.n = len(ring)
        half = self.half = n // 2
        self.partner = [(i, i ^ 1) for i in range(devices)]
        self.onward_by_core = [
            [(ring[i] * CORES + c, ring[(i + 1 - 2 * c) % n] * CORES + c) for i in range(n)] for c in range(CORES)
        ]
        self.onward = self.onward_by_core[0] + self.onward_by_core[1]
        steps = [0] + [-k for k in range(1, half)] + list(range(1, half)) + [half]
        self.table = np.zeros((devices, n), np.int32)
        for i, chip in enumerate(ring):
            for c in range(CORES):
                self.table[chip * CORES + c] = [ring[(i + (1 - 2 * c) * s) % n] for s in steps]
        self.opposite = n - 1

    def behind(self, k):
        return k

    def ahead(self, k):
        return self.half - 1 + k


def after(value, *earlier):
    return lax.optimization_barrier((value, *earlier))[0]


def arrange_inputs_kernel(ids, x_ref, gain_ref, inv_ref, x_out, scaled_out, gain_out):
    x = x_ref[...]
    x_out[0] = x
    gain = gain_ref[...]
    gain_out[0] = gain
    scaled_out[0] = ((x.astype(F32) * inv_ref[...]) * gain).astype(BF16)


def arrange_inputs(ids, x, gain, inverse):
    tokens, width = x.shape
    n = ids.shape[0]
    block = width // n
    by_slot = pl.BlockSpec((1, tokens, block), lambda j, ids: (j, 0, 0))
    return pl.pallas_call(
        arrange_inputs_kernel,
        grid_spec=pltpu.PrefetchScalarGridSpec(
            num_scalar_prefetch=1,
            grid=(n,),
            in_specs=[
                pl.BlockSpec((tokens, block), lambda j, ids: (0, ids[j])),
                pl.BlockSpec((1, block), lambda j, ids: (0, ids[j])),
                pl.BlockSpec((tokens, 1), lambda j, ids: (0, 0)),
            ],
            out_specs=[by_slot, by_slot, pl.BlockSpec((1, 1, block), lambda j, ids: (j, 0, 0))],
        ),
        out_shape=[
            jax.ShapeDtypeStruct((n, tokens, block), BF16),
            jax.ShapeDtypeStruct((n, tokens, block), BF16),
            jax.ShapeDtypeStruct((n, 1, block), F32),
        ],
        cost_estimate=pl.CostEstimate(flops=4 * tokens * width, bytes_accessed=6 * tokens * width, transcendentals=0),
        name="arrange_inputs",
    )(ids, x, gain, inverse)


def arrange_teacher_kernel(ids, t_ref, t_out):
    t_out[0] = t_ref[...]


def arrange_teacher(ids, teacher):
    tokens, width = teacher.shape
    n = ids.shape[0]
    block = width // n
    return pl.pallas_call(
        arrange_teacher_kernel,
        grid_spec=pltpu.PrefetchScalarGridSpec(
            num_scalar_prefetch=1,
            grid=(n,),
            in_specs=[pl.BlockSpec((tokens, block), lambda j, ids: (0, ids[j]))],
            out_specs=pl.BlockSpec((1, tokens, block), lambda j, ids: (j, 0, 0)),
        ),
        out_shape=jax.ShapeDtypeStruct((n, tokens, block), BF16),
        cost_estimate=pl.CostEstimate(flops=0, bytes_accessed=4 * tokens * width, transcendentals=0),
        name="arrange_teacher",
    )(ids, teacher)


def finish_kernel(ids, cot_ref, x_ref, down_ref, gain_ref, pre_ref, inv_ref, mean_ref, *rest):
    out_ref = rest[-1]
    grad = lax.dot_general(pre_ref[...], down_ref[...], (((1,), (1,)), ((), ())), preferred_element_type=F32)
    normed = x_ref[0].astype(F32) * inv_ref[...]
    out = cot_ref[...].astype(F32) + inv_ref[...] * (grad * gain_ref[0] - normed * mean_ref[...])
    out_ref[...] = out.astype(BF16)


def finish(ids, slot, cot, x_slots, down, gain_slots, pre_grad, inverse, mean, so_far):
    n, tokens, block = x_slots.shape
    rank = pre_grad.shape[1]

    def whole(*shape):
        return pl.BlockSpec(shape, lambda i, ids: (0,) * len(shape))

    given = [] if so_far is None else [so_far]
    return pl.pallas_call(
        finish_kernel,
        grid_spec=pltpu.PrefetchScalarGridSpec(
            num_scalar_prefetch=1,
            grid=(1,),
            in_specs=[
                whole(tokens, block),
                pl.BlockSpec((1, tokens, block), lambda i, ids: (slot, 0, 0)),
                whole(block, rank),
                pl.BlockSpec((1, 1, block), lambda i, ids: (slot, 0, 0)),
                whole(tokens, rank),
                whole(tokens, 1),
                whole(tokens, 1),
            ]
            + [pl.BlockSpec(memory_space=pl.ANY)] * len(given),
            out_specs=pl.BlockSpec((tokens, block), lambda i, ids: (0, ids[slot])),
        ),
        out_shape=jax.ShapeDtypeStruct((tokens, n * block), BF16),
        input_output_aliases={8: 0} if given else {},
        cost_estimate=pl.CostEstimate(
            flops=2 * tokens * block * rank, bytes_accessed=6 * tokens * block + 2 * block * rank, transcendentals=0
        ),
        name="finish",
    )(ids, cot, x_slots, down, gain_slots, pre_grad, inverse, mean, *given)


def local(section_inputs, teacher_states, confidence, gains, w_down, w_up):
    sections = lax.axis_size("section")
    devices = lax.axis_size("dp")
    section_index = lax.axis_index("section")
    dp_index = lax.axis_index("dp")
    first = dp_index % CORES == 0
    is_last = section_index == sections - 1
    routes = Routes(devices)
    half, opposite = routes.half, routes.opposite
    x = section_inputs[0]
    tokens, width = x.shape
    back = [(s, s - 1) for s in range(1, sections)]
    ahead_section = [(s, s + 1) for s in range(sections - 1)]

    def swap(block):
        return lax.ppermute(block, "dp", routes.partner)

    def onward(block):
        return lax.ppermute(block, "dp", routes.onward)

    def of_chip(own, other):
        return jnp.where(first, jnp.concatenate([own, other]), jnp.concatenate([other, own]))

    def own_half(block):
        rows = block.shape[0] // CORES
        return jnp.where(first, block[:rows], block[rows:])

    order = [0]
    for k in range(1, half):
        order += [routes.behind(k), routes.ahead(k)]
    order.append(opposite)
    leaving = [opposite]
    for k in range(half - 1, 0, -1):
        leaving += [routes.ahead(k), routes.behind(k)]
    leaving.append(0)

    downs, ups, next_ups = {}, {}, {}
    down, up = w_down[0], w_up[0]
    downs[0] = of_chip(down, swap(down))
    ups[0] = of_chip(up, swap(up))
    for k in range(1, half):
        downs[k] = onward(downs[k - 1])
        ups[k] = onward(ups[k - 1])
        downs[routes.ahead(k)] = swap(downs[k])
        ups[routes.ahead(k)] = swap(ups[k])
    down_far = onward(own_half(downs[half - 1]))
    up_far = onward(own_half(ups[half - 1]))
    downs[opposite] = of_chip(down_far, swap(down_far))
    ups[opposite] = of_chip(up_far, swap(up_far))

    relayed = {0: up}
    for k in range(1, half):
        relayed[k] = ups[k]
    relayed[opposite] = up_far
    for j, block in relayed.items():
        block = lax.ppermute(block, "section", ahead_section)
        other = swap(block)
        if j in (0, opposite):
            next_ups[j] = of_chip(block, other)
        else:
            next_ups[j], next_ups[routes.ahead(j)] = block, other

    values = x.astype(F32)
    inverse = lax.rsqrt(jnp.mean(values * values, axis=-1, keepdims=True) + EPSILON)
    table = after(jnp.asarray(routes.table), downs[0])
    ids = lax.dynamic_slice_in_dim(table, dp_index, 1, 0)[0]
    x_slots, scaled_slots, gain_slots = arrange_inputs(ids, after(x, downs[1]), gains, inverse)
    teacher_slots = arrange_teacher(ids, after(teacher_states, downs[2], scaled_slots))
    weight_rows = (confidence.astype(F32) / 256.0)[:, None]
    preact = 0.0
    for j in order:
        preact = preact + jnp.dot(scaled_slots[j], downs[j], preferred_element_type=F32)
    hidden = jax.nn.silu(preact).astype(BF16)
    sigmoid_val = jax.nn.sigmoid(preact)
    slope = sigmoid_val * (1.0 + preact * (1.0 - sigmoid_val))

    def top_of(j):
        branch = jnp.einsum("tr,dr->td", hidden, ups[j], preferred_element_type=F32)
        return (weight_rows * (x_slots[j].astype(F32) + branch - teacher_slots[j].astype(F32))).astype(BF16)

    tops = {j: top_of(j) for j in order}

    def through_rank(cots, matrices):
        total = 0.0
        for j in order:
            total = total + jnp.dot(cots[j], matrices[j], preferred_element_type=F32)
        return total

    def pre_grad_of(hidden_grad):
        pre_grad = (hidden_grad * slope).astype(BF16)
        return pre_grad, jnp.sum(pre_grad.astype(F32) * preact, axis=-1, keepdims=True) / width

    def input_grad_of(j, cot, pre_grad, mean):
        grad = jnp.einsum("tr,dr->td", pre_grad, downs[j], preferred_element_type=F32)
        normed = x_slots[j].astype(F32) * inverse
        return (cot.astype(F32) + inverse * (grad * gain_slots[j] - normed * mean)).astype(BF16)

    own_hidden_grad = through_rank(tops, ups)
    pre_grad, mean = pre_grad_of(own_hidden_grad)
    cots = tops
    for _ in range(sections - 1):
        sent = {j: input_grad_of(j, cots[j], pre_grad, mean) for j in leaving}
        next_hidden_grad = through_rank(sent, next_ups)
        arrived = {}
        queue = [sent[j] for j in leaving]
        queue.insert(2, next_hidden_grad)
        done = []
        for i, block in enumerate(queue):
            done.append(lax.ppermute(after(block, done[i - 2]) if i >= 2 else block, "section", back))
        hidden_grad = jnp.where(is_last, own_hidden_grad, done.pop(2))
        cots = {j: jnp.where(is_last, tops[j], block) for j, block in zip(leaving, done)}
        pre_grad, mean = pre_grad_of(hidden_grad)

    def scattered(parts, far_core):
        to_far = [(a, b) for a, b in routes.partner if b % CORES == far_core]
        total = parts[opposite].astype(F32) + lax.ppermute(parts[opposite], "dp", to_far).astype(F32)
        total = lax.ppermute(total.astype(BF16), "dp", routes.onward_by_core[far_core]).astype(F32)
        for k in range(half - 1, 0, -1):
            other = swap(parts[routes.behind(k)]).astype(F32)
            total = total + (other + parts[routes.ahead(k)].astype(F32))
            total = onward(total.astype(BF16)).astype(F32)
        total = total + parts[0].astype(F32)
        columns = total.shape[1] // CORES
        low, high = total[:, :columns], total[:, columns:]
        other = swap(jnp.where(first, high, low).astype(BF16))
        return (jnp.where(first, low, high) + other.astype(F32)).T / tokens

    def product(a, b):
        return jnp.dot(a, b, preferred_element_type=F32).astype(BF16)

    pre_t = lax.optimization_barrier(pre_grad.T)
    hidden_t = lax.optimization_barrier(hidden.T)
    grad_down = scattered({j: product(pre_t, scaled_slots[j]) for j in leaving}, 0)
    grad_up = scattered({j: product(hidden_t, cots[j]) for j in leaving}, 1)
    input_grads = None
    for j in leaving:
        input_grads = finish(ids, j, cots[j], x_slots, downs[j], gain_slots, pre_grad, inverse, mean, input_grads)
    own_gain = lax.dynamic_slice_in_dim(gains[0], dp_index * w_down.shape[1], w_down.shape[1], 0)
    grad_gain = jnp.sum(grad_down * down.astype(F32), axis=1) / own_gain
    return input_grads[None], grad_down[None], grad_up[None], grad_gain[None]


def solution(mesh):
    in_specs = (
        P("section", "dp", None),
        P("dp", None),
        P("dp"),
        P("section", None),
        P("section", "dp", None),
        P("section", "dp", None),
    )
    out_specs = (
        P("section", "dp", None),
        P("section", "dp", None),
        P("section", "dp", None),
        P("section", "dp"),
    )
    return jax.shard_map(local, mesh=mesh, in_specs=in_specs, out_specs=out_specs, check_vma=False)
```

time: 197 us -> 221 us (1.12); the launches traced: 196 us -> 217 us
  waiting for transfers between devices: 87.8 us -> 45.9 us
  matrix products: 26.3 us -> 51.8 us
  Pallas kernels: 16.8 us -> 37.2 us
  starting transfers between devices: 48.1 us -> 60.5 us
  other arithmetic: 10.6 us -> 15.7 us
    ppermute x42 -> x55, waiting for transfers between devices: 87.8 us -> 45.9 us  [the longest x9 21.4 us: local(): lax.ppermute(after(block, done[i - 2]) if i >= 2 else block, 'section', b...]
    pallas_call x1 -> x8, Pallas kernels: 8.92 us -> 24.1 us  [finish(): pl.pallas_call(finish_kernel, grid_spec=pltpu.PrefetchScalarGridSpec(num_...]
    ppermute x42 -> x55, starting transfers between devices: 48.1 us -> 60.5 us  [the longest x14 19.2 us: onward(): return lax.ppermute(block, 'dp', routes.onward)]
    dot_general x32, matrix products: 19.2 us -> 29.9 us  [the longest x16 18.8 us: product(): return jnp.dot(a, b, preferred_element_type=F32).astype(BF16)]
    dot_general x8, matrix products: 2.7 us -> 8.66 us  [input_grad_of(): jnp.einsum('tr,dr->td', pre_grad, downs[j], preferred_element_type=F32)]
    select_n x4 -> x13, other arithmetic: 0.57 us -> 6.24 us  [the longest x8 3.81 us: local(): jnp.where(is_last, tops[j], block)]
    dot_general x8, matrix products: 1.9 us -> 7.54 us  [local(): jnp.dot(scaled_slots[j], downs[j], preferred_element_type=F32)]
    pallas_call x1 -> x2, Pallas kernels: 7.92 us -> 13.1 us  [the longest x1 6.8 us: arrange_inputs(): pl.pallas_call(arrange_inputs_kernel, grid_spec=pltpu.PrefetchScalarGridS...]
  transfers between devices with their start and end apart: 42 -> 55, of which waited for: 19 -> 13; matrix products, arithmetic and copies ran while one was open for 16% -> 32% of each run, Pallas kernels for 9% -> 17%
where the time goes in v2:
time: 221 us; the launch traced here: 217 us
  starting transfers between devices  60.5 us (27%)
  matrix products  51.8 us (23%)
  waiting for transfers between devices  45.9 us (21%)
  Pallas kernels  37.2 us (17%)
  other arithmetic  15.7 us (7%)
  local copies, waits for them, and re-layouts  4.43 us (2%)
    pallas_call x8, Pallas kernels, finish(): pl.pallas_call(finish_kernel, grid_spec=pltpu.PrefetchScalarGridSpec(num_...  24.1 us
    ppermute x9, waiting for transfers between devices, local(): lax.ppermute(after(block, done[i - 2]) if i >= 2 else block, 'section', b...  21.4 us
    ppermute x14, starting transfers between devices, onward(): return lax.ppermute(block, 'dp', routes.onward)  19.2 us
    dot_general x16, matrix products, product(): return jnp.dot(a, b, preferred_element_type=F32).astype(BF16)  18.8 us
    ppermute x14, waiting for transfers between devices, onward(): return lax.ppermute(block, 'dp', routes.onward)  16 us
    ppermute x5, starting transfers between devices, local(): block = lax.ppermute(block, 'section', ahead_section)  13.8 us
    ppermute x9, starting transfers between devices, local(): lax.ppermute(after(block, done[i - 2]) if i >= 2 else block, 'section', b...  11.6 us
    dot_general x16, matrix products, through_rank(): total = total + jnp.dot(cots[j], matrices[j], preferred_element_type=F32)  11.1 us
  transfers between devices with their start and end apart: 55, of which 13 were waited for; matrix products, arithmetic and copies ran while one was open for 32% of the time, Pallas kernels for 17%

profile of v2, /device:TPU:0, one launch (start us, length us, event | category | flops | bytes accessed | tf_op | source)
XLA Modules:
  0.0 217.5 jit_solution(1692715921701892936)
XLA Ops:
  1.2 5.6 %collective-permute-start.18 = (bf16[512,256]{1,0:T(8,128)(2,1)}, bf16[512,256]{1,0:T(8,128)(2,1)}, u32[]{:S(2)}, u32[]{:S(2)}) collective-permute-start(bf16[512,256]{1,0:T(8,128)(2,1)} %bitcast.273), channel_id=1, source_target_pairs={{0,16},{1,17},{2,18},{3,19},{4,20},{5,21},{6,22},{7,23},{8,24},{9,... | collective-permute-start | bytes 786440 | tf_op jit(solution)/shard_map/ppermute | solution.py:207
  8.0 1.6 collective-permute-start.1
  9.6 2.1 multiply_reduce_fusion
  11.9 1.6 collective-permute-start.10
  14.9 2.5 %collective-permute-done.1.down_ref = bf16[1024,256]{1,0:T(8,128)(2,1)} collective-permute-done((bf16[1024,256]{1,0:T(8,128)(2,1)S(1)}, bf16[1024,256]{1,0:T(8,128)(2,1)}, u32[]{:S(2)}, u32[]{:S(2)}) %collective-permute-start.1) | collective-permute-done | bytes 524320 | tf_op jit(solution)/shard_map/ppermute | solution.py:170
  17.4 1.5 collective-permute-start.3
  20.1 2.9 %collective-permute-done.10 = bf16[1024,256]{1,0:T(8,128)(2,1)} collective-permute-done((bf16[1024,256]{1,0:T(8,128)(2,1)S(1)}, bf16[1024,256]{1,0:T(8,128)(2,1)}, u32[]{:S(2)}, u32[]{:S(2)}) %collective-permute-start.10) | collective-permute-done | bytes 524320 | tf_op jit(solution)/shard_map/ppermute | solution.py:170
  23.0 1.5 collective-permute-start.12
  24.5 6.8 %arrange_inputs.1 = (bf16[8,128,1024]{2,1,0:T(8,128)(2,1)}, bf16[8,128,1024]{2,1,0:T(8,128)(2,1)}, f32[8,1,1024]{2,1,0:T(1,128)}) custom-call(s32[8]{0:T(128)} %dynamic-slice_bitcast_fusion.ids, bf16[128,8192]{1,0:T(8,128)(2,1)} %bitcast.269, f32[1,8192]{1,0:T(1,128)} %gain_ref.1, f32[128,1]{1,0:T(8,128)} %copy.18.inv_ref), custom_call_target="tpu_custom_call" | custom-call | flops 4194304 | bytes 6291456 | tf_op jit(solution)/shard_map/arrange_inputs/pallas_call | solution.py:66
  31.3 1.5 fusion.111
  32.8 1.6 collective-permute-start.5
  35.7 1.3 fusion.142
  37.6 1.4 fusion.106
  39.0 3.2 %collective-permute-done.5.down_ref = bf16[1024,256]{1,0:T(8,128)(2,1)S(1)} collective-permute-done((bf16[1024,256]{1,0:T(8,128)(2,1)}, bf16[1024,256]{1,0:T(8,128)(2,1)S(1)}, u32[]{:S(2)}, u32[]{:S(2)}) %collective-permute-start.5) | collective-permute-done | bytes 524320 | tf_op jit(solution)/shard_map/ppermute | solution.py:170
  42.3 1.6 collective-permute-start.14
  44.6 1.6 collective-permute-start.7
  46.4 6.3 %arrange_teacher.1 = bf16[8,128,1024]{2,1,0:T(8,128)(2,1)} custom-call(s32[8]{0:T(128)} %dynamic-slice_bitcast_fusion.ids, bf16[128,8192]{1,0:T(8,128)(2,1)} %t_ref), custom_call_target="tpu_custom_call" | custom-call | bytes 4194304 | tf_op jit(solution)/shard_map/arrange_teacher/pallas_call | solution.py:96
  52.8 1.3 fusion.101
  54.1 1.3 collective-permute-start.20
  55.6 1.4 fusion.71
  59.1 1.6 collective-permute-start.16
  61.6 1.4 fusion.49
  64.5 1.4 fusion.51
  65.9 1.3 collective-permute-start.22
  67.3 1.4 fusion.50
  71.1 1.3 collective-permute-start.26
  73.6 6.2 %collective-permute-done.22 = bf16[1024,256]{1,0:T(8,128)(2,1)S(1)} collective-permute-done((bf16[1024,256]{1,0:T(8,128)(2,1)}, bf16[1024,256]{1,0:T(8,128)(2,1)S(1)}, u32[]{:S(2)}, u32[]{:S(2)}) %collective-permute-start.22) | collective-permute-done | bytes 524320 | tf_op jit(solution)/shard_map/ppermute | solution.py:207
  79.9 4.3 %collective-permute-start.24 = (bf16[1024,256]{1,0:T(8,128)(2,1)S(1)}, bf16[1024,256]{1,0:T(8,128)(2,1)S(1)}, u32[]{:S(2)}, u32[]{:S(2)}) collective-permute-start(bf16[1024,256]{1,0:T(8,128)(2,1)S(1)} %collective-permute-done.14), channel_id=1, source_target_pairs={{0,16},{1,17},{2,18},{3,19},{4,20},{5,21},{6,22},{7,23},{8,24},{9,... | collective-permute-start | bytes 1572872 | tf_op jit(solution)/shard_map/ppermute | solution.py:207
  86.2 1.3 fusion.69
  89.7 2.1 fusion.60
  93.0 1.4 fusion.59
  96.1 1.3 collective-permute-start.28
  98.0 1.3 collective-permute-start.33
  99.3 1.4 convolution_add_fusion.11
  102.0 2.1 fusion.58
  105.6 6.3 %collective-permute-done.33 = bf16[128,1024]{1,0:T(8,128)(2,1)S(1)} collective-permute-done((bf16[128,1024]{1,0:T(8,128)(2,1)S(1)}, bf16[128,1024]{1,0:T(8,128)(2,1)S(1)}, u32[]{:S(2)}, u32[]{:S(2)}) %collective-permute-start.33) | collective-permute-done | bytes 262176 | tf_op jit(solution)/shard_map/ppermute | solution.py:260
  114.4 2.3 %collective-permute-start.46 = (bf16[256,1024]{0,1:T(8,128)(2,1)}, bf16[256,1024]{0,1:T(8,128)(2,1)}, u32[]{:S(2)}, u32[]{:S(2)}) collective-permute-start(bf16[256,1024]{0,1:T(8,128)(2,1)} %convolution_convert_fusion.7), channel_id=1, source_target_pairs={{0,1},{2,3},{4,5},{6,7},{8,9},{10,11},{12,13},{14,15},{16,17},{18,... | collective-permute-start | bytes 1572872 | tf_op jit(solution)/shard_map/ppermute | solution.py:267
  117.4 3.9 %collective-permute-done.34 = bf16[128,1024]{1,0:T(8,128)(2,1)S(1)} collective-permute-done((bf16[128,1024]{1,0:T(8,128)(2,1)S(1)}, bf16[128,1024]{1,0:T(8,128)(2,1)S(1)}, u32[]{:S(2)}, u32[]{:S(2)}) %collective-permute-start.34) | collective-permute-done | bytes 262176 | tf_op jit(solution)/shard_map/ppermute | solution.py:260
  122.9 1.3 collective-permute-start.29
  125.4 7.4 %collective-permute-done.29 = f32[128,256]{1,0:T(8,128)S(1)} collective-permute-done((f32[128,256]{1,0:T(8,128)S(1)}, f32[128,256]{1,0:T(8,128)S(1)}, u32[]{:S(2)}, u32[]{:S(2)}) %collective-permute-start.29) | collective-permute-done | bytes 131104 | tf_op jit(solution)/shard_map/ppermute | solution.py:260
  138.4 2.9 %finish.8.rest_0_ = bf16[128,8192]{1,0:T(8,128)(2,1)} custom-call(s32[8]{0:T(128)} %dynamic-slice_bitcast_fusion.ids, bf16[128,1024]{1,0:T(8,128)(2,1)} %copy-done.18, bf16[8,128,1024]{2,1,0:T(8,128)(2,1)} %get-tuple-element.19.x_ref, bf16[1024,256]{1,0:T(8,128)(2,1)} %copy-done.13, f32[8,1,1024]{2,1,0:T(1,128)} %get-tuple-element.22.gain_ref, ...), custom_call_target="tpu_custom_call" | custom-call | flops 67108864 | bytes 1310720 | tf_op jit(solution)/shard_map/finish/pallas_call | solution.py:126
  141.4 2.9 %finish.9.rest_0_ = bf16[128,8192]{1,0:T(8,128)(2,1)} custom-call(s32[8]{0:T(128)} %dynamic-slice_bitcast_fusion.ids, bf16[128,1024]{1,0:T(8,128)(2,1)} %broadcast_select_fusion.1.cot_ref, bf16[8,128,1024]{2,1,0:T(8,128)(2,1)} %get-tuple-element.19.x_ref, bf16[1024,256]{1,0:T(8,128)(2,1)} %copy-done.30, ...), custom_call_target="tpu_custom_call", output_to_operand_aliasing={{}: (8, {})} | custom-call | flops 67108864 | bytes 1310720 | tf_op jit(solution)/shard_map/finish/pallas_call | solution.py:126
  144.3 3.1 %finish.10.rest_0_ = bf16[128,8192]{1,0:T(8,128)(2,1)} custom-call(s32[8]{0:T(128)} %dynamic-slice_bitcast_fusion.ids, bf16[128,1024]{1,0:T(8,128)(2,1)} %copy-done.21, bf16[8,128,1024]{2,1,0:T(8,128)(2,1)} %get-tuple-element.19.x_ref, bf16[1024,256]{1,0:T(8,128)(2,1)} %copy-done.11, ...), custom_call_target="tpu_custom_call", output_to_operand_aliasing={{}: (8, {})} | custom-call | flops 67108864 | bytes 1310720 | tf_op jit(solution)/shard_map/finish/pallas_call | solution.py:126
  150.1 1.4 add_convert_fusion.3
  152.6 2.6 %collective-permute-start.39 = (bf16[256,1024]{0,1:T(8,128)(2,1)S(1)}, bf16[256,1024]{0,1:T(8,128)(2,1)S(1)}, u32[]{:S(2)}, u32[]{:S(2)}) collective-permute-start(bf16[256,1024]{0,1:T(8,128)(2,1)S(1)} %copy-done.29), channel_id=1, source_target_pairs={{0,1},{1,0},{2,3},{3,2},{4,5},{5,4},{6,7},{7,6},{8,9},{9,8},{10,11... | collective-permute-start | bytes 1572872 | tf_op jit(solution)/shard_map/ppermute | solution.py:167
  155.4 3.5 %collective-permute-start.38 = (bf16[256,1024]{0,1:T(8,128)(2,1)S(1)}, bf16[256,1024]{0,1:T(8,128)(2,1)S(1)}, u32[]{:S(2)}, u32[]{:S(2)}) collective-permute-start(bf16[256,1024]{0,1:T(8,128)(2,1)S(1)} %add_convert_fusion.7), channel_id=1, source_target_pairs={{2,6},{6,10},{10,14},{14,12},{12,8},{8,4},{4,0},{0,2},{18,22},{22,... | collective-permute-start | bytes 1572872 | tf_op jit(solution)/shard_map/ppermute | solution.py:268
  161.2 1.7 collective-permute-start.50
  162.9 1.4 add_convert_fusion.2
  164.4 3.8 %collective-permute-done.36 = bf16[128,1024]{1,0:T(8,128)(2,1)S(1)} collective-permute-done((bf16[128,1024]{1,0:T(8,128)(2,1)S(1)}, bf16[128,1024]{1,0:T(8,128)(2,1)S(1)}, u32[]{:S(2)}, u32[]{:S(2)}) %collective-permute-start.36) | collective-permute-done | bytes 262176 | tf_op jit(solution)/shard_map/ppermute | solution.py:260
  171.5 1.3 collective-permute-start.40
  174.0 3.4 %collective-permute-done.49 = bf16[256,1024]{0,1:T(8,128)(2,1)S(1)} collective-permute-done((bf16[256,1024]{0,1:T(8,128)(2,1)S(1)}, bf16[256,1024]{0,1:T(8,128)(2,1)S(1)}, u32[]{:S(2)}, u32[]{:S(2)}) %collective-permute-start.49) | collective-permute-done | bytes 524320 | tf_op jit(solution)/shard_map/ppermute | solution.py:170
  179.3 2.9 %finish.11.rest_0_ = bf16[128,8192]{1,0:T(8,128)(2,1)} custom-call(s32[8]{0:T(128)} %dynamic-slice_bitcast_fusion.ids, bf16[128,1024]{1,0:T(8,128)(2,1)} %copy-done.23, bf16[8,128,1024]{2,1,0:T(8,128)(2,1)} %get-tuple-element.19.x_ref, bf16[1024,256]{1,0:T(8,128)(2,1)} %collective-permute-done.4.down_ref, ...), custom_call_target="tpu_custom_call", output_to_operand_aliasing={{}: (8, {})} | custom-call | flops 67108864 | bytes 1310720 | tf_op jit(solution)/shard_map/finish/pallas_call | solution.py:126
  182.2 3.1 %finish.12.rest_0_ = bf16[128,8192]{1,0:T(8,128)(2,1)} custom-call(s32[8]{0:T(128)} %dynamic-slice_bitcast_fusion.ids, bf16[128,1024]{1,0:T(8,128)(2,1)} %copy-done.19, bf16[8,128,1024]{2,1,0:T(8,128)(2,1)} %get-tuple-element.19.x_ref, bf16[1024,256]{1,0:T(8,128)(2,1)} %collective-permute-done.3.down_ref, ...), custom_call_target="tpu_custom_call", output_to_operand_aliasing={{}: (8, {})} | custom-call | flops 67108864 | bytes 1310720 | tf_op jit(solution)/shard_map/finish/pallas_call | solution.py:126
  186.6 2.4 %add_convert_fusion.5 = bf16[256,1024]{0,1:T(8,128)(2,1)} fusion(bf16[256,1024]{0,1:T(8,128)(2,1)} %collective-permute-done.41, bf16[256,1024]{0,1:T(8,128)(2,1)} %collective-permute-done.40, bf16[256,128]{0,1:T(8,128)(2,1)S(1)} %bitcast.266, bf16[8,128,1024]{2,1,0:T(8,128)(2,1)S(1)} %copy-done.6), kind=kOutput, calls=%fused_computation.125 | convolution fusion | flops 68943872 | bytes 1900544 | tf_op jit(solution)/shard_map/dot_general | solution.py:280
  189.0 1.3 collective-permute-start.42
  190.4 1.6 add_convert_fusion
  192.8 2.9 %finish.13.rest_0_ = bf16[128,8192]{1,0:T(8,128)(2,1)} custom-call(s32[8]{0:T(128)} %dynamic-slice_bitcast_fusion.ids, bf16[128,1024]{1,0:T(8,128)(2,1)} %copy-done.25, bf16[8,128,1024]{2,1,0:T(8,128)(2,1)} %get-tuple-element.19.x_ref, bf16[1024,256]{1,0:T(8,128)(2,1)} %copy-done.26, ...), custom_call_target="tpu_custom_call", output_to_operand_aliasing={{}: (8, {})} | custom-call | flops 67108864 | bytes 1310720 | tf_op jit(solution)/shard_map/finish/pallas_call | solution.py:126
  195.8 3.1 %finish.14.rest_0_ = bf16[128,8192]{1,0:T(8,128)(2,1)} custom-call(s32[8]{0:T(128)} %dynamic-slice_bitcast_fusion.ids, bf16[128,1024]{1,0:T(8,128)(2,1)} %copy-done.20, bf16[8,128,1024]{2,1,0:T(8,128)(2,1)} %get-tuple-element.19.x_ref, bf16[1024,256]{1,0:T(8,128)(2,1)} %collective-permute-done.1.down_ref, ...), custom_call_target="tpu_custom_call", output_to_operand_aliasing={{}: (8, {})} | custom-call | flops 67108864 | bytes 1310720 | tf_op jit(solution)/shard_map/finish/pallas_call | solution.py:126
  198.9 1.6 add_convert_fusion.4
  200.4 1.8 collective-permute-start.44
  204.1 1.4 convert_add_fusion
  206.6 3.1 %collective-permute-done.44 = bf16[256,1024]{0,1:T(8,128)(2,1)S(1)} collective-permute-done((bf16[256,1024]{0,1:T(8,128)(2,1)S(1)}, bf16[256,1024]{0,1:T(8,128)(2,1)S(1)}, u32[]{:S(2)}, u32[]{:S(2)}) %collective-permute-start.44) | collective-permute-done | bytes 524320 | tf_op jit(solution)/shard_map/ppermute | solution.py:170
  210.2 3.1 %finish.15 = bf16[128,8192]{1,0:T(8,128)(2,1)} custom-call(s32[8]{0:T(128)} %dynamic-slice_bitcast_fusion.ids, bf16[128,1024]{1,0:T(8,128)(2,1)} %copy-done.24, bf16[8,128,1024]{2,1,0:T(8,128)(2,1)} %get-tuple-element.19.x_ref, bf16[1024,256]{1,0:T(8,128)(2,1)} %copy-done.9, ...), custom_call_target="tpu_custom_call", output_to_operand_aliasing={{}: (8, {})} | custom-call | flops 67108864 | bytes 1310720 | tf_op jit(solution)/shard_map/finish/pallas_call | solution.py:126
  213.3 1.8 multiply_bitcast_fusion
  (226 shorter events, 57.8 us)
Async XLA Ops:
  0.6 6.2 %collective-permute-start = (bf16[512,256]{1,0:T(8,128)(2,1)}, bf16[512,256]{1,0:T(8,128)(2,1)S(1)}, u32[]{:S(2)}, u32[]{:S(2)}) collective-permute-start(bf16[512,256]{1,0:T(8,128)(2,1)} %bitcast.270), channel_id=1, source_target_pairs={{0,1},{1,0},{2,3},{3,2},{4,5},{5,4},{6,7},{7,6},{8,9},{9,8},{10,11... | collective-permute-start | bytes 786440 | tf_op jit(solution)/shard_map/ppermute | solution.py:167
  1.2 10.5 %collective-permute-start.9 = (bf16[512,256]{1,0:T(8,128)(2,1)}, bf16[512,256]{1,0:T(8,128)(2,1)S(1)}, u32[]{:S(2)}, u32[]{:S(2)}) collective-permute-start(bf16[512,256]{1,0:T(8,128)(2,1)} %bitcast.272), channel_id=1, source_target_pairs={{0,1},{1,0},{2,3},{3,2},{4,5},{5,4},{6,7},{7,6},{8,9},{9,8},{10,11... | collective-permute-start | bytes 786440 | tf_op jit(solution)/shard_map/ppermute | solution.py:167
  1.2 69.9 %collective-permute-start.18 = (bf16[512,256]{1,0:T(8,128)(2,1)}, bf16[512,256]{1,0:T(8,128)(2,1)}, u32[]{:S(2)}, u32[]{:S(2)}) collective-permute-start(bf16[512,256]{1,0:T(8,128)(2,1)} %bitcast.273), channel_id=1, source_target_pairs={{0,16},{1,17},{2,18},{3,19},{4,20},{5,21},{6,22},{7,23},{8,24},{9,... | collective-permute-start | bytes 786440 | tf_op jit(solution)/shard_map/ppermute | solution.py:207
  8.0 26.4 %copy-start.9 = (bf16[1024,256]{1,0:T(8,128)(2,1)}, bf16[1024,256]{1,0:T(8,128)(2,1)S(1)}, u32[]{:S(2)}) copy-start(bf16[1024,256]{1,0:T(8,128)(2,1)S(1)} %maximum_select_fusion.down_ref) | copy-start | bytes 1572868
  8.0 9.3 %collective-permute-start.1 = (bf16[1024,256]{1,0:T(8,128)(2,1)S(1)}, bf16[1024,256]{1,0:T(8,128)(2,1)}, u32[]{:S(2)}, u32[]{:S(2)}) collective-permute-start(bf16[1024,256]{1,0:T(8,128)(2,1)S(1)} %maximum_select_fusion.down_ref), channel_id=1, source_target_pairs={{2,6},{6,10},{10,14},{14,12},{12,8},{8,4},{4,0},{0,2},{3,1},{7,3},... | collective-permute-start | bytes 1572872 | tf_op jit(solution)/shard_map/ppermute | solution.py:170
  11.9 11.1 %collective-permute-start.10 = (bf16[1024,256]{1,0:T(8,128)(2,1)S(1)}, bf16[1024,256]{1,0:T(8,128)(2,1)}, u32[]{:S(2)}, u32[]{:S(2)}) collective-permute-start(bf16[1024,256]{1,0:T(8,128)(2,1)S(1)} %maximum_select_fusion.2), channel_id=1, source_target_pairs={{2,6},{6,10},{10,14},{14,12},{12,8},{8,4},{4,0},{0,2},{3,1},{7,3},... | collective-permute-start | bytes 1572872 | tf_op jit(solution)/shard_map/ppermute | solution.py:170
  17.4 15.5 %collective-permute-start.3 = (bf16[1024,256]{1,0:T(8,128)(2,1)}, bf16[1024,256]{1,0:T(8,128)(2,1)}, u32[]{:S(2)}, u32[]{:S(2)}) collective-permute-start(bf16[1024,256]{1,0:T(8,128)(2,1)} %collective-permute-done.1.down_ref), channel_id=1, source_target_pairs={{2,6},{6,10},{10,14},{14,12},{12,8},{8,4},{4,0},{0,2},{3,1},{7,3},... | collective-permute-start | bytes 1572872 | tf_op jit(solution)/shard_map/ppermute | solution.py:170
  23.0 15.9 %collective-permute-start.12 = (bf16[1024,256]{1,0:T(8,128)(2,1)}, bf16[1024,256]{1,0:T(8,128)(2,1)}, u32[]{:S(2)}, u32[]{:S(2)}) collective-permute-start(bf16[1024,256]{1,0:T(8,128)(2,1)} %collective-permute-done.10), channel_id=1, source_target_pairs={{2,6},{6,10},{10,14},{14,12},{12,8},{8,4},{4,0},{0,2},{3,1},{7,3},... | collective-permute-start | bytes 1572872 | tf_op jit(solution)/shard_map/ppermute | solution.py:170
  31.3 14.9 %copy-start.6 = (bf16[8,128,1024]{2,1,0:T(8,128)(2,1)S(1)}, bf16[8,128,1024]{2,1,0:T(8,128)(2,1)}, u32[]{:S(2)}) copy-start(bf16[8,128,1024]{2,1,0:T(8,128)(2,1)} %get-tuple-element.20) | copy-start | bytes 6291460
  32.8 9.4 %collective-permute-start.5 = (bf16[1024,256]{1,0:T(8,128)(2,1)}, bf16[1024,256]{1,0:T(8,128)(2,1)S(1)}, u32[]{:S(2)}, u32[]{:S(2)}) collective-permute-start(bf16[1024,256]{1,0:T(8,128)(2,1)} %collective-permute-done.3.down_ref), channel_id=1, source_target_pairs={{2,6},{6,10},{10,14},{14,12},{12,8},{8,4},{4,0},{0,2},{3,1},{7,3},... | collective-permute-start | bytes 1572872 | tf_op jit(solution)/shard_map/ppermute | solution.py:170
  35.7 8.9 %collective-permute-start.2 = (bf16[1024,256]{1,0:T(8,128)(2,1)}, bf16[1024,256]{1,0:T(8,128)(2,1)S(1)}, u32[]{:S(2)}, u32[]{:S(2)}) collective-permute-start(bf16[1024,256]{1,0:T(8,128)(2,1)} %collective-permute-done.1.down_ref), channel_id=1, source_target_pairs={{0,1},{1,0},{2,3},{3,2},{4,5},{5,4},{6,7},{7,6},{8,9},{9,8},{10,11... | collective-permute-start | bytes 1572872 | tf_op jit(solution)/shard_map/ppermute | solution.py:167
  37.1 28.8 %collective-permute-start.11 = (bf16[1024,256]{1,0:T(8,128)(2,1)}, bf16[1024,256]{1,0:T(8,128)(2,1)}, u32[]{:S(2)}, u32[]{:S(2)}) collective-permute-start(bf16[1024,256]{1,0:T(8,128)(2,1)} %collective-permute-done.10), channel_id=1, source_target_pairs={{0,1},{1,0},{2,3},{3,2},{4,5},{5,4},{6,7},{7,6},{8,9},{9,8},{10,11... | collective-permute-start | bytes 1572872 | tf_op jit(solution)/shard_map/ppermute | solution.py:167
  39.0 15.2 %collective-permute-start.4 = (bf16[1024,256]{1,0:T(8,128)(2,1)}, bf16[1024,256]{1,0:T(8,128)(2,1)}, u32[]{:S(2)}, u32[]{:S(2)}) collective-permute-start(bf16[1024,256]{1,0:T(8,128)(2,1)} %collective-permute-done.3.down_ref), channel_id=1, source_target_pairs={{0,1},{1,0},{2,3},{3,2},{4,5},{5,4},{6,7},{7,6},{8,9},{9,8},{10,11... | collective-permute-start | bytes 1572872 | tf_op jit(solution)/shard_map/ppermute | solution.py:167
  42.3 14.7 %collective-permute-start.14 = (bf16[1024,256]{1,0:T(8,128)(2,1)}, bf16[1024,256]{1,0:T(8,128)(2,1)S(1)}, u32[]{:S(2)}, u32[]{:S(2)}) collective-permute-start(bf16[1024,256]{1,0:T(8,128)(2,1)} %collective-permute-done.12), channel_id=1, source_target_pairs={{2,6},{6,10},{10,14},{14,12},{12,8},{8,4},{4,0},{0,2},{3,1},{7,3},... | collective-permute-start | bytes 1572872 | tf_op jit(solution)/shard_map/ppermute | solution.py:170
  44.6 10.9 %collective-permute-start.7 = (bf16[512,256]{1,0:T(8,128)(2,1)}, bf16[512,256]{1,0:T(8,128)(2,1)S(1)}, u32[]{:S(2)}, u32[]{:S(2)}) collective-permute-start(bf16[512,256]{1,0:T(8,128)(2,1)} %slice_select_fusion.1), channel_id=1, source_target_pairs={{2,6},{6,10},{10,14},{14,12},{12,8},{8,4},{4,0},{0,2},{3,1},{7,3},... | collective-permute-start | bytes 786440 | tf_op jit(solution)/shard_map/ppermute | solution.py:170
  54.1 18.6 %collective-permute-start.20 = (bf16[1024,256]{1,0:T(8,128)(2,1)}, bf16[1024,256]{1,0:T(8,128)(2,1)S(1)}, u32[]{:S(2)}, u32[]{:S(2)}) collective-permute-start(bf16[1024,256]{1,0:T(8,128)(2,1)} %collective-permute-done.10), channel_id=1, source_target_pairs={{0,16},{1,17},{2,18},{3,19},{4,20},{5,21},{6,22},{7,23},{8,24},{9,... | collective-permute-start | bytes 1572872 | tf_op jit(solution)/shard_map/ppermute | solution.py:207
  55.5 2.1 collective-permute-start.8
  57.0 2.1 collective-permute-start.6
  57.6 15.2 %collective-permute-start.13 = (bf16[1024,256]{1,0:T(8,128)(2,1)}, bf16[1024,256]{1,0:T(8,128)(2,1)S(1)}, u32[]{:S(2)}, u32[]{:S(2)}) collective-permute-start(bf16[1024,256]{1,0:T(8,128)(2,1)} %collective-permute-done.12), channel_id=1, source_target_pairs={{0,1},{1,0},{2,3},{3,2},{4,5},{5,4},{6,7},{7,6},{8,9},{9,8},{10,11... | collective-permute-start | bytes 1572872 | tf_op jit(solution)/shard_map/ppermute | solution.py:167
  57.9 31.4 %copy-start.13 = (bf16[1024,256]{1,0:T(8,128)(2,1)}, bf16[1024,256]{1,0:T(8,128)(2,1)S(1)}, u32[]{:S(2)}) copy-start(bf16[1024,256]{1,0:T(8,128)(2,1)S(1)} %maximum_select_fusion.1.down_ref) | copy-start | bytes 1572868
  59.1 38.5 %copy-start.30 = (bf16[1024,256]{1,0:T(8,128)(2,1)}, bf16[1024,256]{1,0:T(8,128)(2,1)S(1)}, u32[]{:S(2)}) copy-start(bf16[1024,256]{1,0:T(8,128)(2,1)S(1)} %collective-permute-done.6.down_ref) | copy-start | bytes 1572868
  59.1 8.1 %collective-permute-start.16 = (bf16[512,256]{1,0:T(8,128)(2,1)S(1)}, bf16[512,256]{1,0:T(8,128)(2,1)S(1)}, u32[]{:S(2)}, u32[]{:S(2)}) collective-permute-start(bf16[512,256]{1,0:T(8,128)(2,1)S(1)} %slice_select_fusion), channel_id=1, source_target_pairs={{2,6},{6,10},{10,14},{14,12},{12,8},{8,4},{4,0},{0,2},{3,1},{7,3},... | collective-permute-start | bytes 786440 | tf_op jit(solution)/shard_map/ppermute | solution.py:170
  61.3 26.9 %copy-start.14 = (bf16[128,1024]{1,0:T(8,128)(2,1)}, bf16[128,1024]{1,0:T(8,128)(2,1)S(1)}, u32[]{:S(2)}) copy-start(bf16[128,1024]{1,0:T(8,128)(2,1)S(1)} %fusion.48) | copy-start | bytes 786436
  65.9 14.0 %collective-permute-start.22 = (bf16[1024,256]{1,0:T(8,128)(2,1)}, bf16[1024,256]{1,0:T(8,128)(2,1)S(1)}, u32[]{:S(2)}, u32[]{:S(2)}) collective-permute-start(bf16[1024,256]{1,0:T(8,128)(2,1)} %collective-permute-done.12), channel_id=1, source_target_pairs={{0,16},{1,17},{2,18},{3,19},{4,20},{5,21},{6,22},{7,23},{8,24},{9,... | collective-permute-start | bytes 1572872 | tf_op jit(solution)/shard_map/ppermute | solution.py:207
  67.2 3.0 %collective-permute-start.17 = (bf16[512,256]{1,0:T(8,128)(2,1)S(1)}, bf16[512,256]{1,0:T(8,128)(2,1)S(1)}, u32[]{:S(2)}, u32[]{:S(2)}) collective-permute-start(bf16[512,256]{1,0:T(8,128)(2,1)S(1)} %collective-permute-done.16), channel_id=1, source_target_pairs={{0,1},{1,0},{2,3},{3,2},{4,5},{5,4},{6,7},{7,6},{8,9},{9,8},{10,11... | collective-permute-start | bytes 786440 | tf_op jit(solution)/shard_map/ppermute | solution.py:167
  70.2 15.2 %collective-permute-start.15 = (bf16[1024,256]{1,0:T(8,128)(2,1)S(1)}, bf16[1024,256]{1,0:T(8,128)(2,1)S(1)}, u32[]{:S(2)}, u32[]{:S(2)}) collective-permute-start(bf16[1024,256]{1,0:T(8,128)(2,1)S(1)} %collective-permute-done.14), channel_id=1, source_target_pairs={{0,1},{1,0},{2,3},{3,2},{4,5},{5,4},{6,7},{7,6},{8,9},{9,8},{10,11... | collective-permute-start | bytes 1572872 | tf_op jit(solution)/shard_map/ppermute | solution.py:167
  71.1 14.3 %collective-permute-start.26 = (bf16[512,256]{1,0:T(8,128)(2,1)S(1)}, bf16[512,256]{1,0:T(8,128)(2,1)S(1)}, u32[]{:S(2)}, u32[]{:S(2)}) collective-permute-start(bf16[512,256]{1,0:T(8,128)(2,1)S(1)} %collective-permute-done.16), channel_id=1, source_target_pairs={{0,16},{1,17},{2,18},{3,19},{4,20},{5,21},{6,22},{7,23},{8,24},{9,... | collective-permute-start | bytes 786440 | tf_op jit(solution)/shard_map/ppermute | solution.py:207
  72.7 25.3 %collective-permute-start.19 = (bf16[512,256]{1,0:T(8,128)(2,1)}, bf16[512,256]{1,0:T(8,128)(2,1)S(1)}, u32[]{:S(2)}, u32[]{:S(2)}) collective-permute-start(bf16[512,256]{1,0:T(8,128)(2,1)} %collective-permute-done.18), channel_id=1, source_target_pairs={{0,1},{1,0},{2,3},{3,2},{4,5},{5,4},{6,7},{7,6},{8,9},{9,8},{10,11... | collective-permute-start | bytes 786440 | tf_op jit(solution)/shard_map/ppermute | solution.py:167
  72.8 27.9 %collective-permute-start.21 = (bf16[1024,256]{1,0:T(8,128)(2,1)S(1)}, bf16[1024,256]{1,0:T(8,128)(2,1)S(1)}, u32[]{:S(2)}, u32[]{:S(2)}) collective-permute-start(bf16[1024,256]{1,0:T(8,128)(2,1)S(1)} %collective-permute-done.20), channel_id=1, source_target_pairs={{0,1},{1,0},{2,3},{3,2},{4,5},{5,4},{6,7},{7,6},{8,9},{9,8},{10,11... | collective-permute-start | bytes 1572872 | tf_op jit(solution)/shard_map/ppermute | solution.py:167
  73.6 28.4 %copy-start.16 = (bf16[128,1024]{1,0:T(8,128)(2,1)}, bf16[128,1024]{1,0:T(8,128)(2,1)S(1)}, u32[]{:S(2)}) copy-start(bf16[128,1024]{1,0:T(8,128)(2,1)S(1)} %fusion.52) | copy-start | bytes 786436
  79.9 16.2 %collective-permute-start.24 = (bf16[1024,256]{1,0:T(8,128)(2,1)S(1)}, bf16[1024,256]{1,0:T(8,128)(2,1)S(1)}, u32[]{:S(2)}, u32[]{:S(2)}) collective-permute-start(bf16[1024,256]{1,0:T(8,128)(2,1)S(1)} %collective-permute-done.14), channel_id=1, source_target_pairs={{0,16},{1,17},{2,18},{3,19},{4,20},{5,21},{6,22},{7,23},{8,24},{9,... | collective-permute-start | bytes 1572872 | tf_op jit(solution)/shard_map/ppermute | solution.py:207
  85.4 18.7 %collective-permute-start.23 = (bf16[1024,256]{1,0:T(8,128)(2,1)S(1)}, bf16[1024,256]{1,0:T(8,128)(2,1)S(1)}, u32[]{:S(2)}, u32[]{:S(2)}) collective-permute-start(bf16[1024,256]{1,0:T(8,128)(2,1)S(1)} %collective-permute-done.22), channel_id=1, source_target_pairs={{0,1},{1,0},{2,3},{3,2},{4,5},{5,4},{6,7},{7,6},{8,9},{9,8},{10,11... | collective-permute-start | bytes 1572872 | tf_op jit(solution)/shard_map/ppermute | solution.py:167
  85.4 19.9 %collective-permute-start.27 = (bf16[512,256]{1,0:T(8,128)(2,1)S(1)}, bf16[512,256]{1,0:T(8,128)(2,1)S(1)}, u32[]{:S(2)}, u32[]{:S(2)}) collective-permute-start(bf16[512,256]{1,0:T(8,128)(2,1)S(1)} %collective-permute-done.26), channel_id=1, source_target_pairs={{0,1},{1,0},{2,3},{3,2},{4,5},{5,4},{6,7},{7,6},{8,9},{9,8},{10,11... | collective-permute-start | bytes 786440 | tf_op jit(solution)/shard_map/ppermute | solution.py:167
  96.1 17.1 %collective-permute-start.28 = (bf16[128,1024]{1,0:T(8,128)(2,1)S(1)}, bf16[128,1024]{1,0:T(8,128)(2,1)S(1)}, u32[]{:S(2)}, u32[]{:S(2)}) collective-permute-start(bf16[128,1024]{1,0:T(8,128)(2,1)S(1)} %fusion.63), channel_id=1, source_target_pairs={{16,0},{17,1},{18,2},{19,3},{20,4},{21,5},{22,6},{23,7},{24,8},{25... | collective-permute-start | bytes 786440 | tf_op jit(solution)/shard_map/ppermute | solution.py:260
  98.0 13.9 %collective-permute-start.33 = (bf16[128,1024]{1,0:T(8,128)(2,1)S(1)}, bf16[128,1024]{1,0:T(8,128)(2,1)S(1)}, u32[]{:S(2)}, u32[]{:S(2)}) collective-permute-start(bf16[128,1024]{1,0:T(8,128)(2,1)S(1)} %fusion.62), channel_id=1, source_target_pairs={{16,0},{17,1},{18,2},{19,3},{20,4},{21,5},{22,6},{23,7},{24,8},{25... | collective-permute-start | bytes 786440 | tf_op jit(solution)/shard_map/ppermute | solution.py:260
  100.7 21.9 %collective-permute-start.25 = (bf16[1024,256]{1,0:T(8,128)(2,1)S(1)}, bf16[1024,256]{1,0:T(8,128)(2,1)S(1)}, u32[]{:S(2)}, u32[]{:S(2)}) collective-permute-start(bf16[1024,256]{1,0:T(8,128)(2,1)S(1)} %collective-permute-done.24), channel_id=1, source_target_pairs={{0,1},{1,0},{2,3},{3,2},{4,5},{5,4},{6,7},{7,6},{8,9},{9,8},{10,11... | collective-permute-start | bytes 1572872 | tf_op jit(solution)/shard_map/ppermute | solution.py:167
  111.9 9.4 %collective-permute-start.34 = (bf16[128,1024]{1,0:T(8,128)(2,1)S(1)}, bf16[128,1024]{1,0:T(8,128)(2,1)S(1)}, u32[]{:S(2)}, u32[]{:S(2)}) collective-permute-start(bf16[128,1024]{1,0:T(8,128)(2,1)S(1)} %fusion.61), channel_id=1, source_target_pairs={{16,0},{17,1},{18,2},{19,3},{20,4},{21,5},{22,6},{23,7},{24,8},{25... | collective-permute-start | bytes 786440 | tf_op jit(solution)/shard_map/ppermute | solution.py:260
  114.4 35.7 %collective-permute-start.46 = (bf16[256,1024]{0,1:T(8,128)(2,1)}, bf16[256,1024]{0,1:T(8,128)(2,1)}, u32[]{:S(2)}, u32[]{:S(2)}) collective-permute-start(bf16[256,1024]{0,1:T(8,128)(2,1)} %convolution_convert_fusion.7), channel_id=1, source_target_pairs={{0,1},{2,3},{4,5},{6,7},{8,9},{10,11},{12,13},{14,15},{16,17},{18,... | collective-permute-start | bytes 1572872 | tf_op jit(solution)/shard_map/ppermute | solution.py:267
  121.3 26.5 %collective-permute-start.35 = (bf16[128,1024]{1,0:T(8,128)(2,1)}, bf16[128,1024]{1,0:T(8,128)(2,1)}, u32[]{:S(2)}, u32[]{:S(2)}) collective-permute-start(bf16[128,1024]{1,0:T(8,128)(2,1)} %fusion.60), channel_id=1, source_target_pairs={{16,0},{17,1},{18,2},{19,3},{20,4},{21,5},{22,6},{23,7},{24,8},{25... | collective-permute-start | bytes 786440 | tf_op jit(solution)/shard_map/ppermute | solution.py:260
  122.6 12.6 %copy-start.21 = (bf16[128,1024]{1,0:T(8,128)(2,1)}, bf16[128,1024]{1,0:T(8,128)(2,1)S(1)}, u32[]{:S(2)}) copy-start(bf16[128,1024]{1,0:T(8,128)(2,1)S(1)} %broadcast_select_fusion.2.cot_ref) | copy-start | bytes 786436
  122.9 9.9 %collective-permute-start.29 = (f32[128,256]{1,0:T(8,128)S(1)}, f32[128,256]{1,0:T(8,128)S(1)}, u32[]{:S(2)}, u32[]{:S(2)}) collective-permute-start(f32[128,256]{1,0:T(8,128)S(1)} %fusion.64), channel_id=1, source_target_pairs={{16,0},{17,1},{18,2},{19,3},{20,4},{21,5},{22,6},{23,7},{24,8},{25... | collective-permute-start | bytes 393224 | tf_op jit(solution)/shard_map/ppermute | solution.py:260
  125.4 34.5 %collective-permute-start.48 = (bf16[256,1024]{0,1:T(8,128)(2,1)}, bf16[256,1024]{0,1:T(8,128)(2,1)}, u32[]{:S(2)}, u32[]{:S(2)}) collective-permute-start(bf16[256,1024]{0,1:T(8,128)(2,1)} %convolution_convert_fusion.6), channel_id=1, source_target_pairs={{0,1},{1,0},{2,3},{3,2},{4,5},{5,4},{6,7},{7,6},{8,9},{9,8},{10,11... | collective-permute-start | bytes 1572872 | tf_op jit(solution)/shard_map/ppermute | solution.py:167
  136.4 19.0 %collective-permute-start.30 = (bf16[128,1024]{1,0:T(8,128)(2,1)}, bf16[128,1024]{1,0:T(8,128)(2,1)}, u32[]{:S(2)}, u32[]{:S(2)}) collective-permute-start(bf16[128,1024]{1,0:T(8,128)(2,1)} %fusion.58), channel_id=1, source_target_pairs={{16,0},{17,1},{18,2},{19,3},{20,4},{21,5},{22,6},{23,7},{24,8},{25... | collective-permute-start | bytes 786440 | tf_op jit(solution)/shard_map/ppermute | solution.py:260
  138.4 46.9 %collective-permute-start.41 = (bf16[256,1024]{0,1:T(8,128)(2,1)}, bf16[256,1024]{0,1:T(8,128)(2,1)}, u32[]{:S(2)}, u32[]{:S(2)}) collective-permute-start(bf16[256,1024]{0,1:T(8,128)(2,1)} %convolution_convert_fusion.12), channel_id=1, source_target_pairs={{0,1},{1,0},{2,3},{3,2},{4,5},{5,4},{6,7},{7,6},{8,9},{9,8},{10,11... | collective-permute-start | bytes 1572872 | tf_op jit(solution)/shard_map/ppermute | solution.py:167
  147.8 4.8 %collective-permute-start.37 = (bf16[256,1024]{0,1:T(8,128)(2,1)S(1)}, bf16[256,1024]{0,1:T(8,128)(2,1)S(1)}, u32[]{:S(2)}, u32[]{:S(2)}) collective-permute-start(bf16[256,1024]{0,1:T(8,128)(2,1)S(1)} %convolution_convert_fusion.15), channel_id=1, source_target_pairs={{1,0},{3,2},{5,4},{7,6},{9,8},{11,10},{13,12},{15,14},{17,16},{19,... | collective-permute-start | bytes 1572872 | tf_op jit(solution)/shard_map/ppermute | solution.py:267
  150.1 12.8 %copy-start.22 = (bf16[128,1024]{1,0:T(8,128)(2,1)S(1)}, bf16[128,1024]{1,0:T(8,128)(2,1)}, u32[]{:S(2)}) copy-start(bf16[128,1024]{1,0:T(8,128)(2,1)} %broadcast_select_fusion.1.cot_ref) | copy-start | bytes 786436
  151.6 9.7 %collective-permute-start.47 = (bf16[256,1024]{0,1:T(8,128)(2,1)S(1)}, bf16[256,1024]{0,1:T(8,128)(2,1)S(1)}, u32[]{:S(2)}, u32[]{:S(2)}) collective-permute-start(bf16[256,1024]{0,1:T(8,128)(2,1)S(1)} %add_convert_fusion.3), channel_id=1, source_target_pairs={{3,1},{7,3},{11,7},{15,11},{13,15},{9,13},{5,9},{1,5},{19,17},{23,... | collective-permute-start | bytes 1572872 | tf_op jit(solution)/shard_map/ppermute | solution.py:268
  152.6 16.3 %collective-permute-start.39 = (bf16[256,1024]{0,1:T(8,128)(2,1)S(1)}, bf16[256,1024]{0,1:T(8,128)(2,1)S(1)}, u32[]{:S(2)}, u32[]{:S(2)}) collective-permute-start(bf16[256,1024]{0,1:T(8,128)(2,1)S(1)} %copy-done.29), channel_id=1, source_target_pairs={{0,1},{1,0},{2,3},{3,2},{4,5},{5,4},{6,7},{7,6},{8,9},{9,8},{10,11... | collective-permute-start | bytes 1572872 | tf_op jit(solution)/shard_map/ppermute | solution.py:167
  155.4 14.9 %collective-permute-start.38 = (bf16[256,1024]{0,1:T(8,128)(2,1)S(1)}, bf16[256,1024]{0,1:T(8,128)(2,1)S(1)}, u32[]{:S(2)}, u32[]{:S(2)}) collective-permute-start(bf16[256,1024]{0,1:T(8,128)(2,1)S(1)} %add_convert_fusion.7), channel_id=1, source_target_pairs={{2,6},{6,10},{10,14},{14,12},{12,8},{8,4},{4,0},{0,2},{18,22},{22,... | collective-permute-start | bytes 1572872 | tf_op jit(solution)/shard_map/ppermute | solution.py:268
  159.9 17.5 %copy-start.23 = (bf16[128,1024]{1,0:T(8,128)(2,1)}, bf16[128,1024]{1,0:T(8,128)(2,1)S(1)}, u32[]{:S(2)}) copy-start(bf16[128,1024]{1,0:T(8,128)(2,1)S(1)} %broadcast_select_fusion.3.cot_ref) | copy-start | bytes 786436
  159.9 8.3 %collective-permute-start.36 = (bf16[128,1024]{1,0:T(8,128)(2,1)S(1)}, bf16[128,1024]{1,0:T(8,128)(2,1)S(1)}, u32[]{:S(2)}, u32[]{:S(2)}) collective-permute-start(bf16[128,1024]{1,0:T(8,128)(2,1)S(1)} %copy-done.32), channel_id=1, source_target_pairs={{16,0},{17,1},{18,2},{19,3},{20,4},{21,5},{22,6},{23,7},{24,8},{25... | collective-permute-start | bytes 786440 | tf_op jit(solution)/shard_map/ppermute | solution.py:260
  161.2 12.7 %collective-permute-start.50 = (bf16[256,1024]{0,1:T(8,128)(2,1)S(1)}, bf16[256,1024]{0,1:T(8,128)(2,1)S(1)}, u32[]{:S(2)}, u32[]{:S(2)}) collective-permute-start(bf16[256,1024]{0,1:T(8,128)(2,1)S(1)} %convolution_convert_fusion.4), channel_id=1, source_target_pairs={{0,1},{1,0},{2,3},{3,2},{4,5},{5,4},{6,7},{7,6},{8,9},{9,8},{10,11... | collective-permute-start | bytes 1572872 | tf_op jit(solution)/shard_map/ppermute | solution.py:167
  168.2 9.2 %collective-permute-start.49 = (bf16[256,1024]{0,1:T(8,128)(2,1)S(1)}, bf16[256,1024]{0,1:T(8,128)(2,1)S(1)}, u32[]{:S(2)}, u32[]{:S(2)}) collective-permute-start(bf16[256,1024]{0,1:T(8,128)(2,1)S(1)} %add_convert_fusion.2), channel_id=1, source_target_pairs={{2,6},{6,10},{10,14},{14,12},{12,8},{8,4},{4,0},{0,2},{3,1},{7,3},... | collective-permute-start | bytes 1572872 | tf_op jit(solution)/shard_map/ppermute | solution.py:170
  169.0 16.3 %collective-permute-start.31 = (bf16[128,1024]{1,0:T(8,128)(2,1)}, bf16[128,1024]{1,0:T(8,128)(2,1)S(1)}, u32[]{:S(2)}, u32[]{:S(2)}) collective-permute-start(bf16[128,1024]{1,0:T(8,128)(2,1)} %fusion.57), channel_id=1, source_target_pairs={{16,0},{17,1},{18,2},{19,3},{20,4},{21,5},{22,6},{23,7},{24,8},{25... | collective-permute-start | bytes 786440 | tf_op jit(solution)/shard_map/ppermute | solution.py:260
  171.5 15.2 %collective-permute-start.40 = (bf16[256,1024]{0,1:T(8,128)(2,1)}, bf16[256,1024]{0,1:T(8,128)(2,1)}, u32[]{:S(2)}, u32[]{:S(2)}) collective-permute-start(bf16[256,1024]{0,1:T(8,128)(2,1)} %add_convert_fusion.6), channel_id=1, source_target_pairs={{2,6},{6,10},{10,14},{14,12},{12,8},{8,4},{4,0},{0,2},{3,1},{7,3},... | collective-permute-start | bytes 1572872 | tf_op jit(solution)/shard_map/ppermute | solution.py:170
  174.0 16.4 %collective-permute-start.52 = (bf16[256,1024]{0,1:T(8,128)(2,1)}, bf16[256,1024]{0,1:T(8,128)(2,1)}, u32[]{:S(2)}, u32[]{:S(2)}) collective-permute-start(bf16[256,1024]{0,1:T(8,128)(2,1)} %convolution_convert_fusion.2), channel_id=1, source_target_pairs={{0,1},{1,0},{2,3},{3,2},{4,5},{5,4},{6,7},{7,6},{8,9},{9,8},{10,11... | collective-permute-start | bytes 1572872 | tf_op jit(solution)/shard_map/ppermute | solution.py:167
  178.6 11.8 %collective-permute-start.51 = (bf16[256,1024]{0,1:T(8,128)(2,1)}, bf16[256,1024]{0,1:T(8,128)(2,1)}, u32[]{:S(2)}, u32[]{:S(2)}) collective-permute-start(bf16[256,1024]{0,1:T(8,128)(2,1)} %add_convert_fusion.1), channel_id=1, source_target_pairs={{2,6},{6,10},{10,14},{14,12},{12,8},{8,4},{4,0},{0,2},{3,1},{7,3},... | collective-permute-start | bytes 1572872 | tf_op jit(solution)/shard_map/ppermute | solution.py:170
  185.3 13.5 %collective-permute-start.43 = (bf16[256,1024]{0,1:T(8,128)(2,1)}, bf16[256,1024]{0,1:T(8,128)(2,1)}, u32[]{:S(2)}, u32[]{:S(2)}) collective-permute-start(bf16[256,1024]{0,1:T(8,128)(2,1)} %convolution_convert_fusion.10), channel_id=1, source_target_pairs={{0,1},{1,0},{2,3},{3,2},{4,5},{5,4},{6,7},{7,6},{8,9},{9,8},{10,11... | collective-permute-start | bytes 1572872 | tf_op jit(solution)/shard_map/ppermute | solution.py:167
  185.3 16.9 %collective-permute-start.32 = (bf16[128,1024]{1,0:T(8,128)(2,1)}, bf16[128,1024]{1,0:T(8,128)(2,1)}, u32[]{:S(2)}, u32[]{:S(2)}) collective-permute-start(bf16[128,1024]{1,0:T(8,128)(2,1)} %fusion.56), channel_id=1, source_target_pairs={{16,0},{17,1},{18,2},{19,3},{20,4},{21,5},{22,6},{23,7},{24,8},{25... | collective-permute-start | bytes 786440 | tf_op jit(solution)/shard_map/ppermute | solution.py:260
  189.0 9.8 %collective-permute-start.42 = (bf16[256,1024]{0,1:T(8,128)(2,1)}, bf16[256,1024]{0,1:T(8,128)(2,1)}, u32[]{:S(2)}, u32[]{:S(2)}) collective-permute-start(bf16[256,1024]{0,1:T(8,128)(2,1)} %add_convert_fusion.5), channel_id=1, source_target_pairs={{2,6},{6,10},{10,14},{14,12},{12,8},{8,4},{4,0},{0,2},{3,1},{7,3},... | collective-permute-start | bytes 1572872 | tf_op jit(solution)/shard_map/ppermute | solution.py:170
  192.0 12.1 %collective-permute-start.53 = (bf16[256,1024]{0,1:T(8,128)(2,1)S(1)}, bf16[256,1024]{0,1:T(8,128)(2,1)}, u32[]{:S(2)}, u32[]{:S(2)}) collective-permute-start(bf16[256,1024]{0,1:T(8,128)(2,1)S(1)} %add_convert_fusion), channel_id=1, source_target_pairs={{2,6},{6,10},{10,14},{14,12},{12,8},{8,4},{4,0},{0,2},{3,1},{7,3},... | collective-permute-start | bytes 1572872 | tf_op jit(solution)/shard_map/ppermute | solution.py:170
  200.4 9.2 %collective-permute-start.44 = (bf16[256,1024]{0,1:T(8,128)(2,1)S(1)}, bf16[256,1024]{0,1:T(8,128)(2,1)S(1)}, u32[]{:S(2)}, u32[]{:S(2)}) collective-permute-start(bf16[256,1024]{0,1:T(8,128)(2,1)S(1)} %add_convert_fusion.4), channel_id=1, source_target_pairs={{2,6},{6,10},{10,14},{14,12},{12,8},{8,4},{4,0},{0,2},{3,1},{7,3},... | collective-permute-start | bytes 1572872 | tf_op jit(solution)/shard_map/ppermute | solution.py:170
  206.4 6.9 %collective-permute-start.54 = (bf16[256,512]{0,1:T(8,128)(2,1)}, bf16[256,512]{0,1:T(8,128)(2,1)}, u32[]{:S(2)}, u32[]{:S(2)}) collective-permute-start(bf16[256,512]{0,1:T(8,128)(2,1)} %select_convert_fusion), channel_id=1, source_target_pairs={{0,1},{1,0},{2,3},{3,2},{4,5},{5,4},{6,7},{7,6},{8,9},{9,8},{10,11... | collective-permute-start | bytes 786440 | tf_op jit(solution)/shard_map/ppermute | solution.py:167
  210.1 5.0 %collective-permute-start.45 = (bf16[256,512]{0,1:T(8,128)(2,1)S(1)}, bf16[256,512]{0,1:T(8,128)(2,1)S(1)}, u32[]{:S(2)}, u32[]{:S(2)}) collective-permute-start(bf16[256,512]{0,1:T(8,128)(2,1)S(1)} %select_convert_fusion.1), channel_id=1, source_target_pairs={{0,1},{1,0},{2,3},{3,2},{4,5},{5,4},{6,7},{7,6},{8,9},{9,8},{10,11... | collective-permute-start | bytes 786440 | tf_op jit(solution)/shard_map/ppermute | solution.py:167
  (32 other events, 157.2 us)

commit v3 on v0

v3 whole, which is shorter than its diff:
```python
import functools

import jax
import jax.numpy as jnp
import numpy as np
from jax import lax
from jax.experimental import pallas as pl
from jax.experimental.pallas import tpu as pltpu
from jax.sharding import PartitionSpec as P

Z_CHIPS = 4
CORES = 2
EPSILON = 1e-05
F32 = jnp.float32
BF16 = jnp.bfloat16
VMEM = pl.BlockSpec(memory_space=pltpu.VMEM)
SMEM = pl.BlockSpec(memory_space=pltpu.SMEM)
ANY = pl.BlockSpec(memory_space=pl.ANY)
NT = (((1,), (1,)), ((), ()))


def ring_of_chips(chips):
    rows = chips // Z_CHIPS
    cycle = []
    for z in range(Z_CHIPS):
        ys = range(1, rows) if z % 2 == 0 else range(rows - 1, 0, -1)
        cycle += [z * rows + y for y in ys]
    return cycle + [z * rows for z in range(Z_CHIPS - 1, -1, -1)]


class Routes:
    def __init__(self, devices):
        ring = ring_of_chips(devices // CORES)
        n = self.n = len(ring)
        half = self.half = n // 2
        self.partner = [(i, i ^ 1) for i in range(devices)]
        self.onward = [
            (ring[i] * CORES + c, ring[(i + 1 - 2 * c) % n] * CORES + c) for c in range(CORES) for i in range(n)
        ]
        steps = [s for k in range(1, half) for s in (-k, k)] + [half, 0]
        self.table = np.zeros((devices, n), np.int32)
        for i, chip in enumerate(ring):
            for c in range(CORES):
                self.table[chip * CORES + c] = [ring[(i + (1 - 2 * c) * s) % n] for s in steps]
        self.opposite, self.own = n - 2, n - 1
        leaving = [self.opposite] + [f(k) for k in range(half - 1, 0, -1) for f in (self.ahead, self.behind)] + [self.own]
        self.groups = [leaving[:3], leaving[3:]]

    def behind(self, k):
        return 2 * k - 2

    def ahead(self, k):
        return 2 * k - 1


def after(value, *earlier):
    return lax.optimization_barrier((value, *earlier))[0] if earlier else value


def call(body, outs, *args, specs=None, out_specs=None, scratch=(), flops=0, aliases=None, vmem=8, name=None):
    single = not isinstance(outs, (list, tuple))
    outs = [outs] if single else list(outs)
    moved = sum(a.size * a.dtype.itemsize for a in args) + sum(o.size * o.dtype.itemsize for o in outs)
    result = pl.pallas_call(
        body,
        in_specs=specs or [VMEM] * len(args),
        out_specs=out_specs or [VMEM] * len(outs),
        out_shape=outs,
        scratch_shapes=scratch,
        input_output_aliases=aliases or {},
        cost_estimate=pl.CostEstimate(flops=flops, bytes_accessed=moved // 4, transcendentals=0),
        compiler_params=pltpu.CompilerParams(vmem_limit_bytes=vmem << 20),
        name=name,
    )(*args)
    return result[0] if single else result


class Place:
    def __init__(self, sections, table_ref):
        self.table, self.sections, self.n = table_ref, sections, table_ref.shape[1]

    def __getitem__(self, slot):
        return self.table[lax.axis_index("dp"), slot]

    def first(self):
        return lax.axis_index("dp") % CORES == 0

    def last(self):
        return lax.axis_index("section") == self.sections - 1


def placed(body, sections):
    def kernel(table_ref, *refs):
        body(Place(sections, table_ref), *refs)

    return kernel


def shape(dtype, *dims):
    return jax.ShapeDtypeStruct(dims, dtype)


def columns(ref, chip, block):
    return ref[:, pl.ds(pl.multiple_of(chip * block, block), block)]


def scale_kernel(block, x_ref, gain_ref, conf_ref, down_ref, inv_ref, scaled_ref, weight_ref, down_t_ref):
    tokens, width = x_ref.shape
    squares = jnp.zeros((tokens, block), F32)
    for at in range(0, width, block):
        values = x_ref[:, at : at + block].astype(F32)
        squares = squares + values * values
    inverse = lax.rsqrt(jnp.sum(squares, axis=-1, keepdims=True) / width + EPSILON)
    inv_ref[...] = inverse
    for at in range(0, width, block):
        values = x_ref[:, at : at + block].astype(F32)
        scaled_ref[:, at : at + block] = ((values * inverse) * gain_ref[:, at : at + block]).astype(BF16)
    weights = jnp.broadcast_to(conf_ref[...].astype(F32) / 256.0, (tokens, tokens))
    row = lax.broadcasted_iota(jnp.int32, (tokens, tokens), 0)
    column = lax.broadcasted_iota(jnp.int32, (tokens, tokens), 1)
    weight_ref[...] = jnp.sum(jnp.where(row == column, weights, 0.0), axis=1, keepdims=True)
    down_t_ref[...] = down_ref[...].astype(F32).T


def fetch(sources, held, sems):
    copies = [pltpu.make_async_copy(ref, held.at[i], sems.at[i]) for i, ref in enumerate(sources)]
    for copy in copies:
        copy.start()
    return copies


def assemble_kernel(mine_ref, other_ref, out_ref, sems):
    rows = mine_ref.shape[0]
    core = lax.axis_index("dp") % CORES
    copies = []
    for i, (ref, place) in enumerate(((mine_ref, core), (other_ref, 1 - core))):
        out = out_ref.at[pl.ds(pl.multiple_of(place * rows, rows), rows)]
        copies.append(pltpu.make_async_copy(ref, out, sems.at[i]))
        copies[-1].start()
    for copy in copies:
        copy.wait()


def pick_kernel(zero_ref, one_ref, out_ref, sem):
    core = lax.axis_index("dp") % CORES
    for at, ref in enumerate((zero_ref, one_ref)):

        @pl.when(core == at)
        def _():
            copy = pltpu.make_async_copy(ref, out_ref, sem)
            copy.start()
            copy.wait()


def pre_grad_of(hidden_grad, slope, preact, width):
    pre_grad = (hidden_grad * slope).astype(BF16)
    return pre_grad, jnp.sum(pre_grad.astype(F32) * preact, axis=-1, keepdims=True) / width


def top_kernel(groups, meta, x_ref, t_ref, scaled_ref, weight_ref, *refs):
    n = meta.n
    held, held_x, sems, sems_x = refs[-4:]
    pre_out, mean_out, hid_out, slope_out, preact_out, sum_out, *tops = refs[2 * n : -4]
    width = x_ref.shape[1]
    block = width // n
    order = [slot for group in groups for slot in group]
    copies = fetch(refs[: 2 * n], held, sems)
    x_copies = {}
    for i, slot in enumerate(order):
        place = pl.ds(pl.multiple_of(meta[slot] * block, block), block)
        for at, ref in enumerate((x_ref, t_ref)):
            x_copies[i, at] = pltpu.make_async_copy(ref.at[:, place], held_x.at[i, at], sems_x.at[i, at])
            x_copies[i, at].start()
    preact = jnp.zeros(preact_out.shape, F32)
    for slot in range(n):
        copies[slot].wait()
        preact = preact + jnp.dot(columns(scaled_ref, meta[slot], block), held[slot], preferred_element_type=F32)
    sigmoid_val = 1.0 / (1.0 + jnp.exp(-preact))
    slope = sigmoid_val * (1.0 + preact * (1.0 - sigmoid_val))
    hidden = preact * sigmoid_val
    preact_out[...] = preact
    slope_out[...] = slope
    hid_out[...] = hidden.T.astype(BF16)
    hidden = hidden.astype(BF16)
    weight = weight_ref[...]
    total = jnp.zeros_like(preact)
    i = 0
    for group, top_ref in zip(groups, tops):
        for at, slot in enumerate(group):
            copies[n + slot].wait()
            branch = lax.dot_general(hidden, held[n + slot], NT, preferred_element_type=F32)
            x_copies[i, 0].wait()
            x_copies[i, 1].wait()
            values = held_x[i, 0].astype(F32) + branch - held_x[i, 1].astype(F32)
            top = (weight * values).astype(BF16)
            top_ref[at] = top
            total = total + jnp.dot(top, held[n + slot], preferred_element_type=F32)
            i += 1
    sum_out[...] = total
    pre_out[...], mean_out[...] = pre_grad_of(total, slope, preact, width)


def input_grad(cot, x, down, gain, pre_grad, inverse, mean):
    grad = lax.dot_general(pre_grad, down, NT, preferred_element_type=F32)
    return (cot.astype(F32) + inverse * (grad * gain - x.astype(F32) * inverse * mean)).astype(BF16)


def leave_kernel(slots, meta, cot_ref, x_ref, gain_ref, pre_ref, inv_ref, mean_ref, *refs):
    downs, out_ref = refs[:-1], refs[-1]
    for at, slot in enumerate(slots):
        block = downs[at].shape[0]
        x, gain = columns(x_ref, meta[slot], block), columns(gain_ref, meta[slot], block)
        out_ref[at] = input_grad(cot_ref[at], x, downs[at][...], gain, pre_ref[...], inv_ref[...], mean_ref[...])


def arrive_kernel(follows, meta, arrived_ref, top_ref, hid_ref, *refs):
    count = arrived_ref.shape[0]
    total = refs[0][...] if follows else 0.0
    refs = refs[1:] if follows else refs
    ups, (cot_ref, sum_out, *parts) = refs[:count], refs[count:]
    for at in range(count):
        cot = jnp.where(meta.last(), top_ref[at], arrived_ref[at])
        cot_ref[at] = cot
        parts[at][...] = jnp.dot(hid_ref[...], cot, preferred_element_type=F32).astype(BF16)
        total = total + jnp.dot(cot, ups[at][...], preferred_element_type=F32)
    sum_out[...] = total


def pre_grad_kernel(width, sum_ref, slope_ref, preact_ref, pre_out, pre_t_out, mean_out):
    hidden_grad = sum_ref[...]
    slope = slope_ref[...]
    pre_out[...], mean_out[...] = pre_grad_of(hidden_grad, slope, preact_ref[...], width)
    pre_t_out[...] = (hidden_grad * slope).T.astype(BF16)


def products_kernel(slots, stacked, meta, scaled_ref, pre_t_ref, *outs):
    block = outs[0].shape[-1]
    for at, slot in enumerate(slots):
        part = jnp.dot(pre_t_ref[...], columns(scaled_ref, meta[slot], block), preferred_element_type=F32)
        if stacked:
            outs[0][at] = part.astype(BF16)
        else:
            outs[at][...] = part.astype(BF16)


def add_kernel(picks, *refs):
    out_ref = refs[-1]
    total = None
    for ref, pick in zip(refs[:-1], picks):
        value = (ref[...] if pick is None else ref[pick]).astype(F32)
        total = value if total is None else total + value
    out_ref[...] = total.astype(out_ref.dtype)


def add(out, *terms):
    arrays = [t[0] if isinstance(t, tuple) else t for t in terms]
    picks = [t[1] if isinstance(t, tuple) else None for t in terms]
    return call(functools.partial(add_kernel, picks), out, *arrays, name="add")


def split_kernel(meta, total_ref, part_ref, mine_ref, other_ref):
    half = mine_ref.shape[1]
    first = meta.first()
    low = total_ref[:, :half].astype(F32) + part_ref[:, :half].astype(F32)
    high = total_ref[:, half:].astype(F32) + part_ref[:, half:].astype(F32)
    mine_ref[...] = jnp.where(first, low, high)
    other_ref[...] = jnp.where(first, high, low).astype(BF16)


def close_kernel(tokens, mine_ref, other_ref, grad_ref):
    grad_ref[0] = ((mine_ref[...] + other_ref[...].astype(F32)) / tokens).T


def close_gain_kernel(tokens, meta, mine_ref, other_ref, down_t_ref, gain_ref, grad_ref, gain_grad_ref):
    grad = (mine_ref[...] + other_ref[...].astype(F32)) / tokens
    grad_ref[0] = grad.T
    columns_own = grad.shape[1]
    gain = columns(gain_ref, lax.axis_index("dp"), columns_own)
    gain_grad_ref[...] = jnp.sum(grad * down_t_ref[...], axis=0, keepdims=True) / gain


def finish_kernel(groups, meta, x_ref, gain_ref, pre_ref, inv_ref, mean_ref, *refs):
    slots = [slot for group in groups for slot in group]
    downs, cots = refs[: len(slots)], refs[len(slots) : len(slots) + len(groups)]
    out_ref, held, sems = refs[-3:]
    copies = []
    for group, cot_ref in zip(groups, cots):
        for at, slot in enumerate(group):
            i = len(copies)
            down = downs[i][...]
            block = down.shape[0]
            chip = meta[slot]
            x, gain = columns(x_ref, chip, block), columns(gain_ref, chip, block)
            held[i] = input_grad(cot_ref[at], x, down, gain, pre_ref[...], inv_ref[...], mean_ref[...])
            place = out_ref.at[:, pl.ds(pl.multiple_of(chip * block, block), block)]
            copies.append(pltpu.make_async_copy(held.at[i], place, sems.at[i]))
            copies[-1].start()
    for copy in copies:
        copy.wait()


def local(section_inputs, teacher_states, confidence, gains, w_down, w_up):
    sections = lax.axis_size("section")
    devices = lax.axis_size("dp")
    routes = Routes(devices)
    n, half, opposite, own, groups = routes.n, routes.half, routes.opposite, routes.own, routes.groups
    behind, ahead = routes.behind, routes.ahead
    x = section_inputs[0]
    tokens, width = x.shape
    block = width // n
    rank = w_down.shape[2]
    half_block = block // CORES
    back = [(s, s - 1) for s in range(1, sections)]
    groups_of = [range(0, 1), range(1, 2)]

    def swap(value):
        return lax.ppermute(value, "dp", routes.partner)

    def onward(value):
        return lax.ppermute(value, "dp", routes.onward)

    chunk, part_shape = shape(BF16, block, rank), shape(BF16, rank, block)

    def of_chip(mine, other):
        return call(
            assemble_kernel, chunk, mine, other, specs=[ANY] * 2, scratch=[pltpu.SemaphoreType.DMA((2,))], name="assemble"
        )

    def pick(zero, one):
        return call(pick_kernel, chunk, zero, one, specs=[ANY] * 2, scratch=[pltpu.SemaphoreType.DMA], name="pick")

    down, up = w_down[0], w_up[0]
    downs, ups = {}, {}
    downs[own] = of_chip(down, swap(down))
    ups[own] = of_chip(up, swap(up))
    table = jnp.asarray(routes.table)

    def with_meta(body, outs, *args, **kw):
        specs = [SMEM] + kw.pop("specs", [VMEM] * len(args))
        return call(placed(body, sections), outs, table, *args, specs=specs, **kw)

    inverse, scaled, weight_rows, down_t = call(
        functools.partial(scale_kernel, block),
        [shape(F32, tokens, 1), shape(BF16, tokens, width), shape(F32, tokens, 1), shape(F32, rank, half_block)],
        after(x, downs[own]), gains, confidence[None], down, name="scale",
    )
    down_block, up_block = downs[own], after(ups[own], scaled)
    for k in range(1, half):
        earlier = [downs[ahead(k - 2)], ups[ahead(k - 2)]] if k >= 3 else []
        downs[behind(k)] = down_block = onward(after(down_block, *earlier))
        ups[behind(k)] = up_block = onward(up_block)
        downs[ahead(k)] = swap(down_block)
        ups[ahead(k)] = swap(up_block)
    earlier = [downs[ahead(half - 2)], ups[ahead(half - 2)]] if half >= 3 else []
    mine = onward(after(pick(down_block, up_block), *earlier))
    other = swap(mine)
    downs[opposite], ups[opposite] = pick(mine, other), pick(other, mine)

    rank_f32, rank_bf16 = shape(F32, tokens, rank), shape(BF16, tokens, rank)
    pre_grad, mean, hidden_t, slope, preact, own_sum, *tops = with_meta(
        functools.partial(top_kernel, groups),
        [rank_bf16, shape(F32, tokens, 1), shape(BF16, rank, tokens), rank_f32, rank_f32, rank_f32]
        + [shape(BF16, len(slots), tokens, block) for slots in groups],
        x, teacher_states, scaled, weight_rows, *(downs[j] for j in range(n)), *(ups[j] for j in range(n)),
        specs=[ANY] * 2 + [VMEM] * 2 + [ANY] * (2 * n),
        scratch=[
            pltpu.VMEM((2 * n, block, rank), BF16),
            pltpu.VMEM((n, 2, tokens, block), BF16),
            pltpu.SemaphoreType.DMA((2 * n,)),
            pltpu.SemaphoreType.DMA((n, 2)),
        ],
        flops=6 * tokens * width * rank, vmem=24, name="top",
    )

    def leave(slots, cot, pre_grad, mean):
        return with_meta(
            functools.partial(leave_kernel, slots), shape(BF16, len(slots), tokens, block),
            cot, x, gains, pre_grad, inverse, mean, *(downs[j] for j in slots),
            flops=2 * len(slots) * tokens * block * rank, name="leave",
        )

    def arrive(slots, value, top, total):
        cot, total, *parts = with_meta(
            functools.partial(arrive_kernel, total is not None),
            [shape(BF16, *value.shape), rank_f32] + [part_shape] * len(slots),
            value, top, hidden_t, *([] if total is None else [total]), *(ups[j] for j in slots),
            flops=4 * len(slots) * tokens * block * rank, name="arrive",
        )
        return cot, parts, total

    def rank_grad(total):
        return call(
            functools.partial(pre_grad_kernel, width),
            [rank_bf16, shape(BF16, rank, tokens), shape(F32, tokens, 1)],
            total, slope, preact, name="pre_grad",
        )


    def split(total, part):
        return with_meta(
            split_kernel, [shape(F32, rank, half_block), shape(BF16, rank, half_block)],
            total, part, name="split",
        )

    cots = tops
    for hop in range(sections - 1):
        sent = [leave(slots, cot, pre_grad, mean) for slots, cot in zip(groups, cots)]
        if hop < sections - 2:
            arrived, cots = [], []
            hidden_grad = None
            for i, value in enumerate(sent):
                arrived.append(lax.ppermute(after(value, *arrived[i - 2 : i - 1] if i >= 2 else ()), "section", back))
                cot, _, hidden_grad = arrive(groups[i], arrived[i], tops[i], hidden_grad)
                cots.append(cot)
            pre_grad, _, mean = rank_grad(hidden_grad)

    arrived = [lax.ppermute(value, "section", back) for value in sent]
    near_cot, parts, hidden_grad = arrive(groups[0], after(arrived[0], sent[1]), tops[0], None)
    total = onward(parts[0])
    total = onward(add(part_shape, total, parts[1], swap(parts[2])))
    cot, parts, hidden_grad = arrive(groups[1], after(arrived[1], total), tops[1], hidden_grad)
    cots = [near_cot, cot]
    for k in range(half - 2, 0, -1):
        at = 2 * (half - 2 - k)
        total = onward(add(part_shape, total, parts[at], swap(parts[at + 1])))
    up_mine, up_other = split(total, parts[-1])
    up_other = swap(up_other)
    grad_up = call(
        functools.partial(close_kernel, tokens), shape(F32, 1, half_block, rank), up_mine, up_other, name="close_up"
    )

    pre_grad, pre_t, mean = rank_grad(hidden_grad)

    def products(slots, stacked=False):
        return with_meta(
            functools.partial(products_kernel, slots, stacked),
            shape(BF16, len(slots), rank, block) if stacked else [part_shape] * len(slots), scaled, pre_t,
            flops=2 * len(slots) * tokens * block * rank, name="products",
        )

    (far,) = products([opposite])
    total = onward(far)
    behinds = products([behind(k) for k in range(1, half)], stacked=True)
    aheads = products([ahead(k) for k in range(1, half)])
    swapped = swap(behinds)

    def finish(some, so_far):
        slots = [j for i in some for j in groups[i]]
        args = [x, gains, pre_grad, inverse, mean, *(downs[j] for j in slots), *(cots[i] for i in some)]
        given = [] if so_far is None else [so_far]
        return with_meta(
            functools.partial(finish_kernel, [groups[i] for i in some]), shape(BF16, tokens, width), *args, *given,
            specs=[VMEM] * len(args) + [ANY] * len(given), out_specs=[ANY],
            scratch=[pltpu.VMEM((len(slots), tokens, block), BF16), pltpu.SemaphoreType.DMA((len(slots),))],
            aliases={len(args) + 1: 0} if given else {},
            flops=2 * len(slots) * tokens * block * rank, name="finish",
        )

    (mine,) = products([own])
    input_grads = finish(groups_of[0], None)
    for at, k in enumerate(range(half - 1, 0, -1)):
        part, other = aheads[k - 1], (swapped, k - 1)
        if at >= 1 and at < len(groups_of):
            input_grads = finish(groups_of[at], input_grads)
        total = after(total, input_grads)
        total = onward(add(part_shape, total, part, other))
    down_mine, down_other = split(total, mine)
    down_other = swap(down_other)
    grad_down, grad_gain = with_meta(
        functools.partial(close_gain_kernel, tokens),
        [shape(F32, 1, half_block, rank), shape(F32, 1, half_block)],
        down_mine, down_other, down_t, gains, name="close_down",
    )
    return input_grads[None], grad_down, grad_up, grad_gain


def solution(mesh):
    in_specs = (
        P("section", "dp", None),
        P("dp", None),
        P("dp"),
        P("section", None),
        P("section", "dp", None),
        P("section", "dp", None),
    )
    out_specs = (
        P("section", "dp", None),
        P("section", "dp", None),
        P("section", "dp", None),
        P("section", "dp"),
    )
    return jax.shard_map(local, mesh=mesh, in_specs=in_specs, out_specs=out_specs, check_vma=False)
```

time: 384 us -> 169 us (0.44)
  waiting for transfers between devices: 212 us -> 101 us
  blocking collectives: 59.9 us -> 0 us
  matrix products: 47.9 us -> 0 us
  Pallas kernels: 0 us -> 31.3 us
  other arithmetic: 26.3 us -> 0 us
  starting transfers between devices: 6.52 us -> 30.5 us
  between operations: 14.5 us -> 0.95 us
  local copies, waits for them, and re-layouts: 15.7 us -> 4.93 us
    all_gather x2 -> x0, waiting for transfers between devices: 106 us -> none  [the longest x1 54.7 us: local(): lax.all_gather(w_down[0], 'dp', axis=0, tiled=True)]
    unnamed x1 -> x0, blocking collectives: 59.9 us -> none
    dot_general x22 -> x0, matrix products: 47.9 us -> none  [the longest x5 16.2 us: run_step(): preact = jnp.dot(scaled, down_matrix, preferred_element_type=jnp.float32)]
    reduce_scatter x1 -> x0, waiting for transfers between devices: 40.4 us -> none  [local(): lax.psum_scatter(jnp.concatenate([down_part, up_part], axis=1).astype(jnp...]
    ppermute x5 -> x32, waiting for transfers between devices: 64.5 us -> 101 us  [the longest x15 64.2 us: onward(): return lax.ppermute(value, 'dp', routes.onward)]
    pallas_call x0 -> x28, Pallas kernels: none -> 31.3 us  [call(): pl.pallas_call(body, in_specs=specs or [VMEM] * len(args), out_specs=out_...]
    ppermute x5 -> x32, starting transfers between devices: 6.4 us -> 30.5 us  [the longest x15 26.1 us: onward(): return lax.ppermute(value, 'dp', routes.onward)]
    dynamic_update_slice x5 -> x0, other arithmetic: 15.1 us -> none  [write_rows(): lax.dynamic_update_slice_in_dim(buffer, jnp.where(active_step, fresh, pre...]
  transfers between devices with their start and end apart: 8 -> 32, of which waited for: 8 -> 21; matrix products, arithmetic and copies ran while one was open for 0% -> 0% of each run, Pallas kernels for 0% -> 10%
where the time goes in v3:
time: 169 us
  waiting for transfers between devices  101 us (60%)
  Pallas kernels  31.3 us (19%)
  starting transfers between devices  30.5 us (18%)
  local copies, waits for them, and re-layouts  4.93 us (3%)
    ppermute x15, waiting for transfers between devices, onward(): return lax.ppermute(value, 'dp', routes.onward)  64.2 us
    ppermute x2, waiting for transfers between devices, local(): arrived = [lax.ppermute(value, 'section', back) for value in sent]  32.4 us
    pallas_call x28, Pallas kernels, call(): pl.pallas_call(body, in_specs=specs or [VMEM] * len(args), out_specs=out_...  31.3 us
    ppermute x15, starting transfers between devices, onward(): return lax.ppermute(value, 'dp', routes.onward)  26.1 us
    unnamed x20, local copies, waits for them, and re-layouts  4.93 us
    ppermute x15, waiting for transfers between devices, swap(): return lax.ppermute(value, 'dp', routes.partner)  4.59 us
  transfers between devices with their start and end apart: 32, of which 21 were waited for; matrix products, arithmetic and copies ran while one was open for 0% of the time, Pallas kernels for 10%

profile of v3, /device:TPU:0, one launch (start us, length us, event | category | flops | bytes accessed | tf_op | source)
XLA Modules:
  0.0 169.0 jit_solution(1412391234414489363)
XLA Ops:
  0.6 0.5 collective-permute-start
  1.2 1.3 collective-permute-done.other_ref
  2.5 0.9 copy-done.6
  3.5 2.9 %collective-permute-start.1 = (bf16[1024,256]{1,0:T(8,128)(2,1)S(1)}, bf16[1024,256]{1,0:T(8,128)(2,1)S(1)}, u32[]{:S(2)}, u32[]{:S(2)}) collective-permute-start(bf16[1024,256]{1,0:T(8,128)(2,1)S(1)} %assemble.2.refs_11_.refs_10_.refs_9_), channel_id=1, source_target_pairs={{2,6},{6,10},{10,14},{14,12},{12,8},{8,4},{4,0},{0,2},{3,1},{7,3},... | collective-permute-start | bytes 1572872 | tf_op jit(solution)/shard_map/ppermute | solution.py:320
  6.5 1.6 copy-done
  8.1 0.8 copy-done.4
  8.8 0.9 copy-done.7
  9.8 0.7 copy-done.9
  10.4 1.1 scale.1
  11.6 1.6 collective-permute-start.6
  13.2 0.5 collective-permute-done.1.refs_4_.refs_9_.refs_8_
  13.7 2.0 %collective-permute-start.3 = (bf16[1024,256]{1,0:T(8,128)(2,1)S(1)}, bf16[1024,256]{1,0:T(8,128)(2,1)S(1)}, u32[]{:S(2)}, u32[]{:S(2)}) collective-permute-start(bf16[1024,256]{1,0:T(8,128)(2,1)S(1)} %collective-permute-done.1.refs_4_.refs_9_.refs_8_), channel_id=1, source_target_pairs={{2,6},{6,10},{10,14},{14,12},{12,8},{8,4},{4,0},{0,2},{3,1},{7,3},... | collective-permute-start | bytes 1572872 | tf_op jit(solution)/shard_map/ppermute | solution.py:320
  15.7 5.2 %collective-permute-done.6.refs_12_.refs_7_ = bf16[1024,256]{1,0:T(8,128)(2,1)S(1)} collective-permute-done((bf16[1024,256]{1,0:T(8,128)(2,1)S(1)}, bf16[1024,256]{1,0:T(8,128)(2,1)S(1)}, u32[]{:S(2)}, u32[]{:S(2)}) %collective-permute-start.6) | collective-permute-done | bytes 524320 | tf_op jit(solution)/shard_map/ppermute | solution.py:320
  20.8 1.6 collective-permute-start.10
  22.4 4.0 %collective-permute-done.3.refs_6_.refs_7_ = bf16[1024,256]{1,0:T(8,128)(2,1)S(1)} collective-permute-done((bf16[1024,256]{1,0:T(8,128)(2,1)S(1)}, bf16[1024,256]{1,0:T(8,128)(2,1)S(1)}, u32[]{:S(2)}, u32[]{:S(2)}) %collective-permute-start.3) | collective-permute-done | bytes 524320 | tf_op jit(solution)/shard_map/ppermute | solution.py:320
  26.5 5.6 %collective-permute-done.10.refs_14_.refs_5_ = bf16[1024,256]{1,0:T(8,128)(2,1)S(1)} collective-permute-done((bf16[1024,256]{1,0:T(8,128)(2,1)S(1)}, bf16[1024,256]{1,0:T(8,128)(2,1)S(1)}, u32[]{:S(2)}, u32[]{:S(2)}) %collective-permute-start.10) | collective-permute-done | bytes 524320 | tf_op jit(solution)/shard_map/ppermute | solution.py:320
  32.1 1.6 collective-permute-start.11
  33.7 1.6 collective-permute-start.8
  35.2 0.5 collective-permute-start.12
  35.7 5.5 %collective-permute-done.11.one_ref.refs_16_.refs_5_ = bf16[1024,256]{1,0:T(8,128)(2,1)S(1)} collective-permute-done((bf16[1024,256]{1,0:T(8,128)(2,1)S(1)}, bf16[1024,256]{1,0:T(8,128)(2,1)S(1)}, u32[]{:S(2)}, u32[]{:S(2)}) %collective-permute-start.11) | collective-permute-done | bytes 524320 | tf_op jit(solution)/shard_map/ppermute | solution.py:320
  41.3 5.6 %collective-permute-done.8.zero_ref.refs_8_.refs_7_ = bf16[1024,256]{1,0:T(8,128)(2,1)S(1)} collective-permute-done((bf16[1024,256]{1,0:T(8,128)(2,1)S(1)}, bf16[1024,256]{1,0:T(8,128)(2,1)S(1)}, u32[]{:S(2)}, u32[]{:S(2)}) %collective-permute-start.8) | collective-permute-done | bytes 524320 | tf_op jit(solution)/shard_map/ppermute | solution.py:320
  47.0 1.6 collective-permute-start.13
  48.6 7.6 %collective-permute-done.13.zero_ref.one_ref = bf16[1024,256]{1,0:T(8,128)(2,1)S(1)} collective-permute-done((bf16[1024,256]{1,0:T(8,128)(2,1)S(1)}, bf16[1024,256]{1,0:T(8,128)(2,1)S(1)}, u32[]{:S(2)}, u32[]{:S(2)}) %collective-permute-start.13) | collective-permute-done | bytes 524320 | tf_op jit(solution)/shard_map/ppermute | solution.py:320
  56.2 0.5 collective-permute-start.15
  56.7 1.4 collective-permute-done.14.one_ref.zero_ref
  58.3 0.6 collective-permute-done.15.refs_17_.refs_4_
  58.9 0.7 collective-permute-done.9.refs_9_.refs_7_.refs_6_
  59.7 8.8 %top.1 = (bf16[128,256]{1,0:T(8,128)(2,1)S(1)}, f32[128,1]{1,0:T(8,128)S(1)}, bf16[256,128]{1,0:T(8,128)(2,1)S(1)}, f32[128,256]{1,0:T(8,128)S(1)}, f32[128,256]...) custom-call(s32[16,8]{1,0:T(8,128)S(1)} %copy-done.3, ...), custom_call_target="tpu_custom_call" | custom-call | flops 1610612736 | bytes 4325760 | tf_op jit(solution)/shard_map/top/pallas_call | solution.py:64
  68.4 1.4 leave.3
  69.8 1.3 collective-permute-start.17
  71.1 1.8 %leave.2 = bf16[5,128,1024]{2,1,0:T(8,128)(2,1)S(1)} custom-call(s32[16,8]{1,0:T(8,128)S(1)} %copy-done.3, bf16[5,128,1024]{2,1,0:T(8,128)(2,1)S(1)} %get-tuple-element.54.refs_0_.refs_1_, bf16[128,8192]{1,0:T(8,128)(2,1)S(1)} %bitcast.8, f32[1,8192]{1,0:T(1,128)S(1)} %copy-done.5, bf16[128,256]{1,0:T(8,128)(2,1)S(1)} %get-tuple-element.55.refs_3_, ...), custom_call_target="tpu_custom_call" | custom-call | flops 335544320 | bytes 1859968 | tf_op jit(solution)/shard_map/leave/pallas_call | solution.py:64
  72.9 1.3 collective-permute-start.16
  74.2 17.9 %collective-permute-done.17.refs_0_ = bf16[3,128,1024]{2,1,0:T(8,128)(2,1)S(1)} collective-permute-done((bf16[3,128,1024]{2,1,0:T(8,128)(2,1)S(1)}, bf16[3,128,1024]{2,1,0:T(8,128)(2,1)S(1)}, u32[]{:S(2)}, u32[]{:S(2)}) %collective-permute-start.17) | collective-permute-done | bytes 786464 | tf_op jit(solution)/shard_map/ppermute | solution.py:417
  92.1 1.5 arrive.2
  93.6 1.6 collective-permute-start.18
  95.2 7.6 %collective-permute-done.18.refs_0_ = bf16[256,1024]{1,0:T(8,128)(2,1)S(1)} collective-permute-done((bf16[256,1024]{1,0:T(8,128)(2,1)S(1)}, bf16[256,1024]{1,0:T(8,128)(2,1)S(1)}, u32[]{:S(2)}, u32[]{:S(2)}) %collective-permute-start.18) | collective-permute-done | bytes 524320 | tf_op jit(solution)/shard_map/ppermute | solution.py:320
  103.0 1.8 %collective-permute-start.20 = (bf16[256,1024]{1,0:T(8,128)(2,1)S(1)}, bf16[256,1024]{1,0:T(8,128)(2,1)S(1)}, u32[]{:S(2)}, u32[]{:S(2)}) collective-permute-start(bf16[256,1024]{1,0:T(8,128)(2,1)S(1)} %add.6), channel_id=1, source_target_pairs={{2,6},{6,10},{10,14},{14,12},{12,8},{8,4},{4,0},{0,2},{3,1},{7,3},... | collective-permute-start | bytes 1572872 | tf_op jit(solution)/shard_map/ppermute | solution.py:320
  104.8 14.6 %collective-permute-done.16.refs_0_ = bf16[5,128,1024]{2,1,0:T(8,128)(2,1)S(1)} collective-permute-done((bf16[5,128,1024]{2,1,0:T(8,128)(2,1)S(1)}, bf16[5,128,1024]{2,1,0:T(8,128)(2,1)S(1)}, u32[]{:S(2)}, u32[]{:S(2)}) %collective-permute-start.16) | collective-permute-done | bytes 1310752 | tf_op jit(solution)/shard_map/ppermute | solution.py:417
  119.4 1.9 %arrive.3 = (bf16[5,128,1024]{2,1,0:T(8,128)(2,1)S(1)}, f32[128,256]{1,0:T(8,128)S(1)}, bf16[256,1024]{1,0:T(8,128)(2,1)S(1)}, bf16[256,1024]{1,0:T(8,128)(2,1)S...) custom-call(s32[16,8]{1,0:T(8,128)S(1)} %copy-done.3, ...), custom_call_target="tpu_custom_call" | custom-call | flops 671088640 | bytes 2375808 | tf_op jit(solution)/shard_map/arrive/pallas_call | solution.py:64
  121.4 1.2 products.6
  122.7 1.0 products.4
  123.7 1.6 collective-permute-start.21
  125.3 1.2 products.5
  126.6 2.1 %finish.2.refs_11_ = bf16[128,8192]{1,0:T(8,128)(2,1)} custom-call(s32[16,8]{1,0:T(8,128)S(1)} %copy-done.3, bf16[128,8192]{1,0:T(8,128)(2,1)S(1)} %bitcast.9, f32[1,8192]{1,0:T(1,128)S(1)} %copy-done.5, bf16[128,256]{1,0:T(8,128)(2,1)S(1)} %get-tuple-element.69.refs_2_, f32[128,1]{1,0:T(8,128)S(1)} %get-tuple-element.56.refs_4_.refs_3_, ...), custom_call_target="tpu_custom_call" | custom-call | flops 201326592 | bytes 1663360 | tf_op jit(solution)/shard_map/finish/pallas_call | solution.py:64
  128.7 4.2 %collective-permute-done.21.refs_0_ = bf16[256,1024]{1,0:T(8,128)(2,1)S(1)} collective-permute-done((bf16[256,1024]{1,0:T(8,128)(2,1)S(1)}, bf16[256,1024]{1,0:T(8,128)(2,1)S(1)}, u32[]{:S(2)}, u32[]{:S(2)}) %collective-permute-start.21) | collective-permute-done | bytes 524320 | tf_op jit(solution)/shard_map/ppermute | solution.py:320
  132.9 0.2 add.7
  133.1 1.6 collective-permute-start.23
  134.8 0.2 add.10
  135.0 1.6 collective-permute-start.28
  136.6 2.6 %finish.3 = bf16[128,8192]{1,0:T(8,128)(2,1)} custom-call(s32[16,8]{1,0:T(8,128)S(1)} %copy-done.3, bf16[128,8192]{1,0:T(8,128)(2,1)S(1)} %bitcast.10, f32[1,8192]{1,0:T(1,128)S(1)} %copy-done.5, bf16[128,256]{1,0:T(8,128)(2,1)S(1)} %get-tuple-element.69.refs_2_, f32[128,1]{1,0:T(8,128)S(1)} %get-tuple-element.56.refs_4_.refs_3_, ...), custom_call_target="tpu_custom_call", output_to_operand_aliasing={{}: (12, {})} | custom-call | flops 335544320 | bytes 2580864 | tf_op jit(solution)/shard_map/finish/pallas_call | solution.py:64
  139.2 3.2 %collective-permute-done.23.refs_0_ = bf16[256,1024]{1,0:T(8,128)(2,1)S(1)} collective-permute-done((bf16[256,1024]{1,0:T(8,128)(2,1)S(1)}, bf16[256,1024]{1,0:T(8,128)(2,1)S(1)}, u32[]{:S(2)}, u32[]{:S(2)}) %collective-permute-start.23) | collective-permute-done | bytes 524320 | tf_op jit(solution)/shard_map/ppermute | solution.py:320
  142.6 1.6 collective-permute-start.24
  144.2 3.8 %collective-permute-done.28.refs_0_ = bf16[256,1024]{1,0:T(8,128)(2,1)S(1)} collective-permute-done((bf16[256,1024]{1,0:T(8,128)(2,1)S(1)}, bf16[256,1024]{1,0:T(8,128)(2,1)S(1)}, u32[]{:S(2)}, u32[]{:S(2)}) %collective-permute-start.28) | collective-permute-done | bytes 524320 | tf_op jit(solution)/shard_map/ppermute | solution.py:320
  148.2 1.6 collective-permute-start.30
  149.8 3.8 %collective-permute-done.24.refs_0_ = bf16[256,1024]{1,0:T(8,128)(2,1)S(1)} collective-permute-done((bf16[256,1024]{1,0:T(8,128)(2,1)S(1)}, bf16[256,1024]{1,0:T(8,128)(2,1)S(1)}, u32[]{:S(2)}, u32[]{:S(2)}) %collective-permute-start.24) | collective-permute-done | bytes 524320 | tf_op jit(solution)/shard_map/ppermute | solution.py:320
  153.8 1.6 collective-permute-start.25
  155.4 1.0 products.7.refs_1_
  156.4 2.8 %collective-permute-done.30.refs_0_ = bf16[256,1024]{1,0:T(8,128)(2,1)S(1)} collective-permute-done((bf16[256,1024]{1,0:T(8,128)(2,1)S(1)}, bf16[256,1024]{1,0:T(8,128)(2,1)S(1)}, u32[]{:S(2)}, u32[]{:S(2)}) %collective-permute-start.30) | collective-permute-done | bytes 524320 | tf_op jit(solution)/shard_map/ppermute | solution.py:320
  159.2 0.8 split.3
  160.1 4.7 %collective-permute-done.25.refs_0_ = bf16[256,1024]{1,0:T(8,128)(2,1)S(1)} collective-permute-done((bf16[256,1024]{1,0:T(8,128)(2,1)S(1)}, bf16[256,1024]{1,0:T(8,128)(2,1)S(1)}, u32[]{:S(2)}, u32[]{:S(2)}) %collective-permute-start.25) | collective-permute-done | bytes 524320 | tf_op jit(solution)/shard_map/ppermute | solution.py:320
  164.8 0.8 split.2
  165.8 1.0 close_up.1
  166.8 0.5 collective-permute-done.26.refs_1_
  167.3 1.7 close_down.1
  (48 shorter events, 1.6 us)
Async XLA Ops:
  0.6 1.9 %collective-permute-start = (bf16[512,256]{1,0:T(8,128)(2,1)}, bf16[512,256]{1,0:T(8,128)(2,1)S(1)}, u32[]{:S(2)}, u32[]{:S(2)}) collective-permute-start(bf16[512,256]{1,0:T(8,128)(2,1)} %bitcast.11), channel_id=1, source_target_pairs={{0,1},{1,0},{2,3},{3,2},{4,5},{5,4},{6,7},{7,6},{8,9},{9,8},{10,11... | collective-permute-start | bytes 786440 | tf_op jit(solution)/shard_map/ppermute | solution.py:317
  1.1 10.4 %collective-permute-start.5 = (bf16[512,256]{1,0:T(8,128)(2,1)}, bf16[512,256]{1,0:T(8,128)(2,1)S(1)}, u32[]{:S(2)}, u32[]{:S(2)}) collective-permute-start(bf16[512,256]{1,0:T(8,128)(2,1)} %bitcast.14), channel_id=1, source_target_pairs={{0,1},{1,0},{2,3},{3,2},{4,5},{5,4},{6,7},{7,6},{8,9},{9,8},{10,11... | collective-permute-start | bytes 786440 | tf_op jit(solution)/shard_map/ppermute | solution.py:317
  2.5 0.9 copy-start.6
  3.5 8.1 %copy-start.8 = (bf16[1,512,256]{2,1,0:T(8,128)(2,1)S(1)}, bf16[1,512,256]{2,1,0:T(8,128)(2,1)}, u32[]{:S(2)}) copy-start(bf16[1,512,256]{2,1,0:T(8,128)(2,1)} %param.12) | copy-start | bytes 786436
  3.5 10.2 %collective-permute-start.1 = (bf16[1024,256]{1,0:T(8,128)(2,1)S(1)}, bf16[1024,256]{1,0:T(8,128)(2,1)S(1)}, u32[]{:S(2)}, u32[]{:S(2)}) collective-permute-start(bf16[1024,256]{1,0:T(8,128)(2,1)S(1)} %assemble.2.refs_11_.refs_10_.refs_9_), channel_id=1, source_target_pairs={{2,6},{6,10},{10,14},{14,12},{12,8},{8,4},{4,0},{0,2},{3,1},{7,3},... | collective-permute-start | bytes 1572872 | tf_op jit(solution)/shard_map/ppermute | solution.py:320
  6.5 1.6 copy-start
  8.1 0.8 copy-start.4
  8.8 0.9 copy-start.7
  9.8 0.7 copy-start.9
  11.6 9.2 %collective-permute-start.6 = (bf16[1024,256]{1,0:T(8,128)(2,1)S(1)}, bf16[1024,256]{1,0:T(8,128)(2,1)S(1)}, u32[]{:S(2)}, u32[]{:S(2)}) collective-permute-start(bf16[1024,256]{1,0:T(8,128)(2,1)S(1)} %assemble.3.refs_19_.refs_8_), channel_id=1, source_target_pairs={{2,6},{6,10},{10,14},{14,12},{12,8},{8,4},{4,0},{0,2},{3,1},{7,3},... | collective-permute-start | bytes 1572872 | tf_op jit(solution)/shard_map/ppermute | solution.py:320
  13.7 12.8 %collective-permute-start.3 = (bf16[1024,256]{1,0:T(8,128)(2,1)S(1)}, bf16[1024,256]{1,0:T(8,128)(2,1)S(1)}, u32[]{:S(2)}, u32[]{:S(2)}) collective-permute-start(bf16[1024,256]{1,0:T(8,128)(2,1)S(1)} %collective-permute-done.1.refs_4_.refs_9_.refs_8_), channel_id=1, source_target_pairs={{2,6},{6,10},{10,14},{14,12},{12,8},{8,4},{4,0},{0,2},{3,1},{7,3},... | collective-permute-start | bytes 1572872 | tf_op jit(solution)/shard_map/ppermute | solution.py:320
  15.7 10.8 %collective-permute-start.2 = (bf16[1024,256]{1,0:T(8,128)(2,1)S(1)}, bf16[1024,256]{1,0:T(8,128)(2,1)S(1)}, u32[]{:S(2)}, u32[]{:S(2)}) collective-permute-start(bf16[1024,256]{1,0:T(8,128)(2,1)S(1)} %collective-permute-done.1.refs_4_.refs_9_.refs_8_), channel_id=1, source_target_pairs={{0,1},{1,0},{2,3},{3,2},{4,5},{5,4},{6,7},{7,6},{8,9},{9,8},{10,11... | collective-permute-start | bytes 1572872 | tf_op jit(solution)/shard_map/ppermute | solution.py:317
  20.8 5.6 %collective-permute-start.7 = (bf16[1024,256]{1,0:T(8,128)(2,1)S(1)}, bf16[1024,256]{1,0:T(8,128)(2,1)S(1)}, u32[]{:S(2)}, u32[]{:S(2)}) collective-permute-start(bf16[1024,256]{1,0:T(8,128)(2,1)S(1)} %collective-permute-done.6.refs_12_.refs_7_), channel_id=1, source_target_pairs={{0,1},{1,0},{2,3},{3,2},{4,5},{5,4},{6,7},{7,6},{8,9},{9,8},{10,11... | collective-permute-start | bytes 1572872 | tf_op jit(solution)/shard_map/ppermute | solution.py:317
  20.8 11.2 %collective-permute-start.10 = (bf16[1024,256]{1,0:T(8,128)(2,1)S(1)}, bf16[1024,256]{1,0:T(8,128)(2,1)S(1)}, u32[]{:S(2)}, u32[]{:S(2)}) collective-permute-start(bf16[1024,256]{1,0:T(8,128)(2,1)S(1)} %collective-permute-done.6.refs_12_.refs_7_), channel_id=1, source_target_pairs={{2,6},{6,10},{10,14},{14,12},{12,8},{8,4},{4,0},{0,2},{3,1},{7,3},... | collective-permute-start | bytes 1572872 | tf_op jit(solution)/shard_map/ppermute | solution.py:320
  32.1 9.2 %collective-permute-start.11 = (bf16[1024,256]{1,0:T(8,128)(2,1)S(1)}, bf16[1024,256]{1,0:T(8,128)(2,1)S(1)}, u32[]{:S(2)}, u32[]{:S(2)}) collective-permute-start(bf16[1024,256]{1,0:T(8,128)(2,1)S(1)} %collective-permute-done.10.refs_14_.refs_5_), channel_id=1, source_target_pairs={{2,6},{6,10},{10,14},{14,12},{12,8},{8,4},{4,0},{0,2},{3,1},{7,3},... | collective-permute-start | bytes 1572872 | tf_op jit(solution)/shard_map/ppermute | solution.py:320
  33.7 13.2 %collective-permute-start.8 = (bf16[1024,256]{1,0:T(8,128)(2,1)S(1)}, bf16[1024,256]{1,0:T(8,128)(2,1)S(1)}, u32[]{:S(2)}, u32[]{:S(2)}) collective-permute-start(bf16[1024,256]{1,0:T(8,128)(2,1)S(1)} %collective-permute-done.3.refs_6_.refs_7_), channel_id=1, source_target_pairs={{2,6},{6,10},{10,14},{14,12},{12,8},{8,4},{4,0},{0,2},{3,1},{7,3},... | collective-permute-start | bytes 1572872 | tf_op jit(solution)/shard_map/ppermute | solution.py:320
  35.2 11.7 %collective-permute-start.4 = (bf16[1024,256]{1,0:T(8,128)(2,1)S(1)}, bf16[1024,256]{1,0:T(8,128)(2,1)S(1)}, u32[]{:S(2)}, u32[]{:S(2)}) collective-permute-start(bf16[1024,256]{1,0:T(8,128)(2,1)S(1)} %collective-permute-done.3.refs_6_.refs_7_), channel_id=1, source_target_pairs={{0,1},{1,0},{2,3},{3,2},{4,5},{5,4},{6,7},{7,6},{8,9},{9,8},{10,11... | collective-permute-start | bytes 1572872 | tf_op jit(solution)/shard_map/ppermute | solution.py:317
  35.2 11.7 %collective-permute-start.12 = (bf16[1024,256]{1,0:T(8,128)(2,1)S(1)}, bf16[1024,256]{1,0:T(8,128)(2,1)S(1)}, u32[]{:S(2)}, u32[]{:S(2)}) collective-permute-start(bf16[1024,256]{1,0:T(8,128)(2,1)S(1)} %collective-permute-done.10.refs_14_.refs_5_), channel_id=1, source_target_pairs={{0,1},{1,0},{2,3},{3,2},{4,5},{5,4},{6,7},{7,6},{8,9},{9,8},{10,11... | collective-permute-start | bytes 1572872 | tf_op jit(solution)/shard_map/ppermute | solution.py:317
  46.9 12.7 %copy-start.2 = (bf16[128,8192]{1,0:T(8,128)(2,1)S(1)}, bf16[128,8192]{1,0:T(8,128)(2,1)}, u32[]{:S(2)}) copy-start(bf16[128,8192]{1,0:T(8,128)(2,1)} %refs_1_.3) | copy-start | bytes 6291460
  46.9 12.7 %copy-start.1 = (bf16[1,128,8192]{2,1,0:T(8,128)(2,1)S(1)}, bf16[1,128,8192]{2,1,0:T(8,128)(2,1)}, u32[]{:S(2)}) copy-start(bf16[1,128,8192]{2,1,0:T(8,128)(2,1)} %param.7) | copy-start | bytes 6291460
  46.9 12.7 %copy-start.3 = (s32[16,8]{1,0:T(8,128)S(1)}, s32[16,8]{1,0:T(8,128)}, u32[]{:S(2)}) copy-start(s32[16,8]{1,0:T(8,128)} %constant.2.clone.table_ref) | copy-start | bytes 1540
  47.0 9.2 %collective-permute-start.13 = (bf16[1024,256]{1,0:T(8,128)(2,1)S(1)}, bf16[1024,256]{1,0:T(8,128)(2,1)S(1)}, u32[]{:S(2)}, u32[]{:S(2)}) collective-permute-start(bf16[1024,256]{1,0:T(8,128)(2,1)S(1)} %pick.3), channel_id=1, source_target_pairs={{2,6},{6,10},{10,14},{14,12},{12,8},{8,4},{4,0},{0,2},{3,1},{7,3},... | collective-permute-start | bytes 1572872 | tf_op jit(solution)/shard_map/ppermute | solution.py:320
  56.2 1.9 %collective-permute-start.14 = (bf16[1024,256]{1,0:T(8,128)(2,1)S(1)}, bf16[1024,256]{1,0:T(8,128)(2,1)S(1)}, u32[]{:S(2)}, u32[]{:S(2)}) collective-permute-start(bf16[1024,256]{1,0:T(8,128)(2,1)S(1)} %collective-permute-done.13.zero_ref.one_ref), channel_id=1, source_target_pairs={{0,1},{1,0},{2,3},{3,2},{4,5},{5,4},{6,7},{7,6},{8,9},{9,8},{10,11... | collective-permute-start | bytes 1572872 | tf_op jit(solution)/shard_map/ppermute | solution.py:317
  56.2 2.7 %collective-permute-start.15 = (bf16[1024,256]{1,0:T(8,128)(2,1)S(1)}, bf16[1024,256]{1,0:T(8,128)(2,1)S(1)}, u32[]{:S(2)}, u32[]{:S(2)}) collective-permute-start(bf16[1024,256]{1,0:T(8,128)(2,1)S(1)} %collective-permute-done.11.one_ref.refs_16_.refs_5_), channel_id=1, source_target_pairs={{0,1},{1,0},{2,3},{3,2},{4,5},{5,4},{6,7},{7,6},{8,9},{9,8},{10,11... | collective-permute-start | bytes 1572872 | tf_op jit(solution)/shard_map/ppermute | solution.py:317
  56.7 2.9 %collective-permute-start.9 = (bf16[1024,256]{1,0:T(8,128)(2,1)S(1)}, bf16[1024,256]{1,0:T(8,128)(2,1)S(1)}, u32[]{:S(2)}, u32[]{:S(2)}) collective-permute-start(bf16[1024,256]{1,0:T(8,128)(2,1)S(1)} %collective-permute-done.8.zero_ref.refs_8_.refs_7_), channel_id=1, source_target_pairs={{0,1},{1,0},{2,3},{3,2},{4,5},{5,4},{6,7},{7,6},{8,9},{9,8},{10,11... | collective-permute-start | bytes 1572872 | tf_op jit(solution)/shard_map/ppermute | solution.py:317
  59.6 8.8 %copy-start.5 = (f32[1,8192]{1,0:T(1,128)S(1)}, f32[1,8192]{1,0:T(1,128)}, u32[]{:S(2)}) copy-start(f32[1,8192]{1,0:T(1,128)} %refs_3_.1) | copy-start | bytes 98308
  69.8 22.3 %collective-permute-start.17 = (bf16[3,128,1024]{2,1,0:T(8,128)(2,1)S(1)}, bf16[3,128,1024]{2,1,0:T(8,128)(2,1)S(1)}, u32[]{:S(2)}, u32[]{:S(2)}) collective-permute-start(bf16[3,128,1024]{2,1,0:T(8,128)(2,1)S(1)} %leave.3), channel_id=1, source_target_pairs={{16,0},{17,1},{18,2},{19,3},{20,4},{21,5},{22,6},{23,7},{24,8},{25... | collective-permute-start | bytes 2359304 | tf_op jit(solution)/shard_map/ppermute | solution.py:417
  72.9 46.5 %collective-permute-start.16 = (bf16[5,128,1024]{2,1,0:T(8,128)(2,1)S(1)}, bf16[5,128,1024]{2,1,0:T(8,128)(2,1)S(1)}, u32[]{:S(2)}, u32[]{:S(2)}) collective-permute-start(bf16[5,128,1024]{2,1,0:T(8,128)(2,1)S(1)} %leave.2), channel_id=1, source_target_pairs={{16,0},{17,1},{18,2},{19,3},{20,4},{21,5},{22,6},{23,7},{24,8},{25... | collective-permute-start | bytes 3932168 | tf_op jit(solution)/shard_map/ppermute | solution.py:417
  93.6 9.2 %collective-permute-start.18 = (bf16[256,1024]{1,0:T(8,128)(2,1)S(1)}, bf16[256,1024]{1,0:T(8,128)(2,1)S(1)}, u32[]{:S(2)}, u32[]{:S(2)}) collective-permute-start(bf16[256,1024]{1,0:T(8,128)(2,1)S(1)} %get-tuple-element.61), channel_id=1, source_target_pairs={{2,6},{6,10},{10,14},{14,12},{12,8},{8,4},{4,0},{0,2},{3,1},{7,3},... | collective-permute-start | bytes 1572872 | tf_op jit(solution)/shard_map/ppermute | solution.py:320
  95.2 7.6 %collective-permute-start.19 = (bf16[256,1024]{1,0:T(8,128)(2,1)S(1)}, bf16[256,1024]{1,0:T(8,128)(2,1)S(1)}, u32[]{:S(2)}, u32[]{:S(2)}) collective-permute-start(bf16[256,1024]{1,0:T(8,128)(2,1)S(1)} %get-tuple-element.63), channel_id=1, source_target_pairs={{0,1},{1,0},{2,3},{3,2},{4,5},{5,4},{6,7},{7,6},{8,9},{9,8},{10,11... | collective-permute-start | bytes 1572872 | tf_op jit(solution)/shard_map/ppermute | solution.py:317
  103.0 16.4 %collective-permute-start.20 = (bf16[256,1024]{1,0:T(8,128)(2,1)S(1)}, bf16[256,1024]{1,0:T(8,128)(2,1)S(1)}, u32[]{:S(2)}, u32[]{:S(2)}) collective-permute-start(bf16[256,1024]{1,0:T(8,128)(2,1)S(1)} %add.6), channel_id=1, source_target_pairs={{2,6},{6,10},{10,14},{14,12},{12,8},{8,4},{4,0},{0,2},{3,1},{7,3},... | collective-permute-start | bytes 1572872 | tf_op jit(solution)/shard_map/ppermute | solution.py:320
  122.7 10.3 %collective-permute-start.22 = (bf16[3,256,1024]{2,1,0:T(8,128)(2,1)S(1)}, bf16[3,256,1024]{2,1,0:T(8,128)(2,1)S(1)}, u32[]{:S(2)}, u32[]{:S(2)}) collective-permute-start(bf16[3,256,1024]{2,1,0:T(8,128)(2,1)S(1)} %products.6), channel_id=1, source_target_pairs={{0,1},{1,0},{2,3},{3,2},{4,5},{5,4},{6,7},{7,6},{8,9},{9,8},{10,11... | collective-permute-start | bytes 4718600 | tf_op jit(solution)/shard_map/ppermute | solution.py:317
  123.7 9.2 %collective-permute-start.21 = (bf16[256,1024]{1,0:T(8,128)(2,1)S(1)}, bf16[256,1024]{1,0:T(8,128)(2,1)S(1)}, u32[]{:S(2)}, u32[]{:S(2)}) collective-permute-start(bf16[256,1024]{1,0:T(8,128)(2,1)S(1)} %products.4), channel_id=1, source_target_pairs={{2,6},{6,10},{10,14},{14,12},{12,8},{8,4},{4,0},{0,2},{3,1},{7,3},... | collective-permute-start | bytes 1572872 | tf_op jit(solution)/shard_map/ppermute | solution.py:320
  125.3 9.4 %collective-permute-start.27 = (bf16[256,1024]{1,0:T(8,128)(2,1)S(1)}, bf16[256,1024]{1,0:T(8,128)(2,1)S(1)}, u32[]{:S(2)}, u32[]{:S(2)}) collective-permute-start(bf16[256,1024]{1,0:T(8,128)(2,1)S(1)} %get-tuple-element.85), channel_id=1, source_target_pairs={{0,1},{1,0},{2,3},{3,2},{4,5},{5,4},{6,7},{7,6},{8,9},{9,8},{10,11... | collective-permute-start | bytes 1572872 | tf_op jit(solution)/shard_map/ppermute | solution.py:317
  133.1 9.2 %collective-permute-start.23 = (bf16[256,1024]{1,0:T(8,128)(2,1)S(1)}, bf16[256,1024]{1,0:T(8,128)(2,1)S(1)}, u32[]{:S(2)}, u32[]{:S(2)}) collective-permute-start(bf16[256,1024]{1,0:T(8,128)(2,1)S(1)} %add.7), channel_id=1, source_target_pairs={{2,6},{6,10},{10,14},{14,12},{12,8},{8,4},{4,0},{0,2},{3,1},{7,3},... | collective-permute-start | bytes 1572872 | tf_op jit(solution)/shard_map/ppermute | solution.py:320
  134.8 9.4 %collective-permute-start.29 = (bf16[256,1024]{1,0:T(8,128)(2,1)S(1)}, bf16[256,1024]{1,0:T(8,128)(2,1)S(1)}, u32[]{:S(2)}, u32[]{:S(2)}) collective-permute-start(bf16[256,1024]{1,0:T(8,128)(2,1)S(1)} %get-tuple-element.87), channel_id=1, source_target_pairs={{0,1},{1,0},{2,3},{3,2},{4,5},{5,4},{6,7},{7,6},{8,9},{9,8},{10,11... | collective-permute-start | bytes 1572872 | tf_op jit(solution)/shard_map/ppermute | solution.py:317
  135.0 13.0 %collective-permute-start.28 = (bf16[256,1024]{1,0:T(8,128)(2,1)S(1)}, bf16[256,1024]{1,0:T(8,128)(2,1)S(1)}, u32[]{:S(2)}, u32[]{:S(2)}) collective-permute-start(bf16[256,1024]{1,0:T(8,128)(2,1)S(1)} %add.10), channel_id=1, source_target_pairs={{2,6},{6,10},{10,14},{14,12},{12,8},{8,4},{4,0},{0,2},{3,1},{7,3},... | collective-permute-start | bytes 1572872 | tf_op jit(solution)/shard_map/ppermute | solution.py:320
  142.6 11.0 %collective-permute-start.24 = (bf16[256,1024]{1,0:T(8,128)(2,1)S(1)}, bf16[256,1024]{1,0:T(8,128)(2,1)S(1)}, u32[]{:S(2)}, u32[]{:S(2)}) collective-permute-start(bf16[256,1024]{1,0:T(8,128)(2,1)S(1)} %add.8), channel_id=1, source_target_pairs={{2,6},{6,10},{10,14},{14,12},{12,8},{8,4},{4,0},{0,2},{3,1},{7,3},... | collective-permute-start | bytes 1572872 | tf_op jit(solution)/shard_map/ppermute | solution.py:320
  148.2 11.0 %collective-permute-start.30 = (bf16[256,1024]{1,0:T(8,128)(2,1)S(1)}, bf16[256,1024]{1,0:T(8,128)(2,1)S(1)}, u32[]{:S(2)}, u32[]{:S(2)}) collective-permute-start(bf16[256,1024]{1,0:T(8,128)(2,1)S(1)} %add.11), channel_id=1, source_target_pairs={{2,6},{6,10},{10,14},{14,12},{12,8},{8,4},{4,0},{0,2},{3,1},{7,3},... | collective-permute-start | bytes 1572872 | tf_op jit(solution)/shard_map/ppermute | solution.py:320
  153.8 11.0 %collective-permute-start.25 = (bf16[256,1024]{1,0:T(8,128)(2,1)S(1)}, bf16[256,1024]{1,0:T(8,128)(2,1)S(1)}, u32[]{:S(2)}, u32[]{:S(2)}) collective-permute-start(bf16[256,1024]{1,0:T(8,128)(2,1)S(1)} %add.9), channel_id=1, source_target_pairs={{2,6},{6,10},{10,14},{14,12},{12,8},{8,4},{4,0},{0,2},{3,1},{7,3},... | collective-permute-start | bytes 1572872 | tf_op jit(solution)/shard_map/ppermute | solution.py:320
  160.1 5.7 %collective-permute-start.31 = (bf16[256,512]{1,0:T(8,128)(2,1)S(1)}, bf16[256,512]{1,0:T(8,128)(2,1)S(1)}, u32[]{:S(2)}, u32[]{:S(2)}) collective-permute-start(bf16[256,512]{1,0:T(8,128)(2,1)S(1)} %get-tuple-element.90), channel_id=1, source_target_pairs={{0,1},{1,0},{2,3},{3,2},{4,5},{5,4},{6,7},{7,6},{8,9},{9,8},{10,11... | collective-permute-start | bytes 786440 | tf_op jit(solution)/shard_map/ppermute | solution.py:317
  165.7 1.6 collective-permute-start.26

commit v4 on v3

--- a/solution.py
+++ b/solution.py
@@ -122,13 +122,6 @@
     down_t_ref[...] = down_ref[...].astype(F32).T
 
 
-def fetch(sources, held, sems):
-    copies = [pltpu.make_async_copy(ref, held.at[i], sems.at[i]) for i, ref in enumerate(sources)]
-    for copy in copies:
-        copy.start()
-    return copies
-
-
 def assemble_kernel(mine_ref, other_ref, out_ref, sems):
     rows = mine_ref.shape[0]
     core = lax.axis_index("dp") % CORES
@@ -157,24 +150,22 @@
     return pre_grad, jnp.sum(pre_grad.astype(F32) * preact, axis=-1, keepdims=True) / width
 
 
-def top_kernel(groups, meta, x_ref, t_ref, scaled_ref, weight_ref, *refs):
+def preact_kernel(slots, meta, scaled_ref, *refs):
+    downs, out_ref = refs[:-1], refs[-1]
+    total = 0.0
+    for slot, down_ref in zip(slots, downs):
+        scaled = columns(scaled_ref, meta[slot], down_ref.shape[0])
+        total = total + jnp.dot(scaled, down_ref[...], preferred_element_type=F32)
+    out_ref[...] = total
+
+
+def top_kernel(groups, opposite, meta, x_ref, t_ref, scaled_ref, weight_ref, sum_ref, down_ref, *refs):
     n = meta.n
-    held, held_x, sems, sems_x = refs[-4:]
-    pre_out, mean_out, hid_out, slope_out, preact_out, sum_out, *tops = refs[2 * n : -4]
+    ups, (pre_out, mean_out, hid_out, slope_out, preact_out, sum_out, *tops) = refs[:n], refs[n:]
     width = x_ref.shape[1]
     block = width // n
-    order = [slot for group in groups for slot in group]
-    copies = fetch(refs[: 2 * n], held, sems)
-    x_copies = {}
-    for i, slot in enumerate(order):
-        place = pl.ds(pl.multiple_of(meta[slot] * block, block), block)
-        for at, ref in enumerate((x_ref, t_ref)):
-            x_copies[i, at] = pltpu.make_async_copy(ref.at[:, place], held_x.at[i, at], sems_x.at[i, at])
-            x_copies[i, at].start()
-    preact = jnp.zeros(preact_out.shape, F32)
-    for slot in range(n):
-        copies[slot].wait()
-        preact = preact + jnp.dot(columns(scaled_ref, meta[slot], block), held[slot], preferred_element_type=F32)
+    far = columns(scaled_ref, meta[opposite], block)
+    preact = sum_ref[...] + jnp.dot(far, down_ref[...], preferred_element_type=F32)
     sigmoid_val = 1.0 / (1.0 + jnp.exp(-preact))
     slope = sigmoid_val * (1.0 + preact * (1.0 - sigmoid_val))
     hidden = preact * sigmoid_val
@@ -184,18 +175,14 @@
     hidden = hidden.astype(BF16)
     weight = weight_ref[...]
     total = jnp.zeros_like(preact)
-    i = 0
     for group, top_ref in zip(groups, tops):
         for at, slot in enumerate(group):
-            copies[n + slot].wait()
-            branch = lax.dot_general(hidden, held[n + slot], NT, preferred_element_type=F32)
-            x_copies[i, 0].wait()
-            x_copies[i, 1].wait()
-            values = held_x[i, 0].astype(F32) + branch - held_x[i, 1].astype(F32)
+            branch = lax.dot_general(hidden, ups[slot][...], NT, preferred_element_type=F32)
+            chip = meta[slot]
+            values = columns(x_ref, chip, block).astype(F32) + branch - columns(t_ref, chip, block).astype(F32)
             top = (weight * values).astype(BF16)
             top_ref[at] = top
-            total = total + jnp.dot(top, held[n + slot], preferred_element_type=F32)
-            i += 1
+            total = total + jnp.dot(top, ups[slot][...], preferred_element_type=F32)
     sum_out[...] = total
     pre_out[...], mean_out[...] = pre_grad_of(total, slope, preact, width)
 
@@ -213,34 +200,47 @@
         out_ref[at] = input_grad(cot_ref[at], x, downs[at][...], gain, pre_ref[...], inv_ref[...], mean_ref[...])
 
 
-def arrive_kernel(follows, meta, arrived_ref, top_ref, hid_ref, *refs):
+def arrive_kernel(follows, width, opposite, meta, arrived_ref, top_ref, hid_ref, *refs):
     count = arrived_ref.shape[0]
-    total = refs[0][...] if follows else 0.0
-    refs = refs[1:] if follows else refs
-    ups, (cot_ref, sum_out, *parts) = refs[:count], refs[count:]
+    ups, refs = refs[:count], refs[count:]
+    total = 0.0
+    if follows:
+        sum_ref, slope_ref, preact_ref, scaled_ref, cot_ref, pre_out, pre_t_out, mean_out, *outs = refs
+        total = sum_ref[...]
+        outs, parts = outs[:2], outs[2:]
+    else:
+        cot_ref, sum_out, *parts = refs
     for at in range(count):
         cot = jnp.where(meta.last(), top_ref[at], arrived_ref[at])
         cot_ref[at] = cot
+        total = total + jnp.dot(cot, ups[at][...], preferred_element_type=F32)
         parts[at][...] = jnp.dot(hid_ref[...], cot, preferred_element_type=F32).astype(BF16)
-        total = total + jnp.dot(cot, ups[at][...], preferred_element_type=F32)
-    sum_out[...] = total
-
-
-def pre_grad_kernel(width, sum_ref, slope_ref, preact_ref, pre_out, pre_t_out, mean_out):
-    hidden_grad = sum_ref[...]
-    slope = slope_ref[...]
-    pre_out[...], mean_out[...] = pre_grad_of(hidden_grad, slope, preact_ref[...], width)
-    pre_t_out[...] = (hidden_grad * slope).T.astype(BF16)
-
-
-def products_kernel(slots, stacked, meta, scaled_ref, pre_t_ref, *outs):
-    block = outs[0].shape[-1]
+    if not follows:
+        sum_out[...] = total
+        return
+    pre_out[...], mean_out[...] = pre_grad_of(total, slope_ref[...], preact_ref[...], width)
+    pre_t = (total * slope_ref[...]).T.astype(BF16)
+    pre_t_out[...] = pre_t
+    put_product(pre_t, columns(scaled_ref, meta[opposite], ups[0].shape[0]), outs)
+
+
+def put_product(pre_t, scaled, halves):
+    part = jnp.dot(pre_t, scaled, preferred_element_type=F32).astype(BF16)
+    half = part.shape[1] // 2
+    halves[0][...] = part[:, :half]
+    halves[1][...] = part[:, half:]
+
+
+def products_kernel(slots, meta, scaled_ref, pre_t_ref, *outs):
     for at, slot in enumerate(slots):
-        part = jnp.dot(pre_t_ref[...], columns(scaled_ref, meta[slot], block), preferred_element_type=F32)
-        if stacked:
-            outs[0][at] = part.astype(BF16)
-        else:
-            outs[at][...] = part.astype(BF16)
+        halves = outs[2 * at : 2 * at + 2]
+        put_product(pre_t_ref[...], columns(scaled_ref, meta[slot], 2 * halves[0].shape[1]), halves)
+
+
+def stack_kernel(slots, meta, scaled_ref, pre_t_ref, out_ref):
+    for at, slot in enumerate(slots):
+        halves = out_ref.at[2 * at], out_ref.at[2 * at + 1]
+        put_product(pre_t_ref[...], columns(scaled_ref, meta[slot], 2 * out_ref.shape[2]), halves)
 
 
 def add_kernel(picks, *refs):
@@ -263,6 +263,14 @@
     first = meta.first()
     low = total_ref[:, :half].astype(F32) + part_ref[:, :half].astype(F32)
     high = total_ref[:, half:].astype(F32) + part_ref[:, half:].astype(F32)
+    mine_ref[...] = jnp.where(first, low, high)
+    other_ref[...] = jnp.where(first, high, low).astype(BF16)
+
+
+def split_halves_kernel(meta, low_ref, high_ref, low_part, high_part, mine_ref, other_ref):
+    first = meta.first()
+    low = low_ref[...].astype(F32) + low_part[...].astype(F32)
+    high = high_ref[...].astype(F32) + high_part[...].astype(F32)
     mine_ref[...] = jnp.where(first, low, high)
     other_ref[...] = jnp.where(first, high, low).astype(BF16)
 
@@ -311,7 +319,6 @@
     rank = w_down.shape[2]
     half_block = block // CORES
     back = [(s, s - 1) for s in range(1, sections)]
-    groups_of = [range(0, 1), range(1, 2)]
 
     def swap(value):
         return lax.ppermute(value, "dp", routes.partner)
@@ -319,6 +326,8 @@
     def onward(value):
         return lax.ppermute(value, "dp", routes.onward)
 
+    rank_f32, rank_bf16 = shape(F32, tokens, rank), shape(BF16, tokens, rank)
+    half_part = shape(BF16, rank, block // CORES)
     chunk, part_shape = shape(BF16, block, rank), shape(BF16, rank, block)
 
     def of_chip(mine, other):
@@ -344,32 +353,30 @@
         [shape(F32, tokens, 1), shape(BF16, tokens, width), shape(F32, tokens, 1), shape(F32, rank, half_block)],
         after(x, downs[own]), gains, confidence[None], down, name="scale",
     )
-    down_block, up_block = downs[own], after(ups[own], scaled)
+    down_block, up_block = downs[own], ups[own]
     for k in range(1, half):
         earlier = [downs[ahead(k - 2)], ups[ahead(k - 2)]] if k >= 3 else []
         downs[behind(k)] = down_block = onward(after(down_block, *earlier))
         ups[behind(k)] = up_block = onward(up_block)
         downs[ahead(k)] = swap(down_block)
         ups[ahead(k)] = swap(up_block)
-    earlier = [downs[ahead(half - 2)], ups[ahead(half - 2)]] if half >= 3 else []
+    earlier = [downs[ahead(half - 2)], ups[ahead(half - 2)]]
     mine = onward(after(pick(down_block, up_block), *earlier))
+    near = [j for j in range(n) if j != opposite]
+    preact = with_meta(
+        functools.partial(preact_kernel, near), rank_f32, scaled, *(downs[j] for j in near),
+        flops=2 * tokens * width * rank, name="preact",
+    )
+    mine = after(mine, preact)
     other = swap(mine)
     downs[opposite], ups[opposite] = pick(mine, other), pick(other, mine)
 
-    rank_f32, rank_bf16 = shape(F32, tokens, rank), shape(BF16, tokens, rank)
     pre_grad, mean, hidden_t, slope, preact, own_sum, *tops = with_meta(
-        functools.partial(top_kernel, groups),
+        functools.partial(top_kernel, groups, opposite),
         [rank_bf16, shape(F32, tokens, 1), shape(BF16, rank, tokens), rank_f32, rank_f32, rank_f32]
         + [shape(BF16, len(slots), tokens, block) for slots in groups],
-        x, teacher_states, scaled, weight_rows, *(downs[j] for j in range(n)), *(ups[j] for j in range(n)),
-        specs=[ANY] * 2 + [VMEM] * 2 + [ANY] * (2 * n),
-        scratch=[
-            pltpu.VMEM((2 * n, block, rank), BF16),
-            pltpu.VMEM((n, 2, tokens, block), BF16),
-            pltpu.SemaphoreType.DMA((2 * n,)),
-            pltpu.SemaphoreType.DMA((n, 2)),
-        ],
-        flops=6 * tokens * width * rank, vmem=24, name="top",
+        x, teacher_states, scaled, weight_rows, preact, downs[opposite], *(ups[j] for j in range(n)),
+        flops=4 * tokens * width * rank, name="top",
     )
 
     def leave(slots, cot, pre_grad, mean):
@@ -379,21 +386,18 @@
             flops=2 * len(slots) * tokens * block * rank, name="leave",
         )
 
-    def arrive(slots, value, top, total):
-        cot, total, *parts = with_meta(
-            functools.partial(arrive_kernel, total is not None),
-            [shape(BF16, *value.shape), rank_f32] + [part_shape] * len(slots),
-            value, top, hidden_t, *([] if total is None else [total]), *(ups[j] for j in slots),
+    def arrive(i, value, total):
+        slots, kind = groups[i], shape(BF16, *value.shape)
+        body = functools.partial(arrive_kernel, total is not None, width, opposite)
+        more, outs = [], [kind, rank_f32]
+        if total is not None:
+            more = [total, slope, preact, scaled]
+            outs = [kind, rank_bf16, shape(BF16, rank, tokens), shape(F32, tokens, 1), half_part, half_part]
+        outs = with_meta(
+            body, outs + [part_shape] * len(slots), value, tops[i], hidden_t, *(ups[j] for j in slots), *more,
             flops=4 * len(slots) * tokens * block * rank, name="arrive",
         )
-        return cot, parts, total
-
-    def rank_grad(total):
-        return call(
-            functools.partial(pre_grad_kernel, width),
-            [rank_bf16, shape(BF16, rank, tokens), shape(F32, tokens, 1)],
-            total, slope, preact, name="pre_grad",
-        )
+        return outs[: -len(slots)], outs[-len(slots) :]
 
 
     def split(total, part):
@@ -405,44 +409,11 @@
     cots = tops
     for hop in range(sections - 1):
         sent = [leave(slots, cot, pre_grad, mean) for slots, cot in zip(groups, cots)]
+        arrived = [lax.ppermute(value, "section", back) for value in sent]
         if hop < sections - 2:
-            arrived, cots = [], []
-            hidden_grad = None
-            for i, value in enumerate(sent):
-                arrived.append(lax.ppermute(after(value, *arrived[i - 2 : i - 1] if i >= 2 else ()), "section", back))
-                cot, _, hidden_grad = arrive(groups[i], arrived[i], tops[i], hidden_grad)
-                cots.append(cot)
-            pre_grad, _, mean = rank_grad(hidden_grad)
-
-    arrived = [lax.ppermute(value, "section", back) for value in sent]
-    near_cot, parts, hidden_grad = arrive(groups[0], after(arrived[0], sent[1]), tops[0], None)
-    total = onward(parts[0])
-    total = onward(add(part_shape, total, parts[1], swap(parts[2])))
-    cot, parts, hidden_grad = arrive(groups[1], after(arrived[1], total), tops[1], hidden_grad)
-    cots = [near_cot, cot]
-    for k in range(half - 2, 0, -1):
-        at = 2 * (half - 2 - k)
-        total = onward(add(part_shape, total, parts[at], swap(parts[at + 1])))
-    up_mine, up_other = split(total, parts[-1])
-    up_other = swap(up_other)
-    grad_up = call(
-        functools.partial(close_kernel, tokens), shape(F32, 1, half_block, rank), up_mine, up_other, name="close_up"
-    )
-
-    pre_grad, pre_t, mean = rank_grad(hidden_grad)
-
-    def products(slots, stacked=False):
-        return with_meta(
-            functools.partial(products_kernel, slots, stacked),
-            shape(BF16, len(slots), rank, block) if stacked else [part_shape] * len(slots), scaled, pre_t,
-            flops=2 * len(slots) * tokens * block * rank, name="products",
-        )
-
-    (far,) = products([opposite])
-    total = onward(far)
-    behinds = products([behind(k) for k in range(1, half)], stacked=True)
-    aheads = products([ahead(k) for k in range(1, half)])
-    swapped = swap(behinds)
+            (near_cot, hidden_grad), _ = arrive(0, arrived[0], None)
+            (cot, pre_grad, _, mean, _, _), _ = arrive(1, arrived[1], hidden_grad)
+            cots = [near_cot, cot]
 
     def finish(some, so_far):
         slots = [j for i in some for j in groups[i]]
@@ -456,15 +427,40 @@
             flops=2 * len(slots) * tokens * block * rank, name="finish",
         )
 
-    (mine,) = products([own])
-    input_grads = finish(groups_of[0], None)
+    (near_cot, hidden_grad), parts = arrive(0, after(arrived[0], sent[1]), None)
+    up_total = onward(parts[0])
+    up_total = onward(add(part_shape, up_total, parts[1], swap(parts[2])))
+    (cot, pre_grad, pre_t, mean, *far), parts = arrive(1, after(arrived[1], up_total), hidden_grad)
+    cots = [near_cot, cot]
+    down_totals = [onward(value) for value in far]
+    behinds = with_meta(
+        functools.partial(stack_kernel, [behind(k) for k in range(1, half)]),
+        shape(BF16, 2 * (half - 1), rank, half_block), scaled, pre_t, name="products",
+    )
+    swapped = swap(behinds)
+    slots = [ahead(k) for k in range(1, half)] + [own]
+    halves = with_meta(
+        functools.partial(products_kernel, slots), [half_part] * (2 * len(slots)), scaled, pre_t, name="products"
+    )
+    input_grads = None
     for at, k in enumerate(range(half - 1, 0, -1)):
-        part, other = aheads[k - 1], (swapped, k - 1)
-        if at >= 1 and at < len(groups_of):
-            input_grads = finish(groups_of[at], input_grads)
-        total = after(total, input_grads)
-        total = onward(add(part_shape, total, part, other))
-    down_mine, down_other = split(total, mine)
+        if k < half - 1:
+            i = 2 * (half - 2 - k)
+            up_total = onward(add(part_shape, up_total, parts[i], swap(parts[i + 1])))
+        down_totals = [
+            onward(add(half_part, down_totals[c], halves[2 * (k - 1) + c], (swapped, 2 * (k - 1) + c))) for c in (0, 1)
+        ]
+        if at < len(groups):
+            input_grads = finish([at], input_grads)
+            down_totals[1] = after(down_totals[1], input_grads)
+    up_mine, up_other = split(up_total, parts[-1])
+    up_other = swap(up_other)
+    grad_up = call(
+        functools.partial(close_kernel, tokens), shape(F32, 1, half_block, rank), up_mine, up_other, name="close_up"
+    )
+    down_mine, down_other = with_meta(
+        split_halves_kernel, [shape(F32, rank, half_block), half_part], *down_totals, *halves[-2:], name="split"
+    )
     down_other = swap(down_other)
     grad_down, grad_gain = with_meta(
         functools.partial(close_gain_kernel, tokens),

time: 169 us -> 162 us (0.959)
  starting transfers between devices: 30.5 us -> 40.3 us
  waiting for transfers between devices: 101 us -> 92.7 us
  Pallas kernels: 31.3 us -> 26.1 us
  local copies, waits for them, and re-layouts: 4.93 us -> 1.93 us
    ppermute x15 -> x19, starting transfers between devices: 26.1 us -> 35.4 us  [onward(): return lax.ppermute(value, 'dp', routes.onward)]
    ppermute x15 -> x19, waiting for transfers between devices: 64.2 us -> 54.9 us  [onward(): return lax.ppermute(value, 'dp', routes.onward)]
    pallas_call x28 -> x29, Pallas kernels: 31.3 us -> 26.1 us  [call(): pl.pallas_call(body, in_specs=specs or [VMEM] * len(args), out_specs=out_...]
    unnamed x20 -> x14, local copies, waits for them, and re-layouts: 4.93 us -> 1.93 us
  transfers between devices with their start and end apart: 32 -> 36, of which waited for: 21 -> 20; matrix products, arithmetic and copies ran while one was open for 0% -> 0% of each run, Pallas kernels for 10% -> 10%
where the time goes in v4:
time: 162 us
  waiting for transfers between devices  92.7 us (57%)
  starting transfers between devices  40.3 us (25%)
  Pallas kernels  26.1 us (16%)
  local copies, waits for them, and re-layouts  1.93 us (1%)
    ppermute x19, waiting for transfers between devices, onward(): return lax.ppermute(value, 'dp', routes.onward)  54.9 us
    ppermute x19, starting transfers between devices, onward(): return lax.ppermute(value, 'dp', routes.onward)  35.4 us
    ppermute x2, waiting for transfers between devices, local(): arrived = [lax.ppermute(value, 'section', back) for value in sent]  32.3 us
    pallas_call x29, Pallas kernels, call(): pl.pallas_call(body, in_specs=specs or [VMEM] * len(args), out_specs=out_...  26.1 us
    ppermute x15, waiting for transfers between devices, swap(): return lax.ppermute(value, 'dp', routes.partner)  5.53 us
  transfers between devices with their start and end apart: 36, of which 20 were waited for; matrix products, arithmetic and copies ran while one was open for 0% of the time, Pallas kernels for 10%

profile of v4, /device:TPU:0, one launch (start us, length us, event | category | flops | bytes accessed | tf_op | source)
XLA Modules:
  0.0 162.0 jit_solution(15783952580450002254)
XLA Ops:
  0.6 0.5 collective-permute-start.5
  1.2 1.3 collective-permute-done.5.other_ref
  2.5 0.9 copy-done.5
  3.6 2.9 %collective-permute-start.6 = (bf16[1024,256]{1,0:T(8,128)(2,1)S(1)}, bf16[1024,256]{1,0:T(8,128)(2,1)S(1)}, u32[]{:S(2)}, u32[]{:S(2)}) collective-permute-start(bf16[1024,256]{1,0:T(8,128)(2,1)S(1)} %assemble.3.refs_13_.refs_7_), channel_id=1, source_target_pairs={{2,6},{6,10},{10,14},{14,12},{12,8},{8,4},{4,0},{0,2},{3,1},{7,3},... | collective-permute-start | bytes 1572872 | tf_op jit(solution)/shard_map/ppermute | solution.py:327
  6.5 0.9 copy-done.4
  7.5 1.6 %collective-permute-start.1 = (bf16[1024,256]{1,0:T(8,128)(2,1)S(1)}, bf16[1024,256]{1,0:T(8,128)(2,1)S(1)}, u32[]{:S(2)}, u32[]{:S(2)}) collective-permute-start(bf16[1024,256]{1,0:T(8,128)(2,1)S(1)} %assemble.2.refs_7_.refs_10_.refs_9_), channel_id=1, source_target_pairs={{2,6},{6,10},{10,14},{14,12},{12,8},{8,4},{4,0},{0,2},{3,1},{7,3},... | collective-permute-start | bytes 1572872 | tf_op jit(solution)/shard_map/ppermute | solution.py:327
  9.2 4.6 %collective-permute-done.6.refs_6_ = bf16[1024,256]{1,0:T(8,128)(2,1)S(1)} collective-permute-done((bf16[1024,256]{1,0:T(8,128)(2,1)S(1)}, bf16[1024,256]{1,0:T(8,128)(2,1)S(1)}, u32[]{:S(2)}, u32[]{:S(2)}) %collective-permute-start.6) | collective-permute-done | bytes 524320 | tf_op jit(solution)/shard_map/ppermute | solution.py:327
  13.7 5.6 %collective-permute-done.1.refs_1_.refs_9_.refs_8_ = bf16[1024,256]{1,0:T(8,128)(2,1)S(1)} collective-permute-done((bf16[1024,256]{1,0:T(8,128)(2,1)S(1)}, bf16[1024,256]{1,0:T(8,128)(2,1)S(1)}, u32[]{:S(2)}, u32[]{:S(2)}) %collective-permute-start.1) | collective-permute-done | bytes 524320 | tf_op jit(solution)/shard_map/ppermute | solution.py:327
  19.3 2.0 %collective-permute-start.3 = (bf16[1024,256]{1,0:T(8,128)(2,1)S(1)}, bf16[1024,256]{1,0:T(8,128)(2,1)S(1)}, u32[]{:S(2)}, u32[]{:S(2)}) collective-permute-start(bf16[1024,256]{1,0:T(8,128)(2,1)S(1)} %collective-permute-done.1.refs_1_.refs_9_.refs_8_), channel_id=1, source_target_pairs={{2,6},{6,10},{10,14},{14,12},{12,8},{8,4},{4,0},{0,2},{3,1},{7,3},... | collective-permute-start | bytes 1572872 | tf_op jit(solution)/shard_map/ppermute | solution.py:327
  21.3 1.6 collective-permute-start.10
  22.9 5.6 %collective-permute-done.3.refs_3_.refs_7_.refs_6_ = bf16[1024,256]{1,0:T(8,128)(2,1)S(1)} collective-permute-done((bf16[1024,256]{1,0:T(8,128)(2,1)S(1)}, bf16[1024,256]{1,0:T(8,128)(2,1)S(1)}, u32[]{:S(2)}, u32[]{:S(2)}) %collective-permute-start.3) | collective-permute-done | bytes 524320 | tf_op jit(solution)/shard_map/ppermute | solution.py:327
  28.5 2.0 %collective-permute-start.8 = (bf16[1024,256]{1,0:T(8,128)(2,1)S(1)}, bf16[1024,256]{1,0:T(8,128)(2,1)S(1)}, u32[]{:S(2)}, u32[]{:S(2)}) collective-permute-start(bf16[1024,256]{1,0:T(8,128)(2,1)S(1)} %collective-permute-done.3.refs_3_.refs_7_.refs_6_), channel_id=1, source_target_pairs={{2,6},{6,10},{10,14},{14,12},{12,8},{8,4},{4,0},{0,2},{3,1},{7,3},... | collective-permute-start | bytes 1572872 | tf_op jit(solution)/shard_map/ppermute | solution.py:327
  30.5 3.6 %collective-permute-done.10.refs_8_.refs_4_ = bf16[1024,256]{1,0:T(8,128)(2,1)S(1)} collective-permute-done((bf16[1024,256]{1,0:T(8,128)(2,1)S(1)}, bf16[1024,256]{1,0:T(8,128)(2,1)S(1)}, u32[]{:S(2)}, u32[]{:S(2)}) %collective-permute-start.10) | collective-permute-done | bytes 524320 | tf_op jit(solution)/shard_map/ppermute | solution.py:327
  34.1 2.0 %collective-permute-start.11 = (bf16[1024,256]{1,0:T(8,128)(2,1)S(1)}, bf16[1024,256]{1,0:T(8,128)(2,1)S(1)}, u32[]{:S(2)}, u32[]{:S(2)}) collective-permute-start(bf16[1024,256]{1,0:T(8,128)(2,1)S(1)} %collective-permute-done.10.refs_8_.refs_4_), channel_id=1, source_target_pairs={{2,6},{6,10},{10,14},{14,12},{12,8},{8,4},{4,0},{0,2},{3,1},{7,3},... | collective-permute-start | bytes 1572872 | tf_op jit(solution)/shard_map/ppermute | solution.py:327
  36.1 0.5 collective-permute-start.4
  36.6 3.1 %collective-permute-done.8.refs_5_.zero_ref.refs_8_.refs_7_ = bf16[1024,256]{1,0:T(8,128)(2,1)S(1)} collective-permute-done((bf16[1024,256]{1,0:T(8,128)(2,1)S(1)}, bf16[1024,256]{1,0:T(8,128)(2,1)S(1)}, u32[]{:S(2)}, u32[]{:S(2)}) %collective-permute-start.8) | collective-permute-done | bytes 524320 | tf_op jit(solution)/shard_map/ppermute | solution.py:327
  39.8 5.6 %collective-permute-done.11.one_ref.refs_10_.refs_5_ = bf16[1024,256]{1,0:T(8,128)(2,1)S(1)} collective-permute-done((bf16[1024,256]{1,0:T(8,128)(2,1)S(1)}, bf16[1024,256]{1,0:T(8,128)(2,1)S(1)}, u32[]{:S(2)}, u32[]{:S(2)}) %collective-permute-start.11) | collective-permute-done | bytes 524320 | tf_op jit(solution)/shard_map/ppermute | solution.py:327
  45.5 2.0 %collective-permute-start.13 = (bf16[1024,256]{1,0:T(8,128)(2,1)S(1)}, bf16[1024,256]{1,0:T(8,128)(2,1)S(1)}, u32[]{:S(2)}, u32[]{:S(2)}) collective-permute-start(bf16[1024,256]{1,0:T(8,128)(2,1)S(1)} %pick.3), channel_id=1, source_target_pairs={{2,6},{6,10},{10,14},{14,12},{12,8},{8,4},{4,0},{0,2},{3,1},{7,3},... | collective-permute-start | bytes 1572872 | tf_op jit(solution)/shard_map/ppermute | solution.py:327
  47.5 1.1 scale.1
  48.6 1.3 preact.1.refs_4_
  49.9 4.8 %collective-permute-done.13.zero_ref.one_ref = bf16[1024,256]{1,0:T(8,128)(2,1)S(1)} collective-permute-done((bf16[1024,256]{1,0:T(8,128)(2,1)S(1)}, bf16[1024,256]{1,0:T(8,128)(2,1)S(1)}, u32[]{:S(2)}, u32[]{:S(2)}) %collective-permute-start.13) | collective-permute-done | bytes 524320 | tf_op jit(solution)/shard_map/ppermute | solution.py:327
  54.7 0.5 collective-permute-start.15
  55.2 1.4 collective-permute-done.14.one_ref.zero_ref
  56.7 0.6 collective-permute-done.15.refs_11_.refs_4_
  57.4 3.9 %top.1 = (bf16[128,256]{1,0:T(8,128)(2,1)S(1)}, f32[128,1]{1,0:T(8,128)S(1)}, bf16[256,128]{1,0:T(8,128)(2,1)S(1)}, f32[128,256]{1,0:T(8,128)S(1)}, f32[128,256]...) custom-call(s32[16,8]{1,0:T(8,128)S(1)} %copy-done.2, ...), custom_call_target="tpu_custom_call" | custom-call | flops 1073741824 | bytes 3441024 | tf_op jit(solution)/shard_map/top/pallas_call | solution.py:64
  61.2 1.4 leave.3
  62.6 1.3 collective-permute-start.17
  63.9 1.8 %leave.2 = bf16[5,128,1024]{2,1,0:T(8,128)(2,1)S(1)} custom-call(s32[16,8]{1,0:T(8,128)S(1)} %copy-done.2, bf16[5,128,1024]{2,1,0:T(8,128)(2,1)S(1)} %get-tuple-element.59.refs_0_.refs_1_, bf16[128,8192]{1,0:T(8,128)(2,1)S(1)} %bitcast.8, f32[1,8192]{1,0:T(1,128)S(1)} %copy-done.3, bf16[128,256]{1,0:T(8,128)(2,1)S(1)} %get-tuple-element.60.refs_3_, ...), custom_call_target="tpu_custom_call" | custom-call | flops 335544320 | bytes 1859968 | tf_op jit(solution)/shard_map/leave/pallas_call | solution.py:64
  65.7 1.3 collective-permute-start.16
  67.0 17.9 %collective-permute-done.17.refs_0_ = bf16[3,128,1024]{2,1,0:T(8,128)(2,1)S(1)} collective-permute-done((bf16[3,128,1024]{2,1,0:T(8,128)(2,1)S(1)}, bf16[3,128,1024]{2,1,0:T(8,128)(2,1)S(1)}, u32[]{:S(2)}, u32[]{:S(2)}) %collective-permute-start.17) | collective-permute-done | bytes 786464 | tf_op jit(solution)/shard_map/ppermute | solution.py:412
  84.9 1.5 arrive.2
  86.4 2.0 %collective-permute-start.18 = (bf16[256,1024]{1,0:T(8,128)(2,1)S(1)}, bf16[256,1024]{1,0:T(8,128)(2,1)S(1)}, u32[]{:S(2)}, u32[]{:S(2)}) collective-permute-start(bf16[256,1024]{1,0:T(8,128)(2,1)S(1)} %get-tuple-element.66), channel_id=1, source_target_pairs={{2,6},{6,10},{10,14},{14,12},{12,8},{8,4},{4,0},{0,2},{3,1},{7,3},... | collective-permute-start | bytes 1572872 | tf_op jit(solution)/shard_map/ppermute | solution.py:327
  88.4 7.2 %collective-permute-done.18.refs_0_ = bf16[256,1024]{1,0:T(8,128)(2,1)S(1)} collective-permute-done((bf16[256,1024]{1,0:T(8,128)(2,1)S(1)}, bf16[256,1024]{1,0:T(8,128)(2,1)S(1)}, u32[]{:S(2)}, u32[]{:S(2)}) %collective-permute-start.18) | collective-permute-done | bytes 524320 | tf_op jit(solution)/shard_map/ppermute | solution.py:327
  95.6 0.2 add.9
  95.8 2.0 %collective-permute-start.20 = (bf16[256,1024]{1,0:T(8,128)(2,1)S(1)}, bf16[256,1024]{1,0:T(8,128)(2,1)S(1)}, u32[]{:S(2)}, u32[]{:S(2)}) collective-permute-start(bf16[256,1024]{1,0:T(8,128)(2,1)S(1)} %add.9), channel_id=1, source_target_pairs={{2,6},{6,10},{10,14},{14,12},{12,8},{8,4},{4,0},{0,2},{3,1},{7,3},... | collective-permute-start | bytes 1572872 | tf_op jit(solution)/shard_map/ppermute | solution.py:327
  97.8 14.4 %collective-permute-done.16.refs_0_ = bf16[5,128,1024]{2,1,0:T(8,128)(2,1)S(1)} collective-permute-done((bf16[5,128,1024]{2,1,0:T(8,128)(2,1)S(1)}, bf16[5,128,1024]{2,1,0:T(8,128)(2,1)S(1)}, u32[]{:S(2)}, u32[]{:S(2)}) %collective-permute-start.16) | collective-permute-done | bytes 1310752 | tf_op jit(solution)/shard_map/ppermute | solution.py:412
  112.2 2.1 %arrive.3 = (bf16[5,128,1024]{2,1,0:T(8,128)(2,1)S(1)}, bf16[128,256]{1,0:T(8,128)(2,1)S(1)}, bf16[256,128]{1,0:T(8,128)(2,1)S(1)}, f32[128,1]{1,0:T(8,128)S(1)}...) custom-call(s32[16,8]{1,0:T(8,128)S(1)} %copy-done.2, ...), custom_call_target="tpu_custom_call" | custom-call | flops 671088640 | bytes 3096832 | tf_op jit(solution)/shard_map/arrive/pallas_call | solution.py:64
  114.3 1.2 products.3
  115.7 0.5 collective-permute-start.31
  116.2 2.0 %collective-permute-start.21 = (bf16[256,512]{1,0:T(8,128)(2,1)S(1)}, bf16[256,512]{1,0:T(8,128)(2,1)S(1)}, u32[]{:S(2)}, u32[]{:S(2)}) collective-permute-start(bf16[256,512]{1,0:T(8,128)(2,1)S(1)} %get-tuple-element.77), channel_id=1, source_target_pairs={{2,6},{6,10},{10,14},{14,12},{12,8},{8,4},{4,0},{0,2},{3,1},{7,3},... | collective-permute-start | bytes 786440 | tf_op jit(solution)/shard_map/ppermute | solution.py:327
  118.1 1.7 %collective-permute-done.31.refs_2_ = bf16[256,1024]{1,0:T(8,128)(2,1)S(1)} collective-permute-done((bf16[256,1024]{1,0:T(8,128)(2,1)S(1)}, bf16[256,1024]{1,0:T(8,128)(2,1)S(1)}, u32[]{:S(2)}, u32[]{:S(2)}) %collective-permute-start.31) | collective-permute-done | bytes 524320 | tf_op jit(solution)/shard_map/ppermute | solution.py:324
  120.0 2.0 %collective-permute-start.32 = (bf16[256,1024]{1,0:T(8,128)(2,1)S(1)}, bf16[256,1024]{1,0:T(8,128)(2,1)S(1)}, u32[]{:S(2)}, u32[]{:S(2)}) collective-permute-start(bf16[256,1024]{1,0:T(8,128)(2,1)S(1)} %add.16), channel_id=1, source_target_pairs={{2,6},{6,10},{10,14},{14,12},{12,8},{8,4},{4,0},{0,2},{3,1},{7,3},... | collective-permute-start | bytes 1572872 | tf_op jit(solution)/shard_map/ppermute | solution.py:327
  122.0 1.6 collective-permute-start.26
  123.6 1.4 products.2
  125.1 1.6 %collective-permute-start.23 = (bf16[256,512]{1,0:T(8,128)(2,1)S(1)}, bf16[256,512]{1,0:T(8,128)(2,1)S(1)}, u32[]{:S(2)}, u32[]{:S(2)}) collective-permute-start(bf16[256,512]{1,0:T(8,128)(2,1)S(1)} %add.10), channel_id=1, source_target_pairs={{2,6},{6,10},{10,14},{14,12},{12,8},{8,4},{4,0},{0,2},{3,1},{7,3},... | collective-permute-start | bytes 786440 | tf_op jit(solution)/shard_map/ppermute | solution.py:327
  126.7 5.3 %collective-permute-done.26.refs_0_ = bf16[256,512]{1,0:T(8,128)(2,1)S(1)} collective-permute-done((bf16[256,512]{1,0:T(8,128)(2,1)S(1)}, bf16[256,512]{1,0:T(8,128)(2,1)S(1)}, u32[]{:S(2)}, u32[]{:S(2)}) %collective-permute-start.26) | collective-permute-done | bytes 262176 | tf_op jit(solution)/shard_map/ppermute | solution.py:327
  132.1 2.0 %collective-permute-start.27 = (bf16[256,512]{1,0:T(8,128)(2,1)S(1)}, bf16[256,512]{1,0:T(8,128)(2,1)S(1)}, u32[]{:S(2)}, u32[]{:S(2)}) collective-permute-start(bf16[256,512]{1,0:T(8,128)(2,1)S(1)} %add.13), channel_id=1, source_target_pairs={{2,6},{6,10},{10,14},{14,12},{12,8},{8,4},{4,0},{0,2},{3,1},{7,3},... | collective-permute-start | bytes 786440 | tf_op jit(solution)/shard_map/ppermute | solution.py:327
  134.2 2.1 %finish.2.refs_11_ = bf16[128,8192]{1,0:T(8,128)(2,1)} custom-call(s32[16,8]{1,0:T(8,128)S(1)} %copy-done.2, bf16[128,8192]{1,0:T(8,128)(2,1)S(1)} %bitcast.9, f32[1,8192]{1,0:T(1,128)S(1)} %copy-done.3, bf16[128,256]{1,0:T(8,128)(2,1)S(1)} %get-tuple-element.73.refs_2_, f32[128,1]{1,0:T(8,128)S(1)} %get-tuple-element.61.refs_4_.refs_3_, ...), custom_call_target="tpu_custom_call" | custom-call | flops 201326592 | bytes 1663360 | tf_op jit(solution)/shard_map/finish/pallas_call | solution.py:64
  136.3 0.2 add.17
  136.5 1.6 %collective-permute-start.34 = (bf16[256,1024]{1,0:T(8,128)(2,1)S(1)}, bf16[256,1024]{1,0:T(8,128)(2,1)S(1)}, u32[]{:S(2)}, u32[]{:S(2)}) collective-permute-start(bf16[256,1024]{1,0:T(8,128)(2,1)S(1)} %add.17), channel_id=1, source_target_pairs={{2,6},{6,10},{10,14},{14,12},{12,8},{8,4},{4,0},{0,2},{3,1},{7,3},... | collective-permute-start | bytes 1572872 | tf_op jit(solution)/shard_map/ppermute | solution.py:327
  138.3 1.6 %collective-permute-start.24 = (bf16[256,512]{1,0:T(8,128)(2,1)S(1)}, bf16[256,512]{1,0:T(8,128)(2,1)S(1)}, u32[]{:S(2)}, u32[]{:S(2)}) collective-permute-start(bf16[256,512]{1,0:T(8,128)(2,1)S(1)} %add.11), channel_id=1, source_target_pairs={{2,6},{6,10},{10,14},{14,12},{12,8},{8,4},{4,0},{0,2},{3,1},{7,3},... | collective-permute-start | bytes 786440 | tf_op jit(solution)/shard_map/ppermute | solution.py:327
  140.0 1.6 collective-permute-start.28
  141.6 2.6 %finish.3 = bf16[128,8192]{1,0:T(8,128)(2,1)} custom-call(s32[16,8]{1,0:T(8,128)S(1)} %copy-done.2, bf16[128,8192]{1,0:T(8,128)(2,1)S(1)} %bitcast.10, f32[1,8192]{1,0:T(1,128)S(1)} %copy-done.3, bf16[128,256]{1,0:T(8,128)(2,1)S(1)} %get-tuple-element.73.refs_2_, f32[128,1]{1,0:T(8,128)S(1)} %get-tuple-element.61.refs_4_.refs_3_, ...), custom_call_target="tpu_custom_call", output_to_operand_aliasing={{}: (12, {})} | custom-call | flops 335544320 | bytes 2580864 | tf_op jit(solution)/shard_map/finish/pallas_call | solution.py:64
  144.2 4.4 %collective-permute-done.24.refs_0_ = bf16[256,512]{1,0:T(8,128)(2,1)S(1)} collective-permute-done((bf16[256,512]{1,0:T(8,128)(2,1)S(1)}, bf16[256,512]{1,0:T(8,128)(2,1)S(1)}, u32[]{:S(2)}, u32[]{:S(2)}) %collective-permute-start.24) | collective-permute-done | bytes 262176 | tf_op jit(solution)/shard_map/ppermute | solution.py:327
  148.7 1.6 %collective-permute-start.25 = (bf16[256,512]{1,0:T(8,128)(2,1)S(1)}, bf16[256,512]{1,0:T(8,128)(2,1)S(1)}, u32[]{:S(2)}, u32[]{:S(2)}) collective-permute-start(bf16[256,512]{1,0:T(8,128)(2,1)S(1)} %add.12), channel_id=1, source_target_pairs={{2,6},{6,10},{10,14},{14,12},{12,8},{8,4},{4,0},{0,2},{3,1},{7,3},... | collective-permute-start | bytes 786440 | tf_op jit(solution)/shard_map/ppermute | solution.py:327
  150.3 1.1 collective-permute-done.28.refs_0_
  151.5 1.6 %collective-permute-start.29 = (bf16[256,512]{1,0:T(8,128)(2,1)S(1)}, bf16[256,512]{1,0:T(8,128)(2,1)S(1)}, u32[]{:S(2)}, u32[]{:S(2)}) collective-permute-start(bf16[256,512]{1,0:T(8,128)(2,1)S(1)} %add.15), channel_id=1, source_target_pairs={{2,6},{6,10},{10,14},{14,12},{12,8},{8,4},{4,0},{0,2},{3,1},{7,3},... | collective-permute-start | bytes 786440 | tf_op jit(solution)/shard_map/ppermute | solution.py:327
  153.1 0.8 split.3
  154.0 1.1 collective-permute-done.25.refs_0_
  155.1 2.8 %collective-permute-done.29.refs_1_ = bf16[256,512]{1,0:T(8,128)(2,1)S(1)} collective-permute-done((bf16[256,512]{1,0:T(8,128)(2,1)S(1)}, bf16[256,512]{1,0:T(8,128)(2,1)S(1)}, u32[]{:S(2)}, u32[]{:S(2)}) %collective-permute-start.29) | collective-permute-done | bytes 262176 | tf_op jit(solution)/shard_map/ppermute | solution.py:327
  157.9 0.8 split.2
  158.8 1.0 close_up.1
  159.8 0.5 collective-permute-done.30.refs_1_
  160.3 1.7 %close_down.1 = (f32[1,512,256]{2,1,0:T(8,128)}, f32[1,512]{1,0:T(1,128)}) custom-call(s32[16,8]{1,0:T(8,128)S(1)} %copy-done.2, f32[256,512]{1,0:T(8,128)S(1)} %get-tuple-element.90.refs_0_, bf16[256,512]{1,0:T(8,128)(2,1)S(1)} %collective-permute-done.30.refs_1_, f32[256,512]{1,0:T(8,128)S(1)} %get-tuple-element.92.refs_2_, f32[1,8192]{1,0:T(1,128)S(1)} %copy-done.3), custom_call_target="tpu_custom_call" | custom-call | bytes 467584 | tf_op jit(solution)/shard_map/close_down/pallas_call | solution.py:64
  (51 shorter events, 1.4 us)
Async XLA Ops:
  0.6 1.9 %collective-permute-start.5 = (bf16[512,256]{1,0:T(8,128)(2,1)}, bf16[512,256]{1,0:T(8,128)(2,1)S(1)}, u32[]{:S(2)}, u32[]{:S(2)}) collective-permute-start(bf16[512,256]{1,0:T(8,128)(2,1)} %bitcast.14), channel_id=1, source_target_pairs={{0,1},{1,0},{2,3},{3,2},{4,5},{5,4},{6,7},{7,6},{8,9},{9,8},{10,11... | collective-permute-start | bytes 786440 | tf_op jit(solution)/shard_map/ppermute | solution.py:324
  1.1 5.4 %collective-permute-start = (bf16[512,256]{1,0:T(8,128)(2,1)}, bf16[512,256]{1,0:T(8,128)(2,1)S(1)}, u32[]{:S(2)}, u32[]{:S(2)}) collective-permute-start(bf16[512,256]{1,0:T(8,128)(2,1)} %bitcast.11), channel_id=1, source_target_pairs={{0,1},{1,0},{2,3},{3,2},{4,5},{5,4},{6,7},{7,6},{8,9},{9,8},{10,11... | collective-permute-start | bytes 786440 | tf_op jit(solution)/shard_map/ppermute | solution.py:324
  2.5 0.9 copy-start.5
  3.5 44.0 %copy-start.6 = (s32[128]{0:T(128)S(1)}, s32[128]{0:T(128)}, u32[]{:S(2)}) copy-start(s32[128]{0:T(128)} %param.9) | copy-start | bytes 1540
  3.5 43.9 %copy-start = (bf16[1,128,8192]{2,1,0:T(8,128)(2,1)S(1)}, bf16[1,128,8192]{2,1,0:T(8,128)(2,1)}, u32[]{:S(2)}) copy-start(bf16[1,128,8192]{2,1,0:T(8,128)(2,1)} %param.7) | copy-start | bytes 6291460
  3.6 43.9 %copy-start.3 = (f32[1,8192]{1,0:T(1,128)S(1)}, f32[1,8192]{1,0:T(1,128)}, u32[]{:S(2)}) copy-start(f32[1,8192]{1,0:T(1,128)} %refs_3_.1) | copy-start | bytes 98308
  3.6 10.2 %collective-permute-start.6 = (bf16[1024,256]{1,0:T(8,128)(2,1)S(1)}, bf16[1024,256]{1,0:T(8,128)(2,1)S(1)}, u32[]{:S(2)}, u32[]{:S(2)}) collective-permute-start(bf16[1024,256]{1,0:T(8,128)(2,1)S(1)} %assemble.3.refs_13_.refs_7_), channel_id=1, source_target_pairs={{2,6},{6,10},{10,14},{14,12},{12,8},{8,4},{4,0},{0,2},{3,1},{7,3},... | collective-permute-start | bytes 1572872 | tf_op jit(solution)/shard_map/ppermute | solution.py:327
  6.5 1.0 copy-start.4
  7.5 11.8 %collective-permute-start.1 = (bf16[1024,256]{1,0:T(8,128)(2,1)S(1)}, bf16[1024,256]{1,0:T(8,128)(2,1)S(1)}, u32[]{:S(2)}, u32[]{:S(2)}) collective-permute-start(bf16[1024,256]{1,0:T(8,128)(2,1)S(1)} %assemble.2.refs_7_.refs_10_.refs_9_), channel_id=1, source_target_pairs={{2,6},{6,10},{10,14},{14,12},{12,8},{8,4},{4,0},{0,2},{3,1},{7,3},... | collective-permute-start | bytes 1572872 | tf_op jit(solution)/shard_map/ppermute | solution.py:327
  13.7 9.2 %collective-permute-start.7 = (bf16[1024,256]{1,0:T(8,128)(2,1)S(1)}, bf16[1024,256]{1,0:T(8,128)(2,1)S(1)}, u32[]{:S(2)}, u32[]{:S(2)}) collective-permute-start(bf16[1024,256]{1,0:T(8,128)(2,1)S(1)} %collective-permute-done.6.refs_6_), channel_id=1, source_target_pairs={{0,1},{1,0},{2,3},{3,2},{4,5},{5,4},{6,7},{7,6},{8,9},{9,8},{10,11... | collective-permute-start | bytes 1572872 | tf_op jit(solution)/shard_map/ppermute | solution.py:324
  19.3 9.2 %collective-permute-start.3 = (bf16[1024,256]{1,0:T(8,128)(2,1)S(1)}, bf16[1024,256]{1,0:T(8,128)(2,1)S(1)}, u32[]{:S(2)}, u32[]{:S(2)}) collective-permute-start(bf16[1024,256]{1,0:T(8,128)(2,1)S(1)} %collective-permute-done.1.refs_1_.refs_9_.refs_8_), channel_id=1, source_target_pairs={{2,6},{6,10},{10,14},{14,12},{12,8},{8,4},{4,0},{0,2},{3,1},{7,3},... | collective-permute-start | bytes 1572872 | tf_op jit(solution)/shard_map/ppermute | solution.py:327
  21.3 7.2 %collective-permute-start.2 = (bf16[1024,256]{1,0:T(8,128)(2,1)S(1)}, bf16[1024,256]{1,0:T(8,128)(2,1)S(1)}, u32[]{:S(2)}, u32[]{:S(2)}) collective-permute-start(bf16[1024,256]{1,0:T(8,128)(2,1)S(1)} %collective-permute-done.1.refs_1_.refs_9_.refs_8_), channel_id=1, source_target_pairs={{0,1},{1,0},{2,3},{3,2},{4,5},{5,4},{6,7},{7,6},{8,9},{9,8},{10,11... | collective-permute-start | bytes 1572872 | tf_op jit(solution)/shard_map/ppermute | solution.py:324
  21.3 12.8 %collective-permute-start.10 = (bf16[1024,256]{1,0:T(8,128)(2,1)S(1)}, bf16[1024,256]{1,0:T(8,128)(2,1)S(1)}, u32[]{:S(2)}, u32[]{:S(2)}) collective-permute-start(bf16[1024,256]{1,0:T(8,128)(2,1)S(1)} %collective-permute-done.6.refs_6_), channel_id=1, source_target_pairs={{2,6},{6,10},{10,14},{14,12},{12,8},{8,4},{4,0},{0,2},{3,1},{7,3},... | collective-permute-start | bytes 1572872 | tf_op jit(solution)/shard_map/ppermute | solution.py:327
  28.5 11.2 %collective-permute-start.8 = (bf16[1024,256]{1,0:T(8,128)(2,1)S(1)}, bf16[1024,256]{1,0:T(8,128)(2,1)S(1)}, u32[]{:S(2)}, u32[]{:S(2)}) collective-permute-start(bf16[1024,256]{1,0:T(8,128)(2,1)S(1)} %collective-permute-done.3.refs_3_.refs_7_.refs_6_), channel_id=1, source_target_pairs={{2,6},{6,10},{10,14},{14,12},{12,8},{8,4},{4,0},{0,2},{3,1},{7,3},... | collective-permute-start | bytes 1572872 | tf_op jit(solution)/shard_map/ppermute | solution.py:327
  34.1 11.2 %collective-permute-start.11 = (bf16[1024,256]{1,0:T(8,128)(2,1)S(1)}, bf16[1024,256]{1,0:T(8,128)(2,1)S(1)}, u32[]{:S(2)}, u32[]{:S(2)}) collective-permute-start(bf16[1024,256]{1,0:T(8,128)(2,1)S(1)} %collective-permute-done.10.refs_8_.refs_4_), channel_id=1, source_target_pairs={{2,6},{6,10},{10,14},{14,12},{12,8},{8,4},{4,0},{0,2},{3,1},{7,3},... | collective-permute-start | bytes 1572872 | tf_op jit(solution)/shard_map/ppermute | solution.py:327
  36.1 9.3 %collective-permute-start.12 = (bf16[1024,256]{1,0:T(8,128)(2,1)S(1)}, bf16[1024,256]{1,0:T(8,128)(2,1)S(1)}, u32[]{:S(2)}, u32[]{:S(2)}) collective-permute-start(bf16[1024,256]{1,0:T(8,128)(2,1)S(1)} %collective-permute-done.10.refs_8_.refs_4_), channel_id=1, source_target_pairs={{0,1},{1,0},{2,3},{3,2},{4,5},{5,4},{6,7},{7,6},{8,9},{9,8},{10,11... | collective-permute-start | bytes 1572872 | tf_op jit(solution)/shard_map/ppermute | solution.py:324
  36.1 9.3 %collective-permute-start.4 = (bf16[1024,256]{1,0:T(8,128)(2,1)S(1)}, bf16[1024,256]{1,0:T(8,128)(2,1)S(1)}, u32[]{:S(2)}, u32[]{:S(2)}) collective-permute-start(bf16[1024,256]{1,0:T(8,128)(2,1)S(1)} %collective-permute-done.3.refs_3_.refs_7_.refs_6_), channel_id=1, source_target_pairs={{0,1},{1,0},{2,3},{3,2},{4,5},{5,4},{6,7},{7,6},{8,9},{9,8},{10,11... | collective-permute-start | bytes 1572872 | tf_op jit(solution)/shard_map/ppermute | solution.py:324
  39.8 8.8 %collective-permute-start.9 = (bf16[1024,256]{1,0:T(8,128)(2,1)S(1)}, bf16[1024,256]{1,0:T(8,128)(2,1)S(1)}, u32[]{:S(2)}, u32[]{:S(2)}) collective-permute-start(bf16[1024,256]{1,0:T(8,128)(2,1)S(1)} %collective-permute-done.8.refs_5_.zero_ref.refs_8_.refs_7_), channel_id=1, source_target_pairs={{0,1},{1,0},{2,3},{3,2},{4,5},{5,4},{6,7},{7,6},{8,9},{9,8},{10,11... | collective-permute-start | bytes 1572872 | tf_op jit(solution)/shard_map/ppermute | solution.py:324
  45.4 3.2 %copy-start.2 = (s32[16,8]{1,0:T(8,128)S(1)}, s32[16,8]{1,0:T(8,128)}, u32[]{:S(2)}) copy-start(s32[16,8]{1,0:T(8,128)} %constant.2.clone.table_ref) | copy-start | bytes 1540
  45.5 9.2 %collective-permute-start.13 = (bf16[1024,256]{1,0:T(8,128)(2,1)S(1)}, bf16[1024,256]{1,0:T(8,128)(2,1)S(1)}, u32[]{:S(2)}, u32[]{:S(2)}) collective-permute-start(bf16[1024,256]{1,0:T(8,128)(2,1)S(1)} %pick.3), channel_id=1, source_target_pairs={{2,6},{6,10},{10,14},{14,12},{12,8},{8,4},{4,0},{0,2},{3,1},{7,3},... | collective-permute-start | bytes 1572872 | tf_op jit(solution)/shard_map/ppermute | solution.py:327
  49.9 7.4 %copy-start.1 = (bf16[128,8192]{1,0:T(8,128)(2,1)S(1)}, bf16[128,8192]{1,0:T(8,128)(2,1)}, u32[]{:S(2)}) copy-start(bf16[128,8192]{1,0:T(8,128)(2,1)} %refs_1_.3) | copy-start | bytes 6291460
  54.7 1.9 %collective-permute-start.14 = (bf16[1024,256]{1,0:T(8,128)(2,1)S(1)}, bf16[1024,256]{1,0:T(8,128)(2,1)S(1)}, u32[]{:S(2)}, u32[]{:S(2)}) collective-permute-start(bf16[1024,256]{1,0:T(8,128)(2,1)S(1)} %collective-permute-done.13.zero_ref.one_ref), channel_id=1, source_target_pairs={{0,1},{1,0},{2,3},{3,2},{4,5},{5,4},{6,7},{7,6},{8,9},{9,8},{10,11... | collective-permute-start | bytes 1572872 | tf_op jit(solution)/shard_map/ppermute | solution.py:324
  54.7 2.7 %collective-permute-start.15 = (bf16[1024,256]{1,0:T(8,128)(2,1)S(1)}, bf16[1024,256]{1,0:T(8,128)(2,1)S(1)}, u32[]{:S(2)}, u32[]{:S(2)}) collective-permute-start(bf16[1024,256]{1,0:T(8,128)(2,1)S(1)} %collective-permute-done.11.one_ref.refs_10_.refs_5_), channel_id=1, source_target_pairs={{0,1},{1,0},{2,3},{3,2},{4,5},{5,4},{6,7},{7,6},{8,9},{9,8},{10,11... | collective-permute-start | bytes 1572872 | tf_op jit(solution)/shard_map/ppermute | solution.py:324
  62.6 22.3 %collective-permute-start.17 = (bf16[3,128,1024]{2,1,0:T(8,128)(2,1)S(1)}, bf16[3,128,1024]{2,1,0:T(8,128)(2,1)S(1)}, u32[]{:S(2)}, u32[]{:S(2)}) collective-permute-start(bf16[3,128,1024]{2,1,0:T(8,128)(2,1)S(1)} %leave.3), channel_id=1, source_target_pairs={{16,0},{17,1},{18,2},{19,3},{20,4},{21,5},{22,6},{23,7},{24,8},{25... | collective-permute-start | bytes 2359304 | tf_op jit(solution)/shard_map/ppermute | solution.py:412
  65.7 46.5 %collective-permute-start.16 = (bf16[5,128,1024]{2,1,0:T(8,128)(2,1)S(1)}, bf16[5,128,1024]{2,1,0:T(8,128)(2,1)S(1)}, u32[]{:S(2)}, u32[]{:S(2)}) collective-permute-start(bf16[5,128,1024]{2,1,0:T(8,128)(2,1)S(1)} %leave.2), channel_id=1, source_target_pairs={{16,0},{17,1},{18,2},{19,3},{20,4},{21,5},{22,6},{23,7},{24,8},{25... | collective-permute-start | bytes 3932168 | tf_op jit(solution)/shard_map/ppermute | solution.py:412
  86.4 9.2 %collective-permute-start.18 = (bf16[256,1024]{1,0:T(8,128)(2,1)S(1)}, bf16[256,1024]{1,0:T(8,128)(2,1)S(1)}, u32[]{:S(2)}, u32[]{:S(2)}) collective-permute-start(bf16[256,1024]{1,0:T(8,128)(2,1)S(1)} %get-tuple-element.66), channel_id=1, source_target_pairs={{2,6},{6,10},{10,14},{14,12},{12,8},{8,4},{4,0},{0,2},{3,1},{7,3},... | collective-permute-start | bytes 1572872 | tf_op jit(solution)/shard_map/ppermute | solution.py:327
  88.4 7.2 %collective-permute-start.19 = (bf16[256,1024]{1,0:T(8,128)(2,1)S(1)}, bf16[256,1024]{1,0:T(8,128)(2,1)S(1)}, u32[]{:S(2)}, u32[]{:S(2)}) collective-permute-start(bf16[256,1024]{1,0:T(8,128)(2,1)S(1)} %get-tuple-element.68), channel_id=1, source_target_pairs={{0,1},{1,0},{2,3},{3,2},{4,5},{5,4},{6,7},{7,6},{8,9},{9,8},{10,11... | collective-permute-start | bytes 1572872 | tf_op jit(solution)/shard_map/ppermute | solution.py:324
  95.8 16.4 %collective-permute-start.20 = (bf16[256,1024]{1,0:T(8,128)(2,1)S(1)}, bf16[256,1024]{1,0:T(8,128)(2,1)S(1)}, u32[]{:S(2)}, u32[]{:S(2)}) collective-permute-start(bf16[256,1024]{1,0:T(8,128)(2,1)S(1)} %add.9), channel_id=1, source_target_pairs={{2,6},{6,10},{10,14},{14,12},{12,8},{8,4},{4,0},{0,2},{3,1},{7,3},... | collective-permute-start | bytes 1572872 | tf_op jit(solution)/shard_map/ppermute | solution.py:327
  115.6 9.4 %collective-permute-start.22 = (bf16[6,256,512]{2,1,0:T(8,128)(2,1)S(1)}, bf16[6,256,512]{2,1,0:T(8,128)(2,1)S(1)}, u32[]{:S(2)}, u32[]{:S(2)}) collective-permute-start(bf16[6,256,512]{2,1,0:T(8,128)(2,1)S(1)} %products.3), channel_id=1, source_target_pairs={{0,1},{1,0},{2,3},{3,2},{4,5},{5,4},{6,7},{7,6},{8,9},{9,8},{10,11... | collective-permute-start | bytes 4718600 | tf_op jit(solution)/shard_map/ppermute | solution.py:324
  115.7 4.1 %collective-permute-start.31 = (bf16[256,1024]{1,0:T(8,128)(2,1)S(1)}, bf16[256,1024]{1,0:T(8,128)(2,1)S(1)}, u32[]{:S(2)}, u32[]{:S(2)}) collective-permute-start(bf16[256,1024]{1,0:T(8,128)(2,1)S(1)} %get-tuple-element.95), channel_id=1, source_target_pairs={{0,1},{1,0},{2,3},{3,2},{4,5},{5,4},{6,7},{7,6},{8,9},{9,8},{10,11... | collective-permute-start | bytes 1572872 | tf_op jit(solution)/shard_map/ppermute | solution.py:324
  116.2 8.8 %collective-permute-start.21 = (bf16[256,512]{1,0:T(8,128)(2,1)S(1)}, bf16[256,512]{1,0:T(8,128)(2,1)S(1)}, u32[]{:S(2)}, u32[]{:S(2)}) collective-permute-start(bf16[256,512]{1,0:T(8,128)(2,1)S(1)} %get-tuple-element.77), channel_id=1, source_target_pairs={{2,6},{6,10},{10,14},{14,12},{12,8},{8,4},{4,0},{0,2},{3,1},{7,3},... | collective-permute-start | bytes 786440 | tf_op jit(solution)/shard_map/ppermute | solution.py:327
  118.1 18.2 %collective-permute-start.33 = (bf16[256,1024]{1,0:T(8,128)(2,1)S(1)}, bf16[256,1024]{1,0:T(8,128)(2,1)S(1)}, u32[]{:S(2)}, u32[]{:S(2)}) collective-permute-start(bf16[256,1024]{1,0:T(8,128)(2,1)S(1)} %get-tuple-element.97), channel_id=1, source_target_pairs={{0,1},{1,0},{2,3},{3,2},{4,5},{5,4},{6,7},{7,6},{8,9},{9,8},{10,11... | collective-permute-start | bytes 1572872 | tf_op jit(solution)/shard_map/ppermute | solution.py:324
  120.0 16.3 %collective-permute-start.32 = (bf16[256,1024]{1,0:T(8,128)(2,1)S(1)}, bf16[256,1024]{1,0:T(8,128)(2,1)S(1)}, u32[]{:S(2)}, u32[]{:S(2)}) collective-permute-start(bf16[256,1024]{1,0:T(8,128)(2,1)S(1)} %add.16), channel_id=1, source_target_pairs={{2,6},{6,10},{10,14},{14,12},{12,8},{8,4},{4,0},{0,2},{3,1},{7,3},... | collective-permute-start | bytes 1572872 | tf_op jit(solution)/shard_map/ppermute | solution.py:327
  122.0 10.0 %collective-permute-start.26 = (bf16[256,512]{1,0:T(8,128)(2,1)S(1)}, bf16[256,512]{1,0:T(8,128)(2,1)S(1)}, u32[]{:S(2)}, u32[]{:S(2)}) collective-permute-start(bf16[256,512]{1,0:T(8,128)(2,1)S(1)} %get-tuple-element.82), channel_id=1, source_target_pairs={{2,6},{6,10},{10,14},{14,12},{12,8},{8,4},{4,0},{0,2},{3,1},{7,3},... | collective-permute-start | bytes 786440 | tf_op jit(solution)/shard_map/ppermute | solution.py:327
  125.1 13.1 %collective-permute-start.23 = (bf16[256,512]{1,0:T(8,128)(2,1)S(1)}, bf16[256,512]{1,0:T(8,128)(2,1)S(1)}, u32[]{:S(2)}, u32[]{:S(2)}) collective-permute-start(bf16[256,512]{1,0:T(8,128)(2,1)S(1)} %add.10), channel_id=1, source_target_pairs={{2,6},{6,10},{10,14},{14,12},{12,8},{8,4},{4,0},{0,2},{3,1},{7,3},... | collective-permute-start | bytes 786440 | tf_op jit(solution)/shard_map/ppermute | solution.py:327
  132.1 7.8 %collective-permute-start.27 = (bf16[256,512]{1,0:T(8,128)(2,1)S(1)}, bf16[256,512]{1,0:T(8,128)(2,1)S(1)}, u32[]{:S(2)}, u32[]{:S(2)}) collective-permute-start(bf16[256,512]{1,0:T(8,128)(2,1)S(1)} %add.13), channel_id=1, source_target_pairs={{2,6},{6,10},{10,14},{14,12},{12,8},{8,4},{4,0},{0,2},{3,1},{7,3},... | collective-permute-start | bytes 786440 | tf_op jit(solution)/shard_map/ppermute | solution.py:327
  136.5 16.6 %collective-permute-start.34 = (bf16[256,1024]{1,0:T(8,128)(2,1)S(1)}, bf16[256,1024]{1,0:T(8,128)(2,1)S(1)}, u32[]{:S(2)}, u32[]{:S(2)}) collective-permute-start(bf16[256,1024]{1,0:T(8,128)(2,1)S(1)} %add.17), channel_id=1, source_target_pairs={{2,6},{6,10},{10,14},{14,12},{12,8},{8,4},{4,0},{0,2},{3,1},{7,3},... | collective-permute-start | bytes 1572872 | tf_op jit(solution)/shard_map/ppermute | solution.py:327
  138.3 10.3 %collective-permute-start.24 = (bf16[256,512]{1,0:T(8,128)(2,1)S(1)}, bf16[256,512]{1,0:T(8,128)(2,1)S(1)}, u32[]{:S(2)}, u32[]{:S(2)}) collective-permute-start(bf16[256,512]{1,0:T(8,128)(2,1)S(1)} %add.11), channel_id=1, source_target_pairs={{2,6},{6,10},{10,14},{14,12},{12,8},{8,4},{4,0},{0,2},{3,1},{7,3},... | collective-permute-start | bytes 786440 | tf_op jit(solution)/shard_map/ppermute | solution.py:327
  140.0 11.4 %collective-permute-start.28 = (bf16[256,512]{1,0:T(8,128)(2,1)S(1)}, bf16[256,512]{1,0:T(8,128)(2,1)S(1)}, u32[]{:S(2)}, u32[]{:S(2)}) collective-permute-start(bf16[256,512]{1,0:T(8,128)(2,1)S(1)} %add.14), channel_id=1, source_target_pairs={{2,6},{6,10},{10,14},{14,12},{12,8},{8,4},{4,0},{0,2},{3,1},{7,3},... | collective-permute-start | bytes 786440 | tf_op jit(solution)/shard_map/ppermute | solution.py:327
  148.7 6.4 %collective-permute-start.25 = (bf16[256,512]{1,0:T(8,128)(2,1)S(1)}, bf16[256,512]{1,0:T(8,128)(2,1)S(1)}, u32[]{:S(2)}, u32[]{:S(2)}) collective-permute-start(bf16[256,512]{1,0:T(8,128)(2,1)S(1)} %add.12), channel_id=1, source_target_pairs={{2,6},{6,10},{10,14},{14,12},{12,8},{8,4},{4,0},{0,2},{3,1},{7,3},... | collective-permute-start | bytes 786440 | tf_op jit(solution)/shard_map/ppermute | solution.py:327
  151.5 6.4 %collective-permute-start.29 = (bf16[256,512]{1,0:T(8,128)(2,1)S(1)}, bf16[256,512]{1,0:T(8,128)(2,1)S(1)}, u32[]{:S(2)}, u32[]{:S(2)}) collective-permute-start(bf16[256,512]{1,0:T(8,128)(2,1)S(1)} %add.15), channel_id=1, source_target_pairs={{2,6},{6,10},{10,14},{14,12},{12,8},{8,4},{4,0},{0,2},{3,1},{7,3},... | collective-permute-start | bytes 786440 | tf_op jit(solution)/shard_map/ppermute | solution.py:327
  153.9 4.9 %collective-permute-start.35 = (bf16[256,512]{1,0:T(8,128)(2,1)S(1)}, bf16[256,512]{1,0:T(8,128)(2,1)S(1)}, u32[]{:S(2)}, u32[]{:S(2)}) collective-permute-start(bf16[256,512]{1,0:T(8,128)(2,1)S(1)} %get-tuple-element.100), channel_id=1, source_target_pairs={{0,1},{1,0},{2,3},{3,2},{4,5},{5,4},{6,7},{7,6},{8,9},{9,8},{10,11... | collective-permute-start | bytes 786440 | tf_op jit(solution)/shard_map/ppermute | solution.py:324
  158.7 1.6 collective-permute-start.30

commit v5 on v4

--- a/solution.py
+++ b/solution.py
@@ -44,7 +44,7 @@
                 self.table[chip * CORES + c] = [ring[(i + (1 - 2 * c) * s) % n] for s in steps]
         self.opposite, self.own = n - 2, n - 1
         leaving = [self.opposite] + [f(k) for k in range(half - 1, 0, -1) for f in (self.ahead, self.behind)] + [self.own]
-        self.groups = [leaving[:3], leaving[3:]]
+        self.groups = [leaving[:3], leaving[3:-3], leaving[-3:]]
 
     def behind(self, k):
         return 2 * k - 2
@@ -200,13 +200,15 @@
         out_ref[at] = input_grad(cot_ref[at], x, downs[at][...], gain, pre_ref[...], inv_ref[...], mean_ref[...])
 
 
-def arrive_kernel(follows, width, opposite, meta, arrived_ref, top_ref, hid_ref, *refs):
+def arrive_kernel(follows, ends, width, opposite, meta, arrived_ref, top_ref, hid_ref, *refs):
     count = arrived_ref.shape[0]
     ups, refs = refs[:count], refs[count:]
     total = 0.0
     if follows:
-        sum_ref, slope_ref, preact_ref, scaled_ref, cot_ref, pre_out, pre_t_out, mean_out, *outs = refs
-        total = sum_ref[...]
+        total = refs[0][...]
+        refs = refs[1:]
+    if ends:
+        slope_ref, preact_ref, scaled_ref, cot_ref, pre_out, pre_t_out, mean_out, *outs = refs
         outs, parts = outs[:2], outs[2:]
     else:
         cot_ref, sum_out, *parts = refs
@@ -215,7 +217,7 @@
         cot_ref[at] = cot
         total = total + jnp.dot(cot, ups[at][...], preferred_element_type=F32)
         parts[at][...] = jnp.dot(hid_ref[...], cot, preferred_element_type=F32).astype(BF16)
-    if not follows:
+    if not ends:
         sum_out[...] = total
         return
     pre_out[...], mean_out[...] = pre_grad_of(total, slope_ref[...], preact_ref[...], width)
@@ -388,10 +390,11 @@
 
     def arrive(i, value, total):
         slots, kind = groups[i], shape(BF16, *value.shape)
-        body = functools.partial(arrive_kernel, total is not None, width, opposite)
-        more, outs = [], [kind, rank_f32]
-        if total is not None:
-            more = [total, slope, preact, scaled]
+        ends = i == len(groups) - 1
+        body = functools.partial(arrive_kernel, total is not None, ends, width, opposite)
+        more, outs = [] if total is None else [total], [kind, rank_f32]
+        if ends:
+            more += [slope, preact, scaled]
             outs = [kind, rank_bf16, shape(BF16, rank, tokens), shape(F32, tokens, 1), half_part, half_part]
         outs = with_meta(
             body, outs + [part_shape] * len(slots), value, tops[i], hidden_t, *(ups[j] for j in slots), *more,
@@ -411,9 +414,10 @@
         sent = [leave(slots, cot, pre_grad, mean) for slots, cot in zip(groups, cots)]
         arrived = [lax.ppermute(value, "section", back) for value in sent]
         if hop < sections - 2:
-            (near_cot, hidden_grad), _ = arrive(0, arrived[0], None)
-            (cot, pre_grad, _, mean, _, _), _ = arrive(1, arrived[1], hidden_grad)
-            cots = [near_cot, cot]
+            (first_cot, hidden_grad), _ = arrive(0, arrived[0], None)
+            (second_cot, hidden_grad), _ = arrive(1, arrived[1], hidden_grad)
+            (third_cot, pre_grad, _, mean, _, _), _ = arrive(2, arrived[2], hidden_grad)
+            cots = [first_cot, second_cot, third_cot]
 
     def finish(some, so_far):
         slots = [j for i in some for j in groups[i]]
@@ -427,11 +431,18 @@
             flops=2 * len(slots) * tokens * block * rank, name="finish",
         )
 
-    (near_cot, hidden_grad), parts = arrive(0, after(arrived[0], sent[1]), None)
+    def step(total, part, other):
+        return add(part_shape, total, part, swap(other))
+
+    (first_cot, hidden_grad), parts = arrive(0, after(arrived[0], *sent[1:]), None)
     up_total = onward(parts[0])
-    up_total = onward(add(part_shape, up_total, parts[1], swap(parts[2])))
-    (cot, pre_grad, pre_t, mean, *far), parts = arrive(1, after(arrived[1], up_total), hidden_grad)
-    cots = [near_cot, cot]
+    (second_cot, hidden_grad), more_parts = arrive(1, after(arrived[1], up_total), hidden_grad)
+    up_sent = step(up_total, parts[1], parts[2])
+    for at in range(0, len(more_parts), 2):
+        up_sent = step(onward(up_sent), more_parts[at], more_parts[at + 1])
+    (third_cot, pre_grad, pre_t, mean, *far), parts = arrive(2, after(arrived[2], up_sent), hidden_grad)
+    cots = [first_cot, second_cot, third_cot]
+    up_total = onward(step(onward(up_sent), parts[0], parts[1]))
     down_totals = [onward(value) for value in far]
     behinds = with_meta(
         functools.partial(stack_kernel, [behind(k) for k in range(1, half)]),
@@ -444,15 +455,14 @@
     )
     input_grads = None
     for at, k in enumerate(range(half - 1, 0, -1)):
-        if k < half - 1:
-            i = 2 * (half - 2 - k)
-            up_total = onward(add(part_shape, up_total, parts[i], swap(parts[i + 1])))
         down_totals = [
             onward(add(half_part, down_totals[c], halves[2 * (k - 1) + c], (swapped, 2 * (k - 1) + c))) for c in (0, 1)
         ]
-        if at < len(groups):
-            input_grads = finish([at], input_grads)
+        if at == 0:
+            input_grads = finish([0, 1], None)
             down_totals[1] = after(down_totals[1], input_grads)
+    input_grads = finish([2], input_grads)
+    down_totals[1] = after(down_totals[1], input_grads)
     up_mine, up_other = split(up_total, parts[-1])
     up_other = swap(up_other)
     grad_up = call(

time: 162 us -> 159 us (0.981)
  waiting for transfers between devices: 92.7 us -> 85.8 us
  starting transfers between devices: 40.3 us -> 42 us
  Pallas kernels: 26.1 us -> 27.8 us
    ppermute x2 -> x3, waiting for transfers between devices: 32.3 us -> 28.6 us  [local(): arrived = [lax.ppermute(value, 'section', back) for value in sent]]
    pallas_call x29 -> x31, Pallas kernels: 26.1 us -> 27.8 us  [call(): pl.pallas_call(body, in_specs=specs or [VMEM] * len(args), out_specs=out_...]
    ppermute x15, waiting for transfers between devices: 5.53 us -> 3.86 us  [swap(): return lax.ppermute(value, 'dp', routes.partner)]
    ppermute x2 -> x3, starting transfers between devices: 2.58 us -> 3.86 us  [local(): arrived = [lax.ppermute(value, 'section', back) for value in sent]]
  transfers between devices with their start and end apart: 36 -> 37, of which waited for: 20 -> 20; matrix products, arithmetic and copies ran while one was open for 0% -> 0% of each run, Pallas kernels for 10% -> 11%
where the time goes in v5:
time: 159 us; the launch traced here: 158 us
  waiting for transfers between devices  85.8 us (54%)
  starting transfers between devices  42 us (26%)
  Pallas kernels  27.8 us (17%)
  local copies, waits for them, and re-layouts  1.93 us (1%)
    ppermute x19, waiting for transfers between devices, onward(): return lax.ppermute(value, 'dp', routes.onward)  53.4 us
    ppermute x19, starting transfers between devices, onward(): return lax.ppermute(value, 'dp', routes.onward)  36 us
    ppermute x3, waiting for transfers between devices, local(): arrived = [lax.ppermute(value, 'section', back) for value in sent]  28.6 us
    pallas_call x31, Pallas kernels, call(): pl.pallas_call(body, in_specs=specs or [VMEM] * len(args), out_specs=out_...  27.8 us
    ppermute x3, starting transfers between devices, local(): arrived = [lax.ppermute(value, 'section', back) for value in sent]  3.86 us
    ppermute x15, waiting for transfers between devices, swap(): return lax.ppermute(value, 'dp', routes.partner)  3.86 us
  transfers between devices with their start and end apart: 37, of which 20 were waited for; matrix products, arithmetic and copies ran while one was open for 0% of the time, Pallas kernels for 11%

profile of v5, /device:TPU:0, one launch (start us, length us, event | category | flops | bytes accessed | tf_op | source)
XLA Modules:
  0.0 158.5 jit_solution(8069752038278125994)
XLA Ops:
  0.7 0.5 collective-permute-start.5
  1.2 1.3 collective-permute-done.5.other_ref
  2.5 0.9 copy-done.5
  3.6 2.9 %collective-permute-start.6 = (bf16[1024,256]{1,0:T(8,128)(2,1)S(1)}, bf16[1024,256]{1,0:T(8,128)(2,1)S(1)}, u32[]{:S(2)}, u32[]{:S(2)}) collective-permute-start(bf16[1024,256]{1,0:T(8,128)(2,1)S(1)} %assemble.3.refs_13_.refs_5_), channel_id=1, source_target_pairs={{2,6},{6,10},{10,14},{14,12},{12,8},{8,4},{4,0},{0,2},{3,1},{7,3},... | collective-permute-start | bytes 1572872 | tf_op jit(solution)/shard_map/ppermute | solution.py:329
  6.5 0.9 copy-done.4
  7.5 1.6 %collective-permute-start.1 = (bf16[1024,256]{1,0:T(8,128)(2,1)S(1)}, bf16[1024,256]{1,0:T(8,128)(2,1)S(1)}, u32[]{:S(2)}, u32[]{:S(2)}) collective-permute-start(bf16[1024,256]{1,0:T(8,128)(2,1)S(1)} %assemble.2.refs_7_.refs_8_), channel_id=1, source_target_pairs={{2,6},{6,10},{10,14},{14,12},{12,8},{8,4},{4,0},{0,2},{3,1},{7,3},... | collective-permute-start | bytes 1572872 | tf_op jit(solution)/shard_map/ppermute | solution.py:329
  9.2 4.6 %collective-permute-done.6.refs_6_.refs_4_ = bf16[1024,256]{1,0:T(8,128)(2,1)S(1)} collective-permute-done((bf16[1024,256]{1,0:T(8,128)(2,1)S(1)}, bf16[1024,256]{1,0:T(8,128)(2,1)S(1)}, u32[]{:S(2)}, u32[]{:S(2)}) %collective-permute-start.6) | collective-permute-done | bytes 524320 | tf_op jit(solution)/shard_map/ppermute | solution.py:329
  13.7 5.6 %collective-permute-done.1.refs_1_.refs_7_.refs_6_ = bf16[1024,256]{1,0:T(8,128)(2,1)S(1)} collective-permute-done((bf16[1024,256]{1,0:T(8,128)(2,1)S(1)}, bf16[1024,256]{1,0:T(8,128)(2,1)S(1)}, u32[]{:S(2)}, u32[]{:S(2)}) %collective-permute-start.1) | collective-permute-done | bytes 524320 | tf_op jit(solution)/shard_map/ppermute | solution.py:329
  19.3 2.0 %collective-permute-start.3 = (bf16[1024,256]{1,0:T(8,128)(2,1)S(1)}, bf16[1024,256]{1,0:T(8,128)(2,1)S(1)}, u32[]{:S(2)}, u32[]{:S(2)}) collective-permute-start(bf16[1024,256]{1,0:T(8,128)(2,1)S(1)} %collective-permute-done.1.refs_1_.refs_7_.refs_6_), channel_id=1, source_target_pairs={{2,6},{6,10},{10,14},{14,12},{12,8},{8,4},{4,0},{0,2},{3,1},{7,3},... | collective-permute-start | bytes 1572872 | tf_op jit(solution)/shard_map/ppermute | solution.py:329
  21.3 1.6 collective-permute-start.10
  22.9 5.6 %collective-permute-done.3.refs_3_.refs_7_.refs_9_ = bf16[1024,256]{1,0:T(8,128)(2,1)S(1)} collective-permute-done((bf16[1024,256]{1,0:T(8,128)(2,1)S(1)}, bf16[1024,256]{1,0:T(8,128)(2,1)S(1)}, u32[]{:S(2)}, u32[]{:S(2)}) %collective-permute-start.3) | collective-permute-done | bytes 524320 | tf_op jit(solution)/shard_map/ppermute | solution.py:329
  28.5 2.0 %collective-permute-start.8 = (bf16[1024,256]{1,0:T(8,128)(2,1)S(1)}, bf16[1024,256]{1,0:T(8,128)(2,1)S(1)}, u32[]{:S(2)}, u32[]{:S(2)}) collective-permute-start(bf16[1024,256]{1,0:T(8,128)(2,1)S(1)} %collective-permute-done.3.refs_3_.refs_7_.refs_9_), channel_id=1, source_target_pairs={{2,6},{6,10},{10,14},{14,12},{12,8},{8,4},{4,0},{0,2},{3,1},{7,3},... | collective-permute-start | bytes 1572872 | tf_op jit(solution)/shard_map/ppermute | solution.py:329
  30.5 3.6 %collective-permute-done.10.refs_8_.refs_4_ = bf16[1024,256]{1,0:T(8,128)(2,1)S(1)} collective-permute-done((bf16[1024,256]{1,0:T(8,128)(2,1)S(1)}, bf16[1024,256]{1,0:T(8,128)(2,1)S(1)}, u32[]{:S(2)}, u32[]{:S(2)}) %collective-permute-start.10) | collective-permute-done | bytes 524320 | tf_op jit(solution)/shard_map/ppermute | solution.py:329
  34.1 2.0 %collective-permute-start.11 = (bf16[1024,256]{1,0:T(8,128)(2,1)S(1)}, bf16[1024,256]{1,0:T(8,128)(2,1)S(1)}, u32[]{:S(2)}, u32[]{:S(2)}) collective-permute-start(bf16[1024,256]{1,0:T(8,128)(2,1)S(1)} %collective-permute-done.10.refs_8_.refs_4_), channel_id=1, source_target_pairs={{2,6},{6,10},{10,14},{14,12},{12,8},{8,4},{4,0},{0,2},{3,1},{7,3},... | collective-permute-start | bytes 1572872 | tf_op jit(solution)/shard_map/ppermute | solution.py:329
  36.1 0.5 collective-permute-start.4
  36.6 3.1 %collective-permute-done.8.refs_5_.zero_ref.refs_8_.refs_7_ = bf16[1024,256]{1,0:T(8,128)(2,1)S(1)} collective-permute-done((bf16[1024,256]{1,0:T(8,128)(2,1)S(1)}, bf16[1024,256]{1,0:T(8,128)(2,1)S(1)}, u32[]{:S(2)}, u32[]{:S(2)}) %collective-permute-start.8) | collective-permute-done | bytes 524320 | tf_op jit(solution)/shard_map/ppermute | solution.py:329
  39.8 5.6 %collective-permute-done.11.one_ref.refs_10_.refs_5_ = bf16[1024,256]{1,0:T(8,128)(2,1)S(1)} collective-permute-done((bf16[1024,256]{1,0:T(8,128)(2,1)S(1)}, bf16[1024,256]{1,0:T(8,128)(2,1)S(1)}, u32[]{:S(2)}, u32[]{:S(2)}) %collective-permute-start.11) | collective-permute-done | bytes 524320 | tf_op jit(solution)/shard_map/ppermute | solution.py:329
  45.4 2.0 %collective-permute-start.13 = (bf16[1024,256]{1,0:T(8,128)(2,1)S(1)}, bf16[1024,256]{1,0:T(8,128)(2,1)S(1)}, u32[]{:S(2)}, u32[]{:S(2)}) collective-permute-start(bf16[1024,256]{1,0:T(8,128)(2,1)S(1)} %pick.3), channel_id=1, source_target_pairs={{2,6},{6,10},{10,14},{14,12},{12,8},{8,4},{4,0},{0,2},{3,1},{7,3},... | collective-permute-start | bytes 1572872 | tf_op jit(solution)/shard_map/ppermute | solution.py:329
  47.5 1.1 scale.1
  48.6 1.3 preact.1.refs_4_
  49.9 4.8 %collective-permute-done.13.zero_ref.one_ref = bf16[1024,256]{1,0:T(8,128)(2,1)S(1)} collective-permute-done((bf16[1024,256]{1,0:T(8,128)(2,1)S(1)}, bf16[1024,256]{1,0:T(8,128)(2,1)S(1)}, u32[]{:S(2)}, u32[]{:S(2)}) %collective-permute-start.13) | collective-permute-done | bytes 524320 | tf_op jit(solution)/shard_map/ppermute | solution.py:329
  54.7 0.5 collective-permute-start.15
  55.2 1.4 collective-permute-done.14.one_ref.zero_ref
  56.7 0.6 collective-permute-done.15.refs_11_.refs_4_
  57.3 3.9 %top.1 = (bf16[128,256]{1,0:T(8,128)(2,1)S(1)}, f32[128,1]{1,0:T(8,128)S(1)}, bf16[256,128]{1,0:T(8,128)(2,1)S(1)}, f32[128,256]{1,0:T(8,128)S(1)}, f32[128,256]...) custom-call(s32[16,8]{1,0:T(8,128)S(1)} %copy-done.2, ...), custom_call_target="tpu_custom_call" | custom-call | flops 1073741824 | bytes 3441024 | tf_op jit(solution)/shard_map/top/pallas_call | solution.py:64
  61.2 1.4 leave.4
  62.6 1.3 collective-permute-start.17
  63.9 1.2 leave.5
  65.1 1.3 collective-permute-start.21
  66.4 1.4 leave.3
  67.9 17.0 %collective-permute-done.17.refs_0_ = bf16[3,128,1024]{2,1,0:T(8,128)(2,1)S(1)} collective-permute-done((bf16[3,128,1024]{2,1,0:T(8,128)(2,1)S(1)}, bf16[3,128,1024]{2,1,0:T(8,128)(2,1)S(1)}, u32[]{:S(2)}, u32[]{:S(2)}) %collective-permute-start.17) | collective-permute-done | bytes 786464 | tf_op jit(solution)/shard_map/ppermute | solution.py:415
  84.9 1.5 arrive.3
  86.4 2.0 %collective-permute-start.18 = (bf16[256,1024]{1,0:T(8,128)(2,1)S(1)}, bf16[256,1024]{1,0:T(8,128)(2,1)S(1)}, u32[]{:S(2)}, u32[]{:S(2)}) collective-permute-start(bf16[256,1024]{1,0:T(8,128)(2,1)S(1)} %get-tuple-element.71), channel_id=1, source_target_pairs={{2,6},{6,10},{10,14},{14,12},{12,8},{8,4},{4,0},{0,2},{3,1},{7,3},... | collective-permute-start | bytes 1572872 | tf_op jit(solution)/shard_map/ppermute | solution.py:329
  88.4 1.3 collective-permute-start.16
  89.7 6.5 %collective-permute-done.21.refs_0_ = bf16[2,128,1024]{2,1,0:T(8,128)(2,1)S(1)} collective-permute-done((bf16[2,128,1024]{2,1,0:T(8,128)(2,1)S(1)}, bf16[2,128,1024]{2,1,0:T(8,128)(2,1)S(1)}, u32[]{:S(2)}, u32[]{:S(2)}) %collective-permute-start.21) | collective-permute-done | bytes 524320 | tf_op jit(solution)/shard_map/ppermute | solution.py:415
  96.1 1.3 arrive.4
  97.7 2.0 %collective-permute-start.20 = (bf16[256,1024]{1,0:T(8,128)(2,1)S(1)}, bf16[256,1024]{1,0:T(8,128)(2,1)S(1)}, u32[]{:S(2)}, u32[]{:S(2)}) collective-permute-start(bf16[256,1024]{1,0:T(8,128)(2,1)S(1)} %add.9), channel_id=1, source_target_pairs={{2,6},{6,10},{10,14},{14,12},{12,8},{8,4},{4,0},{0,2},{3,1},{7,3},... | collective-permute-start | bytes 1572872 | tf_op jit(solution)/shard_map/ppermute | solution.py:329
  99.7 7.2 %collective-permute-done.20.refs_0_ = bf16[256,1024]{1,0:T(8,128)(2,1)S(1)} collective-permute-done((bf16[256,1024]{1,0:T(8,128)(2,1)S(1)}, bf16[256,1024]{1,0:T(8,128)(2,1)S(1)}, u32[]{:S(2)}, u32[]{:S(2)}) %collective-permute-start.20) | collective-permute-done | bytes 524320 | tf_op jit(solution)/shard_map/ppermute | solution.py:329
  107.1 5.1 %collective-permute-done.16.refs_0_ = bf16[3,128,1024]{2,1,0:T(8,128)(2,1)S(1)} collective-permute-done((bf16[3,128,1024]{2,1,0:T(8,128)(2,1)S(1)}, bf16[3,128,1024]{2,1,0:T(8,128)(2,1)S(1)}, u32[]{:S(2)}, u32[]{:S(2)}) %collective-permute-start.16) | collective-permute-done | bytes 786464 | tf_op jit(solution)/shard_map/ppermute | solution.py:415
  112.2 1.7 %arrive.5 = (bf16[3,128,1024]{2,1,0:T(8,128)(2,1)S(1)}, bf16[128,256]{1,0:T(8,128)(2,1)S(1)}, bf16[256,128]{1,0:T(8,128)(2,1)S(1)}, f32[128,1]{1,0:T(8,128)S(1)}...) custom-call(s32[16,8]{1,0:T(8,128)S(1)} %copy-done.2, ...), custom_call_target="tpu_custom_call" | custom-call | flops 402653184 | bytes 2179328 | tf_op jit(solution)/shard_map/arrive/pallas_call | solution.py:64
  113.9 1.2 products.3
  115.2 2.0 %collective-permute-start.33 = (bf16[256,1024]{1,0:T(8,128)(2,1)S(1)}, bf16[256,1024]{1,0:T(8,128)(2,1)S(1)}, u32[]{:S(2)}, u32[]{:S(2)}) collective-permute-start(bf16[256,1024]{1,0:T(8,128)(2,1)S(1)} %add.10), channel_id=1, source_target_pairs={{2,6},{6,10},{10,14},{14,12},{12,8},{8,4},{4,0},{0,2},{3,1},{7,3},... | collective-permute-start | bytes 1572872 | tf_op jit(solution)/shard_map/ppermute | solution.py:329
  117.4 1.4 collective-permute-start.28
  118.8 1.6 collective-permute-start.23
  120.4 1.4 products.2
  121.8 5.5 %collective-permute-done.28.refs_0_ = bf16[256,512]{1,0:T(8,128)(2,1)S(1)} collective-permute-done((bf16[256,512]{1,0:T(8,128)(2,1)S(1)}, bf16[256,512]{1,0:T(8,128)(2,1)S(1)}, u32[]{:S(2)}, u32[]{:S(2)}) %collective-permute-start.28) | collective-permute-done | bytes 262176 | tf_op jit(solution)/shard_map/ppermute | solution.py:329
  127.4 2.0 %collective-permute-start.29 = (bf16[256,512]{1,0:T(8,128)(2,1)S(1)}, bf16[256,512]{1,0:T(8,128)(2,1)S(1)}, u32[]{:S(2)}, u32[]{:S(2)}) collective-permute-start(bf16[256,512]{1,0:T(8,128)(2,1)S(1)} %add.14), channel_id=1, source_target_pairs={{2,6},{6,10},{10,14},{14,12},{12,8},{8,4},{4,0},{0,2},{3,1},{7,3},... | collective-permute-start | bytes 786440 | tf_op jit(solution)/shard_map/ppermute | solution.py:329
  129.4 0.7 collective-permute-done.23.refs_0_
  130.2 2.0 %collective-permute-start.25 = (bf16[256,512]{1,0:T(8,128)(2,1)S(1)}, bf16[256,512]{1,0:T(8,128)(2,1)S(1)}, u32[]{:S(2)}, u32[]{:S(2)}) collective-permute-start(bf16[256,512]{1,0:T(8,128)(2,1)S(1)} %add.11), channel_id=1, source_target_pairs={{2,6},{6,10},{10,14},{14,12},{12,8},{8,4},{4,0},{0,2},{3,1},{7,3},... | collective-permute-start | bytes 786440 | tf_op jit(solution)/shard_map/ppermute | solution.py:329
  132.4 1.6 %collective-permute-start.35 = (bf16[256,1024]{1,0:T(8,128)(2,1)S(1)}, bf16[256,1024]{1,0:T(8,128)(2,1)S(1)}, u32[]{:S(2)}, u32[]{:S(2)}) collective-permute-start(bf16[256,1024]{1,0:T(8,128)(2,1)S(1)} %add.17), channel_id=1, source_target_pairs={{2,6},{6,10},{10,14},{14,12},{12,8},{8,4},{4,0},{0,2},{3,1},{7,3},... | collective-permute-start | bytes 1572872 | tf_op jit(solution)/shard_map/ppermute | solution.py:329
  134.0 2.6 %finish.2.refs_9_ = bf16[128,8192]{1,0:T(8,128)(2,1)} custom-call(s32[16,8]{1,0:T(8,128)S(1)} %copy-done.2, bf16[128,8192]{1,0:T(8,128)(2,1)S(1)} %bitcast.10, f32[1,8192]{1,0:T(1,128)S(1)} %copy-done.3, bf16[128,256]{1,0:T(8,128)(2,1)S(1)} %get-tuple-element.82.refs_2_, f32[128,1]{1,0:T(8,128)S(1)} %get-tuple-element.65.refs_4_.refs_3_, ...), custom_call_target="tpu_custom_call" | custom-call | flops 335544320 | bytes 2056576 | tf_op jit(solution)/shard_map/finish/pallas_call | solution.py:64
  136.7 1.6 %collective-permute-start.30 = (bf16[256,512]{1,0:T(8,128)(2,1)S(1)}, bf16[256,512]{1,0:T(8,128)(2,1)S(1)}, u32[]{:S(2)}, u32[]{:S(2)}) collective-permute-start(bf16[256,512]{1,0:T(8,128)(2,1)S(1)} %add.15), channel_id=1, source_target_pairs={{2,6},{6,10},{10,14},{14,12},{12,8},{8,4},{4,0},{0,2},{3,1},{7,3},... | collective-permute-start | bytes 786440 | tf_op jit(solution)/shard_map/ppermute | solution.py:329
  138.4 1.6 %collective-permute-start.26 = (bf16[256,512]{1,0:T(8,128)(2,1)S(1)}, bf16[256,512]{1,0:T(8,128)(2,1)S(1)}, u32[]{:S(2)}, u32[]{:S(2)}) collective-permute-start(bf16[256,512]{1,0:T(8,128)(2,1)S(1)} %add.12), channel_id=1, source_target_pairs={{2,6},{6,10},{10,14},{14,12},{12,8},{8,4},{4,0},{0,2},{3,1},{7,3},... | collective-permute-start | bytes 786440 | tf_op jit(solution)/shard_map/ppermute | solution.py:329
  140.1 5.0 %collective-permute-done.30.refs_0_ = bf16[256,512]{1,0:T(8,128)(2,1)S(1)} collective-permute-done((bf16[256,512]{1,0:T(8,128)(2,1)S(1)}, bf16[256,512]{1,0:T(8,128)(2,1)S(1)}, u32[]{:S(2)}, u32[]{:S(2)}) %collective-permute-start.30) | collective-permute-done | bytes 262176 | tf_op jit(solution)/shard_map/ppermute | solution.py:329
  145.1 2.0 %collective-permute-start.31 = (bf16[256,512]{1,0:T(8,128)(2,1)S(1)}, bf16[256,512]{1,0:T(8,128)(2,1)S(1)}, u32[]{:S(2)}, u32[]{:S(2)}) collective-permute-start(bf16[256,512]{1,0:T(8,128)(2,1)S(1)} %add.16), channel_id=1, source_target_pairs={{2,6},{6,10},{10,14},{14,12},{12,8},{8,4},{4,0},{0,2},{3,1},{7,3},... | collective-permute-start | bytes 786440 | tf_op jit(solution)/shard_map/ppermute | solution.py:329
  147.1 0.7 collective-permute-done.26.refs_0_
  147.9 2.0 %collective-permute-start.27 = (bf16[256,512]{1,0:T(8,128)(2,1)S(1)}, bf16[256,512]{1,0:T(8,128)(2,1)S(1)}, u32[]{:S(2)}, u32[]{:S(2)}) collective-permute-start(bf16[256,512]{1,0:T(8,128)(2,1)S(1)} %add.13), channel_id=1, source_target_pairs={{2,6},{6,10},{10,14},{14,12},{12,8},{8,4},{4,0},{0,2},{3,1},{7,3},... | collective-permute-start | bytes 786440 | tf_op jit(solution)/shard_map/ppermute | solution.py:329
  149.9 0.8 split.3
  150.9 2.2 %finish.3 = bf16[128,8192]{1,0:T(8,128)(2,1)} custom-call(s32[16,8]{1,0:T(8,128)S(1)} %copy-done.2, bf16[128,8192]{1,0:T(8,128)(2,1)S(1)} %bitcast.11, f32[1,8192]{1,0:T(1,128)S(1)} %copy-done.3, bf16[128,256]{1,0:T(8,128)(2,1)S(1)} %get-tuple-element.82.refs_2_, f32[128,1]{1,0:T(8,128)S(1)} %get-tuple-element.65.refs_4_.refs_3_, ...), custom_call_target="tpu_custom_call", output_to_operand_aliasing={{}: (10, {})} | custom-call | flops 201326592 | bytes 2187648 | tf_op jit(solution)/shard_map/finish/pallas_call | solution.py:64
  153.0 1.3 collective-permute-done.27.refs_0_
  154.4 0.8 split.2
  155.3 1.0 close_up.1
  156.3 0.5 collective-permute-done.32.refs_1_
  156.8 1.7 %close_down.1 = (f32[1,512,256]{2,1,0:T(8,128)}, f32[1,512]{1,0:T(1,128)}) custom-call(s32[16,8]{1,0:T(8,128)S(1)} %copy-done.2, f32[256,512]{1,0:T(8,128)S(1)} %get-tuple-element.100.refs_0_, bf16[256,512]{1,0:T(8,128)(2,1)S(1)} %collective-permute-done.32.refs_1_, f32[256,512]{1,0:T(8,128)S(1)} %get-tuple-element.102.refs_2_, f32[1,8192]{1,0:T(1,128)S(1)} %copy-done.3), custom_call_target="tpu_custom_call" | custom-call | bytes 467584 | tf_op jit(solution)/shard_map/close_down/pallas_call | solution.py:64
  (55 shorter events, 2.1 us)
Async XLA Ops:
  0.6 46.8 %copy-start = (bf16[1,128,8192]{2,1,0:T(8,128)(2,1)S(1)}, bf16[1,128,8192]{2,1,0:T(8,128)(2,1)}, u32[]{:S(2)}) copy-start(bf16[1,128,8192]{2,1,0:T(8,128)(2,1)} %param.7) | copy-start | bytes 6291460
  0.6 46.8 %copy-start.3 = (f32[1,8192]{1,0:T(1,128)S(1)}, f32[1,8192]{1,0:T(1,128)}, u32[]{:S(2)}) copy-start(f32[1,8192]{1,0:T(1,128)} %refs_3_.1) | copy-start | bytes 98308
  0.7 1.9 %collective-permute-start.5 = (bf16[512,256]{1,0:T(8,128)(2,1)}, bf16[512,256]{1,0:T(8,128)(2,1)S(1)}, u32[]{:S(2)}, u32[]{:S(2)}) collective-permute-start(bf16[512,256]{1,0:T(8,128)(2,1)} %bitcast.15), channel_id=1, source_target_pairs={{0,1},{1,0},{2,3},{3,2},{4,5},{5,4},{6,7},{7,6},{8,9},{9,8},{10,11... | collective-permute-start | bytes 786440 | tf_op jit(solution)/shard_map/ppermute | solution.py:326
  1.2 5.3 %collective-permute-start = (bf16[512,256]{1,0:T(8,128)(2,1)}, bf16[512,256]{1,0:T(8,128)(2,1)S(1)}, u32[]{:S(2)}, u32[]{:S(2)}) collective-permute-start(bf16[512,256]{1,0:T(8,128)(2,1)} %bitcast.12), channel_id=1, source_target_pairs={{0,1},{1,0},{2,3},{3,2},{4,5},{5,4},{6,7},{7,6},{8,9},{9,8},{10,11... | collective-permute-start | bytes 786440 | tf_op jit(solution)/shard_map/ppermute | solution.py:326
  2.5 0.9 copy-start.5
  3.6 10.2 %collective-permute-start.6 = (bf16[1024,256]{1,0:T(8,128)(2,1)S(1)}, bf16[1024,256]{1,0:T(8,128)(2,1)S(1)}, u32[]{:S(2)}, u32[]{:S(2)}) collective-permute-start(bf16[1024,256]{1,0:T(8,128)(2,1)S(1)} %assemble.3.refs_13_.refs_5_), channel_id=1, source_target_pairs={{2,6},{6,10},{10,14},{14,12},{12,8},{8,4},{4,0},{0,2},{3,1},{7,3},... | collective-permute-start | bytes 1572872 | tf_op jit(solution)/shard_map/ppermute | solution.py:329
  6.5 1.0 copy-start.4
  7.5 40.0 %copy-start.6 = (s32[128]{0:T(128)S(1)}, s32[128]{0:T(128)}, u32[]{:S(2)}) copy-start(s32[128]{0:T(128)} %param.9) | copy-start | bytes 1540
  7.5 41.1 %copy-start.2 = (s32[16,8]{1,0:T(8,128)S(1)}, s32[16,8]{1,0:T(8,128)}, u32[]{:S(2)}) copy-start(s32[16,8]{1,0:T(8,128)} %constant.2.clone.table_ref) | copy-start | bytes 1540
  7.5 11.8 %collective-permute-start.1 = (bf16[1024,256]{1,0:T(8,128)(2,1)S(1)}, bf16[1024,256]{1,0:T(8,128)(2,1)S(1)}, u32[]{:S(2)}, u32[]{:S(2)}) collective-permute-start(bf16[1024,256]{1,0:T(8,128)(2,1)S(1)} %assemble.2.refs_7_.refs_8_), channel_id=1, source_target_pairs={{2,6},{6,10},{10,14},{14,12},{12,8},{8,4},{4,0},{0,2},{3,1},{7,3},... | collective-permute-start | bytes 1572872 | tf_op jit(solution)/shard_map/ppermute | solution.py:329
  13.7 9.2 %collective-permute-start.7 = (bf16[1024,256]{1,0:T(8,128)(2,1)S(1)}, bf16[1024,256]{1,0:T(8,128)(2,1)S(1)}, u32[]{:S(2)}, u32[]{:S(2)}) collective-permute-start(bf16[1024,256]{1,0:T(8,128)(2,1)S(1)} %collective-permute-done.6.refs_6_.refs_4_), channel_id=1, source_target_pairs={{0,1},{1,0},{2,3},{3,2},{4,5},{5,4},{6,7},{7,6},{8,9},{9,8},{10,11... | collective-permute-start | bytes 1572872 | tf_op jit(solution)/shard_map/ppermute | solution.py:326
  19.3 9.2 %collective-permute-start.3 = (bf16[1024,256]{1,0:T(8,128)(2,1)S(1)}, bf16[1024,256]{1,0:T(8,128)(2,1)S(1)}, u32[]{:S(2)}, u32[]{:S(2)}) collective-permute-start(bf16[1024,256]{1,0:T(8,128)(2,1)S(1)} %collective-permute-done.1.refs_1_.refs_7_.refs_6_), channel_id=1, source_target_pairs={{2,6},{6,10},{10,14},{14,12},{12,8},{8,4},{4,0},{0,2},{3,1},{7,3},... | collective-permute-start | bytes 1572872 | tf_op jit(solution)/shard_map/ppermute | solution.py:329
  21.3 7.2 %collective-permute-start.2 = (bf16[1024,256]{1,0:T(8,128)(2,1)S(1)}, bf16[1024,256]{1,0:T(8,128)(2,1)S(1)}, u32[]{:S(2)}, u32[]{:S(2)}) collective-permute-start(bf16[1024,256]{1,0:T(8,128)(2,1)S(1)} %collective-permute-done.1.refs_1_.refs_7_.refs_6_), channel_id=1, source_target_pairs={{0,1},{1,0},{2,3},{3,2},{4,5},{5,4},{6,7},{7,6},{8,9},{9,8},{10,11... | collective-permute-start | bytes 1572872 | tf_op jit(solution)/shard_map/ppermute | solution.py:326
  21.3 12.8 %collective-permute-start.10 = (bf16[1024,256]{1,0:T(8,128)(2,1)S(1)}, bf16[1024,256]{1,0:T(8,128)(2,1)S(1)}, u32[]{:S(2)}, u32[]{:S(2)}) collective-permute-start(bf16[1024,256]{1,0:T(8,128)(2,1)S(1)} %collective-permute-done.6.refs_6_.refs_4_), channel_id=1, source_target_pairs={{2,6},{6,10},{10,14},{14,12},{12,8},{8,4},{4,0},{0,2},{3,1},{7,3},... | collective-permute-start | bytes 1572872 | tf_op jit(solution)/shard_map/ppermute | solution.py:329
  28.5 11.2 %collective-permute-start.8 = (bf16[1024,256]{1,0:T(8,128)(2,1)S(1)}, bf16[1024,256]{1,0:T(8,128)(2,1)S(1)}, u32[]{:S(2)}, u32[]{:S(2)}) collective-permute-start(bf16[1024,256]{1,0:T(8,128)(2,1)S(1)} %collective-permute-done.3.refs_3_.refs_7_.refs_9_), channel_id=1, source_target_pairs={{2,6},{6,10},{10,14},{14,12},{12,8},{8,4},{4,0},{0,2},{3,1},{7,3},... | collective-permute-start | bytes 1572872 | tf_op jit(solution)/shard_map/ppermute | solution.py:329
  34.1 11.2 %collective-permute-start.11 = (bf16[1024,256]{1,0:T(8,128)(2,1)S(1)}, bf16[1024,256]{1,0:T(8,128)(2,1)S(1)}, u32[]{:S(2)}, u32[]{:S(2)}) collective-permute-start(bf16[1024,256]{1,0:T(8,128)(2,1)S(1)} %collective-permute-done.10.refs_8_.refs_4_), channel_id=1, source_target_pairs={{2,6},{6,10},{10,14},{14,12},{12,8},{8,4},{4,0},{0,2},{3,1},{7,3},... | collective-permute-start | bytes 1572872 | tf_op jit(solution)/shard_map/ppermute | solution.py:329
  36.1 9.3 %collective-permute-start.12 = (bf16[1024,256]{1,0:T(8,128)(2,1)S(1)}, bf16[1024,256]{1,0:T(8,128)(2,1)S(1)}, u32[]{:S(2)}, u32[]{:S(2)}) collective-permute-start(bf16[1024,256]{1,0:T(8,128)(2,1)S(1)} %collective-permute-done.10.refs_8_.refs_4_), channel_id=1, source_target_pairs={{0,1},{1,0},{2,3},{3,2},{4,5},{5,4},{6,7},{7,6},{8,9},{9,8},{10,11... | collective-permute-start | bytes 1572872 | tf_op jit(solution)/shard_map/ppermute | solution.py:326
  36.1 9.3 %collective-permute-start.4 = (bf16[1024,256]{1,0:T(8,128)(2,1)S(1)}, bf16[1024,256]{1,0:T(8,128)(2,1)S(1)}, u32[]{:S(2)}, u32[]{:S(2)}) collective-permute-start(bf16[1024,256]{1,0:T(8,128)(2,1)S(1)} %collective-permute-done.3.refs_3_.refs_7_.refs_9_), channel_id=1, source_target_pairs={{0,1},{1,0},{2,3},{3,2},{4,5},{5,4},{6,7},{7,6},{8,9},{9,8},{10,11... | collective-permute-start | bytes 1572872 | tf_op jit(solution)/shard_map/ppermute | solution.py:326
  39.8 8.8 %collective-permute-start.9 = (bf16[1024,256]{1,0:T(8,128)(2,1)S(1)}, bf16[1024,256]{1,0:T(8,128)(2,1)S(1)}, u32[]{:S(2)}, u32[]{:S(2)}) collective-permute-start(bf16[1024,256]{1,0:T(8,128)(2,1)S(1)} %collective-permute-done.8.refs_5_.zero_ref.refs_8_.refs_7_), channel_id=1, source_target_pairs={{0,1},{1,0},{2,3},{3,2},{4,5},{5,4},{6,7},{7,6},{8,9},{9,8},{10,11... | collective-permute-start | bytes 1572872 | tf_op jit(solution)/shard_map/ppermute | solution.py:326
  45.4 9.2 %collective-permute-start.13 = (bf16[1024,256]{1,0:T(8,128)(2,1)S(1)}, bf16[1024,256]{1,0:T(8,128)(2,1)S(1)}, u32[]{:S(2)}, u32[]{:S(2)}) collective-permute-start(bf16[1024,256]{1,0:T(8,128)(2,1)S(1)} %pick.3), channel_id=1, source_target_pairs={{2,6},{6,10},{10,14},{14,12},{12,8},{8,4},{4,0},{0,2},{3,1},{7,3},... | collective-permute-start | bytes 1572872 | tf_op jit(solution)/shard_map/ppermute | solution.py:329
  49.9 7.4 %copy-start.1 = (bf16[128,8192]{1,0:T(8,128)(2,1)S(1)}, bf16[128,8192]{1,0:T(8,128)(2,1)}, u32[]{:S(2)}) copy-start(bf16[128,8192]{1,0:T(8,128)(2,1)} %refs_1_.3) | copy-start | bytes 6291460
  54.7 1.9 %collective-permute-start.14 = (bf16[1024,256]{1,0:T(8,128)(2,1)S(1)}, bf16[1024,256]{1,0:T(8,128)(2,1)S(1)}, u32[]{:S(2)}, u32[]{:S(2)}) collective-permute-start(bf16[1024,256]{1,0:T(8,128)(2,1)S(1)} %collective-permute-done.13.zero_ref.one_ref), channel_id=1, source_target_pairs={{0,1},{1,0},{2,3},{3,2},{4,5},{5,4},{6,7},{7,6},{8,9},{9,8},{10,11... | collective-permute-start | bytes 1572872 | tf_op jit(solution)/shard_map/ppermute | solution.py:326
  54.7 2.7 %collective-permute-start.15 = (bf16[1024,256]{1,0:T(8,128)(2,1)S(1)}, bf16[1024,256]{1,0:T(8,128)(2,1)S(1)}, u32[]{:S(2)}, u32[]{:S(2)}) collective-permute-start(bf16[1024,256]{1,0:T(8,128)(2,1)S(1)} %collective-permute-done.11.one_ref.refs_10_.refs_5_), channel_id=1, source_target_pairs={{0,1},{1,0},{2,3},{3,2},{4,5},{5,4},{6,7},{7,6},{8,9},{9,8},{10,11... | collective-permute-start | bytes 1572872 | tf_op jit(solution)/shard_map/ppermute | solution.py:326
  62.6 22.3 %collective-permute-start.17 = (bf16[3,128,1024]{2,1,0:T(8,128)(2,1)S(1)}, bf16[3,128,1024]{2,1,0:T(8,128)(2,1)S(1)}, u32[]{:S(2)}, u32[]{:S(2)}) collective-permute-start(bf16[3,128,1024]{2,1,0:T(8,128)(2,1)S(1)} %leave.4), channel_id=1, source_target_pairs={{16,0},{17,1},{18,2},{19,3},{20,4},{21,5},{22,6},{23,7},{24,8},{25... | collective-permute-start | bytes 2359304 | tf_op jit(solution)/shard_map/ppermute | solution.py:415
  65.1 31.0 %collective-permute-start.21 = (bf16[2,128,1024]{2,1,0:T(8,128)(2,1)S(1)}, bf16[2,128,1024]{2,1,0:T(8,128)(2,1)S(1)}, u32[]{:S(2)}, u32[]{:S(2)}) collective-permute-start(bf16[2,128,1024]{2,1,0:T(8,128)(2,1)S(1)} %leave.5), channel_id=1, source_target_pairs={{16,0},{17,1},{18,2},{19,3},{20,4},{21,5},{22,6},{23,7},{24,8},{25... | collective-permute-start | bytes 1572872 | tf_op jit(solution)/shard_map/ppermute | solution.py:415
  86.4 9.8 %collective-permute-start.18 = (bf16[256,1024]{1,0:T(8,128)(2,1)S(1)}, bf16[256,1024]{1,0:T(8,128)(2,1)S(1)}, u32[]{:S(2)}, u32[]{:S(2)}) collective-permute-start(bf16[256,1024]{1,0:T(8,128)(2,1)S(1)} %get-tuple-element.71), channel_id=1, source_target_pairs={{2,6},{6,10},{10,14},{14,12},{12,8},{8,4},{4,0},{0,2},{3,1},{7,3},... | collective-permute-start | bytes 1572872 | tf_op jit(solution)/shard_map/ppermute | solution.py:329
  88.4 9.1 %collective-permute-start.19 = (bf16[256,1024]{1,0:T(8,128)(2,1)S(1)}, bf16[256,1024]{1,0:T(8,128)(2,1)S(1)}, u32[]{:S(2)}, u32[]{:S(2)}) collective-permute-start(bf16[256,1024]{1,0:T(8,128)(2,1)S(1)} %get-tuple-element.73), channel_id=1, source_target_pairs={{0,1},{1,0},{2,3},{3,2},{4,5},{5,4},{6,7},{7,6},{8,9},{9,8},{10,11... | collective-permute-start | bytes 1572872 | tf_op jit(solution)/shard_map/ppermute | solution.py:326
  88.4 23.8 %collective-permute-start.16 = (bf16[3,128,1024]{2,1,0:T(8,128)(2,1)S(1)}, bf16[3,128,1024]{2,1,0:T(8,128)(2,1)S(1)}, u32[]{:S(2)}, u32[]{:S(2)}) collective-permute-start(bf16[3,128,1024]{2,1,0:T(8,128)(2,1)S(1)} %leave.3), channel_id=1, source_target_pairs={{16,0},{17,1},{18,2},{19,3},{20,4},{21,5},{22,6},{23,7},{24,8},{25... | collective-permute-start | bytes 2359304 | tf_op jit(solution)/shard_map/ppermute | solution.py:415
  97.4 2.3 %collective-permute-start.22 = (bf16[256,1024]{1,0:T(8,128)(2,1)S(1)}, bf16[256,1024]{1,0:T(8,128)(2,1)S(1)}, u32[]{:S(2)}, u32[]{:S(2)}) collective-permute-start(bf16[256,1024]{1,0:T(8,128)(2,1)S(1)} %get-tuple-element.77), channel_id=1, source_target_pairs={{0,1},{1,0},{2,3},{3,2},{4,5},{5,4},{6,7},{7,6},{8,9},{9,8},{10,11... | collective-permute-start | bytes 1572872 | tf_op jit(solution)/shard_map/ppermute | solution.py:326
  97.7 9.2 %collective-permute-start.20 = (bf16[256,1024]{1,0:T(8,128)(2,1)S(1)}, bf16[256,1024]{1,0:T(8,128)(2,1)S(1)}, u32[]{:S(2)}, u32[]{:S(2)}) collective-permute-start(bf16[256,1024]{1,0:T(8,128)(2,1)S(1)} %add.9), channel_id=1, source_target_pairs={{2,6},{6,10},{10,14},{14,12},{12,8},{8,4},{4,0},{0,2},{3,1},{7,3},... | collective-permute-start | bytes 1572872 | tf_op jit(solution)/shard_map/ppermute | solution.py:329
  115.1 12.1 %collective-permute-start.24 = (bf16[6,256,512]{2,1,0:T(8,128)(2,1)S(1)}, bf16[6,256,512]{2,1,0:T(8,128)(2,1)S(1)}, u32[]{:S(2)}, u32[]{:S(2)}) collective-permute-start(bf16[6,256,512]{2,1,0:T(8,128)(2,1)S(1)} %products.3), channel_id=1, source_target_pairs={{0,1},{1,0},{2,3},{3,2},{4,5},{5,4},{6,7},{7,6},{8,9},{9,8},{10,11... | collective-permute-start | bytes 4718600 | tf_op jit(solution)/shard_map/ppermute | solution.py:326
  115.2 17.0 %collective-permute-start.33 = (bf16[256,1024]{1,0:T(8,128)(2,1)S(1)}, bf16[256,1024]{1,0:T(8,128)(2,1)S(1)}, u32[]{:S(2)}, u32[]{:S(2)}) collective-permute-start(bf16[256,1024]{1,0:T(8,128)(2,1)S(1)} %add.10), channel_id=1, source_target_pairs={{2,6},{6,10},{10,14},{14,12},{12,8},{8,4},{4,0},{0,2},{3,1},{7,3},... | collective-permute-start | bytes 1572872 | tf_op jit(solution)/shard_map/ppermute | solution.py:329
  117.2 15.0 %collective-permute-start.34 = (bf16[256,1024]{1,0:T(8,128)(2,1)S(1)}, bf16[256,1024]{1,0:T(8,128)(2,1)S(1)}, u32[]{:S(2)}, u32[]{:S(2)}) collective-permute-start(bf16[256,1024]{1,0:T(8,128)(2,1)S(1)} %get-tuple-element.105), channel_id=1, source_target_pairs={{0,1},{1,0},{2,3},{3,2},{4,5},{5,4},{6,7},{7,6},{8,9},{9,8},{10,11... | collective-permute-start | bytes 1572872 | tf_op jit(solution)/shard_map/ppermute | solution.py:326
  117.4 9.8 %collective-permute-start.28 = (bf16[256,512]{1,0:T(8,128)(2,1)S(1)}, bf16[256,512]{1,0:T(8,128)(2,1)S(1)}, u32[]{:S(2)}, u32[]{:S(2)}) collective-permute-start(bf16[256,512]{1,0:T(8,128)(2,1)S(1)} %get-tuple-element.92), channel_id=1, source_target_pairs={{2,6},{6,10},{10,14},{14,12},{12,8},{8,4},{4,0},{0,2},{3,1},{7,3},... | collective-permute-start | bytes 786440 | tf_op jit(solution)/shard_map/ppermute | solution.py:329
  118.8 11.3 %collective-permute-start.23 = (bf16[256,512]{1,0:T(8,128)(2,1)S(1)}, bf16[256,512]{1,0:T(8,128)(2,1)S(1)}, u32[]{:S(2)}, u32[]{:S(2)}) collective-permute-start(bf16[256,512]{1,0:T(8,128)(2,1)S(1)} %get-tuple-element.87), channel_id=1, source_target_pairs={{2,6},{6,10},{10,14},{14,12},{12,8},{8,4},{4,0},{0,2},{3,1},{7,3},... | collective-permute-start | bytes 786440 | tf_op jit(solution)/shard_map/ppermute | solution.py:329
  127.4 9.2 %collective-permute-start.29 = (bf16[256,512]{1,0:T(8,128)(2,1)S(1)}, bf16[256,512]{1,0:T(8,128)(2,1)S(1)}, u32[]{:S(2)}, u32[]{:S(2)}) collective-permute-start(bf16[256,512]{1,0:T(8,128)(2,1)S(1)} %add.14), channel_id=1, source_target_pairs={{2,6},{6,10},{10,14},{14,12},{12,8},{8,4},{4,0},{0,2},{3,1},{7,3},... | collective-permute-start | bytes 786440 | tf_op jit(solution)/shard_map/ppermute | solution.py:329
  130.2 8.1 %collective-permute-start.25 = (bf16[256,512]{1,0:T(8,128)(2,1)S(1)}, bf16[256,512]{1,0:T(8,128)(2,1)S(1)}, u32[]{:S(2)}, u32[]{:S(2)}) collective-permute-start(bf16[256,512]{1,0:T(8,128)(2,1)S(1)} %add.11), channel_id=1, source_target_pairs={{2,6},{6,10},{10,14},{14,12},{12,8},{8,4},{4,0},{0,2},{3,1},{7,3},... | collective-permute-start | bytes 786440 | tf_op jit(solution)/shard_map/ppermute | solution.py:329
  132.4 17.6 %collective-permute-start.35 = (bf16[256,1024]{1,0:T(8,128)(2,1)S(1)}, bf16[256,1024]{1,0:T(8,128)(2,1)S(1)}, u32[]{:S(2)}, u32[]{:S(2)}) collective-permute-start(bf16[256,1024]{1,0:T(8,128)(2,1)S(1)} %add.17), channel_id=1, source_target_pairs={{2,6},{6,10},{10,14},{14,12},{12,8},{8,4},{4,0},{0,2},{3,1},{7,3},... | collective-permute-start | bytes 1572872 | tf_op jit(solution)/shard_map/ppermute | solution.py:329
  136.7 8.3 %collective-permute-start.30 = (bf16[256,512]{1,0:T(8,128)(2,1)S(1)}, bf16[256,512]{1,0:T(8,128)(2,1)S(1)}, u32[]{:S(2)}, u32[]{:S(2)}) collective-permute-start(bf16[256,512]{1,0:T(8,128)(2,1)S(1)} %add.15), channel_id=1, source_target_pairs={{2,6},{6,10},{10,14},{14,12},{12,8},{8,4},{4,0},{0,2},{3,1},{7,3},... | collective-permute-start | bytes 786440 | tf_op jit(solution)/shard_map/ppermute | solution.py:329
  138.4 9.4 %collective-permute-start.26 = (bf16[256,512]{1,0:T(8,128)(2,1)S(1)}, bf16[256,512]{1,0:T(8,128)(2,1)S(1)}, u32[]{:S(2)}, u32[]{:S(2)}) collective-permute-start(bf16[256,512]{1,0:T(8,128)(2,1)S(1)} %add.12), channel_id=1, source_target_pairs={{2,6},{6,10},{10,14},{14,12},{12,8},{8,4},{4,0},{0,2},{3,1},{7,3},... | collective-permute-start | bytes 786440 | tf_op jit(solution)/shard_map/ppermute | solution.py:329
  145.1 7.9 %collective-permute-start.31 = (bf16[256,512]{1,0:T(8,128)(2,1)S(1)}, bf16[256,512]{1,0:T(8,128)(2,1)S(1)}, u32[]{:S(2)}, u32[]{:S(2)}) collective-permute-start(bf16[256,512]{1,0:T(8,128)(2,1)S(1)} %add.16), channel_id=1, source_target_pairs={{2,6},{6,10},{10,14},{14,12},{12,8},{8,4},{4,0},{0,2},{3,1},{7,3},... | collective-permute-start | bytes 786440 | tf_op jit(solution)/shard_map/ppermute | solution.py:329
  147.9 6.4 %collective-permute-start.27 = (bf16[256,512]{1,0:T(8,128)(2,1)S(1)}, bf16[256,512]{1,0:T(8,128)(2,1)S(1)}, u32[]{:S(2)}, u32[]{:S(2)}) collective-permute-start(bf16[256,512]{1,0:T(8,128)(2,1)S(1)} %add.13), channel_id=1, source_target_pairs={{2,6},{6,10},{10,14},{14,12},{12,8},{8,4},{4,0},{0,2},{3,1},{7,3},... | collective-permute-start | bytes 786440 | tf_op jit(solution)/shard_map/ppermute | solution.py:329
  150.8 4.5 %collective-permute-start.36 = (bf16[256,512]{1,0:T(8,128)(2,1)S(1)}, bf16[256,512]{1,0:T(8,128)(2,1)S(1)}, u32[]{:S(2)}, u32[]{:S(2)}) collective-permute-start(bf16[256,512]{1,0:T(8,128)(2,1)S(1)} %get-tuple-element.108), channel_id=1, source_target_pairs={{0,1},{1,0},{2,3},{3,2},{4,5},{5,4},{6,7},{7,6},{8,9},{9,8},{10,11... | collective-permute-start | bytes 786440 | tf_op jit(solution)/shard_map/ppermute | solution.py:326
  155.2 1.6 %collective-permute-start.32 = (bf16[256,512]{1,0:T(8,128)(2,1)S(1)}, bf16[256,512]{1,0:T(8,128)(2,1)S(1)}, u32[]{:S(2)}, u32[]{:S(2)}) collective-permute-start(bf16[256,512]{1,0:T(8,128)(2,1)S(1)} %get-tuple-element.101), channel_id=1, source_target_pairs={{0,1},{1,0},{2,3},{3,2},{4,5},{5,4},{6,7},{7,6},{8,9},{9,8},{10,11... | collective-permute-start | bytes 786440 | tf_op jit(solution)/shard_map/ppermute | solution.py:326

commit v6 on v5

--- a/solution.py
+++ b/solution.py
@@ -357,7 +357,7 @@
     )
     down_block, up_block = downs[own], ups[own]
     for k in range(1, half):
-        earlier = [downs[ahead(k - 2)], ups[ahead(k - 2)]] if k >= 3 else []
+        earlier = []
         downs[behind(k)] = down_block = onward(after(down_block, *earlier))
         ups[behind(k)] = up_block = onward(up_block)
         downs[ahead(k)] = swap(down_block)

time: 159 us -> 156 us (0.981)
  waiting for transfers between devices: 85.8 us -> 82.6 us
    ppermute x19, waiting for transfers between devices: 53.4 us -> 49.4 us  [onward(): return lax.ppermute(value, 'dp', routes.onward)]
  transfers between devices with their start and end apart: 37 -> 37, of which waited for: 20 -> 21; matrix products, arithmetic and copies ran while one was open for 0% -> 0% of each run, Pallas kernels for 11% -> 11%
where the time goes in v6:
time: 156 us
  waiting for transfers between devices  82.6 us (53%)
  starting transfers between devices  42.3 us (27%)
  Pallas kernels  27.8 us (18%)
  local copies, waits for them, and re-layouts  1.93 us (1%)
    ppermute x19, waiting for transfers between devices, onward(): return lax.ppermute(value, 'dp', routes.onward)  49.4 us
    ppermute x19, starting transfers between devices, onward(): return lax.ppermute(value, 'dp', routes.onward)  36.3 us
    ppermute x3, waiting for transfers between devices, local(): arrived = [lax.ppermute(value, 'section', back) for value in sent]  28.6 us
    pallas_call x31, Pallas kernels, call(): pl.pallas_call(body, in_specs=specs or [VMEM] * len(args), out_specs=out_...  27.8 us
    ppermute x15, waiting for transfers between devices, swap(): return lax.ppermute(value, 'dp', routes.partner)  4.6 us
    ppermute x3, starting transfers between devices, local(): arrived = [lax.ppermute(value, 'section', back) for value in sent]  3.86 us
  transfers between devices with their start and end apart: 37, of which 21 were waited for; matrix products, arithmetic and copies ran while one was open for 0% of the time, Pallas kernels for 11%

profile of v6, /device:TPU:0, one launch (start us, length us, event | category | flops | bytes accessed | tf_op | source)
XLA Modules:
  0.0 155.7 jit_solution(3906750253504419218)
XLA Ops:
  0.7 0.5 collective-permute-start
  1.2 1.3 collective-permute-done.other_ref
  2.5 0.9 copy-done.4
  3.6 2.9 %collective-permute-start.1 = (bf16[1024,256]{1,0:T(8,128)(2,1)S(1)}, bf16[1024,256]{1,0:T(8,128)(2,1)S(1)}, u32[]{:S(2)}, u32[]{:S(2)}) collective-permute-start(bf16[1024,256]{1,0:T(8,128)(2,1)S(1)} %assemble.2.refs_7_.refs_8_), channel_id=1, source_target_pairs={{2,6},{6,10},{10,14},{14,12},{12,8},{8,4},{4,0},{0,2},{3,1},{7,3},... | collective-permute-start | bytes 1572872 | tf_op jit(solution)/shard_map/ppermute | solution.py:329
  6.5 0.9 copy-done.6
  7.5 1.6 %collective-permute-start.8 = (bf16[1024,256]{1,0:T(8,128)(2,1)S(1)}, bf16[1024,256]{1,0:T(8,128)(2,1)S(1)}, u32[]{:S(2)}, u32[]{:S(2)}) collective-permute-start(bf16[1024,256]{1,0:T(8,128)(2,1)S(1)} %assemble.3.refs_13_.refs_5_), channel_id=1, source_target_pairs={{2,6},{6,10},{10,14},{14,12},{12,8},{8,4},{4,0},{0,2},{3,1},{7,3},... | collective-permute-start | bytes 1572872 | tf_op jit(solution)/shard_map/ppermute | solution.py:329
  9.2 4.6 %collective-permute-done.1.refs_1_.refs_7_.refs_6_ = bf16[1024,256]{1,0:T(8,128)(2,1)S(1)} collective-permute-done((bf16[1024,256]{1,0:T(8,128)(2,1)S(1)}, bf16[1024,256]{1,0:T(8,128)(2,1)S(1)}, u32[]{:S(2)}, u32[]{:S(2)}) %collective-permute-start.1) | collective-permute-done | bytes 524320 | tf_op jit(solution)/shard_map/ppermute | solution.py:329
  13.7 2.0 %collective-permute-start.3 = (bf16[1024,256]{1,0:T(8,128)(2,1)S(1)}, bf16[1024,256]{1,0:T(8,128)(2,1)S(1)}, u32[]{:S(2)}, u32[]{:S(2)}) collective-permute-start(bf16[1024,256]{1,0:T(8,128)(2,1)S(1)} %collective-permute-done.1.refs_1_.refs_7_.refs_6_), channel_id=1, source_target_pairs={{2,6},{6,10},{10,14},{14,12},{12,8},{8,4},{4,0},{0,2},{3,1},{7,3},... | collective-permute-start | bytes 1572872 | tf_op jit(solution)/shard_map/ppermute | solution.py:329
  15.7 3.7 %collective-permute-done.8.refs_6_.refs_4_ = bf16[1024,256]{1,0:T(8,128)(2,1)S(1)} collective-permute-done((bf16[1024,256]{1,0:T(8,128)(2,1)S(1)}, bf16[1024,256]{1,0:T(8,128)(2,1)S(1)}, u32[]{:S(2)}, u32[]{:S(2)}) %collective-permute-start.8) | collective-permute-done | bytes 524320 | tf_op jit(solution)/shard_map/ppermute | solution.py:329
  19.3 2.0 %collective-permute-start.9 = (bf16[1024,256]{1,0:T(8,128)(2,1)S(1)}, bf16[1024,256]{1,0:T(8,128)(2,1)S(1)}, u32[]{:S(2)}, u32[]{:S(2)}) collective-permute-start(bf16[1024,256]{1,0:T(8,128)(2,1)S(1)} %collective-permute-done.8.refs_6_.refs_4_), channel_id=1, source_target_pairs={{2,6},{6,10},{10,14},{14,12},{12,8},{8,4},{4,0},{0,2},{3,1},{7,3},... | collective-permute-start | bytes 1572872 | tf_op jit(solution)/shard_map/ppermute | solution.py:329
  21.3 3.7 %collective-permute-done.3.refs_3_.refs_7_.refs_9_ = bf16[1024,256]{1,0:T(8,128)(2,1)S(1)} collective-permute-done((bf16[1024,256]{1,0:T(8,128)(2,1)S(1)}, bf16[1024,256]{1,0:T(8,128)(2,1)S(1)}, u32[]{:S(2)}, u32[]{:S(2)}) %collective-permute-start.3) | collective-permute-done | bytes 524320 | tf_op jit(solution)/shard_map/ppermute | solution.py:329
  25.0 2.0 %collective-permute-start.5 = (bf16[1024,256]{1,0:T(8,128)(2,1)S(1)}, bf16[1024,256]{1,0:T(8,128)(2,1)S(1)}, u32[]{:S(2)}, u32[]{:S(2)}) collective-permute-start(bf16[1024,256]{1,0:T(8,128)(2,1)S(1)} %collective-permute-done.3.refs_3_.refs_7_.refs_9_), channel_id=1, source_target_pairs={{2,6},{6,10},{10,14},{14,12},{12,8},{8,4},{4,0},{0,2},{3,1},{7,3},... | collective-permute-start | bytes 1572872 | tf_op jit(solution)/shard_map/ppermute | solution.py:329
  26.9 3.7 %collective-permute-done.9.refs_8_.refs_4_ = bf16[1024,256]{1,0:T(8,128)(2,1)S(1)} collective-permute-done((bf16[1024,256]{1,0:T(8,128)(2,1)S(1)}, bf16[1024,256]{1,0:T(8,128)(2,1)S(1)}, u32[]{:S(2)}, u32[]{:S(2)}) %collective-permute-start.9) | collective-permute-done | bytes 524320 | tf_op jit(solution)/shard_map/ppermute | solution.py:329
  30.6 2.0 %collective-permute-start.10 = (bf16[1024,256]{1,0:T(8,128)(2,1)S(1)}, bf16[1024,256]{1,0:T(8,128)(2,1)S(1)}, u32[]{:S(2)}, u32[]{:S(2)}) collective-permute-start(bf16[1024,256]{1,0:T(8,128)(2,1)S(1)} %collective-permute-done.9.refs_8_.refs_4_), channel_id=1, source_target_pairs={{2,6},{6,10},{10,14},{14,12},{12,8},{8,4},{4,0},{0,2},{3,1},{7,3},... | collective-permute-start | bytes 1572872 | tf_op jit(solution)/shard_map/ppermute | solution.py:329
  32.5 0.5 collective-permute-start.4
  33.0 3.1 %collective-permute-done.5.refs_5_.zero_ref.refs_8_.refs_7_ = bf16[1024,256]{1,0:T(8,128)(2,1)S(1)} collective-permute-done((bf16[1024,256]{1,0:T(8,128)(2,1)S(1)}, bf16[1024,256]{1,0:T(8,128)(2,1)S(1)}, u32[]{:S(2)}, u32[]{:S(2)}) %collective-permute-start.5) | collective-permute-done | bytes 524320 | tf_op jit(solution)/shard_map/ppermute | solution.py:329
  36.2 5.6 %collective-permute-done.10.one_ref.refs_10_.refs_5_ = bf16[1024,256]{1,0:T(8,128)(2,1)S(1)} collective-permute-done((bf16[1024,256]{1,0:T(8,128)(2,1)S(1)}, bf16[1024,256]{1,0:T(8,128)(2,1)S(1)}, u32[]{:S(2)}, u32[]{:S(2)}) %collective-permute-start.10) | collective-permute-done | bytes 524320 | tf_op jit(solution)/shard_map/ppermute | solution.py:329
  41.9 2.0 %collective-permute-start.12 = (bf16[1024,256]{1,0:T(8,128)(2,1)S(1)}, bf16[1024,256]{1,0:T(8,128)(2,1)S(1)}, u32[]{:S(2)}, u32[]{:S(2)}) collective-permute-start(bf16[1024,256]{1,0:T(8,128)(2,1)S(1)} %pick.3), channel_id=1, source_target_pairs={{2,6},{6,10},{10,14},{14,12},{12,8},{8,4},{4,0},{0,2},{3,1},{7,3},... | collective-permute-start | bytes 1572872 | tf_op jit(solution)/shard_map/ppermute | solution.py:329
  43.9 1.1 scale.1
  45.0 1.3 preact.1.refs_4_
  46.4 4.7 %collective-permute-done.12.zero_ref.one_ref = bf16[1024,256]{1,0:T(8,128)(2,1)S(1)} collective-permute-done((bf16[1024,256]{1,0:T(8,128)(2,1)S(1)}, bf16[1024,256]{1,0:T(8,128)(2,1)S(1)}, u32[]{:S(2)}, u32[]{:S(2)}) %collective-permute-start.12) | collective-permute-done | bytes 524320 | tf_op jit(solution)/shard_map/ppermute | solution.py:329
  51.6 1.4 collective-permute-done.13.one_ref.zero_ref
  53.2 0.6 collective-permute-done.14.refs_7_.refs_3_
  53.8 0.7 collective-permute-done.15.refs_11_.refs_4_
  54.5 3.9 %top.1 = (bf16[128,256]{1,0:T(8,128)(2,1)S(1)}, f32[128,1]{1,0:T(8,128)S(1)}, bf16[256,128]{1,0:T(8,128)(2,1)S(1)}, f32[128,256]{1,0:T(8,128)S(1)}, f32[128,256]...) custom-call(s32[16,8]{1,0:T(8,128)S(1)} %copy-done.2, ...), custom_call_target="tpu_custom_call" | custom-call | flops 1073741824 | bytes 3441024 | tf_op jit(solution)/shard_map/top/pallas_call | solution.py:64
  58.4 1.4 leave.4
  59.8 1.3 collective-permute-start.17
  61.1 1.2 leave.5
  62.3 1.3 collective-permute-start.21
  63.6 1.4 leave.3
  65.0 17.0 %collective-permute-done.17.refs_0_ = bf16[3,128,1024]{2,1,0:T(8,128)(2,1)S(1)} collective-permute-done((bf16[3,128,1024]{2,1,0:T(8,128)(2,1)S(1)}, bf16[3,128,1024]{2,1,0:T(8,128)(2,1)S(1)}, u32[]{:S(2)}, u32[]{:S(2)}) %collective-permute-start.17) | collective-permute-done | bytes 786464 | tf_op jit(solution)/shard_map/ppermute | solution.py:415
  82.1 1.5 arrive.3
  83.6 2.0 %collective-permute-start.18 = (bf16[256,1024]{1,0:T(8,128)(2,1)S(1)}, bf16[256,1024]{1,0:T(8,128)(2,1)S(1)}, u32[]{:S(2)}, u32[]{:S(2)}) collective-permute-start(bf16[256,1024]{1,0:T(8,128)(2,1)S(1)} %get-tuple-element.69), channel_id=1, source_target_pairs={{2,6},{6,10},{10,14},{14,12},{12,8},{8,4},{4,0},{0,2},{3,1},{7,3},... | collective-permute-start | bytes 1572872 | tf_op jit(solution)/shard_map/ppermute | solution.py:329
  85.6 1.3 collective-permute-start.16
  86.9 6.5 %collective-permute-done.21.refs_0_ = bf16[2,128,1024]{2,1,0:T(8,128)(2,1)S(1)} collective-permute-done((bf16[2,128,1024]{2,1,0:T(8,128)(2,1)S(1)}, bf16[2,128,1024]{2,1,0:T(8,128)(2,1)S(1)}, u32[]{:S(2)}, u32[]{:S(2)}) %collective-permute-start.21) | collective-permute-done | bytes 524320 | tf_op jit(solution)/shard_map/ppermute | solution.py:415
  93.3 1.3 arrive.4
  94.9 2.0 %collective-permute-start.20 = (bf16[256,1024]{1,0:T(8,128)(2,1)S(1)}, bf16[256,1024]{1,0:T(8,128)(2,1)S(1)}, u32[]{:S(2)}, u32[]{:S(2)}) collective-permute-start(bf16[256,1024]{1,0:T(8,128)(2,1)S(1)} %add.9), channel_id=1, source_target_pairs={{2,6},{6,10},{10,14},{14,12},{12,8},{8,4},{4,0},{0,2},{3,1},{7,3},... | collective-permute-start | bytes 1572872 | tf_op jit(solution)/shard_map/ppermute | solution.py:329
  96.9 7.2 %collective-permute-done.20.refs_0_ = bf16[256,1024]{1,0:T(8,128)(2,1)S(1)} collective-permute-done((bf16[256,1024]{1,0:T(8,128)(2,1)S(1)}, bf16[256,1024]{1,0:T(8,128)(2,1)S(1)}, u32[]{:S(2)}, u32[]{:S(2)}) %collective-permute-start.20) | collective-permute-done | bytes 524320 | tf_op jit(solution)/shard_map/ppermute | solution.py:329
  104.3 5.1 %collective-permute-done.16.refs_0_ = bf16[3,128,1024]{2,1,0:T(8,128)(2,1)S(1)} collective-permute-done((bf16[3,128,1024]{2,1,0:T(8,128)(2,1)S(1)}, bf16[3,128,1024]{2,1,0:T(8,128)(2,1)S(1)}, u32[]{:S(2)}, u32[]{:S(2)}) %collective-permute-start.16) | collective-permute-done | bytes 786464 | tf_op jit(solution)/shard_map/ppermute | solution.py:415
  109.4 1.7 %arrive.5 = (bf16[3,128,1024]{2,1,0:T(8,128)(2,1)S(1)}, bf16[128,256]{1,0:T(8,128)(2,1)S(1)}, bf16[256,128]{1,0:T(8,128)(2,1)S(1)}, f32[128,1]{1,0:T(8,128)S(1)}...) custom-call(s32[16,8]{1,0:T(8,128)S(1)} %copy-done.2, ...), custom_call_target="tpu_custom_call" | custom-call | flops 402653184 | bytes 2179328 | tf_op jit(solution)/shard_map/arrive/pallas_call | solution.py:64
  111.1 1.2 products.3
  112.4 2.0 %collective-permute-start.33 = (bf16[256,1024]{1,0:T(8,128)(2,1)S(1)}, bf16[256,1024]{1,0:T(8,128)(2,1)S(1)}, u32[]{:S(2)}, u32[]{:S(2)}) collective-permute-start(bf16[256,1024]{1,0:T(8,128)(2,1)S(1)} %add.10), channel_id=1, source_target_pairs={{2,6},{6,10},{10,14},{14,12},{12,8},{8,4},{4,0},{0,2},{3,1},{7,3},... | collective-permute-start | bytes 1572872 | tf_op jit(solution)/shard_map/ppermute | solution.py:329
  114.6 1.3 collective-permute-start.28
  116.0 1.6 %collective-permute-start.23 = (bf16[256,512]{1,0:T(8,128)(2,1)S(1)}, bf16[256,512]{1,0:T(8,128)(2,1)S(1)}, u32[]{:S(2)}, u32[]{:S(2)}) collective-permute-start(bf16[256,512]{1,0:T(8,128)(2,1)S(1)} %get-tuple-element.85), channel_id=1, source_target_pairs={{2,6},{6,10},{10,14},{14,12},{12,8},{8,4},{4,0},{0,2},{3,1},{7,3},... | collective-permute-start | bytes 786440 | tf_op jit(solution)/shard_map/ppermute | solution.py:329
  117.6 1.4 products.2
  118.9 5.5 %collective-permute-done.28.refs_0_ = bf16[256,512]{1,0:T(8,128)(2,1)S(1)} collective-permute-done((bf16[256,512]{1,0:T(8,128)(2,1)S(1)}, bf16[256,512]{1,0:T(8,128)(2,1)S(1)}, u32[]{:S(2)}, u32[]{:S(2)}) %collective-permute-start.28) | collective-permute-done | bytes 262176 | tf_op jit(solution)/shard_map/ppermute | solution.py:329
  124.5 2.0 %collective-permute-start.29 = (bf16[256,512]{1,0:T(8,128)(2,1)S(1)}, bf16[256,512]{1,0:T(8,128)(2,1)S(1)}, u32[]{:S(2)}, u32[]{:S(2)}) collective-permute-start(bf16[256,512]{1,0:T(8,128)(2,1)S(1)} %add.14), channel_id=1, source_target_pairs={{2,6},{6,10},{10,14},{14,12},{12,8},{8,4},{4,0},{0,2},{3,1},{7,3},... | collective-permute-start | bytes 786440 | tf_op jit(solution)/shard_map/ppermute | solution.py:329
  126.6 0.7 collective-permute-done.23.refs_0_
  127.4 2.0 %collective-permute-start.25 = (bf16[256,512]{1,0:T(8,128)(2,1)S(1)}, bf16[256,512]{1,0:T(8,128)(2,1)S(1)}, u32[]{:S(2)}, u32[]{:S(2)}) collective-permute-start(bf16[256,512]{1,0:T(8,128)(2,1)S(1)} %add.11), channel_id=1, source_target_pairs={{2,6},{6,10},{10,14},{14,12},{12,8},{8,4},{4,0},{0,2},{3,1},{7,3},... | collective-permute-start | bytes 786440 | tf_op jit(solution)/shard_map/ppermute | solution.py:329
  129.6 1.6 %collective-permute-start.35 = (bf16[256,1024]{1,0:T(8,128)(2,1)S(1)}, bf16[256,1024]{1,0:T(8,128)(2,1)S(1)}, u32[]{:S(2)}, u32[]{:S(2)}) collective-permute-start(bf16[256,1024]{1,0:T(8,128)(2,1)S(1)} %add.17), channel_id=1, source_target_pairs={{2,6},{6,10},{10,14},{14,12},{12,8},{8,4},{4,0},{0,2},{3,1},{7,3},... | collective-permute-start | bytes 1572872 | tf_op jit(solution)/shard_map/ppermute | solution.py:329
  131.2 2.6 %finish.2.refs_9_ = bf16[128,8192]{1,0:T(8,128)(2,1)} custom-call(s32[16,8]{1,0:T(8,128)S(1)} %copy-done.2, bf16[128,8192]{1,0:T(8,128)(2,1)S(1)} %bitcast.10, f32[1,8192]{1,0:T(1,128)S(1)} %copy-done.3, bf16[128,256]{1,0:T(8,128)(2,1)S(1)} %get-tuple-element.80.refs_2_, f32[128,1]{1,0:T(8,128)S(1)} %get-tuple-element.63.refs_4_.refs_3_, ...), custom_call_target="tpu_custom_call" | custom-call | flops 335544320 | bytes 2056576 | tf_op jit(solution)/shard_map/finish/pallas_call | solution.py:64
  133.9 1.6 %collective-permute-start.30 = (bf16[256,512]{1,0:T(8,128)(2,1)S(1)}, bf16[256,512]{1,0:T(8,128)(2,1)S(1)}, u32[]{:S(2)}, u32[]{:S(2)}) collective-permute-start(bf16[256,512]{1,0:T(8,128)(2,1)S(1)} %add.15), channel_id=1, source_target_pairs={{2,6},{6,10},{10,14},{14,12},{12,8},{8,4},{4,0},{0,2},{3,1},{7,3},... | collective-permute-start | bytes 786440 | tf_op jit(solution)/shard_map/ppermute | solution.py:329
  135.6 1.6 %collective-permute-start.26 = (bf16[256,512]{1,0:T(8,128)(2,1)S(1)}, bf16[256,512]{1,0:T(8,128)(2,1)S(1)}, u32[]{:S(2)}, u32[]{:S(2)}) collective-permute-start(bf16[256,512]{1,0:T(8,128)(2,1)S(1)} %add.12), channel_id=1, source_target_pairs={{2,6},{6,10},{10,14},{14,12},{12,8},{8,4},{4,0},{0,2},{3,1},{7,3},... | collective-permute-start | bytes 786440 | tf_op jit(solution)/shard_map/ppermute | solution.py:329
  137.2 5.0 %collective-permute-done.30.refs_0_ = bf16[256,512]{1,0:T(8,128)(2,1)S(1)} collective-permute-done((bf16[256,512]{1,0:T(8,128)(2,1)S(1)}, bf16[256,512]{1,0:T(8,128)(2,1)S(1)}, u32[]{:S(2)}, u32[]{:S(2)}) %collective-permute-start.30) | collective-permute-done | bytes 262176 | tf_op jit(solution)/shard_map/ppermute | solution.py:329
  142.3 2.0 %collective-permute-start.31 = (bf16[256,512]{1,0:T(8,128)(2,1)S(1)}, bf16[256,512]{1,0:T(8,128)(2,1)S(1)}, u32[]{:S(2)}, u32[]{:S(2)}) collective-permute-start(bf16[256,512]{1,0:T(8,128)(2,1)S(1)} %add.16), channel_id=1, source_target_pairs={{2,6},{6,10},{10,14},{14,12},{12,8},{8,4},{4,0},{0,2},{3,1},{7,3},... | collective-permute-start | bytes 786440 | tf_op jit(solution)/shard_map/ppermute | solution.py:329
  144.3 0.7 collective-permute-done.26.refs_0_
  145.1 2.0 %collective-permute-start.27 = (bf16[256,512]{1,0:T(8,128)(2,1)S(1)}, bf16[256,512]{1,0:T(8,128)(2,1)S(1)}, u32[]{:S(2)}, u32[]{:S(2)}) collective-permute-start(bf16[256,512]{1,0:T(8,128)(2,1)S(1)} %add.13), channel_id=1, source_target_pairs={{2,6},{6,10},{10,14},{14,12},{12,8},{8,4},{4,0},{0,2},{3,1},{7,3},... | collective-permute-start | bytes 786440 | tf_op jit(solution)/shard_map/ppermute | solution.py:329
  147.1 0.8 split.3
  148.0 2.2 %finish.3 = bf16[128,8192]{1,0:T(8,128)(2,1)} custom-call(s32[16,8]{1,0:T(8,128)S(1)} %copy-done.2, bf16[128,8192]{1,0:T(8,128)(2,1)S(1)} %bitcast.11, f32[1,8192]{1,0:T(1,128)S(1)} %copy-done.3, bf16[128,256]{1,0:T(8,128)(2,1)S(1)} %get-tuple-element.80.refs_2_, f32[128,1]{1,0:T(8,128)S(1)} %get-tuple-element.63.refs_4_.refs_3_, ...), custom_call_target="tpu_custom_call", output_to_operand_aliasing={{}: (10, {})} | custom-call | flops 201326592 | bytes 2187648 | tf_op jit(solution)/shard_map/finish/pallas_call | solution.py:64
  150.2 1.3 collective-permute-done.27.refs_0_
  151.5 0.8 split.2
  152.5 1.0 close_up.1
  153.5 0.5 collective-permute-done.32.refs_1_
  154.0 1.7 %close_down.1 = (f32[1,512,256]{2,1,0:T(8,128)}, f32[1,512]{1,0:T(1,128)}) custom-call(s32[16,8]{1,0:T(8,128)S(1)} %copy-done.2, f32[256,512]{1,0:T(8,128)S(1)} %get-tuple-element.98.refs_0_, bf16[256,512]{1,0:T(8,128)(2,1)S(1)} %collective-permute-done.32.refs_1_, f32[256,512]{1,0:T(8,128)S(1)} %get-tuple-element.100.refs_2_, f32[1,8192]{1,0:T(1,128)S(1)} %copy-done.3), custom_call_target="tpu_custom_call" | custom-call | bytes 467584 | tf_op jit(solution)/shard_map/close_down/pallas_call | solution.py:64
  (57 shorter events, 2.6 us)
Async XLA Ops:
  0.6 43.3 %copy-start = (bf16[1,128,8192]{2,1,0:T(8,128)(2,1)S(1)}, bf16[1,128,8192]{2,1,0:T(8,128)(2,1)}, u32[]{:S(2)}) copy-start(bf16[1,128,8192]{2,1,0:T(8,128)(2,1)} %param.7) | copy-start | bytes 6291460
  0.6 43.3 %copy-start.3 = (f32[1,8192]{1,0:T(1,128)S(1)}, f32[1,8192]{1,0:T(1,128)}, u32[]{:S(2)}) copy-start(f32[1,8192]{1,0:T(1,128)} %refs_3_.1) | copy-start | bytes 98308
  0.7 1.9 %collective-permute-start = (bf16[512,256]{1,0:T(8,128)(2,1)}, bf16[512,256]{1,0:T(8,128)(2,1)S(1)}, u32[]{:S(2)}, u32[]{:S(2)}) collective-permute-start(bf16[512,256]{1,0:T(8,128)(2,1)} %bitcast.12), channel_id=1, source_target_pairs={{0,1},{1,0},{2,3},{3,2},{4,5},{5,4},{6,7},{7,6},{8,9},{9,8},{10,11... | collective-permute-start | bytes 786440 | tf_op jit(solution)/shard_map/ppermute | solution.py:326
  1.2 5.3 %collective-permute-start.7 = (bf16[512,256]{1,0:T(8,128)(2,1)}, bf16[512,256]{1,0:T(8,128)(2,1)S(1)}, u32[]{:S(2)}, u32[]{:S(2)}) collective-permute-start(bf16[512,256]{1,0:T(8,128)(2,1)} %bitcast.15), channel_id=1, source_target_pairs={{0,1},{1,0},{2,3},{3,2},{4,5},{5,4},{6,7},{7,6},{8,9},{9,8},{10,11... | collective-permute-start | bytes 786440 | tf_op jit(solution)/shard_map/ppermute | solution.py:326
  2.5 0.9 copy-start.4
  3.5 40.4 %copy-start.5 = (bf16[1,512,256]{2,1,0:T(8,128)(2,1)S(1)}, bf16[1,512,256]{2,1,0:T(8,128)(2,1)}, u32[]{:S(2)}) copy-start(bf16[1,512,256]{2,1,0:T(8,128)(2,1)} %param.11) | copy-start | bytes 786436
  3.6 10.2 %collective-permute-start.1 = (bf16[1024,256]{1,0:T(8,128)(2,1)S(1)}, bf16[1024,256]{1,0:T(8,128)(2,1)S(1)}, u32[]{:S(2)}, u32[]{:S(2)}) collective-permute-start(bf16[1024,256]{1,0:T(8,128)(2,1)S(1)} %assemble.2.refs_7_.refs_8_), channel_id=1, source_target_pairs={{2,6},{6,10},{10,14},{14,12},{12,8},{8,4},{4,0},{0,2},{3,1},{7,3},... | collective-permute-start | bytes 1572872 | tf_op jit(solution)/shard_map/ppermute | solution.py:329
  6.5 1.0 copy-start.6
  7.5 36.5 %copy-start.7 = (s32[128]{0:T(128)S(1)}, s32[128]{0:T(128)}, u32[]{:S(2)}) copy-start(s32[128]{0:T(128)} %param.9) | copy-start | bytes 1540
  7.5 37.5 %copy-start.2 = (s32[16,8]{1,0:T(8,128)S(1)}, s32[16,8]{1,0:T(8,128)}, u32[]{:S(2)}) copy-start(s32[16,8]{1,0:T(8,128)} %constant.2.clone.table_ref) | copy-start | bytes 1540
  7.5 11.8 %collective-permute-start.8 = (bf16[1024,256]{1,0:T(8,128)(2,1)S(1)}, bf16[1024,256]{1,0:T(8,128)(2,1)S(1)}, u32[]{:S(2)}, u32[]{:S(2)}) collective-permute-start(bf16[1024,256]{1,0:T(8,128)(2,1)S(1)} %assemble.3.refs_13_.refs_5_), channel_id=1, source_target_pairs={{2,6},{6,10},{10,14},{14,12},{12,8},{8,4},{4,0},{0,2},{3,1},{7,3},... | collective-permute-start | bytes 1572872 | tf_op jit(solution)/shard_map/ppermute | solution.py:329
  13.7 11.2 %collective-permute-start.3 = (bf16[1024,256]{1,0:T(8,128)(2,1)S(1)}, bf16[1024,256]{1,0:T(8,128)(2,1)S(1)}, u32[]{:S(2)}, u32[]{:S(2)}) collective-permute-start(bf16[1024,256]{1,0:T(8,128)(2,1)S(1)} %collective-permute-done.1.refs_1_.refs_7_.refs_6_), channel_id=1, source_target_pairs={{2,6},{6,10},{10,14},{14,12},{12,8},{8,4},{4,0},{0,2},{3,1},{7,3},... | collective-permute-start | bytes 1572872 | tf_op jit(solution)/shard_map/ppermute | solution.py:329
  19.3 11.2 %collective-permute-start.9 = (bf16[1024,256]{1,0:T(8,128)(2,1)S(1)}, bf16[1024,256]{1,0:T(8,128)(2,1)S(1)}, u32[]{:S(2)}, u32[]{:S(2)}) collective-permute-start(bf16[1024,256]{1,0:T(8,128)(2,1)S(1)} %collective-permute-done.8.refs_6_.refs_4_), channel_id=1, source_target_pairs={{2,6},{6,10},{10,14},{14,12},{12,8},{8,4},{4,0},{0,2},{3,1},{7,3},... | collective-permute-start | bytes 1572872 | tf_op jit(solution)/shard_map/ppermute | solution.py:329
  25.0 11.2 %collective-permute-start.5 = (bf16[1024,256]{1,0:T(8,128)(2,1)S(1)}, bf16[1024,256]{1,0:T(8,128)(2,1)S(1)}, u32[]{:S(2)}, u32[]{:S(2)}) collective-permute-start(bf16[1024,256]{1,0:T(8,128)(2,1)S(1)} %collective-permute-done.3.refs_3_.refs_7_.refs_9_), channel_id=1, source_target_pairs={{2,6},{6,10},{10,14},{14,12},{12,8},{8,4},{4,0},{0,2},{3,1},{7,3},... | collective-permute-start | bytes 1572872 | tf_op jit(solution)/shard_map/ppermute | solution.py:329
  30.6 11.2 %collective-permute-start.10 = (bf16[1024,256]{1,0:T(8,128)(2,1)S(1)}, bf16[1024,256]{1,0:T(8,128)(2,1)S(1)}, u32[]{:S(2)}, u32[]{:S(2)}) collective-permute-start(bf16[1024,256]{1,0:T(8,128)(2,1)S(1)} %collective-permute-done.9.refs_8_.refs_4_), channel_id=1, source_target_pairs={{2,6},{6,10},{10,14},{14,12},{12,8},{8,4},{4,0},{0,2},{3,1},{7,3},... | collective-permute-start | bytes 1572872 | tf_op jit(solution)/shard_map/ppermute | solution.py:329
  32.5 9.3 %collective-permute-start.11 = (bf16[1024,256]{1,0:T(8,128)(2,1)S(1)}, bf16[1024,256]{1,0:T(8,128)(2,1)S(1)}, u32[]{:S(2)}, u32[]{:S(2)}) collective-permute-start(bf16[1024,256]{1,0:T(8,128)(2,1)S(1)} %collective-permute-done.9.refs_8_.refs_4_), channel_id=1, source_target_pairs={{0,1},{1,0},{2,3},{3,2},{4,5},{5,4},{6,7},{7,6},{8,9},{9,8},{10,11... | collective-permute-start | bytes 1572872 | tf_op jit(solution)/shard_map/ppermute | solution.py:326
  32.5 9.3 %collective-permute-start.4 = (bf16[1024,256]{1,0:T(8,128)(2,1)S(1)}, bf16[1024,256]{1,0:T(8,128)(2,1)S(1)}, u32[]{:S(2)}, u32[]{:S(2)}) collective-permute-start(bf16[1024,256]{1,0:T(8,128)(2,1)S(1)} %collective-permute-done.3.refs_3_.refs_7_.refs_9_), channel_id=1, source_target_pairs={{0,1},{1,0},{2,3},{3,2},{4,5},{5,4},{6,7},{7,6},{8,9},{9,8},{10,11... | collective-permute-start | bytes 1572872 | tf_op jit(solution)/shard_map/ppermute | solution.py:326
  33.0 12.0 %collective-permute-start.2 = (bf16[1024,256]{1,0:T(8,128)(2,1)S(1)}, bf16[1024,256]{1,0:T(8,128)(2,1)S(1)}, u32[]{:S(2)}, u32[]{:S(2)}) collective-permute-start(bf16[1024,256]{1,0:T(8,128)(2,1)S(1)} %collective-permute-done.1.refs_1_.refs_7_.refs_6_), channel_id=1, source_target_pairs={{0,1},{1,0},{2,3},{3,2},{4,5},{5,4},{6,7},{7,6},{8,9},{9,8},{10,11... | collective-permute-start | bytes 1572872 | tf_op jit(solution)/shard_map/ppermute | solution.py:326
  36.2 8.8 %collective-permute-start.6 = (bf16[1024,256]{1,0:T(8,128)(2,1)S(1)}, bf16[1024,256]{1,0:T(8,128)(2,1)S(1)}, u32[]{:S(2)}, u32[]{:S(2)}) collective-permute-start(bf16[1024,256]{1,0:T(8,128)(2,1)S(1)} %collective-permute-done.5.refs_5_.zero_ref.refs_8_.refs_7_), channel_id=1, source_target_pairs={{0,1},{1,0},{2,3},{3,2},{4,5},{5,4},{6,7},{7,6},{8,9},{9,8},{10,11... | collective-permute-start | bytes 1572872 | tf_op jit(solution)/shard_map/ppermute | solution.py:326
  41.9 9.2 %collective-permute-start.12 = (bf16[1024,256]{1,0:T(8,128)(2,1)S(1)}, bf16[1024,256]{1,0:T(8,128)(2,1)S(1)}, u32[]{:S(2)}, u32[]{:S(2)}) collective-permute-start(bf16[1024,256]{1,0:T(8,128)(2,1)S(1)} %pick.3), channel_id=1, source_target_pairs={{2,6},{6,10},{10,14},{14,12},{12,8},{8,4},{4,0},{0,2},{3,1},{7,3},... | collective-permute-start | bytes 1572872 | tf_op jit(solution)/shard_map/ppermute | solution.py:329
  46.4 8.2 %copy-start.1 = (bf16[128,8192]{1,0:T(8,128)(2,1)S(1)}, bf16[128,8192]{1,0:T(8,128)(2,1)}, u32[]{:S(2)}) copy-start(bf16[128,8192]{1,0:T(8,128)(2,1)} %refs_1_.3) | copy-start | bytes 6291460
  51.1 1.9 %collective-permute-start.13 = (bf16[1024,256]{1,0:T(8,128)(2,1)S(1)}, bf16[1024,256]{1,0:T(8,128)(2,1)S(1)}, u32[]{:S(2)}, u32[]{:S(2)}) collective-permute-start(bf16[1024,256]{1,0:T(8,128)(2,1)S(1)} %collective-permute-done.12.zero_ref.one_ref), channel_id=1, source_target_pairs={{0,1},{1,0},{2,3},{3,2},{4,5},{5,4},{6,7},{7,6},{8,9},{9,8},{10,11... | collective-permute-start | bytes 1572872 | tf_op jit(solution)/shard_map/ppermute | solution.py:326
  51.1 2.7 %collective-permute-start.14 = (bf16[1024,256]{1,0:T(8,128)(2,1)S(1)}, bf16[1024,256]{1,0:T(8,128)(2,1)S(1)}, u32[]{:S(2)}, u32[]{:S(2)}) collective-permute-start(bf16[1024,256]{1,0:T(8,128)(2,1)S(1)} %collective-permute-done.8.refs_6_.refs_4_), channel_id=1, source_target_pairs={{0,1},{1,0},{2,3},{3,2},{4,5},{5,4},{6,7},{7,6},{8,9},{9,8},{10,11... | collective-permute-start | bytes 1572872 | tf_op jit(solution)/shard_map/ppermute | solution.py:326
  51.6 2.9 %collective-permute-start.15 = (bf16[1024,256]{1,0:T(8,128)(2,1)S(1)}, bf16[1024,256]{1,0:T(8,128)(2,1)S(1)}, u32[]{:S(2)}, u32[]{:S(2)}) collective-permute-start(bf16[1024,256]{1,0:T(8,128)(2,1)S(1)} %collective-permute-done.10.one_ref.refs_10_.refs_5_), channel_id=1, source_target_pairs={{0,1},{1,0},{2,3},{3,2},{4,5},{5,4},{6,7},{7,6},{8,9},{9,8},{10,11... | collective-permute-start | bytes 1572872 | tf_op jit(solution)/shard_map/ppermute | solution.py:326
  59.8 22.3 %collective-permute-start.17 = (bf16[3,128,1024]{2,1,0:T(8,128)(2,1)S(1)}, bf16[3,128,1024]{2,1,0:T(8,128)(2,1)S(1)}, u32[]{:S(2)}, u32[]{:S(2)}) collective-permute-start(bf16[3,128,1024]{2,1,0:T(8,128)(2,1)S(1)} %leave.4), channel_id=1, source_target_pairs={{16,0},{17,1},{18,2},{19,3},{20,4},{21,5},{22,6},{23,7},{24,8},{25... | collective-permute-start | bytes 2359304 | tf_op jit(solution)/shard_map/ppermute | solution.py:415
  62.3 31.0 %collective-permute-start.21 = (bf16[2,128,1024]{2,1,0:T(8,128)(2,1)S(1)}, bf16[2,128,1024]{2,1,0:T(8,128)(2,1)S(1)}, u32[]{:S(2)}, u32[]{:S(2)}) collective-permute-start(bf16[2,128,1024]{2,1,0:T(8,128)(2,1)S(1)} %leave.5), channel_id=1, source_target_pairs={{16,0},{17,1},{18,2},{19,3},{20,4},{21,5},{22,6},{23,7},{24,8},{25... | collective-permute-start | bytes 1572872 | tf_op jit(solution)/shard_map/ppermute | solution.py:415
  83.6 9.8 %collective-permute-start.18 = (bf16[256,1024]{1,0:T(8,128)(2,1)S(1)}, bf16[256,1024]{1,0:T(8,128)(2,1)S(1)}, u32[]{:S(2)}, u32[]{:S(2)}) collective-permute-start(bf16[256,1024]{1,0:T(8,128)(2,1)S(1)} %get-tuple-element.69), channel_id=1, source_target_pairs={{2,6},{6,10},{10,14},{14,12},{12,8},{8,4},{4,0},{0,2},{3,1},{7,3},... | collective-permute-start | bytes 1572872 | tf_op jit(solution)/shard_map/ppermute | solution.py:329
  85.6 9.1 %collective-permute-start.19 = (bf16[256,1024]{1,0:T(8,128)(2,1)S(1)}, bf16[256,1024]{1,0:T(8,128)(2,1)S(1)}, u32[]{:S(2)}, u32[]{:S(2)}) collective-permute-start(bf16[256,1024]{1,0:T(8,128)(2,1)S(1)} %get-tuple-element.71), channel_id=1, source_target_pairs={{0,1},{1,0},{2,3},{3,2},{4,5},{5,4},{6,7},{7,6},{8,9},{9,8},{10,11... | collective-permute-start | bytes 1572872 | tf_op jit(solution)/shard_map/ppermute | solution.py:326
  85.6 23.8 %collective-permute-start.16 = (bf16[3,128,1024]{2,1,0:T(8,128)(2,1)S(1)}, bf16[3,128,1024]{2,1,0:T(8,128)(2,1)S(1)}, u32[]{:S(2)}, u32[]{:S(2)}) collective-permute-start(bf16[3,128,1024]{2,1,0:T(8,128)(2,1)S(1)} %leave.3), channel_id=1, source_target_pairs={{16,0},{17,1},{18,2},{19,3},{20,4},{21,5},{22,6},{23,7},{24,8},{25... | collective-permute-start | bytes 2359304 | tf_op jit(solution)/shard_map/ppermute | solution.py:415
  94.6 2.3 %collective-permute-start.22 = (bf16[256,1024]{1,0:T(8,128)(2,1)S(1)}, bf16[256,1024]{1,0:T(8,128)(2,1)S(1)}, u32[]{:S(2)}, u32[]{:S(2)}) collective-permute-start(bf16[256,1024]{1,0:T(8,128)(2,1)S(1)} %get-tuple-element.75), channel_id=1, source_target_pairs={{0,1},{1,0},{2,3},{3,2},{4,5},{5,4},{6,7},{7,6},{8,9},{9,8},{10,11... | collective-permute-start | bytes 1572872 | tf_op jit(solution)/shard_map/ppermute | solution.py:326
  94.9 9.2 %collective-permute-start.20 = (bf16[256,1024]{1,0:T(8,128)(2,1)S(1)}, bf16[256,1024]{1,0:T(8,128)(2,1)S(1)}, u32[]{:S(2)}, u32[]{:S(2)}) collective-permute-start(bf16[256,1024]{1,0:T(8,128)(2,1)S(1)} %add.9), channel_id=1, source_target_pairs={{2,6},{6,10},{10,14},{14,12},{12,8},{8,4},{4,0},{0,2},{3,1},{7,3},... | collective-permute-start | bytes 1572872 | tf_op jit(solution)/shard_map/ppermute | solution.py:329
  112.3 12.1 %collective-permute-start.24 = (bf16[6,256,512]{2,1,0:T(8,128)(2,1)S(1)}, bf16[6,256,512]{2,1,0:T(8,128)(2,1)S(1)}, u32[]{:S(2)}, u32[]{:S(2)}) collective-permute-start(bf16[6,256,512]{2,1,0:T(8,128)(2,1)S(1)} %products.3), channel_id=1, source_target_pairs={{0,1},{1,0},{2,3},{3,2},{4,5},{5,4},{6,7},{7,6},{8,9},{9,8},{10,11... | collective-permute-start | bytes 4718600 | tf_op jit(solution)/shard_map/ppermute | solution.py:326
  112.4 17.0 %collective-permute-start.33 = (bf16[256,1024]{1,0:T(8,128)(2,1)S(1)}, bf16[256,1024]{1,0:T(8,128)(2,1)S(1)}, u32[]{:S(2)}, u32[]{:S(2)}) collective-permute-start(bf16[256,1024]{1,0:T(8,128)(2,1)S(1)} %add.10), channel_id=1, source_target_pairs={{2,6},{6,10},{10,14},{14,12},{12,8},{8,4},{4,0},{0,2},{3,1},{7,3},... | collective-permute-start | bytes 1572872 | tf_op jit(solution)/shard_map/ppermute | solution.py:329
  114.4 15.0 %collective-permute-start.34 = (bf16[256,1024]{1,0:T(8,128)(2,1)S(1)}, bf16[256,1024]{1,0:T(8,128)(2,1)S(1)}, u32[]{:S(2)}, u32[]{:S(2)}) collective-permute-start(bf16[256,1024]{1,0:T(8,128)(2,1)S(1)} %get-tuple-element.103), channel_id=1, source_target_pairs={{0,1},{1,0},{2,3},{3,2},{4,5},{5,4},{6,7},{7,6},{8,9},{9,8},{10,11... | collective-permute-start | bytes 1572872 | tf_op jit(solution)/shard_map/ppermute | solution.py:326
  114.6 9.8 %collective-permute-start.28 = (bf16[256,512]{1,0:T(8,128)(2,1)S(1)}, bf16[256,512]{1,0:T(8,128)(2,1)S(1)}, u32[]{:S(2)}, u32[]{:S(2)}) collective-permute-start(bf16[256,512]{1,0:T(8,128)(2,1)S(1)} %get-tuple-element.90), channel_id=1, source_target_pairs={{2,6},{6,10},{10,14},{14,12},{12,8},{8,4},{4,0},{0,2},{3,1},{7,3},... | collective-permute-start | bytes 786440 | tf_op jit(solution)/shard_map/ppermute | solution.py:329
  116.0 11.3 %collective-permute-start.23 = (bf16[256,512]{1,0:T(8,128)(2,1)S(1)}, bf16[256,512]{1,0:T(8,128)(2,1)S(1)}, u32[]{:S(2)}, u32[]{:S(2)}) collective-permute-start(bf16[256,512]{1,0:T(8,128)(2,1)S(1)} %get-tuple-element.85), channel_id=1, source_target_pairs={{2,6},{6,10},{10,14},{14,12},{12,8},{8,4},{4,0},{0,2},{3,1},{7,3},... | collective-permute-start | bytes 786440 | tf_op jit(solution)/shard_map/ppermute | solution.py:329
  124.5 9.2 %collective-permute-start.29 = (bf16[256,512]{1,0:T(8,128)(2,1)S(1)}, bf16[256,512]{1,0:T(8,128)(2,1)S(1)}, u32[]{:S(2)}, u32[]{:S(2)}) collective-permute-start(bf16[256,512]{1,0:T(8,128)(2,1)S(1)} %add.14), channel_id=1, source_target_pairs={{2,6},{6,10},{10,14},{14,12},{12,8},{8,4},{4,0},{0,2},{3,1},{7,3},... | collective-permute-start | bytes 786440 | tf_op jit(solution)/shard_map/ppermute | solution.py:329
  127.4 8.1 %collective-permute-start.25 = (bf16[256,512]{1,0:T(8,128)(2,1)S(1)}, bf16[256,512]{1,0:T(8,128)(2,1)S(1)}, u32[]{:S(2)}, u32[]{:S(2)}) collective-permute-start(bf16[256,512]{1,0:T(8,128)(2,1)S(1)} %add.11), channel_id=1, source_target_pairs={{2,6},{6,10},{10,14},{14,12},{12,8},{8,4},{4,0},{0,2},{3,1},{7,3},... | collective-permute-start | bytes 786440 | tf_op jit(solution)/shard_map/ppermute | solution.py:329
  129.6 17.6 %collective-permute-start.35 = (bf16[256,1024]{1,0:T(8,128)(2,1)S(1)}, bf16[256,1024]{1,0:T(8,128)(2,1)S(1)}, u32[]{:S(2)}, u32[]{:S(2)}) collective-permute-start(bf16[256,1024]{1,0:T(8,128)(2,1)S(1)} %add.17), channel_id=1, source_target_pairs={{2,6},{6,10},{10,14},{14,12},{12,8},{8,4},{4,0},{0,2},{3,1},{7,3},... | collective-permute-start | bytes 1572872 | tf_op jit(solution)/shard_map/ppermute | solution.py:329
  133.9 8.3 %collective-permute-start.30 = (bf16[256,512]{1,0:T(8,128)(2,1)S(1)}, bf16[256,512]{1,0:T(8,128)(2,1)S(1)}, u32[]{:S(2)}, u32[]{:S(2)}) collective-permute-start(bf16[256,512]{1,0:T(8,128)(2,1)S(1)} %add.15), channel_id=1, source_target_pairs={{2,6},{6,10},{10,14},{14,12},{12,8},{8,4},{4,0},{0,2},{3,1},{7,3},... | collective-permute-start | bytes 786440 | tf_op jit(solution)/shard_map/ppermute | solution.py:329
  135.6 9.4 %collective-permute-start.26 = (bf16[256,512]{1,0:T(8,128)(2,1)S(1)}, bf16[256,512]{1,0:T(8,128)(2,1)S(1)}, u32[]{:S(2)}, u32[]{:S(2)}) collective-permute-start(bf16[256,512]{1,0:T(8,128)(2,1)S(1)} %add.12), channel_id=1, source_target_pairs={{2,6},{6,10},{10,14},{14,12},{12,8},{8,4},{4,0},{0,2},{3,1},{7,3},... | collective-permute-start | bytes 786440 | tf_op jit(solution)/shard_map/ppermute | solution.py:329
  142.3 7.9 %collective-permute-start.31 = (bf16[256,512]{1,0:T(8,128)(2,1)S(1)}, bf16[256,512]{1,0:T(8,128)(2,1)S(1)}, u32[]{:S(2)}, u32[]{:S(2)}) collective-permute-start(bf16[256,512]{1,0:T(8,128)(2,1)S(1)} %add.16), channel_id=1, source_target_pairs={{2,6},{6,10},{10,14},{14,12},{12,8},{8,4},{4,0},{0,2},{3,1},{7,3},... | collective-permute-start | bytes 786440 | tf_op jit(solution)/shard_map/ppermute | solution.py:329
  145.1 6.4 %collective-permute-start.27 = (bf16[256,512]{1,0:T(8,128)(2,1)S(1)}, bf16[256,512]{1,0:T(8,128)(2,1)S(1)}, u32[]{:S(2)}, u32[]{:S(2)}) collective-permute-start(bf16[256,512]{1,0:T(8,128)(2,1)S(1)} %add.13), channel_id=1, source_target_pairs={{2,6},{6,10},{10,14},{14,12},{12,8},{8,4},{4,0},{0,2},{3,1},{7,3},... | collective-permute-start | bytes 786440 | tf_op jit(solution)/shard_map/ppermute | solution.py:329
  148.0 4.5 %collective-permute-start.36 = (bf16[256,512]{1,0:T(8,128)(2,1)S(1)}, bf16[256,512]{1,0:T(8,128)(2,1)S(1)}, u32[]{:S(2)}, u32[]{:S(2)}) collective-permute-start(bf16[256,512]{1,0:T(8,128)(2,1)S(1)} %get-tuple-element.106), channel_id=1, source_target_pairs={{0,1},{1,0},{2,3},{3,2},{4,5},{5,4},{6,7},{7,6},{8,9},{9,8},{10,11... | collective-permute-start | bytes 786440 | tf_op jit(solution)/shard_map/ppermute | solution.py:326
  152.4 1.6 %collective-permute-start.32 = (bf16[256,512]{1,0:T(8,128)(2,1)S(1)}, bf16[256,512]{1,0:T(8,128)(2,1)S(1)}, u32[]{:S(2)}, u32[]{:S(2)}) collective-permute-start(bf16[256,512]{1,0:T(8,128)(2,1)S(1)} %get-tuple-element.99), channel_id=1, source_target_pairs={{0,1},{1,0},{2,3},{3,2},{4,5},{5,4},{6,7},{7,6},{8,9},{9,8},{10,11... | collective-permute-start | bytes 786440 | tf_op jit(solution)/shard_map/ppermute | solution.py:326

commit v7 on v6

--- a/solution.py
+++ b/solution.py
@@ -134,15 +134,12 @@
         copy.wait()
 
 
-def pick_kernel(zero_ref, one_ref, out_ref, sem):
+def halve_kernel(block_ref, out_ref, sem):
+    rows = out_ref.shape[0]
     core = lax.axis_index("dp") % CORES
-    for at, ref in enumerate((zero_ref, one_ref)):
-
-        @pl.when(core == at)
-        def _():
-            copy = pltpu.make_async_copy(ref, out_ref, sem)
-            copy.start()
-            copy.wait()
+    copy = pltpu.make_async_copy(block_ref.at[pl.ds(pl.multiple_of(core * rows, rows), rows)], out_ref, sem)
+    copy.start()
+    copy.wait()
 
 
 def pre_grad_of(hidden_grad, slope, preact, width):
@@ -337,8 +334,10 @@
             assemble_kernel, chunk, mine, other, specs=[ANY] * 2, scratch=[pltpu.SemaphoreType.DMA((2,))], name="assemble"
         )
 
-    def pick(zero, one):
-        return call(pick_kernel, chunk, zero, one, specs=[ANY] * 2, scratch=[pltpu.SemaphoreType.DMA], name="pick")
+    def halve(value):
+        return call(
+            halve_kernel, shape(BF16, half_block, rank), value, specs=[ANY], scratch=[pltpu.SemaphoreType.DMA], name="halve"
+        )
 
     down, up = w_down[0], w_up[0]
     downs, ups = {}, {}
@@ -363,15 +362,15 @@
         downs[ahead(k)] = swap(down_block)
         ups[ahead(k)] = swap(up_block)
     earlier = [downs[ahead(half - 2)], ups[ahead(half - 2)]]
-    mine = onward(after(pick(down_block, up_block), *earlier))
+    down_far = onward(after(halve(down_block), *earlier))
+    up_far = onward(halve(up_block))
+    downs[opposite] = of_chip(down_far, swap(down_far))
     near = [j for j in range(n) if j != opposite]
     preact = with_meta(
         functools.partial(preact_kernel, near), rank_f32, scaled, *(downs[j] for j in near),
         flops=2 * tokens * width * rank, name="preact",
     )
-    mine = after(mine, preact)
-    other = swap(mine)
-    downs[opposite], ups[opposite] = pick(mine, other), pick(other, mine)
+    ups[opposite] = of_chip(up_far, swap(after(up_far, preact)))
 
     pre_grad, mean, hidden_t, slope, preact, own_sum, *tops = with_meta(
         functools.partial(top_kernel, groups, opposite),

time: 156 us -> 151 us (0.968)
  waiting for transfers between devices: 82.6 us -> 75.8 us
  starting transfers between devices: 42.3 us -> 44.5 us
    ppermute x19 -> x20, waiting for transfers between devices: 49.4 us -> 43.9 us  [onward(): return lax.ppermute(value, 'dp', routes.onward)]
    ppermute x19 -> x20, starting transfers between devices: 36.3 us -> 38.4 us  [onward(): return lax.ppermute(value, 'dp', routes.onward)]
    ppermute x15 -> x16, waiting for transfers between devices: 4.6 us -> 3.3 us  [swap(): return lax.ppermute(value, 'dp', routes.partner)]
    pallas_call x31 -> x32, Pallas kernels: 27.8 us -> 27.8 us  [call(): pl.pallas_call(body, in_specs=specs or [VMEM] * len(args), out_specs=out_...]
  transfers between devices with their start and end apart: 37 -> 39, of which waited for: 21 -> 19; matrix products, arithmetic and copies ran while one was open for 0% -> 0% of each run, Pallas kernels for 11% -> 12%
where the time goes in v7:
time: 151 us
  waiting for transfers between devices  75.8 us (50%)
  starting transfers between devices  44.5 us (29%)
  Pallas kernels  27.8 us (18%)
  local copies, waits for them, and re-layouts  1.93 us (1%)
    ppermute x20, waiting for transfers between devices, onward(): return lax.ppermute(value, 'dp', routes.onward)  43.9 us
    ppermute x20, starting transfers between devices, onward(): return lax.ppermute(value, 'dp', routes.onward)  38.4 us
    ppermute x3, waiting for transfers between devices, local(): arrived = [lax.ppermute(value, 'section', back) for value in sent]  28.6 us
    pallas_call x32, Pallas kernels, call(): pl.pallas_call(body, in_specs=specs or [VMEM] * len(args), out_specs=out_...  27.8 us
    ppermute x3, starting transfers between devices, local(): arrived = [lax.ppermute(value, 'section', back) for value in sent]  3.86 us
    ppermute x16, waiting for transfers between devices, swap(): return lax.ppermute(value, 'dp', routes.partner)  3.3 us
  transfers between devices with their start and end apart: 39, of which 19 were waited for; matrix products, arithmetic and copies ran while one was open for 0% of the time, Pallas kernels for 12%

profile of v7, /device:TPU:0, one launch (start us, length us, event | category | flops | bytes accessed | tf_op | source)
XLA Modules:
  0.0 151.0 jit_solution(6409784103085632595)
XLA Ops:
  0.7 0.5 collective-permute-start
  1.2 1.3 collective-permute-done.other_ref
  2.5 0.9 copy-done.4
  3.6 2.9 %collective-permute-start.1 = (bf16[1024,256]{1,0:T(8,128)(2,1)S(1)}, bf16[1024,256]{1,0:T(8,128)(2,1)S(1)}, u32[]{:S(2)}, u32[]{:S(2)}) collective-permute-start(bf16[1024,256]{1,0:T(8,128)(2,1)S(1)} %assemble.4.refs_7_.refs_8_), channel_id=1, source_target_pairs={{2,6},{6,10},{10,14},{14,12},{12,8},{8,4},{4,0},{0,2},{3,1},{7,3},... | collective-permute-start | bytes 1572872 | tf_op jit(solution)/shard_map/ppermute | solution.py:326
  6.5 0.9 copy-done.6
  7.5 1.6 %collective-permute-start.8 = (bf16[1024,256]{1,0:T(8,128)(2,1)S(1)}, bf16[1024,256]{1,0:T(8,128)(2,1)S(1)}, u32[]{:S(2)}, u32[]{:S(2)}) collective-permute-start(bf16[1024,256]{1,0:T(8,128)(2,1)S(1)} %assemble.5.refs_13_.refs_5_), channel_id=1, source_target_pairs={{2,6},{6,10},{10,14},{14,12},{12,8},{8,4},{4,0},{0,2},{3,1},{7,3},... | collective-permute-start | bytes 1572872 | tf_op jit(solution)/shard_map/ppermute | solution.py:326
  9.2 4.6 %collective-permute-done.1.refs_1_.refs_7_.refs_6_ = bf16[1024,256]{1,0:T(8,128)(2,1)S(1)} collective-permute-done((bf16[1024,256]{1,0:T(8,128)(2,1)S(1)}, bf16[1024,256]{1,0:T(8,128)(2,1)S(1)}, u32[]{:S(2)}, u32[]{:S(2)}) %collective-permute-start.1) | collective-permute-done | bytes 524320 | tf_op jit(solution)/shard_map/ppermute | solution.py:326
  13.7 2.0 %collective-permute-start.3 = (bf16[1024,256]{1,0:T(8,128)(2,1)S(1)}, bf16[1024,256]{1,0:T(8,128)(2,1)S(1)}, u32[]{:S(2)}, u32[]{:S(2)}) collective-permute-start(bf16[1024,256]{1,0:T(8,128)(2,1)S(1)} %collective-permute-done.1.refs_1_.refs_7_.refs_6_), channel_id=1, source_target_pairs={{2,6},{6,10},{10,14},{14,12},{12,8},{8,4},{4,0},{0,2},{3,1},{7,3},... | collective-permute-start | bytes 1572872 | tf_op jit(solution)/shard_map/ppermute | solution.py:326
  15.7 3.7 %collective-permute-done.8.refs_6_.refs_4_ = bf16[1024,256]{1,0:T(8,128)(2,1)S(1)} collective-permute-done((bf16[1024,256]{1,0:T(8,128)(2,1)S(1)}, bf16[1024,256]{1,0:T(8,128)(2,1)S(1)}, u32[]{:S(2)}, u32[]{:S(2)}) %collective-permute-start.8) | collective-permute-done | bytes 524320 | tf_op jit(solution)/shard_map/ppermute | solution.py:326
  19.3 2.0 %collective-permute-start.9 = (bf16[1024,256]{1,0:T(8,128)(2,1)S(1)}, bf16[1024,256]{1,0:T(8,128)(2,1)S(1)}, u32[]{:S(2)}, u32[]{:S(2)}) collective-permute-start(bf16[1024,256]{1,0:T(8,128)(2,1)S(1)} %collective-permute-done.8.refs_6_.refs_4_), channel_id=1, source_target_pairs={{2,6},{6,10},{10,14},{14,12},{12,8},{8,4},{4,0},{0,2},{3,1},{7,3},... | collective-permute-start | bytes 1572872 | tf_op jit(solution)/shard_map/ppermute | solution.py:326
  21.3 3.7 %collective-permute-done.3.refs_3_.refs_7_.refs_9_ = bf16[1024,256]{1,0:T(8,128)(2,1)S(1)} collective-permute-done((bf16[1024,256]{1,0:T(8,128)(2,1)S(1)}, bf16[1024,256]{1,0:T(8,128)(2,1)S(1)}, u32[]{:S(2)}, u32[]{:S(2)}) %collective-permute-start.3) | collective-permute-done | bytes 524320 | tf_op jit(solution)/shard_map/ppermute | solution.py:326
  25.0 2.0 %collective-permute-start.5 = (bf16[1024,256]{1,0:T(8,128)(2,1)S(1)}, bf16[1024,256]{1,0:T(8,128)(2,1)S(1)}, u32[]{:S(2)}, u32[]{:S(2)}) collective-permute-start(bf16[1024,256]{1,0:T(8,128)(2,1)S(1)} %collective-permute-done.3.refs_3_.refs_7_.refs_9_), channel_id=1, source_target_pairs={{2,6},{6,10},{10,14},{14,12},{12,8},{8,4},{4,0},{0,2},{3,1},{7,3},... | collective-permute-start | bytes 1572872 | tf_op jit(solution)/shard_map/ppermute | solution.py:326
  26.9 3.7 %collective-permute-done.9.refs_8_.refs_4_ = bf16[1024,256]{1,0:T(8,128)(2,1)S(1)} collective-permute-done((bf16[1024,256]{1,0:T(8,128)(2,1)S(1)}, bf16[1024,256]{1,0:T(8,128)(2,1)S(1)}, u32[]{:S(2)}, u32[]{:S(2)}) %collective-permute-start.9) | collective-permute-done | bytes 524320 | tf_op jit(solution)/shard_map/ppermute | solution.py:326
  30.6 0.5 collective-permute-start.4
  31.1 2.0 %collective-permute-start.14 = (bf16[1024,256]{1,0:T(8,128)(2,1)S(1)}, bf16[1024,256]{1,0:T(8,128)(2,1)S(1)}, u32[]{:S(2)}, u32[]{:S(2)}) collective-permute-start(bf16[1024,256]{1,0:T(8,128)(2,1)S(1)} %collective-permute-done.9.refs_8_.refs_4_), channel_id=1, source_target_pairs={{2,6},{6,10},{10,14},{14,12},{12,8},{8,4},{4,0},{0,2},{3,1},{7,3},... | collective-permute-start | bytes 1572872 | tf_op jit(solution)/shard_map/ppermute | solution.py:326
  33.0 3.1 %collective-permute-done.5.refs_5_.block_ref.refs_8_.refs_7_ = bf16[1024,256]{1,0:T(8,128)(2,1)S(1)} collective-permute-done((bf16[1024,256]{1,0:T(8,128)(2,1)S(1)}, bf16[1024,256]{1,0:T(8,128)(2,1)S(1)}, u32[]{:S(2)}, u32[]{:S(2)}) %collective-permute-start.5) | collective-permute-done | bytes 524320 | tf_op jit(solution)/shard_map/ppermute | solution.py:326
  36.3 2.0 %collective-permute-start.11 = (bf16[512,256]{1,0:T(8,128)(2,1)S(1)}, bf16[512,256]{1,0:T(8,128)(2,1)S(1)}, u32[]{:S(2)}, u32[]{:S(2)}) collective-permute-start(bf16[512,256]{1,0:T(8,128)(2,1)S(1)} %halve.2), channel_id=1, source_target_pairs={{2,6},{6,10},{10,14},{14,12},{12,8},{8,4},{4,0},{0,2},{3,1},{7,3},... | collective-permute-start | bytes 786440 | tf_op jit(solution)/shard_map/ppermute | solution.py:326
  38.3 3.5 %collective-permute-done.14.block_ref.refs_10_.refs_5_ = bf16[1024,256]{1,0:T(8,128)(2,1)S(1)} collective-permute-done((bf16[1024,256]{1,0:T(8,128)(2,1)S(1)}, bf16[1024,256]{1,0:T(8,128)(2,1)S(1)}, u32[]{:S(2)}, u32[]{:S(2)}) %collective-permute-start.14) | collective-permute-done | bytes 524320 | tf_op jit(solution)/shard_map/ppermute | solution.py:326
  41.8 2.0 %collective-permute-start.16 = (bf16[512,256]{1,0:T(8,128)(2,1)S(1)}, bf16[512,256]{1,0:T(8,128)(2,1)S(1)}, u32[]{:S(2)}, u32[]{:S(2)}) collective-permute-start(bf16[512,256]{1,0:T(8,128)(2,1)S(1)} %halve.3), channel_id=1, source_target_pairs={{2,6},{6,10},{10,14},{14,12},{12,8},{8,4},{4,0},{0,2},{3,1},{7,3},... | collective-permute-start | bytes 786440 | tf_op jit(solution)/shard_map/ppermute | solution.py:326
  43.9 0.5 collective-permute-start.15
  44.4 1.1 scale.1
  45.6 1.3 preact.1.refs_4_
  46.9 1.3 collective-permute-done.16.mine_ref
  48.3 1.5 collective-permute-done.17.other_ref
  49.9 3.9 %top.1 = (bf16[128,256]{1,0:T(8,128)(2,1)S(1)}, f32[128,1]{1,0:T(8,128)S(1)}, bf16[256,128]{1,0:T(8,128)(2,1)S(1)}, f32[128,256]{1,0:T(8,128)S(1)}, f32[128,256]...) custom-call(s32[16,8]{1,0:T(8,128)S(1)} %copy-done.2, ...), custom_call_target="tpu_custom_call" | custom-call | flops 1073741824 | bytes 3441024 | tf_op jit(solution)/shard_map/top/pallas_call | solution.py:64
  53.8 1.4 leave.4
  55.2 1.3 collective-permute-start.19
  56.5 1.2 leave.5
  57.7 1.3 collective-permute-start.23
  59.0 1.4 leave.3
  60.4 17.0 %collective-permute-done.19.refs_0_ = bf16[3,128,1024]{2,1,0:T(8,128)(2,1)S(1)} collective-permute-done((bf16[3,128,1024]{2,1,0:T(8,128)(2,1)S(1)}, bf16[3,128,1024]{2,1,0:T(8,128)(2,1)S(1)}, u32[]{:S(2)}, u32[]{:S(2)}) %collective-permute-start.19) | collective-permute-done | bytes 786464 | tf_op jit(solution)/shard_map/ppermute | solution.py:414
  77.5 1.5 arrive.3
  79.0 2.0 %collective-permute-start.20 = (bf16[256,1024]{1,0:T(8,128)(2,1)S(1)}, bf16[256,1024]{1,0:T(8,128)(2,1)S(1)}, u32[]{:S(2)}, u32[]{:S(2)}) collective-permute-start(bf16[256,1024]{1,0:T(8,128)(2,1)S(1)} %get-tuple-element.69), channel_id=1, source_target_pairs={{2,6},{6,10},{10,14},{14,12},{12,8},{8,4},{4,0},{0,2},{3,1},{7,3},... | collective-permute-start | bytes 1572872 | tf_op jit(solution)/shard_map/ppermute | solution.py:326
  81.0 1.3 collective-permute-start.18
  82.3 6.5 %collective-permute-done.23.refs_0_ = bf16[2,128,1024]{2,1,0:T(8,128)(2,1)S(1)} collective-permute-done((bf16[2,128,1024]{2,1,0:T(8,128)(2,1)S(1)}, bf16[2,128,1024]{2,1,0:T(8,128)(2,1)S(1)}, u32[]{:S(2)}, u32[]{:S(2)}) %collective-permute-start.23) | collective-permute-done | bytes 524320 | tf_op jit(solution)/shard_map/ppermute | solution.py:414
  88.7 1.3 arrive.4
  90.3 2.0 %collective-permute-start.22 = (bf16[256,1024]{1,0:T(8,128)(2,1)S(1)}, bf16[256,1024]{1,0:T(8,128)(2,1)S(1)}, u32[]{:S(2)}, u32[]{:S(2)}) collective-permute-start(bf16[256,1024]{1,0:T(8,128)(2,1)S(1)} %add.9), channel_id=1, source_target_pairs={{2,6},{6,10},{10,14},{14,12},{12,8},{8,4},{4,0},{0,2},{3,1},{7,3},... | collective-permute-start | bytes 1572872 | tf_op jit(solution)/shard_map/ppermute | solution.py:326
  92.3 7.2 %collective-permute-done.22.refs_0_ = bf16[256,1024]{1,0:T(8,128)(2,1)S(1)} collective-permute-done((bf16[256,1024]{1,0:T(8,128)(2,1)S(1)}, bf16[256,1024]{1,0:T(8,128)(2,1)S(1)}, u32[]{:S(2)}, u32[]{:S(2)}) %collective-permute-start.22) | collective-permute-done | bytes 524320 | tf_op jit(solution)/shard_map/ppermute | solution.py:326
  99.7 5.1 %collective-permute-done.18.refs_0_ = bf16[3,128,1024]{2,1,0:T(8,128)(2,1)S(1)} collective-permute-done((bf16[3,128,1024]{2,1,0:T(8,128)(2,1)S(1)}, bf16[3,128,1024]{2,1,0:T(8,128)(2,1)S(1)}, u32[]{:S(2)}, u32[]{:S(2)}) %collective-permute-start.18) | collective-permute-done | bytes 786464 | tf_op jit(solution)/shard_map/ppermute | solution.py:414
  104.8 1.7 %arrive.5 = (bf16[3,128,1024]{2,1,0:T(8,128)(2,1)S(1)}, bf16[128,256]{1,0:T(8,128)(2,1)S(1)}, bf16[256,128]{1,0:T(8,128)(2,1)S(1)}, f32[128,1]{1,0:T(8,128)S(1)}...) custom-call(s32[16,8]{1,0:T(8,128)S(1)} %copy-done.2, ...), custom_call_target="tpu_custom_call" | custom-call | flops 402653184 | bytes 2179328 | tf_op jit(solution)/shard_map/arrive/pallas_call | solution.py:64
  106.5 1.2 products.3
  107.8 2.0 %collective-permute-start.35 = (bf16[256,1024]{1,0:T(8,128)(2,1)S(1)}, bf16[256,1024]{1,0:T(8,128)(2,1)S(1)}, u32[]{:S(2)}, u32[]{:S(2)}) collective-permute-start(bf16[256,1024]{1,0:T(8,128)(2,1)S(1)} %add.10), channel_id=1, source_target_pairs={{2,6},{6,10},{10,14},{14,12},{12,8},{8,4},{4,0},{0,2},{3,1},{7,3},... | collective-permute-start | bytes 1572872 | tf_op jit(solution)/shard_map/ppermute | solution.py:326
  110.0 1.4 collective-permute-start.30
  111.4 1.6 %collective-permute-start.25 = (bf16[256,512]{1,0:T(8,128)(2,1)S(1)}, bf16[256,512]{1,0:T(8,128)(2,1)S(1)}, u32[]{:S(2)}, u32[]{:S(2)}) collective-permute-start(bf16[256,512]{1,0:T(8,128)(2,1)S(1)} %get-tuple-element.85), channel_id=1, source_target_pairs={{2,6},{6,10},{10,14},{14,12},{12,8},{8,4},{4,0},{0,2},{3,1},{7,3},... | collective-permute-start | bytes 786440 | tf_op jit(solution)/shard_map/ppermute | solution.py:326
  113.0 1.4 products.2
  114.3 5.5 %collective-permute-done.30.refs_0_ = bf16[256,512]{1,0:T(8,128)(2,1)S(1)} collective-permute-done((bf16[256,512]{1,0:T(8,128)(2,1)S(1)}, bf16[256,512]{1,0:T(8,128)(2,1)S(1)}, u32[]{:S(2)}, u32[]{:S(2)}) %collective-permute-start.30) | collective-permute-done | bytes 262176 | tf_op jit(solution)/shard_map/ppermute | solution.py:326
  119.9 2.0 %collective-permute-start.31 = (bf16[256,512]{1,0:T(8,128)(2,1)S(1)}, bf16[256,512]{1,0:T(8,128)(2,1)S(1)}, u32[]{:S(2)}, u32[]{:S(2)}) collective-permute-start(bf16[256,512]{1,0:T(8,128)(2,1)S(1)} %add.14), channel_id=1, source_target_pairs={{2,6},{6,10},{10,14},{14,12},{12,8},{8,4},{4,0},{0,2},{3,1},{7,3},... | collective-permute-start | bytes 786440 | tf_op jit(solution)/shard_map/ppermute | solution.py:326
  122.0 0.7 collective-permute-done.25.refs_0_
  122.7 2.0 %collective-permute-start.27 = (bf16[256,512]{1,0:T(8,128)(2,1)S(1)}, bf16[256,512]{1,0:T(8,128)(2,1)S(1)}, u32[]{:S(2)}, u32[]{:S(2)}) collective-permute-start(bf16[256,512]{1,0:T(8,128)(2,1)S(1)} %add.11), channel_id=1, source_target_pairs={{2,6},{6,10},{10,14},{14,12},{12,8},{8,4},{4,0},{0,2},{3,1},{7,3},... | collective-permute-start | bytes 786440 | tf_op jit(solution)/shard_map/ppermute | solution.py:326
  125.0 1.6 %collective-permute-start.37 = (bf16[256,1024]{1,0:T(8,128)(2,1)S(1)}, bf16[256,1024]{1,0:T(8,128)(2,1)S(1)}, u32[]{:S(2)}, u32[]{:S(2)}) collective-permute-start(bf16[256,1024]{1,0:T(8,128)(2,1)S(1)} %add.17), channel_id=1, source_target_pairs={{2,6},{6,10},{10,14},{14,12},{12,8},{8,4},{4,0},{0,2},{3,1},{7,3},... | collective-permute-start | bytes 1572872 | tf_op jit(solution)/shard_map/ppermute | solution.py:326
  126.6 2.6 %finish.2.refs_9_ = bf16[128,8192]{1,0:T(8,128)(2,1)} custom-call(s32[16,8]{1,0:T(8,128)S(1)} %copy-done.2, bf16[128,8192]{1,0:T(8,128)(2,1)S(1)} %bitcast.10, f32[1,8192]{1,0:T(1,128)S(1)} %copy-done.3, bf16[128,256]{1,0:T(8,128)(2,1)S(1)} %get-tuple-element.80.refs_2_, f32[128,1]{1,0:T(8,128)S(1)} %get-tuple-element.63.refs_4_.refs_3_, ...), custom_call_target="tpu_custom_call" | custom-call | flops 335544320 | bytes 2056576 | tf_op jit(solution)/shard_map/finish/pallas_call | solution.py:64
  129.3 1.6 %collective-permute-start.32 = (bf16[256,512]{1,0:T(8,128)(2,1)S(1)}, bf16[256,512]{1,0:T(8,128)(2,1)S(1)}, u32[]{:S(2)}, u32[]{:S(2)}) collective-permute-start(bf16[256,512]{1,0:T(8,128)(2,1)S(1)} %add.15), channel_id=1, source_target_pairs={{2,6},{6,10},{10,14},{14,12},{12,8},{8,4},{4,0},{0,2},{3,1},{7,3},... | collective-permute-start | bytes 786440 | tf_op jit(solution)/shard_map/ppermute | solution.py:326
  131.0 1.6 %collective-permute-start.28 = (bf16[256,512]{1,0:T(8,128)(2,1)S(1)}, bf16[256,512]{1,0:T(8,128)(2,1)S(1)}, u32[]{:S(2)}, u32[]{:S(2)}) collective-permute-start(bf16[256,512]{1,0:T(8,128)(2,1)S(1)} %add.12), channel_id=1, source_target_pairs={{2,6},{6,10},{10,14},{14,12},{12,8},{8,4},{4,0},{0,2},{3,1},{7,3},... | collective-permute-start | bytes 786440 | tf_op jit(solution)/shard_map/ppermute | solution.py:326
  132.6 5.0 %collective-permute-done.32.refs_0_ = bf16[256,512]{1,0:T(8,128)(2,1)S(1)} collective-permute-done((bf16[256,512]{1,0:T(8,128)(2,1)S(1)}, bf16[256,512]{1,0:T(8,128)(2,1)S(1)}, u32[]{:S(2)}, u32[]{:S(2)}) %collective-permute-start.32) | collective-permute-done | bytes 262176 | tf_op jit(solution)/shard_map/ppermute | solution.py:326
  137.7 2.0 %collective-permute-start.33 = (bf16[256,512]{1,0:T(8,128)(2,1)S(1)}, bf16[256,512]{1,0:T(8,128)(2,1)S(1)}, u32[]{:S(2)}, u32[]{:S(2)}) collective-permute-start(bf16[256,512]{1,0:T(8,128)(2,1)S(1)} %add.16), channel_id=1, source_target_pairs={{2,6},{6,10},{10,14},{14,12},{12,8},{8,4},{4,0},{0,2},{3,1},{7,3},... | collective-permute-start | bytes 786440 | tf_op jit(solution)/shard_map/ppermute | solution.py:326
  139.7 0.7 collective-permute-done.28.refs_0_
  140.5 2.0 %collective-permute-start.29 = (bf16[256,512]{1,0:T(8,128)(2,1)S(1)}, bf16[256,512]{1,0:T(8,128)(2,1)S(1)}, u32[]{:S(2)}, u32[]{:S(2)}) collective-permute-start(bf16[256,512]{1,0:T(8,128)(2,1)S(1)} %add.13), channel_id=1, source_target_pairs={{2,6},{6,10},{10,14},{14,12},{12,8},{8,4},{4,0},{0,2},{3,1},{7,3},... | collective-permute-start | bytes 786440 | tf_op jit(solution)/shard_map/ppermute | solution.py:326
  142.5 0.8 split.3
  143.4 2.2 %finish.3 = bf16[128,8192]{1,0:T(8,128)(2,1)} custom-call(s32[16,8]{1,0:T(8,128)S(1)} %copy-done.2, bf16[128,8192]{1,0:T(8,128)(2,1)S(1)} %bitcast.11, f32[1,8192]{1,0:T(1,128)S(1)} %copy-done.3, bf16[128,256]{1,0:T(8,128)(2,1)S(1)} %get-tuple-element.80.refs_2_, f32[128,1]{1,0:T(8,128)S(1)} %get-tuple-element.63.refs_4_.refs_3_, ...), custom_call_target="tpu_custom_call", output_to_operand_aliasing={{}: (10, {})} | custom-call | flops 201326592 | bytes 2187648 | tf_op jit(solution)/shard_map/finish/pallas_call | solution.py:64
  145.6 1.3 collective-permute-done.29.refs_0_
  146.9 0.8 split.2
  147.9 1.0 close_up.1
  148.9 0.5 collective-permute-done.34.refs_1_
  149.4 1.7 %close_down.1 = (f32[1,512,256]{2,1,0:T(8,128)}, f32[1,512]{1,0:T(1,128)}) custom-call(s32[16,8]{1,0:T(8,128)S(1)} %copy-done.2, f32[256,512]{1,0:T(8,128)S(1)} %get-tuple-element.98.refs_0_, bf16[256,512]{1,0:T(8,128)(2,1)S(1)} %collective-permute-done.34.refs_1_, f32[256,512]{1,0:T(8,128)S(1)} %get-tuple-element.100.refs_2_, f32[1,8192]{1,0:T(1,128)S(1)} %copy-done.3), custom_call_target="tpu_custom_call" | custom-call | bytes 467584 | tf_op jit(solution)/shard_map/close_down/pallas_call | solution.py:64
  (62 shorter events, 2.2 us)
Async XLA Ops:
  0.6 43.7 %copy-start = (bf16[1,128,8192]{2,1,0:T(8,128)(2,1)S(1)}, bf16[1,128,8192]{2,1,0:T(8,128)(2,1)}, u32[]{:S(2)}) copy-start(bf16[1,128,8192]{2,1,0:T(8,128)(2,1)} %param.7) | copy-start | bytes 6291460
  0.6 43.7 %copy-start.3 = (f32[1,8192]{1,0:T(1,128)S(1)}, f32[1,8192]{1,0:T(1,128)}, u32[]{:S(2)}) copy-start(f32[1,8192]{1,0:T(1,128)} %refs_3_.1) | copy-start | bytes 98308
  0.7 1.9 %collective-permute-start = (bf16[512,256]{1,0:T(8,128)(2,1)}, bf16[512,256]{1,0:T(8,128)(2,1)S(1)}, u32[]{:S(2)}, u32[]{:S(2)}) collective-permute-start(bf16[512,256]{1,0:T(8,128)(2,1)} %bitcast.12), channel_id=1, source_target_pairs={{0,1},{1,0},{2,3},{3,2},{4,5},{5,4},{6,7},{7,6},{8,9},{9,8},{10,11... | collective-permute-start | bytes 786440 | tf_op jit(solution)/shard_map/ppermute | solution.py:323
  1.2 5.3 %collective-permute-start.7 = (bf16[512,256]{1,0:T(8,128)(2,1)}, bf16[512,256]{1,0:T(8,128)(2,1)S(1)}, u32[]{:S(2)}, u32[]{:S(2)}) collective-permute-start(bf16[512,256]{1,0:T(8,128)(2,1)} %bitcast.15), channel_id=1, source_target_pairs={{0,1},{1,0},{2,3},{3,2},{4,5},{5,4},{6,7},{7,6},{8,9},{9,8},{10,11... | collective-permute-start | bytes 786440 | tf_op jit(solution)/shard_map/ppermute | solution.py:323
  2.5 0.9 copy-start.4
  3.5 40.9 %copy-start.5 = (bf16[1,512,256]{2,1,0:T(8,128)(2,1)S(1)}, bf16[1,512,256]{2,1,0:T(8,128)(2,1)}, u32[]{:S(2)}) copy-start(bf16[1,512,256]{2,1,0:T(8,128)(2,1)} %param.11) | copy-start | bytes 786436
  3.6 10.2 %collective-permute-start.1 = (bf16[1024,256]{1,0:T(8,128)(2,1)S(1)}, bf16[1024,256]{1,0:T(8,128)(2,1)S(1)}, u32[]{:S(2)}, u32[]{:S(2)}) collective-permute-start(bf16[1024,256]{1,0:T(8,128)(2,1)S(1)} %assemble.4.refs_7_.refs_8_), channel_id=1, source_target_pairs={{2,6},{6,10},{10,14},{14,12},{12,8},{8,4},{4,0},{0,2},{3,1},{7,3},... | collective-permute-start | bytes 1572872 | tf_op jit(solution)/shard_map/ppermute | solution.py:326
  6.5 1.0 copy-start.6
  7.5 36.9 %copy-start.7 = (s32[128]{0:T(128)S(1)}, s32[128]{0:T(128)}, u32[]{:S(2)}) copy-start(s32[128]{0:T(128)} %param.9) | copy-start | bytes 1540
  7.5 38.1 %copy-start.2 = (s32[16,8]{1,0:T(8,128)S(1)}, s32[16,8]{1,0:T(8,128)}, u32[]{:S(2)}) copy-start(s32[16,8]{1,0:T(8,128)} %constant.2.clone.table_ref) | copy-start | bytes 1540
  7.5 11.8 %collective-permute-start.8 = (bf16[1024,256]{1,0:T(8,128)(2,1)S(1)}, bf16[1024,256]{1,0:T(8,128)(2,1)S(1)}, u32[]{:S(2)}, u32[]{:S(2)}) collective-permute-start(bf16[1024,256]{1,0:T(8,128)(2,1)S(1)} %assemble.5.refs_13_.refs_5_), channel_id=1, source_target_pairs={{2,6},{6,10},{10,14},{14,12},{12,8},{8,4},{4,0},{0,2},{3,1},{7,3},... | collective-permute-start | bytes 1572872 | tf_op jit(solution)/shard_map/ppermute | solution.py:326
  13.7 11.2 %collective-permute-start.3 = (bf16[1024,256]{1,0:T(8,128)(2,1)S(1)}, bf16[1024,256]{1,0:T(8,128)(2,1)S(1)}, u32[]{:S(2)}, u32[]{:S(2)}) collective-permute-start(bf16[1024,256]{1,0:T(8,128)(2,1)S(1)} %collective-permute-done.1.refs_1_.refs_7_.refs_6_), channel_id=1, source_target_pairs={{2,6},{6,10},{10,14},{14,12},{12,8},{8,4},{4,0},{0,2},{3,1},{7,3},... | collective-permute-start | bytes 1572872 | tf_op jit(solution)/shard_map/ppermute | solution.py:326
  19.3 11.2 %collective-permute-start.9 = (bf16[1024,256]{1,0:T(8,128)(2,1)S(1)}, bf16[1024,256]{1,0:T(8,128)(2,1)S(1)}, u32[]{:S(2)}, u32[]{:S(2)}) collective-permute-start(bf16[1024,256]{1,0:T(8,128)(2,1)S(1)} %collective-permute-done.8.refs_6_.refs_4_), channel_id=1, source_target_pairs={{2,6},{6,10},{10,14},{14,12},{12,8},{8,4},{4,0},{0,2},{3,1},{7,3},... | collective-permute-start | bytes 1572872 | tf_op jit(solution)/shard_map/ppermute | solution.py:326
  25.0 11.2 %collective-permute-start.5 = (bf16[1024,256]{1,0:T(8,128)(2,1)S(1)}, bf16[1024,256]{1,0:T(8,128)(2,1)S(1)}, u32[]{:S(2)}, u32[]{:S(2)}) collective-permute-start(bf16[1024,256]{1,0:T(8,128)(2,1)S(1)} %collective-permute-done.3.refs_3_.refs_7_.refs_9_), channel_id=1, source_target_pairs={{2,6},{6,10},{10,14},{14,12},{12,8},{8,4},{4,0},{0,2},{3,1},{7,3},... | collective-permute-start | bytes 1572872 | tf_op jit(solution)/shard_map/ppermute | solution.py:326
  30.6 5.7 %collective-permute-start.10 = (bf16[1024,256]{1,0:T(8,128)(2,1)S(1)}, bf16[1024,256]{1,0:T(8,128)(2,1)S(1)}, u32[]{:S(2)}, u32[]{:S(2)}) collective-permute-start(bf16[1024,256]{1,0:T(8,128)(2,1)S(1)} %collective-permute-done.9.refs_8_.refs_4_), channel_id=1, source_target_pairs={{0,1},{1,0},{2,3},{3,2},{4,5},{5,4},{6,7},{7,6},{8,9},{9,8},{10,11... | collective-permute-start | bytes 1572872 | tf_op jit(solution)/shard_map/ppermute | solution.py:323
  30.6 5.7 %collective-permute-start.4 = (bf16[1024,256]{1,0:T(8,128)(2,1)S(1)}, bf16[1024,256]{1,0:T(8,128)(2,1)S(1)}, u32[]{:S(2)}, u32[]{:S(2)}) collective-permute-start(bf16[1024,256]{1,0:T(8,128)(2,1)S(1)} %collective-permute-done.3.refs_3_.refs_7_.refs_9_), channel_id=1, source_target_pairs={{0,1},{1,0},{2,3},{3,2},{4,5},{5,4},{6,7},{7,6},{8,9},{9,8},{10,11... | collective-permute-start | bytes 1572872 | tf_op jit(solution)/shard_map/ppermute | solution.py:323
  31.1 10.7 %collective-permute-start.14 = (bf16[1024,256]{1,0:T(8,128)(2,1)S(1)}, bf16[1024,256]{1,0:T(8,128)(2,1)S(1)}, u32[]{:S(2)}, u32[]{:S(2)}) collective-permute-start(bf16[1024,256]{1,0:T(8,128)(2,1)S(1)} %collective-permute-done.9.refs_8_.refs_4_), channel_id=1, source_target_pairs={{2,6},{6,10},{10,14},{14,12},{12,8},{8,4},{4,0},{0,2},{3,1},{7,3},... | collective-permute-start | bytes 1572872 | tf_op jit(solution)/shard_map/ppermute | solution.py:326
  33.0 10.8 %collective-permute-start.2 = (bf16[1024,256]{1,0:T(8,128)(2,1)S(1)}, bf16[1024,256]{1,0:T(8,128)(2,1)S(1)}, u32[]{:S(2)}, u32[]{:S(2)}) collective-permute-start(bf16[1024,256]{1,0:T(8,128)(2,1)S(1)} %collective-permute-done.1.refs_1_.refs_7_.refs_6_), channel_id=1, source_target_pairs={{0,1},{1,0},{2,3},{3,2},{4,5},{5,4},{6,7},{7,6},{8,9},{9,8},{10,11... | collective-permute-start | bytes 1572872 | tf_op jit(solution)/shard_map/ppermute | solution.py:323
  36.2 9.4 %collective-permute-start.6 = (bf16[1024,256]{1,0:T(8,128)(2,1)S(1)}, bf16[1024,256]{1,0:T(8,128)(2,1)S(1)}, u32[]{:S(2)}, u32[]{:S(2)}) collective-permute-start(bf16[1024,256]{1,0:T(8,128)(2,1)S(1)} %collective-permute-done.5.refs_5_.block_ref.refs_8_.refs_7_), channel_id=1, source_target_pairs={{0,1},{1,0},{2,3},{3,2},{4,5},{5,4},{6,7},{7,6},{8,9},{9,8},{10,11... | collective-permute-start | bytes 1572872 | tf_op jit(solution)/shard_map/ppermute | solution.py:323
  36.3 9.2 %collective-permute-start.11 = (bf16[512,256]{1,0:T(8,128)(2,1)S(1)}, bf16[512,256]{1,0:T(8,128)(2,1)S(1)}, u32[]{:S(2)}, u32[]{:S(2)}) collective-permute-start(bf16[512,256]{1,0:T(8,128)(2,1)S(1)} %halve.2), channel_id=1, source_target_pairs={{2,6},{6,10},{10,14},{14,12},{12,8},{8,4},{4,0},{0,2},{3,1},{7,3},... | collective-permute-start | bytes 786440 | tf_op jit(solution)/shard_map/ppermute | solution.py:326
  41.8 6.4 %collective-permute-start.16 = (bf16[512,256]{1,0:T(8,128)(2,1)S(1)}, bf16[512,256]{1,0:T(8,128)(2,1)S(1)}, u32[]{:S(2)}, u32[]{:S(2)}) collective-permute-start(bf16[512,256]{1,0:T(8,128)(2,1)S(1)} %halve.3), channel_id=1, source_target_pairs={{2,6},{6,10},{10,14},{14,12},{12,8},{8,4},{4,0},{0,2},{3,1},{7,3},... | collective-permute-start | bytes 786440 | tf_op jit(solution)/shard_map/ppermute | solution.py:326
  43.9 6.0 %collective-permute-start.13 = (bf16[1024,256]{1,0:T(8,128)(2,1)S(1)}, bf16[1024,256]{1,0:T(8,128)(2,1)S(1)}, u32[]{:S(2)}, u32[]{:S(2)}) collective-permute-start(bf16[1024,256]{1,0:T(8,128)(2,1)S(1)} %collective-permute-done.8.refs_6_.refs_4_), channel_id=1, source_target_pairs={{0,1},{1,0},{2,3},{3,2},{4,5},{5,4},{6,7},{7,6},{8,9},{9,8},{10,11... | collective-permute-start | bytes 1572872 | tf_op jit(solution)/shard_map/ppermute | solution.py:323
  43.9 6.0 %collective-permute-start.15 = (bf16[1024,256]{1,0:T(8,128)(2,1)S(1)}, bf16[1024,256]{1,0:T(8,128)(2,1)S(1)}, u32[]{:S(2)}, u32[]{:S(2)}) collective-permute-start(bf16[1024,256]{1,0:T(8,128)(2,1)S(1)} %collective-permute-done.14.block_ref.refs_10_.refs_5_), channel_id=1, source_target_pairs={{0,1},{1,0},{2,3},{3,2},{4,5},{5,4},{6,7},{7,6},{8,9},{9,8},{10,11... | collective-permute-start | bytes 1572872 | tf_op jit(solution)/shard_map/ppermute | solution.py:323
  45.5 2.8 %collective-permute-start.12 = (bf16[512,256]{1,0:T(8,128)(2,1)S(1)}, bf16[512,256]{1,0:T(8,128)(2,1)S(1)}, u32[]{:S(2)}, u32[]{:S(2)}) collective-permute-start(bf16[512,256]{1,0:T(8,128)(2,1)S(1)} %collective-permute-done.11.mine_ref), channel_id=1, source_target_pairs={{0,1},{1,0},{2,3},{3,2},{4,5},{5,4},{6,7},{7,6},{8,9},{9,8},{10,11... | collective-permute-start | bytes 786440 | tf_op jit(solution)/shard_map/ppermute | solution.py:323
  46.9 3.0 %copy-start.1 = (bf16[128,8192]{1,0:T(8,128)(2,1)S(1)}, bf16[128,8192]{1,0:T(8,128)(2,1)}, u32[]{:S(2)}) copy-start(bf16[128,8192]{1,0:T(8,128)(2,1)} %refs_1_.3) | copy-start | bytes 6291460
  48.3 1.5 %collective-permute-start.17 = (bf16[512,256]{1,0:T(8,128)(2,1)S(1)}, bf16[512,256]{1,0:T(8,128)(2,1)S(1)}, u32[]{:S(2)}, u32[]{:S(2)}) collective-permute-start(bf16[512,256]{1,0:T(8,128)(2,1)S(1)} %collective-permute-done.16.mine_ref), channel_id=1, source_target_pairs={{0,1},{1,0},{2,3},{3,2},{4,5},{5,4},{6,7},{7,6},{8,9},{9,8},{10,11... | collective-permute-start | bytes 786440 | tf_op jit(solution)/shard_map/ppermute | solution.py:323
  55.2 22.3 %collective-permute-start.19 = (bf16[3,128,1024]{2,1,0:T(8,128)(2,1)S(1)}, bf16[3,128,1024]{2,1,0:T(8,128)(2,1)S(1)}, u32[]{:S(2)}, u32[]{:S(2)}) collective-permute-start(bf16[3,128,1024]{2,1,0:T(8,128)(2,1)S(1)} %leave.4), channel_id=1, source_target_pairs={{16,0},{17,1},{18,2},{19,3},{20,4},{21,5},{22,6},{23,7},{24,8},{25... | collective-permute-start | bytes 2359304 | tf_op jit(solution)/shard_map/ppermute | solution.py:414
  57.7 31.0 %collective-permute-start.23 = (bf16[2,128,1024]{2,1,0:T(8,128)(2,1)S(1)}, bf16[2,128,1024]{2,1,0:T(8,128)(2,1)S(1)}, u32[]{:S(2)}, u32[]{:S(2)}) collective-permute-start(bf16[2,128,1024]{2,1,0:T(8,128)(2,1)S(1)} %leave.5), channel_id=1, source_target_pairs={{16,0},{17,1},{18,2},{19,3},{20,4},{21,5},{22,6},{23,7},{24,8},{25... | collective-permute-start | bytes 1572872 | tf_op jit(solution)/shard_map/ppermute | solution.py:414
  79.0 9.8 %collective-permute-start.20 = (bf16[256,1024]{1,0:T(8,128)(2,1)S(1)}, bf16[256,1024]{1,0:T(8,128)(2,1)S(1)}, u32[]{:S(2)}, u32[]{:S(2)}) collective-permute-start(bf16[256,1024]{1,0:T(8,128)(2,1)S(1)} %get-tuple-element.69), channel_id=1, source_target_pairs={{2,6},{6,10},{10,14},{14,12},{12,8},{8,4},{4,0},{0,2},{3,1},{7,3},... | collective-permute-start | bytes 1572872 | tf_op jit(solution)/shard_map/ppermute | solution.py:326
  81.0 9.1 %collective-permute-start.21 = (bf16[256,1024]{1,0:T(8,128)(2,1)S(1)}, bf16[256,1024]{1,0:T(8,128)(2,1)S(1)}, u32[]{:S(2)}, u32[]{:S(2)}) collective-permute-start(bf16[256,1024]{1,0:T(8,128)(2,1)S(1)} %get-tuple-element.71), channel_id=1, source_target_pairs={{0,1},{1,0},{2,3},{3,2},{4,5},{5,4},{6,7},{7,6},{8,9},{9,8},{10,11... | collective-permute-start | bytes 1572872 | tf_op jit(solution)/shard_map/ppermute | solution.py:323
  81.0 23.8 %collective-permute-start.18 = (bf16[3,128,1024]{2,1,0:T(8,128)(2,1)S(1)}, bf16[3,128,1024]{2,1,0:T(8,128)(2,1)S(1)}, u32[]{:S(2)}, u32[]{:S(2)}) collective-permute-start(bf16[3,128,1024]{2,1,0:T(8,128)(2,1)S(1)} %leave.3), channel_id=1, source_target_pairs={{16,0},{17,1},{18,2},{19,3},{20,4},{21,5},{22,6},{23,7},{24,8},{25... | collective-permute-start | bytes 2359304 | tf_op jit(solution)/shard_map/ppermute | solution.py:414
  90.0 2.3 %collective-permute-start.24 = (bf16[256,1024]{1,0:T(8,128)(2,1)S(1)}, bf16[256,1024]{1,0:T(8,128)(2,1)S(1)}, u32[]{:S(2)}, u32[]{:S(2)}) collective-permute-start(bf16[256,1024]{1,0:T(8,128)(2,1)S(1)} %get-tuple-element.75), channel_id=1, source_target_pairs={{0,1},{1,0},{2,3},{3,2},{4,5},{5,4},{6,7},{7,6},{8,9},{9,8},{10,11... | collective-permute-start | bytes 1572872 | tf_op jit(solution)/shard_map/ppermute | solution.py:323
  90.3 9.2 %collective-permute-start.22 = (bf16[256,1024]{1,0:T(8,128)(2,1)S(1)}, bf16[256,1024]{1,0:T(8,128)(2,1)S(1)}, u32[]{:S(2)}, u32[]{:S(2)}) collective-permute-start(bf16[256,1024]{1,0:T(8,128)(2,1)S(1)} %add.9), channel_id=1, source_target_pairs={{2,6},{6,10},{10,14},{14,12},{12,8},{8,4},{4,0},{0,2},{3,1},{7,3},... | collective-permute-start | bytes 1572872 | tf_op jit(solution)/shard_map/ppermute | solution.py:326
  107.7 12.1 %collective-permute-start.26 = (bf16[6,256,512]{2,1,0:T(8,128)(2,1)S(1)}, bf16[6,256,512]{2,1,0:T(8,128)(2,1)S(1)}, u32[]{:S(2)}, u32[]{:S(2)}) collective-permute-start(bf16[6,256,512]{2,1,0:T(8,128)(2,1)S(1)} %products.3), channel_id=1, source_target_pairs={{0,1},{1,0},{2,3},{3,2},{4,5},{5,4},{6,7},{7,6},{8,9},{9,8},{10,11... | collective-permute-start | bytes 4718600 | tf_op jit(solution)/shard_map/ppermute | solution.py:323
  107.8 17.0 %collective-permute-start.35 = (bf16[256,1024]{1,0:T(8,128)(2,1)S(1)}, bf16[256,1024]{1,0:T(8,128)(2,1)S(1)}, u32[]{:S(2)}, u32[]{:S(2)}) collective-permute-start(bf16[256,1024]{1,0:T(8,128)(2,1)S(1)} %add.10), channel_id=1, source_target_pairs={{2,6},{6,10},{10,14},{14,12},{12,8},{8,4},{4,0},{0,2},{3,1},{7,3},... | collective-permute-start | bytes 1572872 | tf_op jit(solution)/shard_map/ppermute | solution.py:326
  109.8 15.0 %collective-permute-start.36 = (bf16[256,1024]{1,0:T(8,128)(2,1)S(1)}, bf16[256,1024]{1,0:T(8,128)(2,1)S(1)}, u32[]{:S(2)}, u32[]{:S(2)}) collective-permute-start(bf16[256,1024]{1,0:T(8,128)(2,1)S(1)} %get-tuple-element.103), channel_id=1, source_target_pairs={{0,1},{1,0},{2,3},{3,2},{4,5},{5,4},{6,7},{7,6},{8,9},{9,8},{10,11... | collective-permute-start | bytes 1572872 | tf_op jit(solution)/shard_map/ppermute | solution.py:323
  110.0 9.8 %collective-permute-start.30 = (bf16[256,512]{1,0:T(8,128)(2,1)S(1)}, bf16[256,512]{1,0:T(8,128)(2,1)S(1)}, u32[]{:S(2)}, u32[]{:S(2)}) collective-permute-start(bf16[256,512]{1,0:T(8,128)(2,1)S(1)} %get-tuple-element.90), channel_id=1, source_target_pairs={{2,6},{6,10},{10,14},{14,12},{12,8},{8,4},{4,0},{0,2},{3,1},{7,3},... | collective-permute-start | bytes 786440 | tf_op jit(solution)/shard_map/ppermute | solution.py:326
  111.4 11.3 %collective-permute-start.25 = (bf16[256,512]{1,0:T(8,128)(2,1)S(1)}, bf16[256,512]{1,0:T(8,128)(2,1)S(1)}, u32[]{:S(2)}, u32[]{:S(2)}) collective-permute-start(bf16[256,512]{1,0:T(8,128)(2,1)S(1)} %get-tuple-element.85), channel_id=1, source_target_pairs={{2,6},{6,10},{10,14},{14,12},{12,8},{8,4},{4,0},{0,2},{3,1},{7,3},... | collective-permute-start | bytes 786440 | tf_op jit(solution)/shard_map/ppermute | solution.py:326
  119.9 9.2 %collective-permute-start.31 = (bf16[256,512]{1,0:T(8,128)(2,1)S(1)}, bf16[256,512]{1,0:T(8,128)(2,1)S(1)}, u32[]{:S(2)}, u32[]{:S(2)}) collective-permute-start(bf16[256,512]{1,0:T(8,128)(2,1)S(1)} %add.14), channel_id=1, source_target_pairs={{2,6},{6,10},{10,14},{14,12},{12,8},{8,4},{4,0},{0,2},{3,1},{7,3},... | collective-permute-start | bytes 786440 | tf_op jit(solution)/shard_map/ppermute | solution.py:326
  122.7 8.2 %collective-permute-start.27 = (bf16[256,512]{1,0:T(8,128)(2,1)S(1)}, bf16[256,512]{1,0:T(8,128)(2,1)S(1)}, u32[]{:S(2)}, u32[]{:S(2)}) collective-permute-start(bf16[256,512]{1,0:T(8,128)(2,1)S(1)} %add.11), channel_id=1, source_target_pairs={{2,6},{6,10},{10,14},{14,12},{12,8},{8,4},{4,0},{0,2},{3,1},{7,3},... | collective-permute-start | bytes 786440 | tf_op jit(solution)/shard_map/ppermute | solution.py:326
  125.0 17.6 %collective-permute-start.37 = (bf16[256,1024]{1,0:T(8,128)(2,1)S(1)}, bf16[256,1024]{1,0:T(8,128)(2,1)S(1)}, u32[]{:S(2)}, u32[]{:S(2)}) collective-permute-start(bf16[256,1024]{1,0:T(8,128)(2,1)S(1)} %add.17), channel_id=1, source_target_pairs={{2,6},{6,10},{10,14},{14,12},{12,8},{8,4},{4,0},{0,2},{3,1},{7,3},... | collective-permute-start | bytes 1572872 | tf_op jit(solution)/shard_map/ppermute | solution.py:326
  129.3 8.3 %collective-permute-start.32 = (bf16[256,512]{1,0:T(8,128)(2,1)S(1)}, bf16[256,512]{1,0:T(8,128)(2,1)S(1)}, u32[]{:S(2)}, u32[]{:S(2)}) collective-permute-start(bf16[256,512]{1,0:T(8,128)(2,1)S(1)} %add.15), channel_id=1, source_target_pairs={{2,6},{6,10},{10,14},{14,12},{12,8},{8,4},{4,0},{0,2},{3,1},{7,3},... | collective-permute-start | bytes 786440 | tf_op jit(solution)/shard_map/ppermute | solution.py:326
  131.0 9.4 %collective-permute-start.28 = (bf16[256,512]{1,0:T(8,128)(2,1)S(1)}, bf16[256,512]{1,0:T(8,128)(2,1)S(1)}, u32[]{:S(2)}, u32[]{:S(2)}) collective-permute-start(bf16[256,512]{1,0:T(8,128)(2,1)S(1)} %add.12), channel_id=1, source_target_pairs={{2,6},{6,10},{10,14},{14,12},{12,8},{8,4},{4,0},{0,2},{3,1},{7,3},... | collective-permute-start | bytes 786440 | tf_op jit(solution)/shard_map/ppermute | solution.py:326
  137.7 7.9 %collective-permute-start.33 = (bf16[256,512]{1,0:T(8,128)(2,1)S(1)}, bf16[256,512]{1,0:T(8,128)(2,1)S(1)}, u32[]{:S(2)}, u32[]{:S(2)}) collective-permute-start(bf16[256,512]{1,0:T(8,128)(2,1)S(1)} %add.16), channel_id=1, source_target_pairs={{2,6},{6,10},{10,14},{14,12},{12,8},{8,4},{4,0},{0,2},{3,1},{7,3},... | collective-permute-start | bytes 786440 | tf_op jit(solution)/shard_map/ppermute | solution.py:326
  140.5 6.4 %collective-permute-start.29 = (bf16[256,512]{1,0:T(8,128)(2,1)S(1)}, bf16[256,512]{1,0:T(8,128)(2,1)S(1)}, u32[]{:S(2)}, u32[]{:S(2)}) collective-permute-start(bf16[256,512]{1,0:T(8,128)(2,1)S(1)} %add.13), channel_id=1, source_target_pairs={{2,6},{6,10},{10,14},{14,12},{12,8},{8,4},{4,0},{0,2},{3,1},{7,3},... | collective-permute-start | bytes 786440 | tf_op jit(solution)/shard_map/ppermute | solution.py:326
  143.4 4.5 %collective-permute-start.38 = (bf16[256,512]{1,0:T(8,128)(2,1)S(1)}, bf16[256,512]{1,0:T(8,128)(2,1)S(1)}, u32[]{:S(2)}, u32[]{:S(2)}) collective-permute-start(bf16[256,512]{1,0:T(8,128)(2,1)S(1)} %get-tuple-element.106), channel_id=1, source_target_pairs={{0,1},{1,0},{2,3},{3,2},{4,5},{5,4},{6,7},{7,6},{8,9},{9,8},{10,11... | collective-permute-start | bytes 786440 | tf_op jit(solution)/shard_map/ppermute | solution.py:323
  147.8 1.6 %collective-permute-start.34 = (bf16[256,512]{1,0:T(8,128)(2,1)S(1)}, bf16[256,512]{1,0:T(8,128)(2,1)S(1)}, u32[]{:S(2)}, u32[]{:S(2)}) collective-permute-start(bf16[256,512]{1,0:T(8,128)(2,1)S(1)} %get-tuple-element.99), channel_id=1, source_target_pairs={{0,1},{1,0},{2,3},{3,2},{4,5},{5,4},{6,7},{7,6},{8,9},{9,8},{10,11... | collective-permute-start | bytes 786440 | tf_op jit(solution)/shard_map/ppermute | solution.py:323

commit v8 on v7

--- a/solution.py
+++ b/solution.py
@@ -206,7 +206,7 @@
         refs = refs[1:]
     if ends:
         slope_ref, preact_ref, scaled_ref, cot_ref, pre_out, pre_t_out, mean_out, *outs = refs
-        outs, parts = outs[:2], outs[2:]
+        far_out, *parts = outs
     else:
         cot_ref, sum_out, *parts = refs
     for at in range(count):
@@ -220,7 +220,8 @@
     pre_out[...], mean_out[...] = pre_grad_of(total, slope_ref[...], preact_ref[...], width)
     pre_t = (total * slope_ref[...]).T.astype(BF16)
     pre_t_out[...] = pre_t
-    put_product(pre_t, columns(scaled_ref, meta[opposite], ups[0].shape[0]), outs)
+    far = jnp.dot(pre_t, columns(scaled_ref, meta[opposite], ups[0].shape[0]), preferred_element_type=F32)
+    far_out[...] = far.astype(BF16)
 
 
 def put_product(pre_t, scaled, halves):
@@ -394,7 +395,7 @@
         more, outs = [] if total is None else [total], [kind, rank_f32]
         if ends:
             more += [slope, preact, scaled]
-            outs = [kind, rank_bf16, shape(BF16, rank, tokens), shape(F32, tokens, 1), half_part, half_part]
+            outs = [kind, rank_bf16, shape(BF16, rank, tokens), shape(F32, tokens, 1), part_shape]
         outs = with_meta(
             body, outs + [part_shape] * len(slots), value, tops[i], hidden_t, *(ups[j] for j in slots), *more,
             flops=4 * len(slots) * tokens * block * rank, name="arrive",
@@ -415,7 +416,7 @@
         if hop < sections - 2:
             (first_cot, hidden_grad), _ = arrive(0, arrived[0], None)
             (second_cot, hidden_grad), _ = arrive(1, arrived[1], hidden_grad)
-            (third_cot, pre_grad, _, mean, _, _), _ = arrive(2, arrived[2], hidden_grad)
+            (third_cot, pre_grad, _, mean, _), _ = arrive(2, arrived[2], hidden_grad)
             cots = [first_cot, second_cot, third_cot]
 
     def finish(some, so_far):
@@ -439,10 +440,11 @@
     up_sent = step(up_total, parts[1], parts[2])
     for at in range(0, len(more_parts), 2):
         up_sent = step(onward(up_sent), more_parts[at], more_parts[at + 1])
-    (third_cot, pre_grad, pre_t, mean, *far), parts = arrive(2, after(arrived[2], up_sent), hidden_grad)
+    (third_cot, pre_grad, pre_t, mean, far), parts = arrive(2, after(arrived[2], up_sent), hidden_grad)
     cots = [first_cot, second_cot, third_cot]
     up_total = onward(step(onward(up_sent), parts[0], parts[1]))
-    down_totals = [onward(value) for value in far]
+    far = onward(far)
+    down_totals = [(far, (slice(None), slice(c * half_block, (c + 1) * half_block))) for c in (0, 1)]
     behinds = with_meta(
         functools.partial(stack_kernel, [behind(k) for k in range(1, half)]),
         shape(BF16, 2 * (half - 1), rank, half_block), scaled, pre_t, name="products",

time: 151 us -> 150 us (level)
  starting transfers between devices: 44.5 us -> 42.9 us
    ppermute x20 -> x19, starting transfers between devices: 38.4 us -> 37 us  [onward(): return lax.ppermute(value, 'dp', routes.onward)]
    ppermute x20 -> x19, waiting for transfers between devices: 43.9 us -> 44.6 us  [onward(): return lax.ppermute(value, 'dp', routes.onward)]
  transfers between devices with their start and end apart: 39 -> 38, of which waited for: 19 -> 19; matrix products, arithmetic and copies ran while one was open for 0% -> 0% of each run, Pallas kernels for 12% -> 12%
where the time goes in v8:
time: 150 us
  waiting for transfers between devices  76.5 us (51%)
  starting transfers between devices  42.9 us (29%)
  Pallas kernels  27.8 us (19%)
  local copies, waits for them, and re-layouts  1.93 us (1%)
    ppermute x19, waiting for transfers between devices, onward(): return lax.ppermute(value, 'dp', routes.onward)  44.6 us
    ppermute x19, starting transfers between devices, onward(): return lax.ppermute(value, 'dp', routes.onward)  37 us
    ppermute x3, waiting for transfers between devices, local(): arrived = [lax.ppermute(value, 'section', back) for value in sent]  28.6 us
    pallas_call x32, Pallas kernels, call(): pl.pallas_call(body, in_specs=specs or [VMEM] * len(args), out_specs=out_...  27.8 us
    ppermute x3, starting transfers between devices, local(): arrived = [lax.ppermute(value, 'section', back) for value in sent]  3.86 us
    ppermute x16, waiting for transfers between devices, swap(): return lax.ppermute(value, 'dp', routes.partner)  3.3 us
  transfers between devices with their start and end apart: 38, of which 19 were waited for; matrix products, arithmetic and copies ran while one was open for 0% of the time, Pallas kernels for 12%

profile of v8, /device:TPU:0, one launch (start us, length us, event | category | flops | bytes accessed | tf_op | source)
XLA Modules:
  0.0 150.1 jit_solution(6750715599058119067)
XLA Ops:
  0.7 0.5 collective-permute-start
  1.2 1.3 collective-permute-done.other_ref
  2.5 0.9 copy-done.4
  3.6 2.9 %collective-permute-start.1 = (bf16[1024,256]{1,0:T(8,128)(2,1)S(1)}, bf16[1024,256]{1,0:T(8,128)(2,1)S(1)}, u32[]{:S(2)}, u32[]{:S(2)}) collective-permute-start(bf16[1024,256]{1,0:T(8,128)(2,1)S(1)} %assemble.4.refs_7_.refs_8_), channel_id=1, source_target_pairs={{2,6},{6,10},{10,14},{14,12},{12,8},{8,4},{4,0},{0,2},{3,1},{7,3},... | collective-permute-start | bytes 1572872 | tf_op jit(solution)/shard_map/ppermute | solution.py:327
  6.5 0.9 copy-done.6
  7.5 1.6 %collective-permute-start.8 = (bf16[1024,256]{1,0:T(8,128)(2,1)S(1)}, bf16[1024,256]{1,0:T(8,128)(2,1)S(1)}, u32[]{:S(2)}, u32[]{:S(2)}) collective-permute-start(bf16[1024,256]{1,0:T(8,128)(2,1)S(1)} %assemble.5.refs_13_.refs_5_), channel_id=1, source_target_pairs={{2,6},{6,10},{10,14},{14,12},{12,8},{8,4},{4,0},{0,2},{3,1},{7,3},... | collective-permute-start | bytes 1572872 | tf_op jit(solution)/shard_map/ppermute | solution.py:327
  9.2 4.6 %collective-permute-done.1.refs_1_.refs_7_.refs_6_ = bf16[1024,256]{1,0:T(8,128)(2,1)S(1)} collective-permute-done((bf16[1024,256]{1,0:T(8,128)(2,1)S(1)}, bf16[1024,256]{1,0:T(8,128)(2,1)S(1)}, u32[]{:S(2)}, u32[]{:S(2)}) %collective-permute-start.1) | collective-permute-done | bytes 524320 | tf_op jit(solution)/shard_map/ppermute | solution.py:327
  13.7 2.0 %collective-permute-start.3 = (bf16[1024,256]{1,0:T(8,128)(2,1)S(1)}, bf16[1024,256]{1,0:T(8,128)(2,1)S(1)}, u32[]{:S(2)}, u32[]{:S(2)}) collective-permute-start(bf16[1024,256]{1,0:T(8,128)(2,1)S(1)} %collective-permute-done.1.refs_1_.refs_7_.refs_6_), channel_id=1, source_target_pairs={{2,6},{6,10},{10,14},{14,12},{12,8},{8,4},{4,0},{0,2},{3,1},{7,3},... | collective-permute-start | bytes 1572872 | tf_op jit(solution)/shard_map/ppermute | solution.py:327
  15.7 3.7 %collective-permute-done.8.refs_6_.refs_4_ = bf16[1024,256]{1,0:T(8,128)(2,1)S(1)} collective-permute-done((bf16[1024,256]{1,0:T(8,128)(2,1)S(1)}, bf16[1024,256]{1,0:T(8,128)(2,1)S(1)}, u32[]{:S(2)}, u32[]{:S(2)}) %collective-permute-start.8) | collective-permute-done | bytes 524320 | tf_op jit(solution)/shard_map/ppermute | solution.py:327
  19.3 2.0 %collective-permute-start.9 = (bf16[1024,256]{1,0:T(8,128)(2,1)S(1)}, bf16[1024,256]{1,0:T(8,128)(2,1)S(1)}, u32[]{:S(2)}, u32[]{:S(2)}) collective-permute-start(bf16[1024,256]{1,0:T(8,128)(2,1)S(1)} %collective-permute-done.8.refs_6_.refs_4_), channel_id=1, source_target_pairs={{2,6},{6,10},{10,14},{14,12},{12,8},{8,4},{4,0},{0,2},{3,1},{7,3},... | collective-permute-start | bytes 1572872 | tf_op jit(solution)/shard_map/ppermute | solution.py:327
  21.3 3.7 %collective-permute-done.3.refs_3_.refs_7_.refs_9_ = bf16[1024,256]{1,0:T(8,128)(2,1)S(1)} collective-permute-done((bf16[1024,256]{1,0:T(8,128)(2,1)S(1)}, bf16[1024,256]{1,0:T(8,128)(2,1)S(1)}, u32[]{:S(2)}, u32[]{:S(2)}) %collective-permute-start.3) | collective-permute-done | bytes 524320 | tf_op jit(solution)/shard_map/ppermute | solution.py:327
  25.0 2.0 %collective-permute-start.5 = (bf16[1024,256]{1,0:T(8,128)(2,1)S(1)}, bf16[1024,256]{1,0:T(8,128)(2,1)S(1)}, u32[]{:S(2)}, u32[]{:S(2)}) collective-permute-start(bf16[1024,256]{1,0:T(8,128)(2,1)S(1)} %collective-permute-done.3.refs_3_.refs_7_.refs_9_), channel_id=1, source_target_pairs={{2,6},{6,10},{10,14},{14,12},{12,8},{8,4},{4,0},{0,2},{3,1},{7,3},... | collective-permute-start | bytes 1572872 | tf_op jit(solution)/shard_map/ppermute | solution.py:327
  26.9 3.7 %collective-permute-done.9.refs_8_.refs_4_ = bf16[1024,256]{1,0:T(8,128)(2,1)S(1)} collective-permute-done((bf16[1024,256]{1,0:T(8,128)(2,1)S(1)}, bf16[1024,256]{1,0:T(8,128)(2,1)S(1)}, u32[]{:S(2)}, u32[]{:S(2)}) %collective-permute-start.9) | collective-permute-done | bytes 524320 | tf_op jit(solution)/shard_map/ppermute | solution.py:327
  30.6 0.5 collective-permute-start.4
  31.1 2.0 %collective-permute-start.14 = (bf16[1024,256]{1,0:T(8,128)(2,1)S(1)}, bf16[1024,256]{1,0:T(8,128)(2,1)S(1)}, u32[]{:S(2)}, u32[]{:S(2)}) collective-permute-start(bf16[1024,256]{1,0:T(8,128)(2,1)S(1)} %collective-permute-done.9.refs_8_.refs_4_), channel_id=1, source_target_pairs={{2,6},{6,10},{10,14},{14,12},{12,8},{8,4},{4,0},{0,2},{3,1},{7,3},... | collective-permute-start | bytes 1572872 | tf_op jit(solution)/shard_map/ppermute | solution.py:327
  33.0 3.1 %collective-permute-done.5.refs_5_.block_ref.refs_8_.refs_7_ = bf16[1024,256]{1,0:T(8,128)(2,1)S(1)} collective-permute-done((bf16[1024,256]{1,0:T(8,128)(2,1)S(1)}, bf16[1024,256]{1,0:T(8,128)(2,1)S(1)}, u32[]{:S(2)}, u32[]{:S(2)}) %collective-permute-start.5) | collective-permute-done | bytes 524320 | tf_op jit(solution)/shard_map/ppermute | solution.py:327
  36.3 2.0 %collective-permute-start.11 = (bf16[512,256]{1,0:T(8,128)(2,1)S(1)}, bf16[512,256]{1,0:T(8,128)(2,1)S(1)}, u32[]{:S(2)}, u32[]{:S(2)}) collective-permute-start(bf16[512,256]{1,0:T(8,128)(2,1)S(1)} %halve.2), channel_id=1, source_target_pairs={{2,6},{6,10},{10,14},{14,12},{12,8},{8,4},{4,0},{0,2},{3,1},{7,3},... | collective-permute-start | bytes 786440 | tf_op jit(solution)/shard_map/ppermute | solution.py:327
  38.3 3.5 %collective-permute-done.14.block_ref.refs_10_.refs_5_ = bf16[1024,256]{1,0:T(8,128)(2,1)S(1)} collective-permute-done((bf16[1024,256]{1,0:T(8,128)(2,1)S(1)}, bf16[1024,256]{1,0:T(8,128)(2,1)S(1)}, u32[]{:S(2)}, u32[]{:S(2)}) %collective-permute-start.14) | collective-permute-done | bytes 524320 | tf_op jit(solution)/shard_map/ppermute | solution.py:327
  41.8 2.0 %collective-permute-start.16 = (bf16[512,256]{1,0:T(8,128)(2,1)S(1)}, bf16[512,256]{1,0:T(8,128)(2,1)S(1)}, u32[]{:S(2)}, u32[]{:S(2)}) collective-permute-start(bf16[512,256]{1,0:T(8,128)(2,1)S(1)} %halve.3), channel_id=1, source_target_pairs={{2,6},{6,10},{10,14},{14,12},{12,8},{8,4},{4,0},{0,2},{3,1},{7,3},... | collective-permute-start | bytes 786440 | tf_op jit(solution)/shard_map/ppermute | solution.py:327
  43.9 0.5 collective-permute-start.15
  44.4 1.1 scale.1
  45.6 1.3 preact.1.refs_4_
  46.9 1.3 collective-permute-done.16.mine_ref
  48.3 1.5 collective-permute-done.17.other_ref
  49.9 3.9 %top.1 = (bf16[128,256]{1,0:T(8,128)(2,1)S(1)}, f32[128,1]{1,0:T(8,128)S(1)}, bf16[256,128]{1,0:T(8,128)(2,1)S(1)}, f32[128,256]{1,0:T(8,128)S(1)}, f32[128,256]...) custom-call(s32[16,8]{1,0:T(8,128)S(1)} %copy-done.2, ...), custom_call_target="tpu_custom_call" | custom-call | flops 1073741824 | bytes 3441024 | tf_op jit(solution)/shard_map/top/pallas_call | solution.py:64
  53.8 1.4 leave.4
  55.2 1.3 collective-permute-start.19
  56.5 1.2 leave.5
  57.7 1.3 collective-permute-start.23
  59.0 1.4 leave.3
  60.4 17.0 %collective-permute-done.19.refs_0_ = bf16[3,128,1024]{2,1,0:T(8,128)(2,1)S(1)} collective-permute-done((bf16[3,128,1024]{2,1,0:T(8,128)(2,1)S(1)}, bf16[3,128,1024]{2,1,0:T(8,128)(2,1)S(1)}, u32[]{:S(2)}, u32[]{:S(2)}) %collective-permute-start.19) | collective-permute-done | bytes 786464 | tf_op jit(solution)/shard_map/ppermute | solution.py:415
  77.5 1.5 arrive.3
  79.0 2.0 %collective-permute-start.20 = (bf16[256,1024]{1,0:T(8,128)(2,1)S(1)}, bf16[256,1024]{1,0:T(8,128)(2,1)S(1)}, u32[]{:S(2)}, u32[]{:S(2)}) collective-permute-start(bf16[256,1024]{1,0:T(8,128)(2,1)S(1)} %get-tuple-element.68), channel_id=1, source_target_pairs={{2,6},{6,10},{10,14},{14,12},{12,8},{8,4},{4,0},{0,2},{3,1},{7,3},... | collective-permute-start | bytes 1572872 | tf_op jit(solution)/shard_map/ppermute | solution.py:327
  81.0 1.3 collective-permute-start.18
  82.3 6.5 %collective-permute-done.23.refs_0_ = bf16[2,128,1024]{2,1,0:T(8,128)(2,1)S(1)} collective-permute-done((bf16[2,128,1024]{2,1,0:T(8,128)(2,1)S(1)}, bf16[2,128,1024]{2,1,0:T(8,128)(2,1)S(1)}, u32[]{:S(2)}, u32[]{:S(2)}) %collective-permute-start.23) | collective-permute-done | bytes 524320 | tf_op jit(solution)/shard_map/ppermute | solution.py:415
  88.7 1.3 arrive.4
  90.1 0.2 add.9
  90.3 2.0 %collective-permute-start.22 = (bf16[256,1024]{1,0:T(8,128)(2,1)S(1)}, bf16[256,1024]{1,0:T(8,128)(2,1)S(1)}, u32[]{:S(2)}, u32[]{:S(2)}) collective-permute-start(bf16[256,1024]{1,0:T(8,128)(2,1)S(1)} %add.9), channel_id=1, source_target_pairs={{2,6},{6,10},{10,14},{14,12},{12,8},{8,4},{4,0},{0,2},{3,1},{7,3},... | collective-permute-start | bytes 1572872 | tf_op jit(solution)/shard_map/ppermute | solution.py:327
  92.3 7.2 %collective-permute-done.22.refs_0_ = bf16[256,1024]{1,0:T(8,128)(2,1)S(1)} collective-permute-done((bf16[256,1024]{1,0:T(8,128)(2,1)S(1)}, bf16[256,1024]{1,0:T(8,128)(2,1)S(1)}, u32[]{:S(2)}, u32[]{:S(2)}) %collective-permute-start.22) | collective-permute-done | bytes 524320 | tf_op jit(solution)/shard_map/ppermute | solution.py:327
  99.7 5.1 %collective-permute-done.18.refs_0_ = bf16[3,128,1024]{2,1,0:T(8,128)(2,1)S(1)} collective-permute-done((bf16[3,128,1024]{2,1,0:T(8,128)(2,1)S(1)}, bf16[3,128,1024]{2,1,0:T(8,128)(2,1)S(1)}, u32[]{:S(2)}, u32[]{:S(2)}) %collective-permute-start.18) | collective-permute-done | bytes 786464 | tf_op jit(solution)/shard_map/ppermute | solution.py:415
  104.8 1.7 %arrive.5 = (bf16[3,128,1024]{2,1,0:T(8,128)(2,1)S(1)}, bf16[128,256]{1,0:T(8,128)(2,1)S(1)}, bf16[256,128]{1,0:T(8,128)(2,1)S(1)}, f32[128,1]{1,0:T(8,128)S(1)}...) custom-call(s32[16,8]{1,0:T(8,128)S(1)} %copy-done.2, ...), custom_call_target="tpu_custom_call" | custom-call | flops 402653184 | bytes 2179328 | tf_op jit(solution)/shard_map/arrive/pallas_call | solution.py:64
  106.5 1.2 products.3
  107.8 2.0 %collective-permute-start.25 = (bf16[256,1024]{1,0:T(8,128)(2,1)S(1)}, bf16[256,1024]{1,0:T(8,128)(2,1)S(1)}, u32[]{:S(2)}, u32[]{:S(2)}) collective-permute-start(bf16[256,1024]{1,0:T(8,128)(2,1)S(1)} %get-tuple-element.84), channel_id=1, source_target_pairs={{2,6},{6,10},{10,14},{14,12},{12,8},{8,4},{4,0},{0,2},{3,1},{7,3},... | collective-permute-start | bytes 1572872 | tf_op jit(solution)/shard_map/ppermute | solution.py:327
  109.8 1.6 %collective-permute-start.34 = (bf16[256,1024]{1,0:T(8,128)(2,1)S(1)}, bf16[256,1024]{1,0:T(8,128)(2,1)S(1)}, u32[]{:S(2)}, u32[]{:S(2)}) collective-permute-start(bf16[256,1024]{1,0:T(8,128)(2,1)S(1)} %add.10), channel_id=1, source_target_pairs={{2,6},{6,10},{10,14},{14,12},{12,8},{8,4},{4,0},{0,2},{3,1},{7,3},... | collective-permute-start | bytes 1572872 | tf_op jit(solution)/shard_map/ppermute | solution.py:327
  111.4 1.4 products.2
  112.8 4.3 %collective-permute-done.25.refs_0_ = bf16[256,1024]{1,0:T(8,128)(2,1)S(1)} collective-permute-done((bf16[256,1024]{1,0:T(8,128)(2,1)S(1)}, bf16[256,1024]{1,0:T(8,128)(2,1)S(1)}, u32[]{:S(2)}, u32[]{:S(2)}) %collective-permute-start.25) | collective-permute-done | bytes 524320 | tf_op jit(solution)/shard_map/ppermute | solution.py:327
  117.1 2.0 %collective-permute-start.30 = (bf16[256,512]{1,0:T(8,128)(2,1)S(1)}, bf16[256,512]{1,0:T(8,128)(2,1)S(1)}, u32[]{:S(2)}, u32[]{:S(2)}) collective-permute-start(bf16[256,512]{1,0:T(8,128)(2,1)S(1)} %add.14), channel_id=1, source_target_pairs={{2,6},{6,10},{10,14},{14,12},{12,8},{8,4},{4,0},{0,2},{3,1},{7,3},... | collective-permute-start | bytes 786440 | tf_op jit(solution)/shard_map/ppermute | solution.py:327
  119.3 1.6 %collective-permute-start.27 = (bf16[256,512]{1,0:T(8,128)(2,1)S(1)}, bf16[256,512]{1,0:T(8,128)(2,1)S(1)}, u32[]{:S(2)}, u32[]{:S(2)}) collective-permute-start(bf16[256,512]{1,0:T(8,128)(2,1)S(1)} %add.11), channel_id=1, source_target_pairs={{2,6},{6,10},{10,14},{14,12},{12,8},{8,4},{4,0},{0,2},{3,1},{7,3},... | collective-permute-start | bytes 786440 | tf_op jit(solution)/shard_map/ppermute | solution.py:327
  120.9 1.8 %collective-permute-done.34.refs_0_ = bf16[256,1024]{1,0:T(8,128)(2,1)S(1)} collective-permute-done((bf16[256,1024]{1,0:T(8,128)(2,1)S(1)}, bf16[256,1024]{1,0:T(8,128)(2,1)S(1)}, u32[]{:S(2)}, u32[]{:S(2)}) %collective-permute-start.34) | collective-permute-done | bytes 524320 | tf_op jit(solution)/shard_map/ppermute | solution.py:327
  122.8 2.0 %collective-permute-start.36 = (bf16[256,1024]{1,0:T(8,128)(2,1)S(1)}, bf16[256,1024]{1,0:T(8,128)(2,1)S(1)}, u32[]{:S(2)}, u32[]{:S(2)}) collective-permute-start(bf16[256,1024]{1,0:T(8,128)(2,1)S(1)} %add.17), channel_id=1, source_target_pairs={{2,6},{6,10},{10,14},{14,12},{12,8},{8,4},{4,0},{0,2},{3,1},{7,3},... | collective-permute-start | bytes 1572872 | tf_op jit(solution)/shard_map/ppermute | solution.py:327
  124.9 2.6 %finish.2.refs_9_ = bf16[128,8192]{1,0:T(8,128)(2,1)} custom-call(s32[16,8]{1,0:T(8,128)S(1)} %copy-done.2, bf16[128,8192]{1,0:T(8,128)(2,1)S(1)} %bitcast.10, f32[1,8192]{1,0:T(1,128)S(1)} %copy-done.3, bf16[128,256]{1,0:T(8,128)(2,1)S(1)} %get-tuple-element.79.refs_2_, f32[128,1]{1,0:T(8,128)S(1)} %get-tuple-element.62.refs_4_.refs_3_, ...), custom_call_target="tpu_custom_call" | custom-call | flops 335544320 | bytes 2056576 | tf_op jit(solution)/shard_map/finish/pallas_call | solution.py:64
  127.5 1.6 %collective-permute-start.31 = (bf16[256,512]{1,0:T(8,128)(2,1)S(1)}, bf16[256,512]{1,0:T(8,128)(2,1)S(1)}, u32[]{:S(2)}, u32[]{:S(2)}) collective-permute-start(bf16[256,512]{1,0:T(8,128)(2,1)S(1)} %add.15), channel_id=1, source_target_pairs={{2,6},{6,10},{10,14},{14,12},{12,8},{8,4},{4,0},{0,2},{3,1},{7,3},... | collective-permute-start | bytes 786440 | tf_op jit(solution)/shard_map/ppermute | solution.py:327
  129.3 1.6 %collective-permute-start.28 = (bf16[256,512]{1,0:T(8,128)(2,1)S(1)}, bf16[256,512]{1,0:T(8,128)(2,1)S(1)}, u32[]{:S(2)}, u32[]{:S(2)}) collective-permute-start(bf16[256,512]{1,0:T(8,128)(2,1)S(1)} %add.12), channel_id=1, source_target_pairs={{2,6},{6,10},{10,14},{14,12},{12,8},{8,4},{4,0},{0,2},{3,1},{7,3},... | collective-permute-start | bytes 786440 | tf_op jit(solution)/shard_map/ppermute | solution.py:327
  130.9 5.8 %collective-permute-done.31.refs_0_ = bf16[256,512]{1,0:T(8,128)(2,1)S(1)} collective-permute-done((bf16[256,512]{1,0:T(8,128)(2,1)S(1)}, bf16[256,512]{1,0:T(8,128)(2,1)S(1)}, u32[]{:S(2)}, u32[]{:S(2)}) %collective-permute-start.31) | collective-permute-done | bytes 262176 | tf_op jit(solution)/shard_map/ppermute | solution.py:327
  136.8 2.0 %collective-permute-start.32 = (bf16[256,512]{1,0:T(8,128)(2,1)S(1)}, bf16[256,512]{1,0:T(8,128)(2,1)S(1)}, u32[]{:S(2)}, u32[]{:S(2)}) collective-permute-start(bf16[256,512]{1,0:T(8,128)(2,1)S(1)} %add.16), channel_id=1, source_target_pairs={{2,6},{6,10},{10,14},{14,12},{12,8},{8,4},{4,0},{0,2},{3,1},{7,3},... | collective-permute-start | bytes 786440 | tf_op jit(solution)/shard_map/ppermute | solution.py:327
  138.8 0.7 collective-permute-done.28.refs_0_
  139.6 2.0 %collective-permute-start.29 = (bf16[256,512]{1,0:T(8,128)(2,1)S(1)}, bf16[256,512]{1,0:T(8,128)(2,1)S(1)}, u32[]{:S(2)}, u32[]{:S(2)}) collective-permute-start(bf16[256,512]{1,0:T(8,128)(2,1)S(1)} %add.13), channel_id=1, source_target_pairs={{2,6},{6,10},{10,14},{14,12},{12,8},{8,4},{4,0},{0,2},{3,1},{7,3},... | collective-permute-start | bytes 786440 | tf_op jit(solution)/shard_map/ppermute | solution.py:327
  141.6 0.8 split.3
  142.5 2.2 %finish.3 = bf16[128,8192]{1,0:T(8,128)(2,1)} custom-call(s32[16,8]{1,0:T(8,128)S(1)} %copy-done.2, bf16[128,8192]{1,0:T(8,128)(2,1)S(1)} %bitcast.11, f32[1,8192]{1,0:T(1,128)S(1)} %copy-done.3, bf16[128,256]{1,0:T(8,128)(2,1)S(1)} %get-tuple-element.79.refs_2_, f32[128,1]{1,0:T(8,128)S(1)} %get-tuple-element.62.refs_4_.refs_3_, ...), custom_call_target="tpu_custom_call", output_to_operand_aliasing={{}: (10, {})} | custom-call | flops 201326592 | bytes 2187648 | tf_op jit(solution)/shard_map/finish/pallas_call | solution.py:64
  144.7 1.3 collective-permute-done.29.refs_0_
  146.0 0.8 split.2
  146.9 1.0 close_up.1
  147.9 0.5 collective-permute-done.33.refs_1_
  148.5 1.7 %close_down.1 = (f32[1,512,256]{2,1,0:T(8,128)}, f32[1,512]{1,0:T(1,128)}) custom-call(s32[16,8]{1,0:T(8,128)S(1)} %copy-done.2, f32[256,512]{1,0:T(8,128)S(1)} %get-tuple-element.96.refs_0_, bf16[256,512]{1,0:T(8,128)(2,1)S(1)} %collective-permute-done.33.refs_1_, f32[256,512]{1,0:T(8,128)S(1)} %get-tuple-element.98.refs_2_, f32[1,8192]{1,0:T(1,128)S(1)} %copy-done.3), custom_call_target="tpu_custom_call" | custom-call | bytes 467584 | tf_op jit(solution)/shard_map/close_down/pallas_call | solution.py:64
  (60 shorter events, 1.8 us)
Async XLA Ops:
  0.6 43.7 %copy-start = (bf16[1,128,8192]{2,1,0:T(8,128)(2,1)S(1)}, bf16[1,128,8192]{2,1,0:T(8,128)(2,1)}, u32[]{:S(2)}) copy-start(bf16[1,128,8192]{2,1,0:T(8,128)(2,1)} %param.7) | copy-start | bytes 6291460
  0.6 43.7 %copy-start.3 = (f32[1,8192]{1,0:T(1,128)S(1)}, f32[1,8192]{1,0:T(1,128)}, u32[]{:S(2)}) copy-start(f32[1,8192]{1,0:T(1,128)} %refs_3_.1) | copy-start | bytes 98308
  0.7 1.9 %collective-permute-start = (bf16[512,256]{1,0:T(8,128)(2,1)}, bf16[512,256]{1,0:T(8,128)(2,1)S(1)}, u32[]{:S(2)}, u32[]{:S(2)}) collective-permute-start(bf16[512,256]{1,0:T(8,128)(2,1)} %bitcast.12), channel_id=1, source_target_pairs={{0,1},{1,0},{2,3},{3,2},{4,5},{5,4},{6,7},{7,6},{8,9},{9,8},{10,11... | collective-permute-start | bytes 786440 | tf_op jit(solution)/shard_map/ppermute | solution.py:324
  1.2 5.3 %collective-permute-start.7 = (bf16[512,256]{1,0:T(8,128)(2,1)}, bf16[512,256]{1,0:T(8,128)(2,1)S(1)}, u32[]{:S(2)}, u32[]{:S(2)}) collective-permute-start(bf16[512,256]{1,0:T(8,128)(2,1)} %bitcast.15), channel_id=1, source_target_pairs={{0,1},{1,0},{2,3},{3,2},{4,5},{5,4},{6,7},{7,6},{8,9},{9,8},{10,11... | collective-permute-start | bytes 786440 | tf_op jit(solution)/shard_map/ppermute | solution.py:324
  2.5 0.9 copy-start.4
  3.5 40.9 %copy-start.5 = (bf16[1,512,256]{2,1,0:T(8,128)(2,1)S(1)}, bf16[1,512,256]{2,1,0:T(8,128)(2,1)}, u32[]{:S(2)}) copy-start(bf16[1,512,256]{2,1,0:T(8,128)(2,1)} %param.11) | copy-start | bytes 786436
  3.6 10.2 %collective-permute-start.1 = (bf16[1024,256]{1,0:T(8,128)(2,1)S(1)}, bf16[1024,256]{1,0:T(8,128)(2,1)S(1)}, u32[]{:S(2)}, u32[]{:S(2)}) collective-permute-start(bf16[1024,256]{1,0:T(8,128)(2,1)S(1)} %assemble.4.refs_7_.refs_8_), channel_id=1, source_target_pairs={{2,6},{6,10},{10,14},{14,12},{12,8},{8,4},{4,0},{0,2},{3,1},{7,3},... | collective-permute-start | bytes 1572872 | tf_op jit(solution)/shard_map/ppermute | solution.py:327
  6.5 1.0 copy-start.6
  7.5 36.9 %copy-start.7 = (s32[128]{0:T(128)S(1)}, s32[128]{0:T(128)}, u32[]{:S(2)}) copy-start(s32[128]{0:T(128)} %param.9) | copy-start | bytes 1540
  7.5 38.1 %copy-start.2 = (s32[16,8]{1,0:T(8,128)S(1)}, s32[16,8]{1,0:T(8,128)}, u32[]{:S(2)}) copy-start(s32[16,8]{1,0:T(8,128)} %constant.2.clone.table_ref) | copy-start | bytes 1540
  7.5 11.8 %collective-permute-start.8 = (bf16[1024,256]{1,0:T(8,128)(2,1)S(1)}, bf16[1024,256]{1,0:T(8,128)(2,1)S(1)}, u32[]{:S(2)}, u32[]{:S(2)}) collective-permute-start(bf16[1024,256]{1,0:T(8,128)(2,1)S(1)} %assemble.5.refs_13_.refs_5_), channel_id=1, source_target_pairs={{2,6},{6,10},{10,14},{14,12},{12,8},{8,4},{4,0},{0,2},{3,1},{7,3},... | collective-permute-start | bytes 1572872 | tf_op jit(solution)/shard_map/ppermute | solution.py:327
  13.7 11.2 %collective-permute-start.3 = (bf16[1024,256]{1,0:T(8,128)(2,1)S(1)}, bf16[1024,256]{1,0:T(8,128)(2,1)S(1)}, u32[]{:S(2)}, u32[]{:S(2)}) collective-permute-start(bf16[1024,256]{1,0:T(8,128)(2,1)S(1)} %collective-permute-done.1.refs_1_.refs_7_.refs_6_), channel_id=1, source_target_pairs={{2,6},{6,10},{10,14},{14,12},{12,8},{8,4},{4,0},{0,2},{3,1},{7,3},... | collective-permute-start | bytes 1572872 | tf_op jit(solution)/shard_map/ppermute | solution.py:327
  19.3 11.2 %collective-permute-start.9 = (bf16[1024,256]{1,0:T(8,128)(2,1)S(1)}, bf16[1024,256]{1,0:T(8,128)(2,1)S(1)}, u32[]{:S(2)}, u32[]{:S(2)}) collective-permute-start(bf16[1024,256]{1,0:T(8,128)(2,1)S(1)} %collective-permute-done.8.refs_6_.refs_4_), channel_id=1, source_target_pairs={{2,6},{6,10},{10,14},{14,12},{12,8},{8,4},{4,0},{0,2},{3,1},{7,3},... | collective-permute-start | bytes 1572872 | tf_op jit(solution)/shard_map/ppermute | solution.py:327
  25.0 11.2 %collective-permute-start.5 = (bf16[1024,256]{1,0:T(8,128)(2,1)S(1)}, bf16[1024,256]{1,0:T(8,128)(2,1)S(1)}, u32[]{:S(2)}, u32[]{:S(2)}) collective-permute-start(bf16[1024,256]{1,0:T(8,128)(2,1)S(1)} %collective-permute-done.3.refs_3_.refs_7_.refs_9_), channel_id=1, source_target_pairs={{2,6},{6,10},{10,14},{14,12},{12,8},{8,4},{4,0},{0,2},{3,1},{7,3},... | collective-permute-start | bytes 1572872 | tf_op jit(solution)/shard_map/ppermute | solution.py:327
  30.6 5.7 %collective-permute-start.10 = (bf16[1024,256]{1,0:T(8,128)(2,1)S(1)}, bf16[1024,256]{1,0:T(8,128)(2,1)S(1)}, u32[]{:S(2)}, u32[]{:S(2)}) collective-permute-start(bf16[1024,256]{1,0:T(8,128)(2,1)S(1)} %collective-permute-done.9.refs_8_.refs_4_), channel_id=1, source_target_pairs={{0,1},{1,0},{2,3},{3,2},{4,5},{5,4},{6,7},{7,6},{8,9},{9,8},{10,11... | collective-permute-start | bytes 1572872 | tf_op jit(solution)/shard_map/ppermute | solution.py:324
  30.6 5.7 %collective-permute-start.4 = (bf16[1024,256]{1,0:T(8,128)(2,1)S(1)}, bf16[1024,256]{1,0:T(8,128)(2,1)S(1)}, u32[]{:S(2)}, u32[]{:S(2)}) collective-permute-start(bf16[1024,256]{1,0:T(8,128)(2,1)S(1)} %collective-permute-done.3.refs_3_.refs_7_.refs_9_), channel_id=1, source_target_pairs={{0,1},{1,0},{2,3},{3,2},{4,5},{5,4},{6,7},{7,6},{8,9},{9,8},{10,11... | collective-permute-start | bytes 1572872 | tf_op jit(solution)/shard_map/ppermute | solution.py:324
  31.1 10.7 %collective-permute-start.14 = (bf16[1024,256]{1,0:T(8,128)(2,1)S(1)}, bf16[1024,256]{1,0:T(8,128)(2,1)S(1)}, u32[]{:S(2)}, u32[]{:S(2)}) collective-permute-start(bf16[1024,256]{1,0:T(8,128)(2,1)S(1)} %collective-permute-done.9.refs_8_.refs_4_), channel_id=1, source_target_pairs={{2,6},{6,10},{10,14},{14,12},{12,8},{8,4},{4,0},{0,2},{3,1},{7,3},... | collective-permute-start | bytes 1572872 | tf_op jit(solution)/shard_map/ppermute | solution.py:327
  33.0 10.8 %collective-permute-start.2 = (bf16[1024,256]{1,0:T(8,128)(2,1)S(1)}, bf16[1024,256]{1,0:T(8,128)(2,1)S(1)}, u32[]{:S(2)}, u32[]{:S(2)}) collective-permute-start(bf16[1024,256]{1,0:T(8,128)(2,1)S(1)} %collective-permute-done.1.refs_1_.refs_7_.refs_6_), channel_id=1, source_target_pairs={{0,1},{1,0},{2,3},{3,2},{4,5},{5,4},{6,7},{7,6},{8,9},{9,8},{10,11... | collective-permute-start | bytes 1572872 | tf_op jit(solution)/shard_map/ppermute | solution.py:324
  36.2 9.4 %collective-permute-start.6 = (bf16[1024,256]{1,0:T(8,128)(2,1)S(1)}, bf16[1024,256]{1,0:T(8,128)(2,1)S(1)}, u32[]{:S(2)}, u32[]{:S(2)}) collective-permute-start(bf16[1024,256]{1,0:T(8,128)(2,1)S(1)} %collective-permute-done.5.refs_5_.block_ref.refs_8_.refs_7_), channel_id=1, source_target_pairs={{0,1},{1,0},{2,3},{3,2},{4,5},{5,4},{6,7},{7,6},{8,9},{9,8},{10,11... | collective-permute-start | bytes 1572872 | tf_op jit(solution)/shard_map/ppermute | solution.py:324
  36.3 9.2 %collective-permute-start.11 = (bf16[512,256]{1,0:T(8,128)(2,1)S(1)}, bf16[512,256]{1,0:T(8,128)(2,1)S(1)}, u32[]{:S(2)}, u32[]{:S(2)}) collective-permute-start(bf16[512,256]{1,0:T(8,128)(2,1)S(1)} %halve.2), channel_id=1, source_target_pairs={{2,6},{6,10},{10,14},{14,12},{12,8},{8,4},{4,0},{0,2},{3,1},{7,3},... | collective-permute-start | bytes 786440 | tf_op jit(solution)/shard_map/ppermute | solution.py:327
  41.8 6.4 %collective-permute-start.16 = (bf16[512,256]{1,0:T(8,128)(2,1)S(1)}, bf16[512,256]{1,0:T(8,128)(2,1)S(1)}, u32[]{:S(2)}, u32[]{:S(2)}) collective-permute-start(bf16[512,256]{1,0:T(8,128)(2,1)S(1)} %halve.3), channel_id=1, source_target_pairs={{2,6},{6,10},{10,14},{14,12},{12,8},{8,4},{4,0},{0,2},{3,1},{7,3},... | collective-permute-start | bytes 786440 | tf_op jit(solution)/shard_map/ppermute | solution.py:327
  43.9 6.0 %collective-permute-start.13 = (bf16[1024,256]{1,0:T(8,128)(2,1)S(1)}, bf16[1024,256]{1,0:T(8,128)(2,1)S(1)}, u32[]{:S(2)}, u32[]{:S(2)}) collective-permute-start(bf16[1024,256]{1,0:T(8,128)(2,1)S(1)} %collective-permute-done.8.refs_6_.refs_4_), channel_id=1, source_target_pairs={{0,1},{1,0},{2,3},{3,2},{4,5},{5,4},{6,7},{7,6},{8,9},{9,8},{10,11... | collective-permute-start | bytes 1572872 | tf_op jit(solution)/shard_map/ppermute | solution.py:324
  43.9 6.0 %collective-permute-start.15 = (bf16[1024,256]{1,0:T(8,128)(2,1)S(1)}, bf16[1024,256]{1,0:T(8,128)(2,1)S(1)}, u32[]{:S(2)}, u32[]{:S(2)}) collective-permute-start(bf16[1024,256]{1,0:T(8,128)(2,1)S(1)} %collective-permute-done.14.block_ref.refs_10_.refs_5_), channel_id=1, source_target_pairs={{0,1},{1,0},{2,3},{3,2},{4,5},{5,4},{6,7},{7,6},{8,9},{9,8},{10,11... | collective-permute-start | bytes 1572872 | tf_op jit(solution)/shard_map/ppermute | solution.py:324
  45.5 2.8 %collective-permute-start.12 = (bf16[512,256]{1,0:T(8,128)(2,1)S(1)}, bf16[512,256]{1,0:T(8,128)(2,1)S(1)}, u32[]{:S(2)}, u32[]{:S(2)}) collective-permute-start(bf16[512,256]{1,0:T(8,128)(2,1)S(1)} %collective-permute-done.11.mine_ref), channel_id=1, source_target_pairs={{0,1},{1,0},{2,3},{3,2},{4,5},{5,4},{6,7},{7,6},{8,9},{9,8},{10,11... | collective-permute-start | bytes 786440 | tf_op jit(solution)/shard_map/ppermute | solution.py:324
  46.9 3.0 %copy-start.1 = (bf16[128,8192]{1,0:T(8,128)(2,1)S(1)}, bf16[128,8192]{1,0:T(8,128)(2,1)}, u32[]{:S(2)}) copy-start(bf16[128,8192]{1,0:T(8,128)(2,1)} %refs_1_.3) | copy-start | bytes 6291460
  48.3 1.5 %collective-permute-start.17 = (bf16[512,256]{1,0:T(8,128)(2,1)S(1)}, bf16[512,256]{1,0:T(8,128)(2,1)S(1)}, u32[]{:S(2)}, u32[]{:S(2)}) collective-permute-start(bf16[512,256]{1,0:T(8,128)(2,1)S(1)} %collective-permute-done.16.mine_ref), channel_id=1, source_target_pairs={{0,1},{1,0},{2,3},{3,2},{4,5},{5,4},{6,7},{7,6},{8,9},{9,8},{10,11... | collective-permute-start | bytes 786440 | tf_op jit(solution)/shard_map/ppermute | solution.py:324
  55.2 22.3 %collective-permute-start.19 = (bf16[3,128,1024]{2,1,0:T(8,128)(2,1)S(1)}, bf16[3,128,1024]{2,1,0:T(8,128)(2,1)S(1)}, u32[]{:S(2)}, u32[]{:S(2)}) collective-permute-start(bf16[3,128,1024]{2,1,0:T(8,128)(2,1)S(1)} %leave.4), channel_id=1, source_target_pairs={{16,0},{17,1},{18,2},{19,3},{20,4},{21,5},{22,6},{23,7},{24,8},{25... | collective-permute-start | bytes 2359304 | tf_op jit(solution)/shard_map/ppermute | solution.py:415
  57.7 31.0 %collective-permute-start.23 = (bf16[2,128,1024]{2,1,0:T(8,128)(2,1)S(1)}, bf16[2,128,1024]{2,1,0:T(8,128)(2,1)S(1)}, u32[]{:S(2)}, u32[]{:S(2)}) collective-permute-start(bf16[2,128,1024]{2,1,0:T(8,128)(2,1)S(1)} %leave.5), channel_id=1, source_target_pairs={{16,0},{17,1},{18,2},{19,3},{20,4},{21,5},{22,6},{23,7},{24,8},{25... | collective-permute-start | bytes 1572872 | tf_op jit(solution)/shard_map/ppermute | solution.py:415
  79.0 9.8 %collective-permute-start.20 = (bf16[256,1024]{1,0:T(8,128)(2,1)S(1)}, bf16[256,1024]{1,0:T(8,128)(2,1)S(1)}, u32[]{:S(2)}, u32[]{:S(2)}) collective-permute-start(bf16[256,1024]{1,0:T(8,128)(2,1)S(1)} %get-tuple-element.68), channel_id=1, source_target_pairs={{2,6},{6,10},{10,14},{14,12},{12,8},{8,4},{4,0},{0,2},{3,1},{7,3},... | collective-permute-start | bytes 1572872 | tf_op jit(solution)/shard_map/ppermute | solution.py:327
  81.0 9.1 %collective-permute-start.21 = (bf16[256,1024]{1,0:T(8,128)(2,1)S(1)}, bf16[256,1024]{1,0:T(8,128)(2,1)S(1)}, u32[]{:S(2)}, u32[]{:S(2)}) collective-permute-start(bf16[256,1024]{1,0:T(8,128)(2,1)S(1)} %get-tuple-element.70), channel_id=1, source_target_pairs={{0,1},{1,0},{2,3},{3,2},{4,5},{5,4},{6,7},{7,6},{8,9},{9,8},{10,11... | collective-permute-start | bytes 1572872 | tf_op jit(solution)/shard_map/ppermute | solution.py:324
  81.0 23.8 %collective-permute-start.18 = (bf16[3,128,1024]{2,1,0:T(8,128)(2,1)S(1)}, bf16[3,128,1024]{2,1,0:T(8,128)(2,1)S(1)}, u32[]{:S(2)}, u32[]{:S(2)}) collective-permute-start(bf16[3,128,1024]{2,1,0:T(8,128)(2,1)S(1)} %leave.3), channel_id=1, source_target_pairs={{16,0},{17,1},{18,2},{19,3},{20,4},{21,5},{22,6},{23,7},{24,8},{25... | collective-permute-start | bytes 2359304 | tf_op jit(solution)/shard_map/ppermute | solution.py:415
  90.0 2.3 %collective-permute-start.24 = (bf16[256,1024]{1,0:T(8,128)(2,1)S(1)}, bf16[256,1024]{1,0:T(8,128)(2,1)S(1)}, u32[]{:S(2)}, u32[]{:S(2)}) collective-permute-start(bf16[256,1024]{1,0:T(8,128)(2,1)S(1)} %get-tuple-element.74), channel_id=1, source_target_pairs={{0,1},{1,0},{2,3},{3,2},{4,5},{5,4},{6,7},{7,6},{8,9},{9,8},{10,11... | collective-permute-start | bytes 1572872 | tf_op jit(solution)/shard_map/ppermute | solution.py:324
  90.3 9.2 %collective-permute-start.22 = (bf16[256,1024]{1,0:T(8,128)(2,1)S(1)}, bf16[256,1024]{1,0:T(8,128)(2,1)S(1)}, u32[]{:S(2)}, u32[]{:S(2)}) collective-permute-start(bf16[256,1024]{1,0:T(8,128)(2,1)S(1)} %add.9), channel_id=1, source_target_pairs={{2,6},{6,10},{10,14},{14,12},{12,8},{8,4},{4,0},{0,2},{3,1},{7,3},... | collective-permute-start | bytes 1572872 | tf_op jit(solution)/shard_map/ppermute | solution.py:327
  107.7 9.3 %collective-permute-start.26 = (bf16[6,256,512]{2,1,0:T(8,128)(2,1)S(1)}, bf16[6,256,512]{2,1,0:T(8,128)(2,1)S(1)}, u32[]{:S(2)}, u32[]{:S(2)}) collective-permute-start(bf16[6,256,512]{2,1,0:T(8,128)(2,1)S(1)} %products.3), channel_id=1, source_target_pairs={{0,1},{1,0},{2,3},{3,2},{4,5},{5,4},{6,7},{7,6},{8,9},{9,8},{10,11... | collective-permute-start | bytes 4718600 | tf_op jit(solution)/shard_map/ppermute | solution.py:324
  107.8 9.2 %collective-permute-start.25 = (bf16[256,1024]{1,0:T(8,128)(2,1)S(1)}, bf16[256,1024]{1,0:T(8,128)(2,1)S(1)}, u32[]{:S(2)}, u32[]{:S(2)}) collective-permute-start(bf16[256,1024]{1,0:T(8,128)(2,1)S(1)} %get-tuple-element.84), channel_id=1, source_target_pairs={{2,6},{6,10},{10,14},{14,12},{12,8},{8,4},{4,0},{0,2},{3,1},{7,3},... | collective-permute-start | bytes 1572872 | tf_op jit(solution)/shard_map/ppermute | solution.py:327
  109.8 12.8 %collective-permute-start.34 = (bf16[256,1024]{1,0:T(8,128)(2,1)S(1)}, bf16[256,1024]{1,0:T(8,128)(2,1)S(1)}, u32[]{:S(2)}, u32[]{:S(2)}) collective-permute-start(bf16[256,1024]{1,0:T(8,128)(2,1)S(1)} %add.10), channel_id=1, source_target_pairs={{2,6},{6,10},{10,14},{14,12},{12,8},{8,4},{4,0},{0,2},{3,1},{7,3},... | collective-permute-start | bytes 1572872 | tf_op jit(solution)/shard_map/ppermute | solution.py:327
  111.4 11.3 %collective-permute-start.35 = (bf16[256,1024]{1,0:T(8,128)(2,1)S(1)}, bf16[256,1024]{1,0:T(8,128)(2,1)S(1)}, u32[]{:S(2)}, u32[]{:S(2)}) collective-permute-start(bf16[256,1024]{1,0:T(8,128)(2,1)S(1)} %get-tuple-element.101), channel_id=1, source_target_pairs={{0,1},{1,0},{2,3},{3,2},{4,5},{5,4},{6,7},{7,6},{8,9},{9,8},{10,11... | collective-permute-start | bytes 1572872 | tf_op jit(solution)/shard_map/ppermute | solution.py:324
  117.1 10.3 %collective-permute-start.30 = (bf16[256,512]{1,0:T(8,128)(2,1)S(1)}, bf16[256,512]{1,0:T(8,128)(2,1)S(1)}, u32[]{:S(2)}, u32[]{:S(2)}) collective-permute-start(bf16[256,512]{1,0:T(8,128)(2,1)S(1)} %add.14), channel_id=1, source_target_pairs={{2,6},{6,10},{10,14},{14,12},{12,8},{8,4},{4,0},{0,2},{3,1},{7,3},... | collective-permute-start | bytes 786440 | tf_op jit(solution)/shard_map/ppermute | solution.py:327
  119.3 9.9 %collective-permute-start.27 = (bf16[256,512]{1,0:T(8,128)(2,1)S(1)}, bf16[256,512]{1,0:T(8,128)(2,1)S(1)}, u32[]{:S(2)}, u32[]{:S(2)}) collective-permute-start(bf16[256,512]{1,0:T(8,128)(2,1)S(1)} %add.11), channel_id=1, source_target_pairs={{2,6},{6,10},{10,14},{14,12},{12,8},{8,4},{4,0},{0,2},{3,1},{7,3},... | collective-permute-start | bytes 786440 | tf_op jit(solution)/shard_map/ppermute | solution.py:327
  122.8 18.8 %collective-permute-start.36 = (bf16[256,1024]{1,0:T(8,128)(2,1)S(1)}, bf16[256,1024]{1,0:T(8,128)(2,1)S(1)}, u32[]{:S(2)}, u32[]{:S(2)}) collective-permute-start(bf16[256,1024]{1,0:T(8,128)(2,1)S(1)} %add.17), channel_id=1, source_target_pairs={{2,6},{6,10},{10,14},{14,12},{12,8},{8,4},{4,0},{0,2},{3,1},{7,3},... | collective-permute-start | bytes 1572872 | tf_op jit(solution)/shard_map/ppermute | solution.py:327
  127.5 9.2 %collective-permute-start.31 = (bf16[256,512]{1,0:T(8,128)(2,1)S(1)}, bf16[256,512]{1,0:T(8,128)(2,1)S(1)}, u32[]{:S(2)}, u32[]{:S(2)}) collective-permute-start(bf16[256,512]{1,0:T(8,128)(2,1)S(1)} %add.15), channel_id=1, source_target_pairs={{2,6},{6,10},{10,14},{14,12},{12,8},{8,4},{4,0},{0,2},{3,1},{7,3},... | collective-permute-start | bytes 786440 | tf_op jit(solution)/shard_map/ppermute | solution.py:327
  129.3 10.2 %collective-permute-start.28 = (bf16[256,512]{1,0:T(8,128)(2,1)S(1)}, bf16[256,512]{1,0:T(8,128)(2,1)S(1)}, u32[]{:S(2)}, u32[]{:S(2)}) collective-permute-start(bf16[256,512]{1,0:T(8,128)(2,1)S(1)} %add.12), channel_id=1, source_target_pairs={{2,6},{6,10},{10,14},{14,12},{12,8},{8,4},{4,0},{0,2},{3,1},{7,3},... | collective-permute-start | bytes 786440 | tf_op jit(solution)/shard_map/ppermute | solution.py:327
  136.8 7.9 %collective-permute-start.32 = (bf16[256,512]{1,0:T(8,128)(2,1)S(1)}, bf16[256,512]{1,0:T(8,128)(2,1)S(1)}, u32[]{:S(2)}, u32[]{:S(2)}) collective-permute-start(bf16[256,512]{1,0:T(8,128)(2,1)S(1)} %add.16), channel_id=1, source_target_pairs={{2,6},{6,10},{10,14},{14,12},{12,8},{8,4},{4,0},{0,2},{3,1},{7,3},... | collective-permute-start | bytes 786440 | tf_op jit(solution)/shard_map/ppermute | solution.py:327
  139.6 6.4 %collective-permute-start.29 = (bf16[256,512]{1,0:T(8,128)(2,1)S(1)}, bf16[256,512]{1,0:T(8,128)(2,1)S(1)}, u32[]{:S(2)}, u32[]{:S(2)}) collective-permute-start(bf16[256,512]{1,0:T(8,128)(2,1)S(1)} %add.13), channel_id=1, source_target_pairs={{2,6},{6,10},{10,14},{14,12},{12,8},{8,4},{4,0},{0,2},{3,1},{7,3},... | collective-permute-start | bytes 786440 | tf_op jit(solution)/shard_map/ppermute | solution.py:327
  142.5 4.5 %collective-permute-start.37 = (bf16[256,512]{1,0:T(8,128)(2,1)S(1)}, bf16[256,512]{1,0:T(8,128)(2,1)S(1)}, u32[]{:S(2)}, u32[]{:S(2)}) collective-permute-start(bf16[256,512]{1,0:T(8,128)(2,1)S(1)} %get-tuple-element.104), channel_id=1, source_target_pairs={{0,1},{1,0},{2,3},{3,2},{4,5},{5,4},{6,7},{7,6},{8,9},{9,8},{10,11... | collective-permute-start | bytes 786440 | tf_op jit(solution)/shard_map/ppermute | solution.py:324
  146.9 1.6 %collective-permute-start.33 = (bf16[256,512]{1,0:T(8,128)(2,1)S(1)}, bf16[256,512]{1,0:T(8,128)(2,1)S(1)}, u32[]{:S(2)}, u32[]{:S(2)}) collective-permute-start(bf16[256,512]{1,0:T(8,128)(2,1)S(1)} %get-tuple-element.97), channel_id=1, source_target_pairs={{0,1},{1,0},{2,3},{3,2},{4,5},{5,4},{6,7},{7,6},{8,9},{9,8},{10,11... | collective-permute-start | bytes 786440 | tf_op jit(solution)/shard_map/ppermute | solution.py:324
